TPU v7x, 32 devices: a whole 2x2x4 slice. The times are simulated.
32 devices in a mesh: grp: 4 (over z), fsdp: 8 (over y, x, core).
Axes of the slice: x: 2, y: 2, z: 4, core: 2. Of those that a mesh axis runs over, the one named last changes fastest.
Arguments:
- tokens: bfloat16 [12288, 1024], P(('grp', 'fsdp')), may hold values from -6 to 6
- segment: int32 [12288], P(('grp', 'fsdp')), may hold values from 0 to 12, as said below
- positions: int32 [12288], P(('grp', 'fsdp')), may hold values from 0 to 233, as said below
- parents: int32 [32, 13], P(('grp', 'fsdp')), may hold values from 0 to 4, as said below
- routes: int32 [12288, 8], P(('grp', 'fsdp')), may hold values from 0 to 15, all different within a row; in each aligned block of 384 rows (0 to 383, 384 to 767, ...) at most 240 rows name the same one
- attn_gain: bfloat16 [1024], P('fsdp'), may hold values from 0.25 to 1.75
- query_weight: bfloat16 [1024, 1024], P('fsdp', 'grp'), may hold values from -0.1875 to 0.1875
- key_matrix: bfloat16 [1024, 512], P('fsdp', 'grp'), may hold values from -0.1875 to 0.1875
- value_matrix: bfloat16 [1024, 512], P('fsdp', 'grp'), may hold values from -0.1875 to 0.1875
- out_weight: bfloat16 [1024, 1024], P('fsdp', 'grp'), may hold values from -0.75 to 0.75
- ffn_gain: bfloat16 [1024], P('fsdp'), may hold values from 0.25 to 1.75
- router_weight: bfloat16 [1024, 16], P('fsdp'), may hold values from -0.09375 to 0.09375
- gate_up_weight: bfloat16 [1024, 16, 1024], P('fsdp', 'grp'), may hold values from -0.1875 to 0.1875
- down_weight: bfloat16 [1024, 16, 512], P('fsdp', 'grp'), may hold values from -1 to 1
- cotangent: bfloat16 [12288, 1024], P(('grp', 'fsdp')), may hold values from -6 to 6
Outputs:
- output: bfloat16 [12288, 1024], P(('grp', 'fsdp'))
- input_grad: float32 [12288, 1024], P(('grp', 'fsdp'))
- attn_gain_grad: float32 [1024], P('fsdp')
- query_grad: float32 [1024, 1024], P('fsdp', 'grp')
- key_grad: float32 [1024, 512], P('fsdp', 'grp')
- value_grad: float32 [1024, 512], P('fsdp', 'grp')
- out_weight_grad: float32 [1024, 1024], P('fsdp', 'grp')
- ffn_gain_grad: float32 [1024], P('fsdp')
- router_grad: float32 [1024, 16], P('fsdp')
- gate_up_grad: float32 [1024, 16, 1024], P('fsdp', 'grp')
- down_grad: float32 [1024, 16, 512], P('fsdp', 'grp')
Inputs may be any that keep to these rules, and one draw needn't show every extreme that they name: Within each tree segment ids never fall; segment 0 (the trunk) comes first, then the 4 branches, then the 8 leaves; every segment has tokens; the trunk has 31 * (6) tokens. parents[t, s] is the parent segment of segment s of tree t: 0 for the trunk itself and for the branches, a branch for every leaf. `positions`: A token's position is the number of tokens of its ancestors' segments plus its index within its own segment. `routes`: each row names 8 different experts; among the rows of one tree no expert is named by more than 240 rows.
All inputs are finite; a program needn't handle non-finite values.
Results may differ from a plain program's by a relative error of at most 0.018.
Values may be sent and summed in bfloat16 or wider, within the bound.
No kernel may reach another device: no remote copies, remote signals or barrier semaphores. Data moves between devices by JAX's collectives and lax.ppermute only.
A program may use at most 384 MiB of HBM per device.

v0:
```python
import math

import jax
import jax.numpy as jnp
from jax import lax
from jax.sharding import PartitionSpec as P

MODEL_WIDTH = 1024
QUERY_HEADS = 16
KEY_VALUE_HEADS = 8
HEAD_SIZE = 64
TOP = 8
EXPERTS = 16
TOKENS_PER_TREE = 384
CAP = 240


EPSILON = 1e-06
ROPE_BASE = 10000.0
NEG_FILL = -1e30


def angle_tables(positions, width):
    half_width = width // 2
    frequency = ROPE_BASE ** (-(jnp.arange(half_width, dtype=jnp.float32) * 2.0) / width)
    turned = positions.astype(jnp.float32)[:, None] * frequency[None, :]
    return (jnp.cos(turned)[:, None, :], jnp.sin(turned)[:, None, :])


def apply_rotation(values, cosine_lookup, sine_lookup):
    half_width = values.shape[-1] // 2
    first_half = values[..., :half_width]
    second_half = values[..., half_width:]
    return jnp.concatenate(
        [
            first_half * cosine_lookup - second_half * sine_lookup,
            second_half * cosine_lookup + first_half * sine_lookup,
        ],
        axis=-1,
    )


def unrotate(values, cosine_lookup, sine_lookup):
    half_width = values.shape[-1] // 2
    first_half = values[..., :half_width]
    second_half = values[..., half_width:]
    return jnp.concatenate(
        [
            first_half * cosine_lookup + second_half * sine_lookup,
            second_half * cosine_lookup - first_half * sine_lookup,
        ],
        axis=-1,
    )


def rms_scale(values, gain):
    return values * lax.rsqrt(jnp.mean(values * values, axis=-1, keepdims=True) + EPSILON) * gain


def softmax_last(values):
    return jax.nn.softmax(values, axis=-1)


def swiglu(values):
    half_width = values.shape[-1] // 2
    return jax.nn.silu(values[..., :half_width]) * values[..., half_width:]


def visible(segment, parents):
    seg_ids = jnp.arange(parents.shape[0], dtype=jnp.int32)
    parent_one = jnp.sum(
        jnp.where(segment[:, None] == seg_ids[None, :], parents[None, :], 0), axis=1
    )
    parent_two = jnp.sum(
        jnp.where(parent_one[:, None] == seg_ids[None, :], parents[None, :], 0), axis=1
    )
    key_seg = segment[None, :]
    related = (
        (key_seg == segment[:, None])
        | (key_seg == parent_one[:, None])
        | (key_seg == parent_two[:, None])
    )
    places = jnp.arange(segment.shape[0], dtype=jnp.int32)
    return related & (places[None, :] <= places[:, None])


def slot_table(route_rows, capacity, experts):
    flat_routes = route_rows.reshape(-1)
    one_hot = (flat_routes[:, None] == jnp.arange(experts, dtype=jnp.int32)[None, :]).astype(
        jnp.int32
    )
    earlier = jnp.cumsum(one_hot, axis=0) - one_hot
    slot_ranks = jnp.sum(earlier * one_hot, axis=1)
    slot_ids = flat_routes * capacity + slot_ranks
    entries = flat_routes.shape[0]
    inverse = (
        jnp.full((experts * capacity,), entries, dtype=jnp.int32)
        .at[slot_ids]
        .set(jnp.arange(entries, dtype=jnp.int32))
    )
    return (slot_ids.reshape(route_rows.shape), inverse)


def shards(
    tokens,
    segment,
    positions,
    parents,
    routes,
    attn_gain,
    query_weight,
    key_matrix,
    value_matrix,
    out_weight,
    ffn_gain,
    router_weight,
    gate_up_weight,
    down_weight,
    cotangent,
):

    def gather_attention():
        columns = (
            lax.all_gather(query_weight, "grp", axis=1, tiled=True),
            lax.all_gather(key_matrix, "grp", axis=1, tiled=True),
            lax.all_gather(value_matrix, "grp", axis=1, tiled=True),
            lax.all_gather(out_weight, "grp", axis=1, tiled=True),
        )
        return (
            lax.all_gather(columns[0], "fsdp", axis=0, tiled=True),
            lax.all_gather(columns[1], "fsdp", axis=0, tiled=True),
            lax.all_gather(columns[2], "fsdp", axis=0, tiled=True),
            lax.all_gather(columns[3], "fsdp", axis=0, tiled=True),
            lax.all_gather(attn_gain, "fsdp", axis=0, tiled=True),
        )

    def gather_experts():
        columns = (
            lax.all_gather(gate_up_weight, "grp", axis=1, tiled=True),
            lax.all_gather(down_weight, "grp", axis=1, tiled=True),
        )
        return (
            lax.all_gather(columns[0], "fsdp", axis=0, tiled=True),
            lax.all_gather(columns[1], "fsdp", axis=0, tiled=True),
            lax.all_gather(router_weight, "fsdp", axis=0, tiled=True),
            lax.all_gather(ffn_gain, "fsdp", axis=0, tiled=True),
        )

    scale_factor = 1.0 / math.sqrt(HEAD_SIZE)
    query_group_width = QUERY_HEADS // KEY_VALUE_HEADS
    rows_in = tokens.astype(jnp.float32)
    attn_fwd = gather_attention()
    query_full, key_full, value_full, out_full, gain_one = (
        attn_fwd[0],
        attn_fwd[1],
        attn_fwd[2],
        attn_fwd[3],
        attn_fwd[4],
    )
    normalized_input, norm_one_back = jax.vjp(rms_scale, rows_in, gain_one.astype(jnp.float32))
    normed_low = normalized_input.astype(jnp.bfloat16)
    cosine_lookup, sine_lookup = angle_tables(positions, HEAD_SIZE)
    query_raw = jnp.dot(normed_low, query_full, preferred_element_type=jnp.float32).reshape(
        TOKENS_PER_TREE, QUERY_HEADS, HEAD_SIZE
    )
    key_raw = jnp.dot(normed_low, key_full, preferred_element_type=jnp.float32).reshape(
        TOKENS_PER_TREE, KEY_VALUE_HEADS, HEAD_SIZE
    )
    value_low = (
        jnp.dot(normed_low, value_full, preferred_element_type=jnp.float32)
        .astype(jnp.bfloat16)
        .reshape(TOKENS_PER_TREE, KEY_VALUE_HEADS, HEAD_SIZE)
    )
    query_heads = jnp.moveaxis(
        apply_rotation(query_raw, cosine_lookup, sine_lookup)
        .astype(jnp.bfloat16)
        .reshape(TOKENS_PER_TREE, KEY_VALUE_HEADS, query_group_width, HEAD_SIZE),
        1,
        0,
    )
    key_heads = jnp.moveaxis(
        apply_rotation(key_raw, cosine_lookup, sine_lookup).astype(jnp.bfloat16), 1, 0
    )
    value_heads = jnp.moveaxis(value_low, 1, 0)
    allowed = visible(segment, parents[0])

    def head_scores(query_one, key_one):
        raw_scores = (
            jnp.einsum("qgd,kd->gqk", query_one, key_one, preferred_element_type=jnp.float32)
            * scale_factor
        )
        return jnp.where(allowed[None], raw_scores, NEG_FILL)

    def attend(operands):
        query_one, key_one, value_one = operands
        scores = head_scores(query_one, key_one)
        row_peak = jnp.max(scores, axis=-1, keepdims=True)
        shifted = jnp.exp(scores - row_peak)
        row_total = jnp.sum(shifted, axis=-1, keepdims=True)
        attn_probs = shifted / row_total
        head_out = jnp.einsum(
            "gqk,kd->qgd",
            attn_probs.astype(jnp.bfloat16),
            value_one,
            preferred_element_type=jnp.float32,
        )
        return (head_out, row_peak + jnp.log(row_total))

    head_outs, log_totals = lax.map(attend, (query_heads, key_heads, value_heads))
    attended_low = (
        jnp.moveaxis(head_outs, 0, 1)
        .reshape(TOKENS_PER_TREE, QUERY_HEADS * HEAD_SIZE)
        .astype(jnp.bfloat16)
    )
    mixed_rows = rows_in + jnp.einsum(
        "tk,dk->td", attended_low, out_full, preferred_element_type=jnp.float32
    )
    experts_fwd = gather_experts()
    up_full, down_full, router_full, gain_two = (
        experts_fwd[0],
        experts_fwd[1],
        experts_fwd[2],
        experts_fwd[3],
    )
    normed_two, norm_two_back = jax.vjp(rms_scale, mixed_rows, gain_two.astype(jnp.float32))
    normed_two_low = normed_two.astype(jnp.bfloat16)
    logits = jnp.dot(normed_two_low, router_full, preferred_element_type=jnp.float32)
    route_hits = routes[:, :, None] == jnp.arange(EXPERTS, dtype=jnp.int32)[None, None, :]
    chosen = jnp.sum(jnp.where(route_hits, logits[:, None, :], 0.0), axis=2)
    gates, gate_back = jax.vjp(softmax_last, chosen)
    slot_ids, inverse = slot_table(routes, CAP, EXPERTS)
    owners = inverse // TOP
    padded = jnp.concatenate([normed_two_low, jnp.zeros((1, MODEL_WIDTH), jnp.bfloat16)], axis=0)
    expert_rows = padded[owners].reshape(EXPERTS, CAP, MODEL_WIDTH)
    gate_up = jnp.einsum("ecd,def->ecf", expert_rows, up_full, preferred_element_type=jnp.float32)
    hidden, swiglu_back = jax.vjp(swiglu, gate_up)
    hidden_low = hidden.astype(jnp.bfloat16)
    expert_out = jnp.einsum(
        "ecf,def->ecd", hidden_low, down_full, preferred_element_type=jnp.float32
    ).reshape(EXPERTS * CAP, MODEL_WIDTH)
    picked = expert_out[slot_ids]
    output = (mixed_rows + jnp.sum(gates[:, :, None] * picked, axis=1)).astype(jnp.bfloat16)
    grad_out = cotangent.astype(jnp.float32)
    experts_back = gather_experts()
    up_back, down_back, router_back = (experts_back[0], experts_back[1], experts_back[2])
    grad_gates = jnp.sum(grad_out[:, None, :] * picked, axis=2)
    grad_chosen = gate_back(grad_gates)[0]
    grad_logits = jnp.sum(jnp.where(route_hits, grad_chosen[:, :, None], 0.0), axis=1).astype(
        jnp.bfloat16
    )
    gate_flat = jnp.concatenate([gates.reshape(-1), jnp.zeros((1,), jnp.float32)], axis=0)
    grad_padded = jnp.concatenate([grad_out, jnp.zeros((1, MODEL_WIDTH), jnp.float32)], axis=0)
    slot_grad = (
        (gate_flat[inverse][:, None] * grad_padded[owners])
        .astype(jnp.bfloat16)
        .reshape(EXPERTS, CAP, MODEL_WIDTH)
    )
    down_grad = jnp.einsum(
        "ecd,ecf->def", slot_grad, hidden_low, preferred_element_type=jnp.float32
    )
    grad_hidden = jnp.einsum(
        "ecd,def->ecf", slot_grad, down_back, preferred_element_type=jnp.float32
    )
    grad_gate_up = swiglu_back(grad_hidden)[0].astype(jnp.bfloat16)
    gate_up_grad = jnp.einsum(
        "ecd,ecf->def", expert_rows, grad_gate_up, preferred_element_type=jnp.float32
    )
    grad_expert_rows = jnp.einsum(
        "ecf,def->ecd", grad_gate_up, up_back, preferred_element_type=jnp.float32
    ).reshape(EXPERTS * CAP, MODEL_WIDTH)
    grad_normed_two = jnp.sum(grad_expert_rows[slot_ids], axis=1) + jnp.einsum(
        "te,de->td", grad_logits, router_back, preferred_element_type=jnp.float32
    )
    router_grad = jnp.einsum(
        "td,te->de", normed_two_low, grad_logits, preferred_element_type=jnp.float32
    )
    grad_mixed_norm, gain_two_grad = norm_two_back(grad_normed_two)
    grad_mixed = grad_out + grad_mixed_norm
    moe_sums = (
        lax.psum(router_grad.astype(jnp.bfloat16), "grp").astype(jnp.float32),
        lax.psum(gain_two_grad.astype(jnp.bfloat16), "grp").astype(jnp.float32),
    )
    moe_parts = (
        lax.psum_scatter(gate_up_grad, "fsdp", scatter_dimension=0, tiled=True),
        lax.psum_scatter(down_grad, "fsdp", scatter_dimension=0, tiled=True),
        lax.psum_scatter(moe_sums[0], "fsdp", scatter_dimension=0, tiled=True),
        lax.psum_scatter(moe_sums[1], "fsdp", scatter_dimension=0, tiled=True),
    )
    moe_cols_done = (
        lax.psum_scatter(
            moe_parts[0].astype(jnp.bfloat16), "grp", scatter_dimension=1, tiled=True
        ).astype(jnp.float32),
        lax.psum_scatter(
            moe_parts[1].astype(jnp.bfloat16), "grp", scatter_dimension=1, tiled=True
        ).astype(jnp.float32),
    )
    gate_up_out, down_out, router_out, gain_two_out = (
        moe_cols_done[0],
        moe_cols_done[1],
        moe_parts[2],
        moe_parts[3],
    )
    attn_back = gather_attention()
    query_back, key_back, value_back, out_back = (
        attn_back[0],
        attn_back[1],
        attn_back[2],
        attn_back[3],
    )
    grad_branch = grad_mixed.astype(jnp.bfloat16)
    out_weight_grad = jnp.einsum(
        "td,tk->dk", grad_branch, attended_low, preferred_element_type=jnp.float32
    )
    attended_gradient = jnp.einsum(
        "td,dk->tk", grad_branch, out_back, preferred_element_type=jnp.float32
    ).astype(jnp.bfloat16)
    heads_gradient = jnp.moveaxis(
        attended_gradient.reshape(TOKENS_PER_TREE, KEY_VALUE_HEADS, query_group_width, HEAD_SIZE),
        1,
        0,
    )

    def attend_back(operands):
        query_one, key_one, value_one, grad_one, log_one = operands
        scores = head_scores(query_one, key_one)
        attn_probs = jnp.exp(scores - log_one)
        grad_probs = jnp.einsum(
            "qgd,kd->gqk", grad_one, value_one, preferred_element_type=jnp.float32
        )
        row_inner = jnp.sum(attn_probs * grad_probs, axis=-1, keepdims=True)
        grad_scores = (attn_probs * (grad_probs - row_inner)).astype(jnp.bfloat16)
        grad_query = (
            jnp.einsum("gqk,kd->qgd", grad_scores, key_one, preferred_element_type=jnp.float32)
            * scale_factor
        )
        grad_key = (
            jnp.einsum("gqk,qgd->kd", grad_scores, query_one, preferred_element_type=jnp.float32)
            * scale_factor
        )
        grad_value = jnp.einsum(
            "gqk,qgd->kd",
            attn_probs.astype(jnp.bfloat16),
            grad_one,
            preferred_element_type=jnp.float32,
        )
        return (grad_query, grad_key, grad_value)

    query_heads_grad, key_heads_grad, value_heads_gradient = lax.map(
        attend_back, (query_heads, key_heads, value_heads, heads_gradient, log_totals)
    )
    grad_query = (
        unrotate(
            jnp.moveaxis(query_heads_grad, 0, 1).reshape(TOKENS_PER_TREE, QUERY_HEADS, HEAD_SIZE),
            cosine_lookup,
            sine_lookup,
        )
        .reshape(TOKENS_PER_TREE, QUERY_HEADS * HEAD_SIZE)
        .astype(jnp.bfloat16)
    )
    grad_key = (
        unrotate(jnp.moveaxis(key_heads_grad, 0, 1), cosine_lookup, sine_lookup)
        .reshape(TOKENS_PER_TREE, KEY_VALUE_HEADS * HEAD_SIZE)
        .astype(jnp.bfloat16)
    )
    grad_value = (
        jnp.moveaxis(value_heads_gradient, 0, 1)
        .reshape(TOKENS_PER_TREE, KEY_VALUE_HEADS * HEAD_SIZE)
        .astype(jnp.bfloat16)
    )
    query_grad = jnp.einsum("td,tk->dk", normed_low, grad_query, preferred_element_type=jnp.float32)
    key_grad = jnp.einsum("td,tk->dk", normed_low, grad_key, preferred_element_type=jnp.float32)
    value_grad = jnp.einsum("td,tk->dk", normed_low, grad_value, preferred_element_type=jnp.float32)
    grad_normed = jnp.einsum(
        "tk,dk->td", grad_query, query_back, preferred_element_type=jnp.float32
    )
    grad_normed = grad_normed + jnp.einsum(
        "tk,dk->td", grad_key, key_back, preferred_element_type=jnp.float32
    )
    grad_normed = grad_normed + jnp.einsum(
        "tk,dk->td", grad_value, value_back, preferred_element_type=jnp.float32
    )
    grad_rows_norm, gain_one_grad = norm_one_back(grad_normed)
    input_grad = grad_mixed + grad_rows_norm
    gain_one_sum = lax.psum(gain_one_grad, "grp")
    attn_parts = (
        lax.psum_scatter(query_grad, "fsdp", scatter_dimension=0, tiled=True),
        lax.psum_scatter(key_grad, "fsdp", scatter_dimension=0, tiled=True),
        lax.psum_scatter(value_grad, "fsdp", scatter_dimension=0, tiled=True),
        lax.psum_scatter(out_weight_grad, "fsdp", scatter_dimension=0, tiled=True),
        lax.psum_scatter(gain_one_sum, "fsdp", scatter_dimension=0, tiled=True),
    )
    attn_cols_done = (
        lax.psum_scatter(
            attn_parts[0].astype(jnp.bfloat16), "grp", scatter_dimension=1, tiled=True
        ).astype(jnp.float32),
        lax.psum_scatter(
            attn_parts[1].astype(jnp.bfloat16), "grp", scatter_dimension=1, tiled=True
        ).astype(jnp.float32),
        lax.psum_scatter(
            attn_parts[2].astype(jnp.bfloat16), "grp", scatter_dimension=1, tiled=True
        ).astype(jnp.float32),
        lax.psum_scatter(
            attn_parts[3].astype(jnp.bfloat16), "grp", scatter_dimension=1, tiled=True
        ).astype(jnp.float32),
    )
    query_out, key_out, value_out, out_weight_out, gain_one_out = (
        attn_cols_done[0],
        attn_cols_done[1],
        attn_cols_done[2],
        attn_cols_done[3],
        attn_parts[4],
    )
    return (
        output,
        input_grad,
        gain_one_out,
        query_out,
        key_out,
        value_out,
        out_weight_out,
        gain_two_out,
        router_out,
        gate_up_out,
        down_out,
    )


def solution(mesh):
    in_specs = (
        P(("grp", "fsdp"), None),
        P(("grp", "fsdp")),
        P(("grp", "fsdp")),
        P(("grp", "fsdp"), None),
        P(("grp", "fsdp"), None),
        P("fsdp"),
        P("fsdp", "grp"),
        P("fsdp", "grp"),
        P("fsdp", "grp"),
        P("fsdp", "grp"),
        P("fsdp"),
        P("fsdp", None),
        P("fsdp", "grp", None),
        P("fsdp", "grp", None),
        P(("grp", "fsdp"), None),
    )
    out_specs = (
        P(("grp", "fsdp"), None),
        P(("grp", "fsdp"), None),
        P("fsdp"),
        P("fsdp", "grp"),
        P("fsdp", "grp"),
        P("fsdp", "grp"),
        P("fsdp", "grp"),
        P("fsdp"),
        P("fsdp", None),
        P("fsdp", "grp", None),
        P("fsdp", "grp", None),
    )
    return jax.shard_map(shards, mesh=mesh, in_specs=in_specs, out_specs=out_specs, check_vma=False)
```

profile of v0, /device:TPU:0, one launch (start us, length us, event | category | flops | bytes accessed | tf_op | source)
XLA Modules:
  0.0 1753.6 jit_solution(12199491386744080068)
XLA Ops:
  43.1 18.2 %all_gather.63 = bf16[128,1024]{1,0:T(8,128)(2,1)} all-gather(bf16[128,256]{1,0:T(8,128)(2,1)S(1)} %copy-done.48), channel_id=1, replica_groups=mesh['grp'=4,'fsdp'=8] {'grp'}, dimensions={1}, use_global_device_ids=true | all-gather | bytes 327680 | tf_op jit(solution)/shard_map/all_gather | solution.py:124
  61.4 18.4 %all_gather.65 = bf16[128,1024]{1,0:T(8,128)(2,1)} all-gather(bf16[128,256]{1,0:T(8,128)(2,1)S(1)} %copy-done.49), channel_id=1, replica_groups=mesh['grp'=4,'fsdp'=8] {'grp'}, dimensions={1}, use_global_device_ids=true | all-gather | bytes 327680 | tf_op jit(solution)/shard_map/all_gather | solution.py:127
  79.8 24.0 %all-gather.19.cloned.1.call-done = bf16[128,16,1024]{2,0,1:T(8,128)(2,1)} async-done(((bf16[128,4,1024]{2,0,1:T(8,128)(2,1)}), bf16[128,16,1024]{2,0,1:T(8,128)(2,1)}) %all-gather.19.cloned.1.call-update) | async-done | bytes 4194320 | tf_op jit(solution)/shard_map/all_gather | solution.py:139
  104.0 46.9 %all-gather.23.cloned.1.call-done = bf16[128,16,512]{2,0,1:T(8,128)(2,1)} async-done(((bf16[128,4,512]{2,0,1:T(8,128)(2,1)}), bf16[128,16,512]{2,0,1:T(8,128)(2,1)}) %all-gather.23.cloned.1.call-update) | async-done | bytes 2097168 | tf_op jit(solution)/shard_map/all_gather | solution.py:140
  278.5 20.2 %gather_fusion.2 = f32[3840]{0:T(1024)S(1)} fusion(f32[3073]{0:T(1024)S(1)} %pad_maximum_fusion.2, s32[4096]{0:T(1024)S(1)} %get-tuple-element.294), kind=kCustom, calls=%fused_computation.2 | custom fusion | bytes 46080 | tf_op jit(solution)/shard_map/gather | solution.py:254
  299.3 123.0 %all-gather.21.cloned.1.call-done = bf16[1024,16,1024]{2,0,1:T(8,128)(2,1)} async-done(((bf16[128,16,1024]{2,0,1:T(8,128)(2,1)}), bf16[1024,16,1024]{2,0,1:T(8,128)(2,1)}) %all-gather.21.cloned.1.call-update) | async-done | bytes 33554448 | tf_op jit(solution)/shard_map/all_gather | solution.py:143
  422.4 24.6 %fusion.98 = f32[16,240,1024]{2,1,0:T(8,128)} fusion(bf16[16,240,1024]{2,1,0:T(8,128)(2,1)} %bitcast.255, bf16[1024,16,1024]{2,0,1:T(8,128)(2,1)} %all-gather.21.cloned.1.call-done), kind=kOutput, calls=%fused_computation.188 | convolution fusion | flops 8053063680 | bytes 57147392 | tf_op jit(solution)/shard_map/ecd,def->ecf/dot_general | solution.py:235
  447.0 67.2 %all-gather.25.cloned.1.call-done = bf16[1024,16,512]{2,0,1:T(8,128)(2,1)} async-done(((bf16[128,16,512]{2,0,1:T(8,128)(2,1)}), bf16[1024,16,512]{2,0,1:T(8,128)(2,1)}) %all-gather.25.cloned.1.call-update) | async-done | bytes 16777232 | tf_op jit(solution)/shard_map/all_gather | solution.py:144
  514.2 27.6 %fusion.65 = (f32[16,240,512]{2,1,0:T(8,128)}, f32[16,240,512]{2,1,0:T(8,128)}, bf16[16,240,512]{2,1,0:T(8,128)(2,1)}) fusion(f32[16,240,1024]{2,1,0:T(8,128)} %fusion.98, bf16[1024,16,512]{2,0,1:T(8,128)(2,1)} %all-gather.25.cloned.1.call-done, f32[16,240,1024]{2,1,0:T(8,128)} %bitcast.253, f32[16,240]{1,0:T(8,128)S(1)} %mul.404), kind=kOutput, calls=%fused_computation.111 | convolution fusion | flops 4061921280 | bytes 67910656 | tf_op jit(solution)/shard_map/ecd,def->ecf/dot_general | solution.py:261
  541.7 22.5 %fusion.64 = f32[16,240,1024]{2,1,0:T(8,128)} fusion(bf16[1024,16,1024]{2,0,1:T(8,128)(2,1)} %all-gather.21.cloned.1.call-done, f32[16,240,512]{2,1,0:T(8,128)} %get-tuple-element.272, f32[16,240,512]{2,1,0:T(8,128)} %get-tuple-element.271), kind=kOutput, calls=%fused_computation.109 | convolution fusion | flops 8060928000 | bytes 65011712 | tf_op jit(solution)/shard_map/ecf,def->ecd/dot_general | solution.py:268
  564.2 22.6 %gather_fusion.4 = f32[3072,1024]{1,0:T(8,128)} fusion(f32[3840,1024]{1,0:T(8,128)} %bitcast.252, s32[3072]{0:T(1024)S(1)} %broadcast_clamp_fusion), kind=kCustom, calls=%fused_computation.4 | custom fusion | bytes 25178112 | tf_op jit(solution)/shard_map/gather | solution.py:271
  606.9 22.6 %gather_fusion.1 = f32[3072,1024]{1,0:T(8,128)} fusion(f32[3840,1024]{1,0:T(8,128)} %bitcast.251, s32[3072]{0:T(1024)S(1)} %broadcast_clamp_fusion), kind=kCustom, calls=%fused_computation.1 | custom fusion | bytes 25178112 | tf_op jit(solution)/shard_map/gather | solution.py:241
  648.7 60.5 %while.31 = (s32[]{:T(128)}, f32[8,384,2,64]{1,3,2,0:T(8,128)}, f32[8,384,64]{1,2,0:T(8,128)}, bf16[8,384,64]{1,2,0:T(8,128)(2,1)S(1)}, bf16[8,384,64]{1,2,0:T(8...) while((s32[]{:T(128)}, f32[8,384,2,64]{1,3,2,0:T(8,128)}, ...), condition=%wide.region_23.24_spmd.clone.clone, body=%wide.region_21.23_spmd.clone.sunk.clone | while | flops 192503040 | bytes 10101377 | solution.py:348
  725.7 17.5 convolution_bitcast_fusion.5
  743.3 33.0 %convolution_bitcast_fusion.4 = f32[1024,16,1024]{0,2,1:T(8,128)} fusion(bf16[16,240,1024]{2,1,0:T(8,128)(2,1)} %bitcast.256, f32[16,240,512]{2,1,0:T(8,128)} %get-tuple-element.272, f32[16,240,512]{2,1,0:T(8,128)} %get-tuple-element.271), kind=kOutput, calls=%fused_computation.69 | convolution fusion | flops 8060928000 | bytes 90701824 | tf_op jit(solution)/shard_map/ecd,ecf->def/dot_general | solution.py:265
  778.2 20.9 %reduce-scatter.24.cloned.1.call-done = f32[128,512]{1,0:T(8,128)} async-done(((f32[1024,512]{1,0:T(8,128)}), f32[128,512]{1,0:T(8,128)}) %reduce-scatter.24.cloned.1.call-update) | async-done | bytes 262160 | tf_op jit(solution)/shard_map/reduce_scatter | solution.py:388
  800.9 52.9 %reduce-scatter.18.cloned.1.call-done = f32[128,1024]{1,0:T(8,128)} async-done(((f32[1024,1024]{1,0:T(8,128)}), f32[128,1024]{1,0:T(8,128)}) %reduce-scatter.18.cloned.1.call-update) | async-done | bytes 524304 | tf_op jit(solution)/shard_map/reduce_scatter | solution.py:386
  855.7 53.1 %reduce-scatter.26.cloned.1.call-done = f32[128,1024]{1,0:T(8,128)} async-done(((f32[1024,1024]{1,0:T(8,128)}), f32[128,1024]{1,0:T(8,128)}) %reduce-scatter.26.cloned.1.call-update) | async-done | bytes 524304 | tf_op jit(solution)/shard_map/reduce_scatter | solution.py:389
  910.7 206.9 %reduce-scatter.36.cloned.1.call-done = f32[128,16,512]{0,2,1:T(8,128)} async-done(((f32[1024,16,512]{0,2,1:T(8,128)}), f32[128,16,512]{0,2,1:T(8,128)}) %reduce-scatter.36.cloned.1.call-update) | async-done | bytes 4194320 | tf_op jit(solution)/shard_map/reduce_scatter | solution.py:285
  1121.6 383.6 %reduce-scatter.32.cloned.1.call-done = f32[128,16,1024]{0,2,1:T(8,128)} async-done(((f32[1024,16,1024]{0,2,1:T(8,128)}), f32[128,16,1024]{0,2,1:T(8,128)}) %reduce-scatter.32.cloned.1.call-update) | async-done | bytes 8388624 | tf_op jit(solution)/shard_map/reduce_scatter | solution.py:284
  1514.2 20.6 %all-reduce.7 = (bf16[1024]{0:T(1024)(128)(2,1)S(1)}, bf16[1024,16]{0,1:T(8,128)(2,1)}) all-reduce(bf16[1024]{0:T(1024)(128)(2,1)} %get-tuple-element.217, bf16[1024,16]{0,1:T(8,128)(2,1)} %convolution_convert_fusion.2), channel_id=1, replica_groups=mesh['grp'=4,'fsdp'=8] {'grp'}, use_global_device_ids=true, to_apply=%region_37.38 | all-reduce | flops 17408 | bytes 69632 | tf_op jit(solution)/shard_map/psum | solution.py:281
  1588.9 43.5 %reduce-scatter.38.cloned.1.call-done = bf16[128,4,512]{0,2,1:T(8,128)(2,1)} async-done(((bf16[128,16,512]{0,2,1:T(8,128)(2,1)}), bf16[128,4,512]{0,2,1:T(8,128)(2,1)}) %reduce-scatter.38.cloned.1.call-update) | async-done | bytes 524304 | tf_op jit(solution)/shard_map/reduce_scatter | solution.py:293
  1634.8 76.0 %reduce-scatter.34.cloned.1.call-done = bf16[128,4,1024]{0,2,1:T(8,128)(2,1)} async-done(((bf16[128,16,1024]{0,2,1:T(8,128)(2,1)}), bf16[128,4,1024]{0,2,1:T(8,128)(2,1)}) %reduce-scatter.34.cloned.1.call-update) | async-done | bytes 1048592 | tf_op jit(solution)/shard_map/reduce_scatter | solution.py:290
  1713.5 32.8 %reduce-scatter.30.cloned.1.call-done = f32[128,16]{0,1:T(8,128)} async-done(((f32[1024,16]{0,1:T(8,128)}), f32[128,16]{0,1:T(8,128)}) %reduce-scatter.30.cloned.1.call-update) | async-done | bytes 8208 | tf_op jit(solution)/shard_map/reduce_scatter | solution.py:286
  (407 shorter events, 371.5 us)
Async XLA Ops:
  7.2 96.7 %all-gather.19.cloned.1.call-start = ((), (), s32[]{:S(2)}) async-start(), calls=%async_computation.17 | async-start | bytes 5242880 | tf_op jit(solution)/shard_map/all_gather | solution.py:139
  9.8 141.1 %all-gather.23.cloned.1.call-start = ((), (), s32[]{:S(2)}) async-start(), calls=%async_computation.19 | async-start | bytes 2621440 | tf_op jit(solution)/shard_map/all_gather | solution.py:140
  10.8 199.0 %all-gather.11.cloned.1.call-start = ((), (), s32[]{:S(2)}) async-start(), calls=%async_computation.13 | async-start | bytes 1179648 | tf_op jit(solution)/shard_map/all_gather | solution.py:132
  25.5 186.6 %all-gather.13.cloned.1.call-start = ((), (), s32[]{:S(2)}) async-start(), calls=%async_computation.14 | async-start | bytes 1179648 | tf_op jit(solution)/shard_map/all_gather | solution.py:131
  43.0 186.9 %all-gather.15.cloned.1.call-start = ((), (), s32[]{:S(2)}) async-start(), calls=%async_computation.15 | async-start | bytes 2359296 | tf_op jit(solution)/shard_map/all_gather | solution.py:130
  61.3 198.3 %all-gather.17.cloned.1.call-start = ((), (), s32[]{:S(2)}) async-start(), calls=%async_computation.16 | async-start | bytes 2359296 | tf_op jit(solution)/shard_map/all_gather | solution.py:133
  79.8 342.6 %all-gather.21.cloned.1.call-start = ((), (), s32[]{:S(2)}) async-start(), calls=%async_computation.18 | async-start | bytes 37748736 | tf_op jit(solution)/shard_map/all_gather | solution.py:143
  104.0 410.2 %all-gather.25.cloned.1.call-start = ((), (), s32[]{:S(2)}) async-start(), calls=%async_computation.20 | async-start | bytes 18874368 | tf_op jit(solution)/shard_map/all_gather | solution.py:144
  150.9 625.5 %reduce-scatter.22.cloned.1.call-start = ((), (), s32[]{:S(2)}) async-start(), calls=%async_computation.23 | async-start | bytes 2359296 | tf_op jit(solution)/shard_map/reduce_scatter | solution.py:387
  160.2 69.8 %copy-start.32 = (f32[8,1,128]{2,1,0:T(1,128)}, f32[8,1,128]{2,1,0:T(1,128)S(1)}, u32[]{:S(2)}) copy-start(f32[8,1,128]{2,1,0:T(1,128)S(1)} %convert_element_type.180) | copy-start | bytes 12292
  168.9 93.6 %copy-start.46 = (f32[8,1,128]{2,1,0:T(1,128)}, f32[8,1,128]{2,1,0:T(1,128)S(1)}, u32[]{:S(2)}) copy-start(f32[8,1,128]{2,1,0:T(1,128)S(1)} %convert_element_type.181) | copy-start | bytes 12292
  298.7 215.5 %copy-start.37 = (f32[16,240]{1,0:T(8,128)}, f32[16,240]{1,0:T(8,128)S(1)}, u32[]{:S(2)}) copy-start(f32[16,240]{1,0:T(8,128)S(1)} %mul.404) | copy-start | bytes 46084
  713.0 86.2 %reduce-scatter.24.cloned.1.call-start = ((), (), s32[]{:S(2)}) async-start(), calls=%async_computation.24 | async-start | bytes 2359296 | tf_op jit(solution)/shard_map/reduce_scatter | solution.py:388
  715.3 138.5 %reduce-scatter.18.cloned.1.call-start = ((), (), s32[]{:S(2)}) async-start(), calls=%async_computation.21 | async-start | bytes 4718592 | tf_op jit(solution)/shard_map/reduce_scatter | solution.py:386
  720.5 188.3 %reduce-scatter.26.cloned.1.call-start = ((), (), s32[]{:S(2)}) async-start(), calls=%async_computation.25 | async-start | bytes 4718592 | tf_op jit(solution)/shard_map/reduce_scatter | solution.py:389
  725.0 392.6 %reduce-scatter.36.cloned.1.call-start = ((), (), s32[]{:S(2)}) async-start(), calls=%async_computation.30 | async-start | bytes 37748736 | tf_op jit(solution)/shard_map/reduce_scatter | solution.py:285
  743.2 762.0 %reduce-scatter.32.cloned.1.call-start = ((), (), s32[]{:S(2)}) async-start(), calls=%async_computation.28 | async-start | bytes 75497472 | tf_op jit(solution)/shard_map/reduce_scatter | solution.py:284
  776.3 789.9 %reduce-scatter.40.cloned.1.call-start = ((), (), s32[]{:S(2)}) async-start(), calls=%async_computation.32 | async-start | bytes 163840
  778.2 789.5 %reduce-scatter.42.cloned.1.call-start = ((), (), s32[]{:S(2)}) async-start(), calls=%async_computation.33 | async-start | bytes 163840
  800.9 768.3 %reduce-scatter.20.cloned.1.call-start = ((), (), s32[]{:S(2)}) async-start(), calls=%async_computation.22 | async-start | bytes 327680 | tf_op jit(solution)/shard_map/reduce_scatter | solution.py:393
  855.7 731.8 %reduce-scatter.28.cloned.1.call-start = ((), (), s32[]{:S(2)}) async-start(), calls=%async_computation.26 | async-start | bytes 327680 | tf_op jit(solution)/shard_map/reduce_scatter | solution.py:402
  910.6 721.8 %reduce-scatter.38.cloned.1.call-start = ((), (), s32[]{:S(2)}) async-start(), calls=%async_computation.31 | async-start | bytes 2621440 | tf_op jit(solution)/shard_map/reduce_scatter | solution.py:293
  1121.5 589.3 %reduce-scatter.34.cloned.1.call-start = ((), (), s32[]{:S(2)}) async-start(), calls=%async_computation.29 | async-start | bytes 5242880 | tf_op jit(solution)/shard_map/reduce_scatter | solution.py:290
  1511.3 235.0 %reduce-scatter.30.cloned.1.call-start = ((), (), s32[]{:S(2)}) async-start(), calls=%async_computation.27 | async-start | bytes 73728 | tf_op jit(solution)/shard_map/reduce_scatter | solution.py:286
  (65 other events, 918.9 us)
Sparse Core Ops, SparseCore 0:
  10.2 93.6 all-gather.18
  106.0 44.8 all-gather.22
  152.8 22.2 all-gather.10
  176.8 23.4 all-gather.12
  202.0 27.8 all-gather.14
  231.7 27.8 all-gather.16
  261.5 160.7 all-gather.20
  424.3 89.8 all-gather.24
  713.1 41.2 reduce-scatter.21
  757.8 41.2 reduce-scatter.23
  802.5 51.3 reduce-scatter.17
  857.4 51.3 reduce-scatter.25
  912.4 205.2 reduce-scatter.35
  1121.5 383.7 reduce-scatter.31
  1507.9 19.3 reduce-scatter.39
  1530.0 17.2 reduce-scatter.41
  1549.4 17.9 reduce-scatter.19
  1569.6 17.7 reduce-scatter.27
  1590.3 42.1 reduce-scatter.37
  1634.7 76.0 reduce-scatter.33
  1714.4 31.8 reduce-scatter.29
where the time goes:
time: 1760 us; the launch traced here: 1750 us
  waiting for transfers between devices  1180 us (67%)
  matrix products  226 us (13%)
  blocking collectives  135 us (8%)
  local copies, waits for them, and re-layouts  131 us (7%)
  other arithmetic  66.8 us (4%)
    reduce_scatter x1, waiting for transfers between devices, shards(): lax.psum_scatter(gate_up_grad, 'fsdp', scatter_dimension=0, tiled=True)  384 us
    reduce_scatter x1, waiting for transfers between devices, shards(): lax.psum_scatter(down_grad, 'fsdp', scatter_dimension=0, tiled=True)  207 us
    all_gather x1, waiting for transfers between devices, gather_experts(): lax.all_gather(columns[0], 'fsdp', axis=0, tiled=True)  123 us
    reduce_scatter x1, waiting for transfers between devices, shards(): lax.psum_scatter(moe_parts[0].astype(jnp.bfloat16), 'grp', scatter_dimens...  76 us
    all_gather x1, waiting for transfers between devices, gather_experts(): lax.all_gather(columns[1], 'fsdp', axis=0, tiled=True)  67.2 us
    reduce_scatter x1, waiting for transfers between devices, shards(): lax.psum_scatter(out_weight_grad, 'fsdp', scatter_dimension=0, tiled=True)  53.1 us
    reduce_scatter x1, waiting for transfers between devices, shards(): lax.psum_scatter(query_grad, 'fsdp', scatter_dimension=0, tiled=True)  52.9 us
    all_gather x1, waiting for transfers between devices, gather_experts(): lax.all_gather(down_weight, 'grp', axis=1, tiled=True)  46.9 us
  transfers between devices with their start and end apart: 21, of which 15 were waited for; matrix products, arithmetic and copies ran while one was open for 12% of the time, Pallas kernels for 0%

commit v1 on v0

v1 whole, which is shorter than its diff:
```python
import math

import jax
import jax.numpy as jnp
from jax import lax
from jax.experimental import pallas as pl
from jax.experimental.pallas import tpu as pltpu
from jax.sharding import PartitionSpec as P

MODEL_WIDTH = 1024
HEAD_SIZE = 64
FF = 512
HALF = FF // 2
EXPERTS = 16
T = 384
LANES = 128
EPSILON = 1e-06
ROPE_BASE = 10000.0
NEG_FILL = -1e30
SCALE = 1.0 / math.sqrt(HEAD_SIZE)
BF = jnp.bfloat16
F32 = jnp.float32

NT = (((1,), (1,)), ((), ()))
TN = (((0,), (0,)), ((), ()))

VM = pl.BlockSpec(memory_space=pltpu.VMEM)
SM = pl.BlockSpec(memory_space=pltpu.SMEM)
ANY = pl.BlockSpec(memory_space=pl.ANY)


def dot(a, b):
    return jnp.dot(a, b, preferred_element_type=F32)


def dotg(a, b, dims, **kw):
    return lax.dot_general(a, b, dims, preferred_element_type=F32, **kw)


def call(body, outs, in_specs, out_specs, scratch, args, name, vmem=48, flops=0):
    nbytes = sum(math.prod(a.shape) * a.dtype.itemsize for a in args)
    nbytes += sum(math.prod(s) * jnp.dtype(d).itemsize for s, d in outs)
    return pl.pallas_call(
        body,
        out_shape=[jax.ShapeDtypeStruct(s, d) for s, d in outs],
        in_specs=in_specs,
        out_specs=out_specs,
        scratch_shapes=scratch,
        compiler_params=pltpu.CompilerParams(vmem_limit_bytes=vmem << 20),
        cost_estimate=pl.CostEstimate(
            flops=int(flops), transcendentals=0, bytes_accessed=int(nbytes)
        ),
        name=name,
    )(*args)


def low_half(shape):
    return lax.broadcasted_iota(jnp.int32, shape, 1) < HEAD_SIZE


def turn(part, cos, sin, first):
    partner = jnp.where(first, pltpu.roll(part, 96, 1), pltpu.roll(part, 32, 1))
    return part * cos + partner * sin


def first_of_head(shape):
    return (lax.broadcasted_iota(jnp.int32, shape, 1) % HEAD_SIZE) < HEAD_SIZE // 2


def attn_fwd(x_ref, gain_ref, w_ref, cos_ref, sin_ref, bias_ref, n1_ref, qkv_ref, att_ref):
    x = x_ref[...].astype(F32)
    r1 = lax.rsqrt(jnp.mean(x * x, axis=1, keepdims=True) + EPSILON)
    n1 = (x * r1 * gain_ref[...]).astype(BF)
    n1_ref[...] = n1
    cos = cos_ref[...]
    sin = sin_ref[...]
    first = first_of_head((T, LANES))
    for b in range(4):
        raw = dot(n1, w_ref[:, b * 512 : (b + 1) * 512])
        for s in range(4):
            part = raw[:, s * LANES : (s + 1) * LANES]
            if s < 3:
                part = turn(part, cos, sin, first)
            qkv_ref[b, :, s * LANES : (s + 1) * LANES] = part.astype(BF)
    low = low_half((LANES, LANES))

    def block(b, carry):
        for c in range(3):
            rows = slice(c * LANES, (c + 1) * LANES)
            seen = (c + 1) * LANES
            keys = qkv_ref[b, :seen, 256:384]
            vals = qkv_ref[b, :seen, 384:512]
            bias = bias_ref[rows, :seen]
            for tile in range(2):
                cols = slice(tile * LANES, (tile + 1) * LANES)
                q = qkv_ref[b, rows, cols]
                parts = []
                for half in range(2):
                    qm = jnp.where(low if half == 0 else ~low, q, jnp.zeros_like(q))
                    s = dotg(qm, keys, NT) * SCALE + bias
                    p = jnp.exp(s - jnp.max(s, axis=1, keepdims=True))
                    p = p * (1.0 / jnp.sum(p, axis=1, keepdims=True))
                    parts.append(dot(p.astype(BF), vals))
                att_ref[b, rows, cols] = jnp.where(low, parts[0], parts[1]).astype(BF)
        return carry

    lax.fori_loop(0, 4, block, 0)


def soft_gates(n2, rt, mask):
    logits = dotg(n2, rt, NT)
    top = jnp.max(jnp.where(mask > 0, logits, NEG_FILL), axis=1, keepdims=True)
    e = jnp.where(mask > 0, jnp.exp(jnp.minimum(logits - top, 0.0)), 0.0)
    return e / jnp.sum(e, axis=1, keepdims=True)


def mid(x_ref, att_ref, wo_ref, gain_ref, rt_ref, mask_ref, h1_ref, n2_ref, gates_ref):
    att = jnp.concatenate([att_ref[b] for b in range(4)], axis=1)
    h1 = x_ref[...].astype(F32) + dotg(att, wo_ref[...], NT)
    h1_ref[...] = h1
    r2 = lax.rsqrt(jnp.mean(h1 * h1, axis=1, keepdims=True) + EPSILON)
    n2 = (h1 * r2 * gain_ref[...]).astype(BF)
    n2_ref[...] = n2
    gates_ref[...] = soft_gates(n2, rt_ref[...], mask_ref[...].astype(F32))


def gate_rest(nx_ref, ny_ref, na_ref, nb_ref, rt_ref, mx_ref, my_ref, md_ref, out_ref):
    rt = rt_ref[...]
    out_ref[0:T] = soft_gates(nx_ref[...], rt, mx_ref[...].astype(F32))
    out_ref[T : 2 * T] = soft_gates(ny_ref[...], rt, my_ref[...].astype(F32))
    nd = jnp.concatenate([na_ref[...], nb_ref[...]], axis=0)
    out_ref[2 * T : 3 * T] = soft_gates(nd, rt, md_ref[...].astype(F32))


ROWS = 4 * T


def expert(e_ref, x0, xx, xy, xa, xb, y0, yx, yy, ya, yb, g0, gr, w0, w1,
           gh_o, dgu_o, dw0_o, dw1_o, dgate_o,
           X, Y, G, W, GH, DGU, DW, si, so):
    half = T // 2
    srcs = [
        (w0, W.at[0]), (w1, W.at[1]),
        (x0, X.at[0:T]), (y0, Y.at[0:T]), (g0, G.at[0:T]), (gr, G.at[T:ROWS]),
        (xx, X.at[T : 2 * T]), (yx, Y.at[T : 2 * T]),
        (xy, X.at[2 * T : 3 * T]), (yy, Y.at[2 * T : 3 * T]),
        (xa, X.at[3 * T : 3 * T + half]), (xb, X.at[3 * T + half : ROWS]),
        (ya, Y.at[3 * T : 3 * T + half]), (yb, Y.at[3 * T + half : ROWS]),
    ]
    copies = [pltpu.make_async_copy(s, d, si.at[i]) for i, (s, d) in enumerate(srcs)]
    for c in copies:
        c.start()
    need = [(0, 1, 2, 3, 4, 5), (6, 7), (8, 9), (10, 11, 12, 13)]
    e = e_ref[0]

    def tree(t, carry):
        for k in range(4):
            @pl.when(t == k)
            def _():
                for i in need[k]:
                    copies[i].wait()
        rows = pl.ds(pl.multiple_of(t * T, T), T)
        xt = X[rows, :]
        yt = Y[rows, :]
        lanes = lax.broadcasted_iota(jnp.int32, (T, LANES), 1)
        gate = jnp.sum(jnp.where(lanes == e, G[rows, :], 0.0), axis=1, keepdims=True)
        dgate = jnp.zeros((T, 1), F32)
        for u in range(2):
            gu = dot(xt, W[u, :, 0 : 2 * HALF])
            dh = dot(yt, W[u, :, 2 * HALF : 3 * HALF])
            g = gu[:, :HALF]
            up = gu[:, HALF:]
            s = 1.0 / (1.0 + jnp.exp(-g))
            silu = g * s
            hid = silu * up
            GH[rows, u * HALF : (u + 1) * HALF] = (gate * hid).astype(BF)
            dgate = dgate + jnp.sum(dh * hid, axis=1, keepdims=True)
            dh = dh * gate
            base = u * 2 * HALF
            DGU[rows, base : base + HALF] = (dh * up * (s * (1.0 + g * (1.0 - s)))).astype(BF)
            DGU[rows, base + HALF : base + 2 * HALF] = (dh * silu).astype(BF)
        dgate_o[rows, :] = jnp.where(lanes == e, dgate, 0.0)
        return carry

    lax.fori_loop(0, 4, tree, 0)
    outs = [pltpu.make_async_copy(GH, gh_o, so.at[0]), pltpu.make_async_copy(DGU, dgu_o, so.at[1])]
    outs[0].start()
    outs[1].start()
    for u in range(2):
        DW[u, :, 0 : 2 * HALF] = dotg(X[...], DGU[:, u * 2 * HALF : (u + 1) * 2 * HALF], TN).astype(BF)
        DW[u, :, 2 * HALF : 3 * HALF] = dotg(Y[...], GH[:, u * HALF : (u + 1) * HALF], TN).astype(BF)
        o = pltpu.make_async_copy(DW.at[u], (dw1_o if u else dw0_o), so.at[2 + u])
        o.start()
        outs.append(o)
    for o in outs:
        o.wait()


def run_expert(e, xs, ys, gs, w0, w1):
    args = (e, *xs, *ys, *gs, w0, w1)
    rows = MODEL_WIDTH
    return call(
        expert,
        [((ROWS, FF), BF), ((ROWS, 2 * FF), BF), ((rows, 3 * HALF), BF), ((rows, 3 * HALF), BF),
         ((ROWS, LANES), F32)],
        [SM] + [ANY] * 14,
        [ANY] * 4 + [VM],
        [
            pltpu.VMEM((ROWS, MODEL_WIDTH), BF), pltpu.VMEM((ROWS, MODEL_WIDTH), BF),
            pltpu.VMEM((ROWS, LANES), F32), pltpu.VMEM((2, rows, 3 * HALF), BF),
            pltpu.VMEM((ROWS, FF), BF), pltpu.VMEM((ROWS, 2 * FF), BF),
            pltpu.VMEM((2, rows, 3 * HALF), BF),
            pltpu.SemaphoreType.DMA((14,)), pltpu.SemaphoreType.DMA((4,)),
        ],
        args, "expert", 56, 2 * ROWS * rows * 3 * FF * 2,
    )


def back_body(lo, m, width, first_col, splits, n):
    def body(*refs):
        acts = refs[0:4]
        ws = refs[4:12]
        outs = refs[12 : 12 + n]
        A, W, sem = refs[12 + n :]
        copies = []
        for k in range(4):
            for u in range(2):
                i = 2 * k + u
                a = acts[k].at[lo : lo + m, u * width : (u + 1) * width]
                w = ws[i].at[:, first_col : first_col + width]
                h, j = i // 4, i % 4
                copies.append((
                    pltpu.make_async_copy(a, A.at[h, :, j * width : (j + 1) * width], sem.at[0, i]),
                    pltpu.make_async_copy(w, W.at[h, :, j * width : (j + 1) * width], sem.at[1, i]),
                ))
        for a, w in copies:
            a.start()
            w.start()
        for a, w in copies[:4]:
            a.wait()
            w.wait()
        total = dotg(A[0], W[0], NT)
        for a, w in copies[4:]:
            a.wait()
            w.wait()
        total = total + dotg(A[1], W[1], NT)
        for o, (r0, r1) in zip(outs, splits):
            o[...] = total[r0:r1].astype(o.dtype)
    return body


def run_back(acts, ws, lo, m, width, first_col, splits, dtypes, name):
    return call(
        back_body(lo, m, width, first_col, splits, len(splits)),
        [((r1 - r0, MODEL_WIDTH), d) for (r0, r1), d in zip(splits, dtypes)],
        [ANY] * 12,
        [VM] * len(splits),
        [
            pltpu.VMEM((2, m, 4 * width), BF), pltpu.VMEM((2, MODEL_WIDTH, 4 * width), BF),
            pltpu.SemaphoreType.DMA((2, 8)),
        ],
        (*acts, *ws), name, 48, 2 * m * MODEL_WIDTH * 8 * width,
    )


def columns_of(rowwise, lane):
    ones = jnp.ones((T, LANES), F32)
    total = dotg(rowwise, ones, TN, precision=lax.Precision.HIGHEST)
    lanes = lax.broadcasted_iota(jnp.int32, total.shape, 1)
    return jnp.where(lanes == lane, total, 0.0)


def join(p_ref, rx_ref, ry_ref, g0_ref, gx_ref, gy_ref, gd_ref, gates_ref, h1_ref, n2_ref,
         gain_ref, rt_ref, dy_ref, wo_ref, att_ref, dh1_ref, datt_ref, dwo_ref):
    gates = gates_ref[...]
    dg = g0_ref[...] + gx_ref[...] + gy_ref[...] + gd_ref[...]
    dl = (gates * (dg - jnp.sum(gates * dg, axis=1, keepdims=True))).astype(BF)
    dn2 = p_ref[...] + rx_ref[...].astype(F32) + ry_ref[...].astype(F32) + dot(dl, rt_ref[...])
    h1 = h1_ref[...]
    gain = gain_ref[...]
    r2 = lax.rsqrt(jnp.mean(h1 * h1, axis=1, keepdims=True) + EPSILON)
    gd = gain * dn2
    inner = jnp.mean(gd * h1, axis=1, keepdims=True)
    dh1 = dy_ref[...].astype(F32) + r2 * gd - h1 * (r2 * r2 * r2 * inner)
    dh1_ref[...] = dh1
    db = dh1.astype(BF)
    for b in range(4):
        cols = slice(b * 256, (b + 1) * 256)
        datt_ref[b] = dot(db, wo_ref[:, cols]).astype(BF)
        dwo_ref[:, cols] = dotg(db, att_ref[b], TN).astype(BF)
    extra = dotg(n2_ref[...], dl, TN) + columns_of(dn2 * h1 * r2, EXPERTS)
    dwo_ref[:, 1024:1152] = extra.astype(BF)


def attn_bwd(x_ref, gain_ref, w_ref, cos_ref, sin_ref, bias_ref, n1_ref, qkv_ref, datt_ref, dh1_ref,
             dx_ref, dw_ref, dqkv, dk, dv):
    low = low_half((LANES, LANES))
    first = first_of_head((T, LANES))

    def block(b, carry):
        dk[...] = jnp.zeros_like(dk)
        dv[...] = jnp.zeros_like(dv)
        for c in range(3):
            rows = slice(c * LANES, (c + 1) * LANES)
            seen = (c + 1) * LANES
            keys = qkv_ref[b, :seen, 256:384]
            vals = qkv_ref[b, :seen, 384:512]
            bias = bias_ref[rows, :seen]
            cos = cos_ref[rows, :]
            sin = sin_ref[rows, :]
            for tile in range(2):
                cols = slice(tile * LANES, (tile + 1) * LANES)
                q = qkv_ref[b, rows, cols]
                do = datt_ref[b, rows, cols]
                dq = []
                for half in range(2):
                    keep = low if half == 0 else ~low
                    qm = jnp.where(keep, q, jnp.zeros_like(q))
                    dm = jnp.where(keep, do, jnp.zeros_like(do))
                    s = dotg(qm, keys, NT) * SCALE + bias
                    p = jnp.exp(s - jnp.max(s, axis=1, keepdims=True))
                    p = p * (1.0 / jnp.sum(p, axis=1, keepdims=True))
                    dp = dotg(dm, vals, NT)
                    ds = (p * (dp - jnp.sum(p * dp, axis=1, keepdims=True))).astype(BF)
                    dq.append(dot(ds, keys))
                    dk[:seen] += dotg(ds, qm, TN)
                    dv[:seen] += dotg(p.astype(BF), dm, TN)
                dqt = jnp.where(low, dq[0], dq[1]) * SCALE
                dqkv[b, rows, cols] = turn(dqt, cos, -sin, first[rows]).astype(BF)
        dqkv[b, :, 256:384] = turn(dk[...] * SCALE, cos_ref[...], -sin_ref[...], first).astype(BF)
        dqkv[b, :, 384:512] = dv[...].astype(BF)
        return carry

    lax.fori_loop(0, 4, block, 0)
    n1 = n1_ref[...]
    dn1 = jnp.zeros((T, MODEL_WIDTH), F32)
    for b in range(4):
        cols = slice(b * 512, (b + 1) * 512)
        dw_ref[:, cols] = dotg(n1, dqkv[b], TN).astype(BF)
        dn1 = dn1 + dotg(dqkv[b], w_ref[:, cols], NT)
    x = x_ref[...].astype(F32)
    gain = gain_ref[...]
    r1 = lax.rsqrt(jnp.mean(x * x, axis=1, keepdims=True) + EPSILON)
    gd = gain * dn1
    inner = jnp.mean(gd * x, axis=1, keepdims=True)
    dx_ref[...] = dh1_ref[...] + r1 * gd - x * (r1 * r1 * r1 * inner)
    dw_ref[:, 2048:2176] = columns_of(dn1 * x * r1, 0).astype(BF)


def visible_bias(segment, parents):
    ids = jnp.arange(parents.shape[0], dtype=jnp.int32)
    one = jnp.sum(jnp.where(segment[:, None] == ids[None, :], parents[None, :], 0), axis=1)
    two = jnp.sum(jnp.where(one[:, None] == ids[None, :], parents[None, :], 0), axis=1)
    key = segment[None, :]
    related = (key == segment[:, None]) | (key == one[:, None]) | (key == two[:, None])
    places = jnp.arange(segment.shape[0], dtype=jnp.int32)
    return jnp.where(related & (places[None, :] <= places[:, None]), 0.0, NEG_FILL).astype(F32)


def turn_tables(positions):
    half = HEAD_SIZE // 2
    lane = jnp.arange(LANES, dtype=jnp.int32)
    frequency = ROPE_BASE ** (-((lane % half).astype(F32) * 2.0) / HEAD_SIZE)
    angle = positions.astype(F32)[:, None] * frequency[None, :]
    sign = jnp.where(lane % HEAD_SIZE < half, -1.0, 1.0).astype(F32)
    return jnp.cos(angle), jnp.sin(angle) * sign[None, :]


def make_shards(groups, fsdp):
    ring = list(range(0, groups, 1))
    if groups == 4:
        ring = [0, 1, 3, 2]
    place = [ring.index(g) for g in range(groups)]
    rest = fsdp // 8

    def shifted(k):
        return [(ring[p], ring[(p + k) % groups]) for p in range(groups)]

    def flip(bits):
        return [(i, i ^ bits) for i in range(fsdp)]

    low_groups = None if rest == 1 else [[8 * r + j for j in range(8)] for r in range(rest)]
    rest_groups = [[8 * r + j for r in range(rest)] for j in range(8)]

    def z_next(a):
        return lax.ppermute(a, "grp", shifted(1))

    def to_x(a):
        return lax.ppermute(a, "fsdp", flip(2))

    def to_y(a):
        return lax.ppermute(a, "fsdp", flip(4))

    def to_diag(a):
        return lax.ppermute(a, "fsdp", flip(6))

    def to_core(a):
        return lax.ppermute(a, "fsdp", flip(1))

    def plane(a):
        half = a.shape[0] // 2
        ax = to_x(a)
        ay = to_y(a)
        return (a, ax, ay, to_x(ay[:half]), to_y(ax[half:]))

    def z_sum(blocks):
        total = blocks[0].astype(F32)
        for k in range(1, groups):
            total = total + lax.ppermute(blocks[k], "grp", shifted(groups - k)).astype(F32)
        return total

    def shards(tokens, segment, positions, parents, routes, attn_gain, query_weight, key_matrix,
               value_matrix, out_weight, ffn_gain, router_weight, gate_up_weight, down_weight, cotangent):
        dr = query_weight.shape[0]
        mine = lax.axis_index("fsdp")
        spot = jnp.array(place, jnp.int32)[lax.axis_index("grp")]
        ring_ids = jnp.array(ring, jnp.int32)

        def swapped(w):
            return [w[:, 0:64], w[:, 128:192], w[:, 64:128], w[:, 192:256]]

        own_qkv = jnp.concatenate(swapped(query_weight) + [key_matrix, value_matrix], axis=1)
        own_out = jnp.concatenate(swapped(out_weight), axis=1)

        def z_gather(a):
            got = [a]
            for _ in range(groups - 1):
                got.append(z_next(got[-1]))
            return got

        w_qkv = lax.all_gather(jnp.concatenate(z_gather(own_qkv), axis=1), "fsdp", axis=0, tiled=True)
        w_out = lax.all_gather(jnp.concatenate(z_gather(own_out), axis=1), "fsdp", axis=0, tiled=True)
        small = jnp.concatenate([router_weight.T, attn_gain[None], ffn_gain[None]], axis=0)
        small = lax.all_gather(small, "fsdp", axis=1, tiled=True)
        router_t = jnp.concatenate([small[:16], jnp.zeros((LANES - 16, MODEL_WIDTH), BF)], axis=0)
        gain_one = small[16:17].astype(F32)
        gain_two = small[17:18].astype(F32)

        gu = gate_up_weight.reshape(dr, 4, 2, 2, HALF)
        dn = down_weight.reshape(dr, 4, 1, 2, HALF)
        parts = jnp.concatenate([gu, dn], axis=2)
        parts = jnp.transpose(parts, (1, 3, 0, 2, 4)).reshape(8, dr, 3 * HALF)
        unit = lax.all_to_all(parts, "fsdp", 0, 0, axis_index_groups=low_groups)
        unit = unit.reshape(8 * dr, 3 * HALF)
        if rest > 1:
            unit = lax.all_gather(unit, "fsdp", axis=0, tiled=True, axis_index_groups=rest_groups)
        units = z_gather(unit)
        pairs = [(u, to_core(u)) for u in units]

        bias = visible_bias(segment, parents[0])
        cos, sin = turn_tables(positions)
        lanes = jnp.arange(LANES, dtype=jnp.int32)
        mask = jnp.sum((routes[:, :, None] == lanes[None, None, :]).astype(F32), axis=1).astype(BF)
        mask_rest = (to_x(mask), to_y(mask), to_diag(mask))
        dys = plane(cotangent)

        n1, qkv, att = call(
            attn_fwd,
            [((T, MODEL_WIDTH), BF), ((4, T, 512), BF), ((4, T, 256), BF)],
            [VM] * 6, [VM] * 3, [],
            (tokens, gain_one, w_qkv, cos, sin, bias), "attn_fwd", 48, 3.0e9,
        )
        h1, n2, gates = call(
            mid,
            [((T, MODEL_WIDTH), F32), ((T, MODEL_WIDTH), BF), ((T, LANES), F32)],
            [VM] * 6, [VM] * 3, [],
            (tokens, att, w_out, gain_two, router_t, mask), "mid", 48, 1.0e9,
        )
        xs = plane(n2)
        gates_rest, = call(
            gate_rest, [((3 * T, LANES), F32)], [VM] * 8, [VM], [],
            (*xs[1:], router_t, *mask_rest), "gate_rest", 48, 0.4e9,
        )

        chip = (mine // 2) % 4
        order = list(range(1, groups)) + [0]
        done = {}
        ring_acc = None
        for k in order:
            e = (4 * ring_ids[(spot - k) % groups] + chip).astype(jnp.int32).reshape(1)
            gh, dgu, dw_own, dw_sib, dgate = run_expert(e, xs, dys, (gates, gates_rest), *pairs[k])
            got = to_core(dw_sib)
            grad = dw_own.astype(F32) + got.astype(F32)
            if ring_acc is not None:
                grad = grad + z_next(ring_acc).astype(F32)
            ring_acc = grad.astype(BF)
            done[k] = (gh, dgu, dgate)
        ghs = [done[k][0] for k in range(groups)]
        dgus = [done[k][1] for k in range(groups)]
        dgate = sum(done[k][2] for k in range(groups))
        ws = [w for pair in pairs for w in pair]
        half = T // 2
        whole = ((0, T),)
        split = ((0, half), (half, T))

        def spread(acts, width, first_col, name):
            da, db = run_back(acts, ws, 3 * T, T, width, first_col, split, (BF, BF), name + "_d")
            ra = to_x(da)
            rb = to_y(db)
            xa, xb, ya, yb = run_back(
                acts, ws, T, 2 * T, width, first_col,
                ((0, half), (half, T), (T, T + half), (T + half, 2 * T)), (BF,) * 4, name + "_xy",
            )
            own, = run_back(acts, ws, 0, T, width, first_col, whole, (F32,), name + "_o")
            xb = (xb.astype(F32) + rb.astype(F32)).astype(BF)
            ya = (ya.astype(F32) + ra.astype(F32)).astype(BF)
            rx = jnp.concatenate([to_x(xa), to_x(xb)], axis=0)
            ry = jnp.concatenate([to_y(ya), to_y(yb)], axis=0)
            return own, rx, ry

        gate_parts = (
            dgate[:T], to_x(dgate[T : 2 * T]), to_y(dgate[2 * T : 3 * T]), to_diag(dgate[3 * T :]),
        )
        p_n2, rx_n2, ry_n2 = spread(dgus, 2 * HALF, 0, "dn2")
        dh1, datt, dwo = call(
            join,
            [((T, MODEL_WIDTH), F32), ((4, T, 256), BF), ((MODEL_WIDTH, 1152), BF)],
            [VM] * 15, [VM] * 3, [],
            (p_n2, rx_n2, ry_n2, *gate_parts, gates, h1, n2, gain_two, router_t, cotangent, w_out, att),
            "join", 48, 2.0e9,
        )
        dx, dwqkv = call(
            attn_bwd,
            [((T, MODEL_WIDTH), F32), ((MODEL_WIDTH, 2176), BF)],
            [VM] * 10, [VM] * 2,
            [pltpu.VMEM((4, T, 512), BF), pltpu.VMEM((T, LANES), F32), pltpu.VMEM((T, LANES), F32)],
            (tokens, gain_one, w_qkv, cos, sin, bias, n1, qkv, datt, dh1), "attn_bwd", 48, 6.0e9,
        )

        p_out, rx_out, ry_out = spread(ghs, HALF, 2 * HALF, "out")
        output = (h1 + p_out + rx_out.astype(F32) + ry_out.astype(F32)).astype(BF)

        if rest > 1:
            ring_acc = lax.psum_scatter(
                ring_acc, "fsdp", scatter_dimension=0, tiled=True, axis_index_groups=rest_groups
            )
        back = lax.all_to_all(ring_acc.reshape(8, dr, 3 * HALF), "fsdp", 0, 0, axis_index_groups=low_groups)
        back = back.astype(F32).reshape(4, 2, dr, 3, HALF)
        back = jnp.transpose(back, (2, 0, 3, 1, 4))
        gate_up_grad = back[:, :, :2].reshape(dr, 4, 2 * FF)
        down_grad = back[:, :, 2].reshape(dr, 4, FF)

        rs_out = lax.psum_scatter(dwo, "fsdp", scatter_dimension=0, tiled=True)
        rs_qkv = lax.psum_scatter(dwqkv, "fsdp", scatter_dimension=0, tiled=True)
        z_out = z_sum([
            jnp.concatenate([rs_out[:, k * 256 : (k + 1) * 256], rs_out[:, 1024:]], axis=1)
            for k in range(groups)
        ])
        z_qkv = z_sum([
            jnp.concatenate([rs_qkv[:, k * 512 : (k + 1) * 512], rs_qkv[:, 2048:]], axis=1)
            for k in range(groups)
        ])
        return (
            output,
            dx,
            z_qkv[:, 512],
            jnp.concatenate(swapped(z_qkv[:, :256]), axis=1),
            z_qkv[:, 256:384],
            z_qkv[:, 384:512],
            jnp.concatenate(swapped(z_out[:, :256]), axis=1),
            z_out[:, 256 + EXPERTS],
            z_out[:, 256 : 256 + EXPERTS],
            gate_up_grad,
            down_grad,
        )

    return shards


def solution(mesh):
    both = ("grp", "fsdp")
    in_specs = (
        P(both, None), P(both), P(both), P(both, None), P(both, None),
        P("fsdp"), P("fsdp", "grp"), P("fsdp", "grp"), P("fsdp", "grp"), P("fsdp", "grp"),
        P("fsdp"), P("fsdp", None), P("fsdp", "grp", None), P("fsdp", "grp", None), P(both, None),
    )
    out_specs = (
        P(both, None), P(both, None), P("fsdp"),
        P("fsdp", "grp"), P("fsdp", "grp"), P("fsdp", "grp"), P("fsdp", "grp"),
        P("fsdp"), P("fsdp", None), P("fsdp", "grp", None), P("fsdp", "grp", None),
    )
    shards = make_shards(mesh.shape["grp"], mesh.shape["fsdp"])
    return jax.shard_map(shards, mesh=mesh, in_specs=in_specs, out_specs=out_specs, check_vma=False)
```

time: 1760 us -> 556 us (0.32)
  waiting for transfers between devices: 1180 us -> 191 us
  matrix products: 226 us -> 0 us
  Pallas kernels: 0 us -> 173 us
  blocking collectives: 135 us -> 8.34 us
  local copies, waits for them, and re-layouts: 131 us -> 59.4 us
  starting transfers between devices: 0.87 us -> 68 us
  other arithmetic: 66.8 us -> 23.1 us
    reduce_scatter x11 -> x2, waiting for transfers between devices: 886 us -> 0.04 us  [the longest x1 0.02 us: shards(): rs_qkv = lax.psum_scatter(dwqkv, 'fsdp', scatter_dimension=0, tiled=True)]
    all_gather x8 -> x2, waiting for transfers between devices: 289 us -> 0.01 us  [the longest x1 0.01 us: shards(): lax.all_gather(jnp.concatenate(z_gather(own_qkv), axis=1), 'fsdp', axis=0...]
    dot_general x77 -> x0, matrix products: 226 us -> none  [the longest x1 33 us: shards(): jnp.einsum('ecd,ecf->def', expert_rows, grad_gate_up, preferred_element_t...]
    ppermute x0 -> x52, waiting for transfers between devices: none -> 176 us  [the longest x12 93.1 us: z_next(): return lax.ppermute(a, 'grp', shifted(1))]
    pallas_call x0 -> x15, Pallas kernels: none -> 173 us  [call(): pl.pallas_call(body, out_shape=[jax.ShapeDtypeStruct(s, d) for s, d in ou...]
    gather x5 -> x0, local copies, waits for them, and re-layouts: 90.9 us -> none  [the longest x1 22.6 us: shards(): picked = expert_out[slot_ids]]
    all_gather x7 -> x1, blocking collectives: 94 us -> 8.34 us  [shards(): small = lax.all_gather(small, 'fsdp', axis=1, tiled=True)]
    ppermute x0 -> x52, starting transfers between devices: none -> 60.6 us  [the longest x12 18.2 us: z_next(): return lax.ppermute(a, 'grp', shifted(1))]
  transfers between devices with their start and end apart: 21 -> 58, of which waited for: 15 -> 23; matrix products, arithmetic and copies ran while one was open for 12% -> 7% of each run, Pallas kernels for 0% -> 27%
where the time goes in v1:
time: 556 us; the launch traced here: 545 us
  waiting for transfers between devices  191 us (34%)
  Pallas kernels  173 us (31%)
  starting transfers between devices  68 us (12%)
  local copies, waits for them, and re-layouts  59.4 us (11%)
  other arithmetic  23.1 us (4%)
  between operations  21.7 us (4%)
  blocking collectives  8.34 us (2%)
    pallas_call x15, Pallas kernels, call(): pl.pallas_call(body, out_shape=[jax.ShapeDtypeStruct(s, d) for s, d in ou...  173 us
    ppermute x12, waiting for transfers between devices, z_next(): return lax.ppermute(a, 'grp', shifted(1))  93.1 us
    unnamed x156, local copies, waits for them, and re-layouts  40.7 us
    ppermute x6, waiting for transfers between devices, z_sum(): lax.ppermute(blocks[k], 'grp', shifted(groups - k)).astype(F32)  35.6 us
    ppermute x12, waiting for transfers between devices, to_y(): return lax.ppermute(a, 'fsdp', flip(4))  29.1 us
    ppermute x12, starting transfers between devices, z_next(): return lax.ppermute(a, 'grp', shifted(1))  18.2 us
    ppermute x12, starting transfers between devices, to_x(): return lax.ppermute(a, 'fsdp', flip(2))  17 us
    ppermute x12, waiting for transfers between devices, to_x(): return lax.ppermute(a, 'fsdp', flip(2))  16.1 us
  transfers between devices with their start and end apart: 58, of which 23 were waited for; matrix products, arithmetic and copies ran while one was open for 7% of the time, Pallas kernels for 27%

profile of v1, /device:TPU:0, one launch (start us, length us, event | category | flops | bytes accessed | tf_op | source)
XLA Modules:
  0.0 544.9 jit_solution(16655390374660415187)
XLA Ops:
  17.5 5.0 collective-permute-done.1
  49.4 15.0 %all-to-all-done = bf16[8,128,768]{1,2,0:T(8,128)(2,1)S(1)} async-done(((bf16[8,128,768]{1,2,0:T(8,128)(2,1)}), bf16[8,128,768]{1,2,0:T(8,128)(2,1)S(1)}, u32[]{:S(2)}, u32[]{:S(2)}) %all-to-all-start) | async-done | bytes 1572896 | tf_op jit(solution)/shard_map/all_to_all | solution.py:443
  67.4 8.3 %all_gather.9 = bf16[18,1024]{1,0:T(8,128)(2,1)S(1)} all-gather(bf16[18,128]{1,0:T(8,128)(2,1)S(1)} %pad_maximum_fusion.11), channel_id=1, replica_groups=mesh['grp'=4,'fsdp'=8] {'fsdp'}, dimensions={1}, use_global_device_ids=true | all-gather | bytes 41472 | tf_op jit(solution)/shard_map/all_gather | solution.py:434
  80.8 18.9 %collective-permute-done.18.w0.refs_6_ = bf16[1024,768]{1,0:T(8,128)(2,1)S(1)} collective-permute-done((bf16[1024,768]{1,0:T(8,128)(2,1)S(1)}, bf16[1024,768]{1,0:T(8,128)(2,1)S(1)}, u32[]{:S(2)}, u32[]{:S(2)}) %collective-permute-start.18) | collective-permute-done | bytes 1572896 | tf_op jit(solution)/shard_map/ppermute | solution.py:386
  108.5 18.6 %attn_fwd.1 = (bf16[384,1024]{1,0:T(8,128)(2,1)S(1)}, bf16[4,384,512]{2,1,0:T(8,128)(2,1)S(1)}, bf16[4,384,256]{2,1,0:T(8,128)(2,1)S(1)}) custom-call(bf16[384,1024]{1,0:T(8,128)(2,1)S(1)} %copy-done.23, f32[1,1024]{1,0:T(1,128)S(1)} %get-tuple-element.170.gain_ref, bf16[1024,2048]{1,0:T(8,128)(2,1)} %all-gather.3.cloned.1.call-done.w_ref, ...), custom_call_target="tpu_custom_call" | custom-call | flops 3000000000 | bytes 9113600 | tf_op jit(solution)/shard_map/attn_fwd/pallas_call | solution.py:43
  145.1 11.6 %collective-permute-done.15.my_ref = bf16[384,128]{1,0:T(8,128)(2,1)S(1)} collective-permute-done((bf16[384,128]{1,0:T(8,128)(2,1)S(1)}, bf16[384,128]{1,0:T(8,128)(2,1)S(1)}, u32[]{:S(2)}, u32[]{:S(2)}) %collective-permute-start.15) | collective-permute-done | bytes 98336 | tf_op jit(solution)/shard_map/ppermute | solution.py:392
  165.5 9.4 %collective-permute-done.11.yy = bf16[384,1024]{1,0:T(8,128)(2,1)S(1)} collective-permute-done((bf16[384,1024]{1,0:T(8,128)(2,1)S(1)}, bf16[384,1024]{1,0:T(8,128)(2,1)S(1)}, u32[]{:S(2)}, u32[]{:S(2)}) %collective-permute-start.11) | collective-permute-done | bytes 786464 | tf_op jit(solution)/shard_map/ppermute | solution.py:392
  176.7 7.1 %collective-permute-done.10.yx = bf16[384,1024]{1,0:T(8,128)(2,1)S(1)} collective-permute-done((bf16[384,1024]{1,0:T(8,128)(2,1)S(1)}, bf16[384,1024]{1,0:T(8,128)(2,1)S(1)}, u32[]{:S(2)}, u32[]{:S(2)}) %collective-permute-start.10) | collective-permute-done | bytes 786464 | tf_op jit(solution)/shard_map/ppermute | solution.py:389
  184.6 7.3 %collective-permute-done.8.na_ref.xa = bf16[192,1024]{1,0:T(8,128)(2,1)S(1)} collective-permute-done((bf16[192,1024]{1,0:T(8,128)(2,1)S(1)}, bf16[192,1024]{1,0:T(8,128)(2,1)S(1)}, u32[]{:S(2)}, u32[]{:S(2)}) %collective-permute-start.8) | collective-permute-done | bytes 393248 | tf_op jit(solution)/shard_map/ppermute | solution.py:389
  213.9 16.2 %expert.5 = (bf16[1536,512]{1,0:T(8,128)(2,1)}, bf16[1536,1024]{1,0:T(8,128)(2,1)}, bf16[1024,768]{1,0:T(8,128)(2,1)}, bf16[1024,768]{1,0:T(8,128)(2,1)}, f32[1536,128]{1,0:T(8,128)}) custom-call(s32[1]{0:T(128)} %bitcast.13.e_ref, bf16[384,1024]{1,0:T(8,128)(2,1)} %copy-done.21, bf16[384,1024]{1,0:T(8,128)(2,1)} %copy-done.17, ...), custom_call_target="tpu_custom_call" | custom-call | flops 9663676416 | bytes 18874372 | tf_op jit(solution)/shard_map/expert/pallas_call | solution.py:43
  230.1 16.2 %expert.6 = (bf16[1536,512]{1,0:T(8,128)(2,1)}, bf16[1536,1024]{1,0:T(8,128)(2,1)}, bf16[1024,768]{1,0:T(8,128)(2,1)}, bf16[1024,768]{1,0:T(8,128)(2,1)}, f32[1536,128]{1,0:T(8,128)}) custom-call(s32[1]{0:T(128)} %bitcast.15.e_ref, bf16[384,1024]{1,0:T(8,128)(2,1)} %copy-done.21, bf16[384,1024]{1,0:T(8,128)(2,1)} %copy-done.17, ...), custom_call_target="tpu_custom_call" | custom-call | flops 9663676416 | bytes 18874372 | tf_op jit(solution)/shard_map/expert/pallas_call | solution.py:43
  247.5 16.2 %expert.7 = (bf16[1536,512]{1,0:T(8,128)(2,1)}, bf16[1536,1024]{1,0:T(8,128)(2,1)}, bf16[1024,768]{1,0:T(8,128)(2,1)}, bf16[1024,768]{1,0:T(8,128)(2,1)}, f32[1536,128]{1,0:T(8,128)}) custom-call(s32[1]{0:T(128)} %bitcast.17.e_ref, bf16[384,1024]{1,0:T(8,128)(2,1)} %copy-done.21, bf16[384,1024]{1,0:T(8,128)(2,1)} %copy-done.17, ...), custom_call_target="tpu_custom_call" | custom-call | flops 9663676416 | bytes 18874372 | tf_op jit(solution)/shard_map/expert/pallas_call | solution.py:43
  264.8 16.4 %expert.4 = (bf16[1536,512]{1,0:T(8,128)(2,1)}, bf16[1536,1024]{1,0:T(8,128)(2,1)}, bf16[1024,768]{1,0:T(8,128)(2,1)}, bf16[1024,768]{1,0:T(8,128)(2,1)}, f32[1536,128]{1,0:T(8,128)}) custom-call(s32[1]{0:T(128)} %bitcast.6.e_ref, bf16[384,1024]{1,0:T(8,128)(2,1)} %copy-done.21, bf16[384,1024]{1,0:T(8,128)(2,1)} %copy-done.17, bf16[384,1024]{1,0:T(8,128)(2,1)} %copy-done.15, ...), custom_call_target="tpu_custom_call" | custom-call | flops 9663676416 | bytes 18874372 | tf_op jit(solution)/shard_map/expert/pallas_call | solution.py:43
  284.3 7.3 %dn2_d.1 = (bf16[192,1024]{1,0:T(8,128)(2,1)S(1)}, bf16[192,1024]{1,0:T(8,128)(2,1)S(1)}) custom-call(bf16[1536,1024]{1,0:T(8,128)(2,1)} %get-tuple-element.70.refs_0_, bf16[1536,1024]{1,0:T(8,128)(2,1)} %get-tuple-element.71.refs_1_, bf16[1536,1024]{1,0:T(8,128)(2,1)} %get-tuple-element.72.refs_2_, bf16[1536,1024]{1,0:T(8,128)(2,1)} %get-tuple-element.73.refs_3_, ...), custom_call_target="tpu_custom_call" | custom-call | flops 3221225472 | bytes 25952256 | tf_op jit(solution)/shard_map/dn2_d/pallas_call | solution.py:43
  292.6 11.5 %dn2_xy.1 = (bf16[192,1024]{1,0:T(8,128)(2,1)S(1)}, bf16[192,1024]{1,0:T(8,128)(2,1)S(1)}, bf16[192,1024]{1,0:T(8,128)(2,1)S(1)}, bf16[192,1024]{1,0:T(8,128)(2,1)S(1)}) custom-call(bf16[1536,1024]{1,0:T(8,128)(2,1)} %get-tuple-element.70.refs_0_, bf16[1536,1024]{1,0:T(8,128)(2,1)} %get-tuple-element.71.refs_1_, ...), custom_call_target="tpu_custom_call" | custom-call | flops 6442450944 | bytes 26738688 | tf_op jit(solution)/shard_map/dn2_xy/pallas_call | solution.py:43
  308.6 7.8 %dn2_o.1.p_ref = f32[384,1024]{1,0:T(8,128)S(1)} custom-call(bf16[1536,1024]{1,0:T(8,128)(2,1)} %get-tuple-element.70.refs_0_, bf16[1536,1024]{1,0:T(8,128)(2,1)} %get-tuple-element.71.refs_1_, bf16[1536,1024]{1,0:T(8,128)(2,1)} %get-tuple-element.72.refs_2_, bf16[1536,1024]{1,0:T(8,128)(2,1)} %get-tuple-element.73.refs_3_, bf16[1024,768]{1,0:T(8,128)(2,1)S(1)} %bitcast.34, ...), custom_call_target="tpu_custom_call" | custom-call | flops 3221225472 | bytes 26738688 | tf_op jit(solution)/shard_map/dn2_o/pallas_call | solution.py:43
  318.3 6.4 %collective-permute-done.34 = bf16[192,1024]{1,0:T(8,128)(2,1)S(1)} collective-permute-done((bf16[192,1024]{1,0:T(8,128)(2,1)S(1)}, bf16[192,1024]{1,0:T(8,128)(2,1)S(1)}, u32[]{:S(2)}, u32[]{:S(2)}) %collective-permute-start.34) | collective-permute-done | bytes 393248 | tf_op jit(solution)/shard_map/ppermute | solution.py:392
  331.3 8.7 %join.1 = (f32[384,1024]{1,0:T(8,128)}, bf16[4,384,256]{2,1,0:T(8,128)(2,1)S(1)}, bf16[1024,1152]{1,0:T(8,128)(2,1)}) custom-call(f32[384,1024]{1,0:T(8,128)} %copy-done.9, bf16[384,1024]{1,0:T(8,128)(2,1)S(1)} %pad_maximum_fusion.rx_ref, bf16[384,1024]{1,0:T(8,128)(2,1)S(1)} %pad_maximum_fusion.1.ry_ref, f32[384,128]{1,0:T(8,128)S(1)} %get-tuple-element.144.g0_ref, ...), custom_call_target="tpu_custom_call" | custom-call | flops 2000000000 | bytes 15142912 | tf_op jit(solution)/shard_map/join/pallas_call | solution.py:43
  344.0 34.5 %attn_bwd.1 = (f32[384,1024]{1,0:T(8,128)}, bf16[1024,2176]{1,0:T(8,128)(2,1)}) custom-call(bf16[384,1024]{1,0:T(8,128)(2,1)S(1)} %copy-done.25, f32[1,1024]{1,0:T(1,128)S(1)} %get-tuple-element.170.gain_ref, bf16[1024,2048]{1,0:T(8,128)(2,1)} %all-gather.3.cloned.1.call-done.w_ref, f32[384,128]{1,0:T(8,128)S(1)} %copy-done.36, f32[384,128]{1,0:T(8,128)S(1)} %copy-done.34, ...), custom_call_target="tpu_custom_call" | custom-call | flops 6000000000 | bytes 16715776 | tf_op jit(solution)/shard_map/attn_bwd/pallas_call | solution.py:43
  382.2 36.2 %collective-permute-done.49 = bf16[1024,768]{1,0:T(8,128)(2,1)S(1)} collective-permute-done((bf16[1024,768]{1,0:T(8,128)(2,1)S(1)}, bf16[1024,768]{1,0:T(8,128)(2,1)S(1)}, u32[]{:S(2)}, u32[]{:S(2)}) %collective-permute-start.49) | collective-permute-done | bytes 1572896 | tf_op jit(solution)/shard_map/ppermute | solution.py:386
  429.0 6.4 %out_xy.1 = (bf16[192,1024]{1,0:T(8,128)(2,1)S(1)}, bf16[192,1024]{1,0:T(8,128)(2,1)S(1)}, bf16[192,1024]{1,0:T(8,128)(2,1)S(1)}, bf16[192,1024]{1,0:T(8,128)(2,1)S(1)}) custom-call(bf16[1536,512]{1,0:T(8,128)(2,1)S(1)} %copy-done.8, bf16[1536,512]{1,0:T(8,128)(2,1)S(1)} %copy-done.6, bf16[1536,512]{1,0:T(8,128)(2,1)} %get-tuple-element.60.refs_2_, ...), custom_call_target="tpu_custom_call" | custom-call | flops 3221225472 | bytes 20447232 | tf_op jit(solution)/shard_map/out_xy/pallas_call | solution.py:43
  436.0 18.7 %collective-permute-done.50 = bf16[1024,768]{1,0:T(8,128)(2,1)S(1)} collective-permute-done((bf16[1024,768]{1,0:T(8,128)(2,1)S(1)}, bf16[1024,768]{1,0:T(8,128)(2,1)S(1)}, u32[]{:S(2)}, u32[]{:S(2)}) %collective-permute-start.50) | collective-permute-done | bytes 1572896 | tf_op jit(solution)/shard_map/ppermute | solution.py:386
  476.7 16.9 %collective-permute-done.42 = bf16[128,384]{1,0:T(8,128)(2,1)S(1)} collective-permute-done((bf16[128,384]{1,0:T(8,128)(2,1)S(1)}, bf16[128,384]{1,0:T(8,128)(2,1)S(1)}, u32[]{:S(2)}, u32[]{:S(2)}) %collective-permute-start.42) | collective-permute-done | bytes 98336 | tf_op jit(solution)/shard_map/ppermute | solution.py:409
  521.2 6.4 %collective-permute-done.41 = bf16[128,640]{1,0:T(8,128)(2,1)S(1)} collective-permute-done((bf16[128,640]{1,0:T(8,128)(2,1)S(1)}, bf16[128,640]{1,0:T(8,128)(2,1)S(1)}, u32[]{:S(2)}, u32[]{:S(2)}) %collective-permute-start.41) | collective-permute-done | bytes 163872 | tf_op jit(solution)/shard_map/ppermute | solution.py:409
  (331 shorter events, 196.3 us)
Async XLA Ops:
  7.2 97.3 %all-gather.3.cloned.1.call-start = ((), (), s32[]{:S(2)}) async-start(), calls=%async_computation.4 | async-start | bytes 4718592 | tf_op jit(solution)/shard_map/all_gather | solution.py:431
  34.0 30.3 %all-to-all-start = ((bf16[8,128,768]{1,2,0:T(8,128)(2,1)}), bf16[8,128,768]{1,2,0:T(8,128)(2,1)S(1)}, u32[]{:S(2)}, u32[]{:S(2)}) async-start(bf16[8,128,768]{1,2,0:T(8,128)(2,1)} %bitcast.10), calls=%async_computation | async-start | bytes 3145728 | tf_op jit(solution)/shard_map/all_to_all | solution.py:443
  37.8 92.3 %all-gather.5.cloned.1.call-start = ((), (), s32[]{:S(2)}) async-start(), calls=%async_computation.5 | async-start | bytes 2359296 | tf_op jit(solution)/shard_map/all_gather | solution.py:432
  49.3 417.8 %reduce-scatter.5.cloned.1.call-start = ((), (), s32[]{:S(2)}) async-start(), calls=%async_computation.7 | async-start | bytes 2654208 | tf_op jit(solution)/shard_map/reduce_scatter | solution.py:543
  65.1 34.6 %collective-permute-start.18 = (bf16[1024,768]{1,0:T(8,128)(2,1)S(1)}, bf16[1024,768]{1,0:T(8,128)(2,1)S(1)}, u32[]{:S(2)}, u32[]{:S(2)}) collective-permute-start(bf16[1024,768]{1,0:T(8,128)(2,1)S(1)} %bitcast.26), channel_id=1, source_target_pairs={{0,8},{8,24},{24,16},{16,0},{1,9},{9,25},{25,17},{17,1},{2,10},{10... | collective-permute-start | bytes 4718600 | tf_op jit(solution)/shard_map/ppermute | solution.py:386
  99.7 59.4 %collective-permute-start.20 = (bf16[1024,768]{1,0:T(8,128)(2,1)S(1)}, bf16[1024,768]{1,0:T(8,128)(2,1)}, u32[]{:S(2)}, u32[]{:S(2)}) collective-permute-start(bf16[1024,768]{1,0:T(8,128)(2,1)S(1)} %collective-permute-done.18.w0.refs_6_), channel_id=1, source_target_pairs={{0,8},{8,24},{24,16},{16,0},{1,9},{9,25},{25,17},{17,1},{2,10},{10... | collective-permute-start | bytes 4718600 | tf_op jit(solution)/shard_map/ppermute | solution.py:386
  136.6 24.9 %collective-permute-start.7 = (bf16[384,1024]{1,0:T(8,128)(2,1)S(1)}, bf16[384,1024]{1,0:T(8,128)(2,1)S(1)}, u32[]{:S(2)}, u32[]{:S(2)}) collective-permute-start(bf16[384,1024]{1,0:T(8,128)(2,1)S(1)} %get-tuple-element.56.x0.n2_ref), channel_id=1, source_target_pairs={{0,4},{1,5},{2,6},{3,7},{4,0},{5,1},{6,2},{7,3},{8,12},{9,13},{10,... | collective-permute-start | bytes 2359304 | tf_op jit(solution)/shard_map/ppermute | solution.py:392
  159.1 54.3 %collective-permute-start.22 = (bf16[1024,768]{1,0:T(8,128)(2,1)}, bf16[1024,768]{1,0:T(8,128)(2,1)}, u32[]{:S(2)}, u32[]{:S(2)}) collective-permute-start(bf16[1024,768]{1,0:T(8,128)(2,1)} %collective-permute-done.20.w0.refs_8_), channel_id=1, source_target_pairs={{0,8},{8,24},{24,16},{16,0},{1,9},{9,25},{25,17},{17,1},{2,10},{10... | collective-permute-start | bytes 4718600 | tf_op jit(solution)/shard_map/ppermute | solution.py:386
  161.5 52.4 %collective-permute-start.19 = (bf16[1024,768]{1,0:T(8,128)(2,1)S(1)}, bf16[1024,768]{1,0:T(8,128)(2,1)}, u32[]{:S(2)}, u32[]{:S(2)}) collective-permute-start(bf16[1024,768]{1,0:T(8,128)(2,1)S(1)} %collective-permute-done.18.w0.refs_6_), channel_id=1, source_target_pairs={{0,1},{1,0},{2,3},{3,2},{4,5},{5,4},{6,7},{7,6},{8,9},{9,8},{10,11... | collective-permute-start | bytes 4718600 | tf_op jit(solution)/shard_map/ppermute | solution.py:398
  165.4 26.5 %collective-permute-start.8 = (bf16[192,1024]{1,0:T(8,128)(2,1)S(1)}, bf16[192,1024]{1,0:T(8,128)(2,1)S(1)}, u32[]{:S(2)}, u32[]{:S(2)}) collective-permute-start(bf16[192,1024]{1,0:T(8,128)(2,1)S(1)} %slice.191), channel_id=1, source_target_pairs={{0,2},{1,3},{2,0},{3,1},{4,6},{5,7},{6,4},{7,5},{8,10},{9,11},{10,... | collective-permute-start | bytes 1179656 | tf_op jit(solution)/shard_map/ppermute | solution.py:389
  183.8 46.3 %collective-permute-start.21 = (bf16[1024,768]{1,0:T(8,128)(2,1)}, bf16[1024,768]{1,0:T(8,128)(2,1)}, u32[]{:S(2)}, u32[]{:S(2)}) collective-permute-start(bf16[1024,768]{1,0:T(8,128)(2,1)} %collective-permute-done.20.w0.refs_8_), channel_id=1, source_target_pairs={{0,1},{1,0},{2,3},{3,2},{4,5},{5,4},{6,7},{7,6},{8,9},{9,8},{10,11... | collective-permute-start | bytes 4718600 | tf_op jit(solution)/shard_map/ppermute | solution.py:398
  213.4 50.3 %collective-permute-start.17 = (bf16[1024,768]{1,0:T(8,128)(2,1)S(1)}, bf16[1024,768]{1,0:T(8,128)(2,1)S(1)}, u32[]{:S(2)}, u32[]{:S(2)}) collective-permute-start(bf16[1024,768]{1,0:T(8,128)(2,1)S(1)} %bitcast.27), channel_id=1, source_target_pairs={{0,1},{1,0},{2,3},{3,2},{4,5},{5,4},{6,7},{7,6},{8,9},{9,8},{10,11... | collective-permute-start | bytes 4718600 | tf_op jit(solution)/shard_map/ppermute | solution.py:398
  213.4 32.9 %collective-permute-start.23 = (bf16[1024,768]{1,0:T(8,128)(2,1)}, bf16[1024,768]{1,0:T(8,128)(2,1)S(1)}, u32[]{:S(2)}, u32[]{:S(2)}) collective-permute-start(bf16[1024,768]{1,0:T(8,128)(2,1)} %collective-permute-done.22.w0.refs_10_), channel_id=1, source_target_pairs={{0,1},{1,0},{2,3},{3,2},{4,5},{5,4},{6,7},{7,6},{8,9},{9,8},{10,11... | collective-permute-start | bytes 4718600 | tf_op jit(solution)/shard_map/ppermute | solution.py:398
  282.8 44.7 %collective-permute-start.36 = (f32[384,128]{1,0:T(8,128)S(1)}, f32[384,128]{1,0:T(8,128)S(1)}, u32[]{:S(2)}, u32[]{:S(2)}) collective-permute-start(f32[384,128]{1,0:T(8,128)S(1)} %get-tuple-element.143), channel_id=1, source_target_pairs={{0,2},{1,3},{2,0},{3,1},{4,6},{5,7},{6,4},{7,5},{8,10},{9,11},{10,... | collective-permute-start | bytes 589832 | tf_op jit(solution)/shard_map/ppermute | solution.py:389
  340.1 168.8 %reduce-scatter.3.cloned.1.call-start = ((), (), s32[]{:S(2)}) async-start(), calls=%async_computation.6 | async-start | bytes 5013504 | tf_op jit(solution)/shard_map/reduce_scatter | solution.py:544
  340.1 38.5 %collective-permute-start.48 = (bf16[1024,768]{1,0:T(8,128)(2,1)}, bf16[1024,768]{1,0:T(8,128)(2,1)}, u32[]{:S(2)}, u32[]{:S(2)}) collective-permute-start(bf16[1024,768]{1,0:T(8,128)(2,1)} %get-tuple-element.96), channel_id=1, source_target_pairs={{0,1},{1,0},{2,3},{3,2},{4,5},{5,4},{6,7},{7,6},{8,9},{9,8},{10,11... | collective-permute-start | bytes 4718600 | tf_op jit(solution)/shard_map/ppermute | solution.py:398
  381.8 36.6 %collective-permute-start.49 = (bf16[1024,768]{1,0:T(8,128)(2,1)S(1)}, bf16[1024,768]{1,0:T(8,128)(2,1)S(1)}, u32[]{:S(2)}, u32[]{:S(2)}) collective-permute-start(bf16[1024,768]{1,0:T(8,128)(2,1)S(1)} %add_convert_fusion.3), channel_id=1, source_target_pairs={{0,8},{8,24},{24,16},{16,0},{1,9},{9,25},{25,17},{17,1},{2,10},{10... | collective-permute-start | bytes 4718600 | tf_op jit(solution)/shard_map/ppermute | solution.py:386
  382.2 53.2 %collective-permute-start.46 = (bf16[1024,768]{1,0:T(8,128)(2,1)S(1)}, bf16[1024,768]{1,0:T(8,128)(2,1)S(1)}, u32[]{:S(2)}, u32[]{:S(2)}) collective-permute-start(bf16[1024,768]{1,0:T(8,128)(2,1)S(1)} %copy-done.74), channel_id=1, source_target_pairs={{0,1},{1,0},{2,3},{3,2},{4,5},{5,4},{6,7},{7,6},{8,9},{9,8},{10,11... | collective-permute-start | bytes 4718600 | tf_op jit(solution)/shard_map/ppermute | solution.py:398
  419.1 35.6 %collective-permute-start.50 = (bf16[1024,768]{1,0:T(8,128)(2,1)S(1)}, bf16[1024,768]{1,0:T(8,128)(2,1)S(1)}, u32[]{:S(2)}, u32[]{:S(2)}) collective-permute-start(bf16[1024,768]{1,0:T(8,128)(2,1)S(1)} %add_convert_fusion.2), channel_id=1, source_target_pairs={{0,8},{8,24},{24,16},{16,0},{1,9},{9,25},{25,17},{17,1},{2,10},{10... | collective-permute-start | bytes 4718600 | tf_op jit(solution)/shard_map/ppermute | solution.py:386
  419.1 82.0 %collective-permute-start.45 = (bf16[1024,768]{1,0:T(8,128)(2,1)}, bf16[1024,768]{1,0:T(8,128)(2,1)}, u32[]{:S(2)}, u32[]{:S(2)}) collective-permute-start(bf16[1024,768]{1,0:T(8,128)(2,1)} %get-tuple-element.90), channel_id=1, source_target_pairs={{0,1},{1,0},{2,3},{3,2},{4,5},{5,4},{6,7},{7,6},{8,9},{9,8},{10,11... | collective-permute-start | bytes 4718600 | tf_op jit(solution)/shard_map/ppermute | solution.py:398
  425.3 32.7 %collective-permute-start.27 = (bf16[192,1024]{1,0:T(8,128)(2,1)S(1)}, bf16[192,1024]{1,0:T(8,128)(2,1)S(1)}, u32[]{:S(2)}, u32[]{:S(2)}) collective-permute-start(bf16[192,1024]{1,0:T(8,128)(2,1)S(1)} %get-tuple-element.66), channel_id=1, source_target_pairs={{0,2},{1,3},{2,0},{3,1},{4,6},{5,7},{6,4},{7,5},{8,10},{9,11},{10,... | collective-permute-start | bytes 1179656 | tf_op jit(solution)/shard_map/ppermute | solution.py:389
  427.0 31.9 %collective-permute-start.25 = (bf16[192,1024]{1,0:T(8,128)(2,1)S(1)}, bf16[192,1024]{1,0:T(8,128)(2,1)S(1)}, u32[]{:S(2)}, u32[]{:S(2)}) collective-permute-start(bf16[192,1024]{1,0:T(8,128)(2,1)S(1)} %get-tuple-element.64), channel_id=1, source_target_pairs={{0,4},{1,5},{2,6},{3,7},{4,0},{5,1},{6,2},{7,3},{8,12},{9,13},{10,... | collective-permute-start | bytes 1179656 | tf_op jit(solution)/shard_map/ppermute | solution.py:392
  458.0 43.1 %collective-permute-start.51 = (bf16[1024,768]{1,0:T(8,128)(2,1)}, bf16[1024,768]{1,0:T(8,128)(2,1)}, u32[]{:S(2)}, u32[]{:S(2)}) collective-permute-start(bf16[1024,768]{1,0:T(8,128)(2,1)} %add_convert_fusion.1), channel_id=1, source_target_pairs={{0,8},{8,24},{24,16},{16,0},{1,9},{9,25},{25,17},{17,1},{2,10},{10... | collective-permute-start | bytes 4718600 | tf_op jit(solution)/shard_map/ppermute | solution.py:386
  473.9 27.1 %collective-permute-start.44 = (bf16[128,384]{1,0:T(8,128)(2,1)S(1)}, bf16[128,384]{1,0:T(8,128)(2,1)S(1)}, u32[]{:S(2)}, u32[]{:S(2)}) collective-permute-start(bf16[128,384]{1,0:T(8,128)(2,1)S(1)} %concatenate.87), channel_id=1, source_target_pairs={{0,8},{8,24},{24,16},{16,0},{1,9},{9,25},{25,17},{17,1},{2,10},{10... | collective-permute-start | bytes 294920 | tf_op jit(solution)/shard_map/ppermute | solution.py:409
  (110 other events, 1504.5 us)
Sparse Core Ops, SparseCore 0:
  30.2 50.7 all-gather.2
  83.5 27.8 all-gather.4
  340.2 41.6 reduce-scatter.4
  385.6 58.3 reduce-scatter.2

commit v2 on v1

--- a/solution.py
+++ b/solution.py
@@ -20,6 +20,7 @@
 SCALE = 1.0 / math.sqrt(HEAD_SIZE)
 BF = jnp.bfloat16
 F32 = jnp.float32
+COST = 0.02
 
 NT = (((1,), (1,)), ((), ()))
 TN = (((0,), (0,)), ((), ()))
@@ -48,10 +49,14 @@
         scratch_shapes=scratch,
         compiler_params=pltpu.CompilerParams(vmem_limit_bytes=vmem << 20),
         cost_estimate=pl.CostEstimate(
-            flops=int(flops), transcendentals=0, bytes_accessed=int(nbytes)
+            flops=int(flops * COST), transcendentals=0, bytes_accessed=int(nbytes * COST)
         ),
         name=name,
     )(*args)
+
+
+def after(x, *deps):
+    return lax.optimization_barrier((x, *deps))[0]
 
 
 def low_half(shape):
@@ -135,7 +140,7 @@
 ROWS = 4 * T
 
 
-def expert(e_ref, x0, xx, xy, xa, xb, y0, yx, yy, ya, yb, g0, gr, w0, w1,
+def expert(e_ref, x0, xx, xy, xa, xb, y0, yx, yy, ya, yb, g0, gr, w0, w1, dgate_i,
            gh_o, dgu_o, dw0_o, dw1_o, dgate_o,
            X, Y, G, W, GH, DGU, DW, si, so):
     half = T // 2
@@ -179,7 +184,7 @@
             base = u * 2 * HALF
             DGU[rows, base : base + HALF] = (dh * up * (s * (1.0 + g * (1.0 - s)))).astype(BF)
             DGU[rows, base + HALF : base + 2 * HALF] = (dh * silu).astype(BF)
-        dgate_o[rows, :] = jnp.where(lanes == e, dgate, 0.0)
+        dgate_o[rows, :] = dgate_i[rows, :] + jnp.where(lanes == e, dgate, 0.0)
         return carry
 
     lax.fori_loop(0, 4, tree, 0)
@@ -196,14 +201,14 @@
         o.wait()
 
 
-def run_expert(e, xs, ys, gs, w0, w1):
-    args = (e, *xs, *ys, *gs, w0, w1)
+def run_expert(e, xs, ys, gs, w0, w1, dgate):
+    args = (e, *xs, *ys, *gs, w0, w1, dgate)
     rows = MODEL_WIDTH
     return call(
         expert,
         [((ROWS, FF), BF), ((ROWS, 2 * FF), BF), ((rows, 3 * HALF), BF), ((rows, 3 * HALF), BF),
          ((ROWS, LANES), F32)],
-        [SM] + [ANY] * 14,
+        [SM] + [ANY] * 14 + [VM],
         [ANY] * 4 + [VM],
         [
             pltpu.VMEM((ROWS, MODEL_WIDTH), BF), pltpu.VMEM((ROWS, MODEL_WIDTH), BF),
@@ -216,12 +221,12 @@
     )
 
 
-def back_body(lo, m, width, first_col, splits, n):
+def back_body(lo, m, width, first_col, splits, n, tail):
     def body(*refs):
         acts = refs[0:4]
         ws = refs[4:12]
-        outs = refs[12 : 12 + n]
-        A, W, sem = refs[12 + n :]
+        outs = refs[12 + tail : 12 + tail + n]
+        A, W, sem = refs[12 + tail + n :]
         copies = []
         for k in range(4):
             for u in range(2):
@@ -245,21 +250,25 @@
             w.wait()
         total = total + dotg(A[1], W[1], NT)
         for o, (r0, r1) in zip(outs, splits):
-            o[...] = total[r0:r1].astype(o.dtype)
+            o[:, 0:MODEL_WIDTH] = total[r0:r1].astype(o.dtype)
+            if tail:
+                o[:, MODEL_WIDTH:] = refs[12][lo + r0 : lo + r1, :].astype(o.dtype)
     return body
 
 
-def run_back(acts, ws, lo, m, width, first_col, splits, dtypes, name):
+def run_back(acts, ws, extra, lo, m, width, first_col, splits, dtypes, name):
+    cols = MODEL_WIDTH + (0 if extra is None else LANES)
+    extras = () if extra is None else (extra,)
     return call(
-        back_body(lo, m, width, first_col, splits, len(splits)),
-        [((r1 - r0, MODEL_WIDTH), d) for (r0, r1), d in zip(splits, dtypes)],
-        [ANY] * 12,
+        back_body(lo, m, width, first_col, splits, len(splits), len(extras)),
+        [((r1 - r0, cols), d) for (r0, r1), d in zip(splits, dtypes)],
+        [ANY] * 12 + [VM] * len(extras),
         [VM] * len(splits),
         [
             pltpu.VMEM((2, m, 4 * width), BF), pltpu.VMEM((2, MODEL_WIDTH, 4 * width), BF),
             pltpu.SemaphoreType.DMA((2, 8)),
         ],
-        (*acts, *ws), name, 48, 2 * m * MODEL_WIDTH * 8 * width,
+        (*acts, *ws, *extras), name, 48, 2 * m * MODEL_WIDTH * 8 * width,
     )
 
 
@@ -270,12 +279,15 @@
     return jnp.where(lanes == lane, total, 0.0)
 
 
-def join(p_ref, rx_ref, ry_ref, g0_ref, gx_ref, gy_ref, gd_ref, gates_ref, h1_ref, n2_ref,
+def join(p_ref, rxa_ref, rxb_ref, rya_ref, ryb_ref, gates_ref, h1_ref, n2_ref,
          gain_ref, rt_ref, dy_ref, wo_ref, att_ref, dh1_ref, datt_ref, dwo_ref):
     gates = gates_ref[...]
-    dg = g0_ref[...] + gx_ref[...] + gy_ref[...] + gd_ref[...]
+    rx = jnp.concatenate([rxa_ref[...], rxb_ref[...]], axis=0).astype(F32)
+    ry = jnp.concatenate([rya_ref[...], ryb_ref[...]], axis=0).astype(F32)
+    total = p_ref[...] + rx + ry
+    dg = total[:, MODEL_WIDTH:]
     dl = (gates * (dg - jnp.sum(gates * dg, axis=1, keepdims=True))).astype(BF)
-    dn2 = p_ref[...] + rx_ref[...].astype(F32) + ry_ref[...].astype(F32) + dot(dl, rt_ref[...])
+    dn2 = total[:, :MODEL_WIDTH] + dot(dl, rt_ref[...])
     h1 = h1_ref[...]
     gain = gain_ref[...]
     r2 = lax.rsqrt(jnp.mean(h1 * h1, axis=1, keepdims=True) + EPSILON)
@@ -419,22 +431,34 @@
         def swapped(w):
             return [w[:, 0:64], w[:, 128:192], w[:, 64:128], w[:, 192:256]]
 
-        own_qkv = jnp.concatenate(swapped(query_weight) + [key_matrix, value_matrix], axis=1)
-        own_out = jnp.concatenate(swapped(out_weight), axis=1)
-
         def z_gather(a):
             got = [a]
             for _ in range(groups - 1):
                 got.append(z_next(got[-1]))
             return got
 
-        w_qkv = lax.all_gather(jnp.concatenate(z_gather(own_qkv), axis=1), "fsdp", axis=0, tiled=True)
-        w_out = lax.all_gather(jnp.concatenate(z_gather(own_out), axis=1), "fsdp", axis=0, tiled=True)
+        own_qkv = jnp.concatenate(swapped(query_weight) + [key_matrix, value_matrix], axis=1)
+        cols_qkv = jnp.concatenate(z_gather(own_qkv), axis=1)
+        w_qkv = lax.all_gather(cols_qkv, "fsdp", axis=0, tiled=True)
+        own_out = after(jnp.concatenate(swapped(out_weight), axis=1), cols_qkv)
+        cols_out = jnp.concatenate(z_gather(own_out), axis=1)
+        w_out = lax.all_gather(cols_out, "fsdp", axis=0, tiled=True)
+
         small = jnp.concatenate([router_weight.T, attn_gain[None], ffn_gain[None]], axis=0)
-        small = lax.all_gather(small, "fsdp", axis=1, tiled=True)
-        router_t = jnp.concatenate([small[:16], jnp.zeros((LANES - 16, MODEL_WIDTH), BF)], axis=0)
-        gain_one = small[16:17].astype(F32)
-        gain_two = small[17:18].astype(F32)
+        small = jnp.concatenate([small.reshape(-1), routes.T.astype(BF).reshape(-1)])
+        small = lax.all_gather(small, "fsdp", axis=0, tiled=False)
+        rows = jnp.transpose(small[:, : 18 * dr].reshape(fsdp, 18, dr), (1, 0, 2)).reshape(18, -1)
+        router_t = jnp.concatenate([rows[:16], jnp.zeros((LANES - 16, MODEL_WIDTH), BF)], axis=0)
+        gain_one = rows[16:17].astype(F32)
+        gain_two = rows[17:18].astype(F32)
+        lanes = jnp.arange(LANES, dtype=jnp.int32)
+
+        def route_mask(bits):
+            got = lax.dynamic_index_in_dim(small, mine ^ bits, 0, keepdims=False)[18 * dr :]
+            got = got.reshape(-1, T).T.astype(jnp.int32)
+            return jnp.sum((got[:, :, None] == lanes[None, None, :]).astype(F32), axis=1).astype(BF)
+
+        masks = [route_mask(bits) for bits in (0, 2, 4, 6)]
 
         gu = gate_up_weight.reshape(dr, 4, 2, 2, HALF)
         dn = down_weight.reshape(dr, 4, 1, 2, HALF)
@@ -444,81 +468,98 @@
         unit = unit.reshape(8 * dr, 3 * HALF)
         if rest > 1:
             unit = lax.all_gather(unit, "fsdp", axis=0, tiled=True, axis_index_groups=rest_groups)
-        units = z_gather(unit)
-        pairs = [(u, to_core(u)) for u in units]
 
         bias = visible_bias(segment, parents[0])
         cos, sin = turn_tables(positions)
-        lanes = jnp.arange(LANES, dtype=jnp.int32)
-        mask = jnp.sum((routes[:, :, None] == lanes[None, None, :]).astype(F32), axis=1).astype(BF)
-        mask_rest = (to_x(mask), to_y(mask), to_diag(mask))
-        dys = plane(cotangent)
-
+
+        tokens_f = after(tokens, unit, cols_out, bias, cos, sin, *masks)
+        dy_x = to_x(cotangent)
+        dy_y = to_y(cotangent)
+        units = z_gather(unit)
         n1, qkv, att = call(
             attn_fwd,
             [((T, MODEL_WIDTH), BF), ((4, T, 512), BF), ((4, T, 256), BF)],
             [VM] * 6, [VM] * 3, [],
-            (tokens, gain_one, w_qkv, cos, sin, bias), "attn_fwd", 48, 3.0e9,
+            (tokens_f, gain_one, w_qkv, cos, sin, bias), "attn_fwd", 48, 3.0e9,
         )
+        half = T // 2
+        att, dy_x, dy_y = lax.optimization_barrier((att, dy_x, dy_y))
+        dy_a = to_x(dy_y[:half])
+        dy_b = to_y(dy_x[half:])
         h1, n2, gates = call(
             mid,
             [((T, MODEL_WIDTH), F32), ((T, MODEL_WIDTH), BF), ((T, LANES), F32)],
             [VM] * 6, [VM] * 3, [],
-            (tokens, att, w_out, gain_two, router_t, mask), "mid", 48, 1.0e9,
+            (tokens, att, w_out, gain_two, router_t, masks[0]), "mid", 48, 1.0e9,
         )
+        n2, dy_a, dy_b, u1 = lax.optimization_barrier((n2, dy_a, dy_b, units[1]))
+        units[1] = u1
+        dys = (cotangent, dy_x, dy_y, dy_a, dy_b)
+        pairs = [(u, to_core(u)) for u in units]
         xs = plane(n2)
         gates_rest, = call(
             gate_rest, [((3 * T, LANES), F32)], [VM] * 8, [VM], [],
-            (*xs[1:], router_t, *mask_rest), "gate_rest", 48, 0.4e9,
+            (*xs[1:], router_t, *masks[1:]), "gate_rest", 48, 0.4e9,
         )
 
         chip = (mine // 2) % 4
         order = list(range(1, groups)) + [0]
-        done = {}
-        ring_acc = None
+        ghs = [None] * groups
+        dgus = [None] * groups
+        mine_dw = []
+        dgate = jnp.zeros((ROWS, LANES), F32)
         for k in order:
             e = (4 * ring_ids[(spot - k) % groups] + chip).astype(jnp.int32).reshape(1)
-            gh, dgu, dw_own, dw_sib, dgate = run_expert(e, xs, dys, (gates, gates_rest), *pairs[k])
-            got = to_core(dw_sib)
-            grad = dw_own.astype(F32) + got.astype(F32)
-            if ring_acc is not None:
-                grad = grad + z_next(ring_acc).astype(F32)
-            ring_acc = grad.astype(BF)
-            done[k] = (gh, dgu, dgate)
-        ghs = [done[k][0] for k in range(groups)]
-        dgus = [done[k][1] for k in range(groups)]
-        dgate = sum(done[k][2] for k in range(groups))
+            ghs[k], dgus[k], dw_own, dw_sib, dgate = run_expert(
+                e, xs, dys, (gates, gates_rest), *pairs[k], dgate
+            )
+            mine_dw.append((dw_own, to_core(dw_sib)))
+
+        def chip_sum(i, *more):
+            total = mine_dw[i][0].astype(F32) + mine_dw[i][1].astype(F32)
+            for m in more:
+                total = total + m.astype(F32)
+            return total.astype(BF)
+
         ws = [w for pair in pairs for w in pair]
-        half = T // 2
-        whole = ((0, T),)
-        split = ((0, half), (half, T))
-
-        def spread(acts, width, first_col, name):
-            da, db = run_back(acts, ws, 3 * T, T, width, first_col, split, (BF, BF), name + "_d")
-            ra = to_x(da)
-            rb = to_y(db)
-            xa, xb, ya, yb = run_back(
-                acts, ws, T, 2 * T, width, first_col,
-                ((0, half), (half, T), (T, T + half), (T + half, 2 * T)), (BF,) * 4, name + "_xy",
-            )
-            own, = run_back(acts, ws, 0, T, width, first_col, whole, (F32,), name + "_o")
-            xb = (xb.astype(F32) + rb.astype(F32)).astype(BF)
-            ya = (ya.astype(F32) + ra.astype(F32)).astype(BF)
-            rx = jnp.concatenate([to_x(xa), to_x(xb)], axis=0)
-            ry = jnp.concatenate([to_y(ya), to_y(yb)], axis=0)
-            return own, rx, ry
-
-        gate_parts = (
-            dgate[:T], to_x(dgate[T : 2 * T]), to_y(dgate[2 * T : 3 * T]), to_diag(dgate[3 * T :]),
-        )
-        p_n2, rx_n2, ry_n2 = spread(dgus, 2 * HALF, 0, "dn2")
+        xy_splits = ((0, half), (half, T), (T, T + half), (T + half, 2 * T))
+
+        def back(acts, extra, width, first_col, lo, m, splits, dtypes, name):
+            return run_back(acts, ws, extra, lo, m, width, first_col, splits, dtypes, name)
+
+        hop = z_next(chip_sum(0))
+        dgus[0], hop = lax.optimization_barrier((dgus[0], hop))
+        args = (dgus, dgate, 2 * HALF, 0)
+        da, db = back(*args, 3 * T, T, ((0, half), (half, T)), (BF, BF), "dn2_d")
+        hop = z_next(chip_sum(1, hop))
+        ra = to_x(da)
+        rb = to_y(db)
+        xa, xb, ya, yb = back(*args, T, 2 * T, xy_splits, (BF,) * 4, "dn2_xy")
+        rxa = to_x(xa)
+        ryb = to_y(yb)
+        ra = after(ra, xa)
+        rxb = to_x((xb.astype(F32) + rb.astype(F32)).astype(BF))
+        rya = to_y((ya.astype(F32) + ra.astype(F32)).astype(BF))
+        own, = back(*args, 0, T, ((0, T),), (F32,), "dn2_o")
+        ghs[0] = after(ghs[0], own)
+        args = (ghs, None, HALF, 2 * HALF)
+        oda, odb = back(*args, 3 * T, T, ((0, half), (half, T)), (BF, BF), "out_d")
+        oxa, oxb, oya, oyb = back(*args, T, 2 * T, xy_splits, (BF,) * 4, "out_xy")
+        own, hop, oda, odb, oxa = lax.optimization_barrier((own, hop, oda, odb, oxa))
         dh1, datt, dwo = call(
             join,
             [((T, MODEL_WIDTH), F32), ((4, T, 256), BF), ((MODEL_WIDTH, 1152), BF)],
-            [VM] * 15, [VM] * 3, [],
-            (p_n2, rx_n2, ry_n2, *gate_parts, gates, h1, n2, gain_two, router_t, cotangent, w_out, att),
+            [VM] * 13, [VM] * 3, [],
+            (own, rxa, rxb, rya, ryb, gates, h1, n2, gain_two, router_t, cotangent, w_out, att),
             "join", 48, 2.0e9,
         )
+        rs_out = lax.psum_scatter(dwo, "fsdp", scatter_dimension=0, tiled=True)
+        hop = z_next(chip_sum(2, hop))
+        oda, odb, oxa, oyb, _ = lax.optimization_barrier((oda, odb, oxa, oyb, dh1))
+        ra = to_x(oda)
+        rb = to_y(odb)
+        orxa = to_x(oxa)
+        oryb = to_y(oyb)
         dx, dwqkv = call(
             attn_bwd,
             [((T, MODEL_WIDTH), F32), ((MODEL_WIDTH, 2176), BF)],
@@ -526,26 +567,32 @@
             [pltpu.VMEM((4, T, 512), BF), pltpu.VMEM((T, LANES), F32), pltpu.VMEM((T, LANES), F32)],
             (tokens, gain_one, w_qkv, cos, sin, bias, n1, qkv, datt, dh1), "attn_bwd", 48, 6.0e9,
         )
-
-        p_out, rx_out, ry_out = spread(ghs, HALF, 2 * HALF, "out")
-        output = (h1 + p_out + rx_out.astype(F32) + ry_out.astype(F32)).astype(BF)
-
+        ra, rb, hop, orxa, oryb, ghs[0], dwqkv = lax.optimization_barrier(
+            (ra, rb, hop, orxa, oryb, ghs[0], dwqkv)
+        )
+        rs_qkv = lax.psum_scatter(dwqkv, "fsdp", scatter_dimension=0, tiled=True)
+        orxb = to_x((oxb.astype(F32) + rb.astype(F32)).astype(BF))
+        orya = to_y((oya.astype(F32) + ra.astype(F32)).astype(BF))
+        oown, = back(ghs, None, HALF, 2 * HALF, 0, T, ((0, T),), (F32,), "out_o")
+
+        acc = chip_sum(3, hop)
         if rest > 1:
-            ring_acc = lax.psum_scatter(
-                ring_acc, "fsdp", scatter_dimension=0, tiled=True, axis_index_groups=rest_groups
+            acc = lax.psum_scatter(
+                acc, "fsdp", scatter_dimension=0, tiled=True, axis_index_groups=rest_groups
             )
-        back = lax.all_to_all(ring_acc.reshape(8, dr, 3 * HALF), "fsdp", 0, 0, axis_index_groups=low_groups)
-        back = back.astype(F32).reshape(4, 2, dr, 3, HALF)
-        back = jnp.transpose(back, (2, 0, 3, 1, 4))
-        gate_up_grad = back[:, :, :2].reshape(dr, 4, 2 * FF)
-        down_grad = back[:, :, 2].reshape(dr, 4, FF)
-
-        rs_out = lax.psum_scatter(dwo, "fsdp", scatter_dimension=0, tiled=True)
-        rs_qkv = lax.psum_scatter(dwqkv, "fsdp", scatter_dimension=0, tiled=True)
+        home = lax.all_to_all(acc.reshape(8, dr, 3 * HALF), "fsdp", 0, 0, axis_index_groups=low_groups)
+        home = home.astype(F32).reshape(4, 2, dr, 3, HALF)
+        home = jnp.transpose(home, (2, 0, 3, 1, 4))
+        gate_up_grad = home[:, :, :2].reshape(dr, 4, 2 * FF)
+        down_grad = home[:, :, 2].reshape(dr, 4, FF)
+
         z_out = z_sum([
             jnp.concatenate([rs_out[:, k * 256 : (k + 1) * 256], rs_out[:, 1024:]], axis=1)
             for k in range(groups)
         ])
+        received = jnp.concatenate([orxa, orxb], axis=0).astype(F32)
+        received = received + jnp.concatenate([orya, oryb], axis=0).astype(F32)
+        output = (h1 + oown + received).astype(BF)
         z_qkv = z_sum([
             jnp.concatenate([rs_qkv[:, k * 512 : (k + 1) * 512], rs_qkv[:, 2048:]], axis=1)
             for k in range(groups)

time: 556 us -> 490 us (0.88)
  waiting for transfers between devices: 191 us -> 102 us
  blocking collectives: 8.34 us -> 29.6 us
  starting transfers between devices: 68 us -> 60.3 us
  other arithmetic: 23.1 us -> 30.6 us
  Pallas kernels: 173 us -> 180 us
    ppermute x12, waiting for transfers between devices: 93.1 us -> 38.2 us  [z_next(): return lax.ppermute(a, 'grp', shifted(1))]
    ppermute x6, waiting for transfers between devices: 35.6 us -> 6.95 us  [z_sum(): lax.ppermute(blocks[k], 'grp', shifted(groups - k)).astype(F32)]
    all_gather x1, blocking collectives: 8.34 us -> 29.6 us  [shards(): small = lax.all_gather(small, 'fsdp', axis=0, tiled=False)]
    ppermute x12 -> x10, waiting for transfers between devices: 16.1 us -> 32 us  [to_x(): return lax.ppermute(a, 'fsdp', flip(2))]
    all_to_all x1, waiting for transfers between devices: 15 us -> 0.01 us  [shards(): unit = lax.all_to_all(parts, 'fsdp', 0, 0, axis_index_groups=low_groups)]
    ppermute x12 -> x10, waiting for transfers between devices: 29.1 us -> 17.9 us  [to_y(): return lax.ppermute(a, 'fsdp', flip(4))]
    unnamed x156 -> x151, local copies, waits for them, and re-layouts: 40.7 us -> 32.9 us
    ppermute x8, waiting for transfers between devices: 0.02 us -> 7.03 us  [to_core(): return lax.ppermute(a, 'fsdp', flip(1))]
  transfers between devices with their start and end apart: 58 -> 52, of which waited for: 23 -> 13; matrix products, arithmetic and copies ran while one was open for 7% -> 12% of each run, Pallas kernels for 27% -> 35%
where the time goes in v2:
time: 490 us; the launch traced here: 483 us
  Pallas kernels  180 us (37%)
  waiting for transfers between devices  102 us (21%)
  starting transfers between devices  60.3 us (12%)
  local copies, waits for them, and re-layouts  58.2 us (12%)
  other arithmetic  30.6 us (6%)
  blocking collectives  29.6 us (6%)
  between operations  21.7 us (4%)
    pallas_call x15, Pallas kernels, call(): pl.pallas_call(body, out_shape=[jax.ShapeDtypeStruct(s, d) for s, d in ou...  180 us
    ppermute x12, waiting for transfers between devices, z_next(): return lax.ppermute(a, 'grp', shifted(1))  38.2 us
    unnamed x151, local copies, waits for them, and re-layouts  32.9 us
    ppermute x10, waiting for transfers between devices, to_x(): return lax.ppermute(a, 'fsdp', flip(2))  32 us
    all_gather x1, blocking collectives, shards(): small = lax.all_gather(small, 'fsdp', axis=0, tiled=False)  29.6 us
    ppermute x12, starting transfers between devices, z_next(): return lax.ppermute(a, 'grp', shifted(1))  18.1 us
    ppermute x10, waiting for transfers between devices, to_y(): return lax.ppermute(a, 'fsdp', flip(4))  17.9 us
    ppermute x10, starting transfers between devices, to_x(): return lax.ppermute(a, 'fsdp', flip(2))  12.9 us
  transfers between devices with their start and end apart: 52, of which 13 were waited for; matrix products, arithmetic and copies ran while one was open for 12% of the time, Pallas kernels for 35%

profile of v2, /device:TPU:0, one launch (start us, length us, event | category | flops | bytes accessed | tf_op | source)
XLA Modules:
  0.0 482.7 jit_solution(2483710524248053972)
XLA Ops:
  12.2 4.5 collective-permute-done
  17.6 5.0 %collective-permute-done.1 = bf16[128,512]{1,0:T(8,128)(2,1)S(1)} collective-permute-done((bf16[128,512]{1,0:T(8,128)(2,1)S(1)}, bf16[128,512]{1,0:T(8,128)(2,1)S(1)}, u32[]{:S(2)}, u32[]{:S(2)}) %collective-permute-start.1) | collective-permute-done | bytes 131104 | tf_op jit(solution)/shard_map/ppermute | solution.py:398
  23.5 5.0 %collective-permute-done.2 = bf16[128,512]{1,0:T(8,128)(2,1)S(1)} collective-permute-done((bf16[128,512]{1,0:T(8,128)(2,1)S(1)}, bf16[128,512]{1,0:T(8,128)(2,1)S(1)}, u32[]{:S(2)}, u32[]{:S(2)}) %collective-permute-start.2) | collective-permute-done | bytes 131104 | tf_op jit(solution)/shard_map/ppermute | solution.py:398
  41.0 4.4 collective-permute-done.3
  56.7 29.6 %all-gather.1 = bf16[8,1,5376]{2,1,0:T(2,128)(2,1)S(1)} all-gather(bf16[1,1,5376]{2,1,0:T(2,128)(2,1)S(1)} %reshape.181), channel_id=2, replica_groups=mesh['grp'=4,'fsdp'=8] {'fsdp'}, dimensions={0}, use_global_device_ids=true | all-gather | bytes 96768 | tf_op jit(solution)/shard_map/all_gather | solution.py:449
  103.3 18.9 %attn_fwd.1 = (bf16[384,1024]{1,0:T(8,128)(2,1)S(1)}, bf16[4,384,512]{2,1,0:T(8,128)(2,1)S(1)}, bf16[4,384,256]{2,1,0:T(8,128)(2,1)S(1)}) custom-call(bf16[384,1024]{1,0:T(8,128)(2,1)S(1)} %copy-done.20, f32[1,1024]{1,0:T(1,128)S(1)} %bitcast.64, bf16[1024,2048]{1,0:T(8,128)(2,1)} %all-gather.5.cloned.1.call-done.w_ref, ...), custom_call_target="tpu_custom_call" | custom-call | flops 60000000 | bytes 182272 | tf_op jit(solution)/shard_map/attn_fwd/pallas_call | solution.py:44
  129.0 5.8 %collective-permute-done.10.w0.refs_6_ = bf16[1024,768]{1,0:T(8,128)(2,1)S(1)} collective-permute-done((bf16[1024,768]{1,0:T(8,128)(2,1)S(1)}, bf16[1024,768]{1,0:T(8,128)(2,1)S(1)}, u32[]{:S(2)}, u32[]{:S(2)}) %collective-permute-start.10) | collective-permute-done | bytes 1572896 | tf_op jit(solution)/shard_map/ppermute | solution.py:398
  145.4 17.9 %collective-permute-done.12.ny_ref.xy = bf16[384,1024]{1,0:T(8,128)(2,1)S(1)} collective-permute-done((bf16[384,1024]{1,0:T(8,128)(2,1)S(1)}, bf16[384,1024]{1,0:T(8,128)(2,1)S(1)}, u32[]{:S(2)}, u32[]{:S(2)}) %collective-permute-start.12) | collective-permute-done | bytes 786464 | tf_op jit(solution)/shard_map/ppermute | solution.py:404
  188.1 17.3 %expert.4 = (bf16[1536,512]{1,0:T(8,128)(2,1)}, bf16[1536,1024]{1,0:T(8,128)(2,1)}, bf16[1024,768]{1,0:T(8,128)(2,1)}, bf16[1024,768]{1,0:T(8,128)(2,1)}, f32[1536,128]{1,0:T(8,128)}) custom-call(s32[1]{0:T(128)} %bitcast.32.e_ref, bf16[384,1024]{1,0:T(8,128)(2,1)} %copy-done.10, bf16[384,1024]{1,0:T(8,128)(2,1)} %copy-done.8, bf16[384,1024]{1,0:T(8,128)(2,1)} %copy-done.6, ...), custom_call_target="tpu_custom_call" | custom-call | flops 193273536 | bytes 393216 | tf_op jit(solution)/shard_map/expert/pallas_call | solution.py:44
  206.7 4.8 %collective-permute-done.17.w0.refs_10_ = bf16[1024,768]{1,0:T(8,128)(2,1)} collective-permute-done((bf16[1024,768]{1,0:T(8,128)(2,1)}, bf16[1024,768]{1,0:T(8,128)(2,1)}, u32[]{:S(2)}, u32[]{:S(2)}) %collective-permute-start.17) | collective-permute-done | bytes 1572896 | tf_op jit(solution)/shard_map/ppermute | solution.py:398
  217.9 17.3 %expert.5 = (bf16[1536,512]{1,0:T(8,128)(2,1)}, bf16[1536,1024]{1,0:T(8,128)(2,1)}, bf16[1024,768]{1,0:T(8,128)(2,1)}, bf16[1024,768]{1,0:T(8,128)(2,1)}, f32[1536,128]{1,0:T(8,128)}) custom-call(s32[1]{0:T(128)} %bitcast.30.e_ref, bf16[384,1024]{1,0:T(8,128)(2,1)} %copy-done.10, bf16[384,1024]{1,0:T(8,128)(2,1)} %copy-done.8, bf16[384,1024]{1,0:T(8,128)(2,1)} %copy-done.6, ...), custom_call_target="tpu_custom_call" | custom-call | flops 193273536 | bytes 393216 | tf_op jit(solution)/shard_map/expert/pallas_call | solution.py:44
  236.8 17.3 %expert.6 = (bf16[1536,512]{1,0:T(8,128)(2,1)}, bf16[1536,1024]{1,0:T(8,128)(2,1)}, bf16[1024,768]{1,0:T(8,128)(2,1)}, bf16[1024,768]{1,0:T(8,128)(2,1)}, f32[1536,128]{1,0:T(8,128)}) custom-call(s32[1]{0:T(128)} %bitcast.28.e_ref, bf16[384,1024]{1,0:T(8,128)(2,1)} %copy-done.10, bf16[384,1024]{1,0:T(8,128)(2,1)} %copy-done.8, bf16[384,1024]{1,0:T(8,128)(2,1)} %copy-done.6, ...), custom_call_target="tpu_custom_call" | custom-call | flops 193273536 | bytes 393216 | tf_op jit(solution)/shard_map/expert/pallas_call | solution.py:44
  255.4 17.4 %expert.7 = (bf16[1536,512]{1,0:T(8,128)(2,1)}, bf16[1536,1024]{1,0:T(8,128)(2,1)}, bf16[1024,768]{1,0:T(8,128)(2,1)}, bf16[1024,768]{1,0:T(8,128)(2,1)}, f32[1536,128]{1,0:T(8,128)}) custom-call(s32[1]{0:T(128)} %bitcast.26.e_ref, bf16[384,1024]{1,0:T(8,128)(2,1)} %copy-done.10, bf16[384,1024]{1,0:T(8,128)(2,1)} %copy-done.8, bf16[384,1024]{1,0:T(8,128)(2,1)} %copy-done.6, ...), custom_call_target="tpu_custom_call" | custom-call | flops 193273536 | bytes 393216 | tf_op jit(solution)/shard_map/expert/pallas_call | solution.py:44
  275.4 7.5 %dn2_d.1 = (bf16[192,1152]{1,0:T(8,128)(2,1)S(1)}, bf16[192,1152]{1,0:T(8,128)(2,1)S(1)}) custom-call(bf16[1536,1024]{1,0:T(8,128)(2,1)} %get-tuple-element.102.refs_0_, bf16[1536,1024]{1,0:T(8,128)(2,1)} %get-tuple-element.103.refs_1_, bf16[1536,1024]{1,0:T(8,128)(2,1)} %get-tuple-element.104.refs_2_, bf16[1536,1024]{1,0:T(8,128)(2,1)} %get-tuple-element.105.refs_3_, ...), custom_call_target="tpu_custom_call" | custom-call | flops 64424508 | bytes 536739 | tf_op jit(solution)/shard_map/dn2_d/pallas_call | solution.py:44
  290.0 11.6 %dn2_xy.1 = (bf16[192,1152]{1,0:T(8,128)(2,1)S(1)}, bf16[192,1152]{1,0:T(8,128)(2,1)S(1)}, bf16[192,1152]{1,0:T(8,128)(2,1)S(1)}, bf16[192,1152]{1,0:T(8,128)(2,1)S(1)}) custom-call(bf16[1536,1024]{1,0:T(8,128)(2,1)} %get-tuple-element.102.refs_0_, bf16[1536,1024]{1,0:T(8,128)(2,1)} %get-tuple-element.103.refs_1_, ...), custom_call_target="tpu_custom_call" | custom-call | flops 128849016 | bytes 554434 | tf_op jit(solution)/shard_map/dn2_xy/pallas_call | solution.py:44
  306.9 8.4 %dn2_o.1.p_ref = f32[384,1152]{1,0:T(8,128)} custom-call(bf16[1536,1024]{1,0:T(8,128)(2,1)} %get-tuple-element.102.refs_0_, bf16[1536,1024]{1,0:T(8,128)(2,1)} %get-tuple-element.103.refs_1_, bf16[1536,1024]{1,0:T(8,128)(2,1)} %get-tuple-element.104.refs_2_, bf16[1536,1024]{1,0:T(8,128)(2,1)} %get-tuple-element.105.refs_3_, bf16[1024,768]{1,0:T(8,128)(2,1)S(1)} %bitcast.63, ...), custom_call_target="tpu_custom_call" | custom-call | flops 64424508 | bytes 554434 | tf_op jit(solution)/shard_map/dn2_o/pallas_call | solution.py:44
  315.3 4.3 out_d.1
  319.7 6.8 %out_xy.1 = (bf16[192,1024]{1,0:T(8,128)(2,1)S(1)}, bf16[192,1024]{1,0:T(8,128)(2,1)S(1)}, bf16[192,1024]{1,0:T(8,128)(2,1)S(1)}, bf16[192,1024]{1,0:T(8,128)(2,1)S(1)}) custom-call(bf16[1536,512]{1,0:T(8,128)(2,1)S(1)} %copy-done.16, bf16[1536,512]{1,0:T(8,128)(2,1)S(1)} %copy-done.13, bf16[1536,512]{1,0:T(8,128)(2,1)} %get-tuple-element.113.refs_2_, ...), custom_call_target="tpu_custom_call" | custom-call | flops 64424508 | bytes 408944 | tf_op jit(solution)/shard_map/out_xy/pallas_call | solution.py:44
  327.7 8.9 %join.1 = (f32[384,1024]{1,0:T(8,128)}, bf16[4,384,256]{2,1,0:T(8,128)(2,1)S(1)}, bf16[1024,1152]{1,0:T(8,128)(2,1)}) custom-call(f32[384,1152]{1,0:T(8,128)} %dn2_o.1.p_ref, bf16[192,1152]{1,0:T(8,128)(2,1)S(1)} %collective-permute-done.25.rxa_ref, bf16[192,1152]{1,0:T(8,128)(2,1)S(1)} %collective-permute-done.27.rxb_ref, ...), custom_call_target="tpu_custom_call" | custom-call | flops 40000000 | bytes 294993 | tf_op jit(solution)/shard_map/join/pallas_call | solution.py:44
  347.7 34.5 %attn_bwd.1 = (f32[384,1024]{1,0:T(8,128)}, bf16[1024,2176]{1,0:T(8,128)(2,1)}) custom-call(bf16[384,1024]{1,0:T(8,128)(2,1)S(1)} %copy-done.22, f32[1,1024]{1,0:T(1,128)S(1)} %bitcast.65, bf16[1024,2048]{1,0:T(8,128)(2,1)} %all-gather.5.cloned.1.call-done.w_ref, f32[384,128]{1,0:T(8,128)S(1)} %copy-done.38, f32[384,128]{1,0:T(8,128)S(1)} %copy-done.36, ...), custom_call_target="tpu_custom_call" | custom-call | flops 120000000 | bytes 334315 | tf_op jit(solution)/shard_map/attn_bwd/pallas_call | solution.py:44
  392.0 4.7 all-to-all-start.1
  400.6 4.5 out_o.1
  405.1 32.0 %collective-permute-done.37 = bf16[192,1024]{1,0:T(8,128)(2,1)S(1)} collective-permute-done((bf16[192,1024]{1,0:T(8,128)(2,1)S(1)}, bf16[192,1024]{1,0:T(8,128)(2,1)S(1)}, u32[]{:S(2)}, u32[]{:S(2)}) %collective-permute-start.37) | collective-permute-done | bytes 393248 | tf_op jit(solution)/shard_map/ppermute | solution.py:401
  466.8 6.9 %collective-permute-done.41 = bf16[128,640]{1,0:T(8,128)(2,1)S(1)} collective-permute-done((bf16[128,640]{1,0:T(8,128)(2,1)S(1)}, bf16[128,640]{1,0:T(8,128)(2,1)S(1)}, u32[]{:S(2)}, u32[]{:S(2)}) %collective-permute-start.41) | collective-permute-done | bytes 163872 | tf_op jit(solution)/shard_map/ppermute | solution.py:421
  (330 shorter events, 165.7 us)
Async XLA Ops:
  7.2 93.9 %all-gather.5.cloned.1.call-start = ((), (), s32[]{:S(2)}) async-start(), calls=%async_computation.4 | async-start | bytes 4718592 | tf_op jit(solution)/shard_map/all_gather | solution.py:442
  30.2 93.2 %collective-permute-start.7 = (bf16[384,1024]{1,0:T(8,128)(2,1)}, bf16[384,1024]{1,0:T(8,128)(2,1)}, u32[]{:S(2)}, u32[]{:S(2)}) collective-permute-start(bf16[384,1024]{1,0:T(8,128)(2,1)} %dy_ref.1), channel_id=1, source_target_pairs={{0,4},{1,5},{2,6},{3,7},{4,0},{5,1},{6,2},{7,3},{8,12},{9,13},{10,... | collective-permute-start | bytes 2359304 | tf_op jit(solution)/shard_map/ppermute | solution.py:404
  31.8 91.6 %collective-permute-start.6 = (bf16[384,1024]{1,0:T(8,128)(2,1)}, bf16[384,1024]{1,0:T(8,128)(2,1)}, u32[]{:S(2)}, u32[]{:S(2)}) collective-permute-start(bf16[384,1024]{1,0:T(8,128)(2,1)} %dy_ref.1), channel_id=1, source_target_pairs={{0,2},{1,3},{2,0},{3,1},{4,6},{5,7},{6,4},{7,5},{8,10},{9,11},{10,... | collective-permute-start | bytes 2359304 | tf_op jit(solution)/shard_map/ppermute | solution.py:401
  36.1 60.2 %all-to-all-start = ((bf16[8,128,768]{1,2,0:T(8,128)(2,1)}), bf16[8,128,768]{1,2,0:T(8,128)(2,1)S(1)}, u32[]{:S(2)}, u32[]{:S(2)}) async-start(bf16[8,128,768]{1,2,0:T(8,128)(2,1)} %bitcast.3), calls=%async_computation | async-start | bytes 3145728 | tf_op jit(solution)/shard_map/all_to_all | solution.py:467
  39.9 95.7 %all-gather.7.cloned.1.call-start = ((), (), s32[]{:S(2)}) async-start(), calls=%async_computation.5 | async-start | bytes 2359296 | tf_op jit(solution)/shard_map/all_gather | solution.py:445
  56.5 382.0 %reduce-scatter.5.cloned.1.call-start = ((), (), s32[]{:S(2)}) async-start(), calls=%async_computation.7 | async-start | bytes 2654208 | tf_op jit(solution)/shard_map/reduce_scatter | solution.py:556
  97.0 37.8 %collective-permute-start.10 = (bf16[1024,768]{1,0:T(8,128)(2,1)S(1)}, bf16[1024,768]{1,0:T(8,128)(2,1)S(1)}, u32[]{:S(2)}, u32[]{:S(2)}) collective-permute-start(bf16[1024,768]{1,0:T(8,128)(2,1)S(1)} %bitcast.55), channel_id=1, source_target_pairs={{0,8},{8,24},{24,16},{16,0},{1,9},{9,25},{25,17},{17,1},{2,10},{10... | collective-permute-start | bytes 4718600 | tf_op jit(solution)/shard_map/ppermute | solution.py:398
  134.8 39.7 %collective-permute-start.16 = (bf16[1024,768]{1,0:T(8,128)(2,1)S(1)}, bf16[1024,768]{1,0:T(8,128)(2,1)}, u32[]{:S(2)}, u32[]{:S(2)}) collective-permute-start(bf16[1024,768]{1,0:T(8,128)(2,1)S(1)} %collective-permute-done.10.w0.refs_6_), channel_id=1, source_target_pairs={{0,8},{8,24},{24,16},{16,0},{1,9},{9,25},{25,17},{17,1},{2,10},{10... | collective-permute-start | bytes 4718600 | tf_op jit(solution)/shard_map/ppermute | solution.py:398
  143.3 43.8 %collective-permute-start.20 = (bf16[1024,768]{1,0:T(8,128)(2,1)S(1)}, bf16[1024,768]{1,0:T(8,128)(2,1)}, u32[]{:S(2)}, u32[]{:S(2)}) collective-permute-start(bf16[1024,768]{1,0:T(8,128)(2,1)S(1)} %collective-permute-done.10.w0.refs_6_), channel_id=1, source_target_pairs={{0,1},{1,0},{2,3},{3,2},{4,5},{5,4},{6,7},{7,6},{8,9},{9,8},{10,11... | collective-permute-start | bytes 4718600 | tf_op jit(solution)/shard_map/ppermute | solution.py:410
  174.5 37.1 %collective-permute-start.17 = (bf16[1024,768]{1,0:T(8,128)(2,1)}, bf16[1024,768]{1,0:T(8,128)(2,1)}, u32[]{:S(2)}, u32[]{:S(2)}) collective-permute-start(bf16[1024,768]{1,0:T(8,128)(2,1)} %collective-permute-done.16.w0.refs_8_), channel_id=1, source_target_pairs={{0,8},{8,24},{24,16},{16,0},{1,9},{9,25},{25,17},{17,1},{2,10},{10... | collective-permute-start | bytes 4718600 | tf_op jit(solution)/shard_map/ppermute | solution.py:398
  206.6 47.5 %collective-permute-start.15 = (bf16[1024,768]{1,0:T(8,128)(2,1)S(1)}, bf16[1024,768]{1,0:T(8,128)(2,1)S(1)}, u32[]{:S(2)}, u32[]{:S(2)}) collective-permute-start(bf16[1024,768]{1,0:T(8,128)(2,1)S(1)} %bitcast.56), channel_id=1, source_target_pairs={{0,1},{1,0},{2,3},{3,2},{4,5},{5,4},{6,7},{7,6},{8,9},{9,8},{10,11... | collective-permute-start | bytes 4718600 | tf_op jit(solution)/shard_map/ppermute | solution.py:410
  211.6 25.2 %collective-permute-start.18 = (bf16[1024,768]{1,0:T(8,128)(2,1)}, bf16[1024,768]{1,0:T(8,128)(2,1)}, u32[]{:S(2)}, u32[]{:S(2)}) collective-permute-start(bf16[1024,768]{1,0:T(8,128)(2,1)} %collective-permute-done.17.w0.refs_10_), channel_id=1, source_target_pairs={{0,1},{1,0},{2,3},{3,2},{4,5},{5,4},{6,7},{7,6},{8,9},{9,8},{10,11... | collective-permute-start | bytes 4718600 | tf_op jit(solution)/shard_map/ppermute | solution.py:410
  215.0 57.8 %collective-permute-start.22 = (bf16[1024,768]{1,0:T(8,128)(2,1)}, bf16[1024,768]{1,0:T(8,128)(2,1)}, u32[]{:S(2)}, u32[]{:S(2)}) collective-permute-start(bf16[1024,768]{1,0:T(8,128)(2,1)} %add_convert_fusion.3), channel_id=1, source_target_pairs={{0,8},{8,24},{24,16},{16,0},{1,9},{9,25},{25,17},{17,1},{2,10},{10... | collective-permute-start | bytes 4718600 | tf_op jit(solution)/shard_map/ppermute | solution.py:398
  235.2 48.2 %collective-permute-start.23 = (bf16[1024,768]{1,0:T(8,128)(2,1)}, bf16[1024,768]{1,0:T(8,128)(2,1)}, u32[]{:S(2)}, u32[]{:S(2)}) collective-permute-start(bf16[1024,768]{1,0:T(8,128)(2,1)} %get-tuple-element.108), channel_id=1, source_target_pairs={{0,1},{1,0},{2,3},{3,2},{4,5},{5,4},{6,7},{7,6},{8,9},{9,8},{10,11... | collective-permute-start | bytes 4718600 | tf_op jit(solution)/shard_map/ppermute | solution.py:410
  287.0 39.5 %collective-permute-start.24 = (bf16[1024,768]{1,0:T(8,128)(2,1)}, bf16[1024,768]{1,0:T(8,128)(2,1)S(1)}, u32[]{:S(2)}, u32[]{:S(2)}) collective-permute-start(bf16[1024,768]{1,0:T(8,128)(2,1)} %add_convert_fusion.2), channel_id=1, source_target_pairs={{0,8},{8,24},{24,16},{16,0},{1,9},{9,25},{25,17},{17,1},{2,10},{10... | collective-permute-start | bytes 4718600 | tf_op jit(solution)/shard_map/ppermute | solution.py:398
  336.6 121.2 %reduce-scatter.3.cloned.1.call-start = ((), (), s32[]{:S(2)}) async-start(), calls=%async_computation.6 | async-start | bytes 5013504 | tf_op jit(solution)/shard_map/reduce_scatter | solution.py:573
  343.1 39.1 %collective-permute-start.34 = (bf16[1024,768]{1,0:T(8,128)(2,1)S(1)}, bf16[1024,768]{1,0:T(8,128)(2,1)}, u32[]{:S(2)}, u32[]{:S(2)}) collective-permute-start(bf16[1024,768]{1,0:T(8,128)(2,1)S(1)} %add_convert_fusion.1), channel_id=1, source_target_pairs={{0,8},{8,24},{24,16},{16,0},{1,9},{9,25},{25,17},{17,1},{2,10},{10... | collective-permute-start | bytes 4718600 | tf_op jit(solution)/shard_map/ppermute | solution.py:398
  343.6 38.6 %collective-permute-start.31 = (bf16[192,1024]{1,0:T(8,128)(2,1)S(1)}, bf16[192,1024]{1,0:T(8,128)(2,1)S(1)}, u32[]{:S(2)}, u32[]{:S(2)}) collective-permute-start(bf16[192,1024]{1,0:T(8,128)(2,1)S(1)} %get-tuple-element.131), channel_id=1, source_target_pairs={{0,2},{1,3},{2,0},{3,1},{4,6},{5,7},{6,4},{7,5},{8,10},{9,11},{10,... | collective-permute-start | bytes 1179656 | tf_op jit(solution)/shard_map/ppermute | solution.py:401
  344.3 37.8 %collective-permute-start.32 = (bf16[192,1024]{1,0:T(8,128)(2,1)S(1)}, bf16[192,1024]{1,0:T(8,128)(2,1)S(1)}, u32[]{:S(2)}, u32[]{:S(2)}) collective-permute-start(bf16[192,1024]{1,0:T(8,128)(2,1)S(1)} %get-tuple-element.132), channel_id=1, source_target_pairs={{0,4},{1,5},{2,6},{3,7},{4,0},{5,1},{6,2},{7,3},{8,12},{9,13},{10,... | collective-permute-start | bytes 1179656 | tf_op jit(solution)/shard_map/ppermute | solution.py:404
  345.4 36.8 %collective-permute-start.35 = (bf16[192,1024]{1,0:T(8,128)(2,1)S(1)}, bf16[192,1024]{1,0:T(8,128)(2,1)S(1)}, u32[]{:S(2)}, u32[]{:S(2)}) collective-permute-start(bf16[192,1024]{1,0:T(8,128)(2,1)S(1)} %get-tuple-element.136), channel_id=1, source_target_pairs={{0,2},{1,3},{2,0},{3,1},{4,6},{5,7},{6,4},{7,5},{8,10},{9,11},{10,... | collective-permute-start | bytes 1179656 | tf_op jit(solution)/shard_map/ppermute | solution.py:401
  346.7 35.5 %collective-permute-start.36 = (bf16[192,1024]{1,0:T(8,128)(2,1)S(1)}, bf16[192,1024]{1,0:T(8,128)(2,1)S(1)}, u32[]{:S(2)}, u32[]{:S(2)}) collective-permute-start(bf16[192,1024]{1,0:T(8,128)(2,1)S(1)} %get-tuple-element.137), channel_id=1, source_target_pairs={{0,4},{1,5},{2,6},{3,7},{4,0},{5,1},{6,2},{7,3},{8,12},{9,13},{10,... | collective-permute-start | bytes 1179656 | tf_op jit(solution)/shard_map/ppermute | solution.py:404
  392.0 56.1 %all-to-all-start.1 = ((bf16[8,128,768]{1,2,0:T(8,128)(2,1)}), bf16[8,128,768]{1,2,0:T(8,128)(2,1)}, u32[]{:S(2)}, u32[]{:S(2)}) async-start(bf16[8,128,768]{1,2,0:T(8,128)(2,1)} %copy.89), calls=%async_computation.3 | async-start | bytes 3145728 | tf_op jit(solution)/shard_map/all_to_all | solution.py:583
  396.9 40.2 %collective-permute-start.37 = (bf16[192,1024]{1,0:T(8,128)(2,1)S(1)}, bf16[192,1024]{1,0:T(8,128)(2,1)S(1)}, u32[]{:S(2)}, u32[]{:S(2)}) collective-permute-start(bf16[192,1024]{1,0:T(8,128)(2,1)S(1)} %add_convert_fusion.8), channel_id=1, source_target_pairs={{0,2},{1,3},{2,0},{3,1},{4,6},{5,7},{6,4},{7,5},{8,10},{9,11},{10,... | collective-permute-start | bytes 1179656 | tf_op jit(solution)/shard_map/ppermute | solution.py:401
  399.1 38.0 %collective-permute-start.38 = (bf16[192,1024]{1,0:T(8,128)(2,1)S(1)}, bf16[192,1024]{1,0:T(8,128)(2,1)S(1)}, u32[]{:S(2)}, u32[]{:S(2)}) collective-permute-start(bf16[192,1024]{1,0:T(8,128)(2,1)S(1)} %add_convert_fusion.7), channel_id=1, source_target_pairs={{0,4},{1,5},{2,6},{3,7},{4,0},{5,1},{6,2},{7,3},{8,12},{9,13},{10,... | collective-permute-start | bytes 1179656 | tf_op jit(solution)/shard_map/ppermute | solution.py:404
  (100 other events, 1085.9 us)
Sparse Core Ops, SparseCore 0:
  30.3 52.9 all-gather.4
  85.8 28.4 all-gather.6
  336.7 45.3 reduce-scatter.4
  385.9 66.1 reduce-scatter.2

commit v3 on v1

v3 whole, which is shorter than its diff:
```python
import math

import jax
import jax.numpy as jnp
from jax import lax
from jax.experimental import pallas as pl
from jax.experimental.pallas import tpu as pltpu
from jax.sharding import PartitionSpec as P

MODEL_WIDTH = 1024
HEAD_SIZE = 64
FF = 512
HALF = FF // 2
EXPERTS = 16
T = 384
LANES = 128
EPSILON = 1e-06
ROPE_BASE = 10000.0
NEG_FILL = -1e30
SCALE = 1.0 / math.sqrt(HEAD_SIZE)
BF = jnp.bfloat16
F32 = jnp.float32
COST = 0.02
VMEM_MIB = 62

NT = (((1,), (1,)), ((), ()))
TN = (((0,), (0,)), ((), ()))

VM = pl.BlockSpec(memory_space=pltpu.VMEM)
SM = pl.BlockSpec(memory_space=pltpu.SMEM)
HB = pl.BlockSpec(memory_space=pltpu.HBM)


def dot(a, b):
    return jnp.dot(a, b, preferred_element_type=F32)


def dotg(a, b, dims, **kw):
    return lax.dot_general(a, b, dims, preferred_element_type=F32, **kw)


def call(body, outs, in_specs, out_specs, scratch, args, name, vmem=48, flops=0):
    nbytes = sum(math.prod(a.shape) * a.dtype.itemsize for a in args)
    nbytes += sum(math.prod(s) * jnp.dtype(d).itemsize for s, d in outs)
    return pl.pallas_call(
        body,
        out_shape=[jax.ShapeDtypeStruct(s, d) for s, d in outs],
        in_specs=in_specs,
        out_specs=out_specs,
        scratch_shapes=scratch,
        compiler_params=pltpu.CompilerParams(vmem_limit_bytes=VMEM_MIB << 20),
        cost_estimate=pl.CostEstimate(
            flops=int(flops * COST), transcendentals=0, bytes_accessed=int(nbytes * COST)
        ),
        name=name,
    )(*args)


def after(x, *deps):
    return lax.optimization_barrier((x, *deps))[0]


def low_half(shape):
    return lax.broadcasted_iota(jnp.int32, shape, 1) < HEAD_SIZE


def turn(part, cos, sin, first):
    partner = jnp.where(first, pltpu.roll(part, 96, 1), pltpu.roll(part, 32, 1))
    return part * cos + partner * sin


def first_of_head(shape):
    return (lax.broadcasted_iota(jnp.int32, shape, 1) % HEAD_SIZE) < HEAD_SIZE // 2


def attn_rows(qkv_ref, bias_ref, b, c, low):
    rows = slice(c * LANES, (c + 1) * LANES)
    seen = (c + 1) * LANES
    qa = qkv_ref[b, rows, 0:LANES]
    qb = qkv_ref[b, rows, LANES : 2 * LANES]
    zero = jnp.zeros_like(qa)
    q = jnp.concatenate(
        [jnp.where(low, qa, zero), jnp.where(low, qb, zero), jnp.where(low, zero, qa), jnp.where(low, zero, qb)], axis=0
    )
    keys = qkv_ref[b, :seen, 256:384]
    bias = bias_ref[rows, :seen]
    s = dotg(q, keys, NT) * SCALE + jnp.concatenate([bias] * 4, axis=0)
    p = jnp.exp(s - jnp.max(s, axis=1, keepdims=True))
    p = p * (1.0 / jnp.sum(p, axis=1, keepdims=True))
    return rows, seen, q, keys, p


def fetch(pairs, sems, first=0):
    copies = [pltpu.make_async_copy(a, b, sems.at[first + i]) for i, (a, b) in enumerate(pairs)]
    for c in copies:
        c.start()
    return copies


def wait(copies):
    for c in copies:
        c.wait()


def attn_fwd(places, dr):
    n = len(places)

    def body(mine_ref, *refs):
        pieces = refs[:n]
        x_h, cos_h, sin_h, bias_h, wo_h = refs[n : n + 5]
        w_h, n1_h, qkv_h, att_h, h1_h, n2_h, rows_h = refs[n + 5 : n + 12]
        x, cos, sin, bias, wo, w, n1, qkv, att, h1, n2, small, si, so = refs[n + 12 :]
        mine = mine_ref[0]
        pairs = [(x_h, x), (cos_h, cos), (sin_h, sin)]
        for p, (bits, off, rows) in zip(pieces, places):
            at = 0 if bits is None else pl.multiple_of((mine ^ bits) * dr + off, math.gcd(dr, off))
            pairs.append((p, w.at[pl.ds(at, rows)]))
        pairs += [(bias_h, bias), (wo_h, wo)]
        copies = fetch(pairs, si)
        wait(copies[:-1])
        outs = fetch([(w.at[:, 0:2048], w_h)], so)
        small[...] = w[:, 2048:2176].astype(F32).T
        outs += fetch([(small, rows_h)], so, 7)
        attn_fwd_body(x, small.at[16:17], w, cos, sin, bias, n1, qkv, att)
        outs += fetch([(n1, n1_h), (qkv, qkv_h), (att, att_h)], so, 1)
        copies[-1].wait()
        mid(x, att, wo, small.at[17:18], h1, n2)
        outs += fetch([(n2, n2_h), (h1, h1_h)], so, 4)
        wait(outs)

    return body


def attn_fwd_body(x_ref, gain_ref, w_ref, cos_ref, sin_ref, bias_ref, n1_ref, qkv_ref, att_ref):
    x = x_ref[...].astype(F32)
    r1 = lax.rsqrt(jnp.mean(x * x, axis=1, keepdims=True) + EPSILON)
    n1 = (x * r1 * gain_ref[...]).astype(BF)
    n1_ref[...] = n1
    cos = cos_ref[...]
    sin = sin_ref[...]
    first = first_of_head((T, LANES))
    low = low_half((LANES, LANES))
    for b in range(4):
        raw = dot(n1, w_ref[:, b * 512 : (b + 1) * 512])
        for s in range(4):
            part = raw[:, s * LANES : (s + 1) * LANES]
            if s < 3:
                part = turn(part, cos, sin, first)
            qkv_ref[b, :, s * LANES : (s + 1) * LANES] = part.astype(BF)

    def block(b, carry):
        for c in range(3):
            rows, seen, q, keys, p = attn_rows(qkv_ref, bias_ref, b, c, low)
            o = dot(p.astype(BF), qkv_ref[b, :seen, 384:512])
            att_ref[b, rows, 0:LANES] = jnp.where(low, o[0:LANES], o[2 * LANES : 3 * LANES]).astype(BF)
            att_ref[b, rows, LANES : 2 * LANES] = jnp.where(low, o[LANES : 2 * LANES], o[3 * LANES :]).astype(BF)
        return carry

    for b in range(4):
        block(b, 0)


def soft_gates(n2, rt, mask):
    logits = dotg(n2, rt, NT)
    top = jnp.max(jnp.where(mask > 0, logits, NEG_FILL), axis=1, keepdims=True)
    e = jnp.where(mask > 0, jnp.exp(jnp.minimum(logits - top, 0.0)), 0.0)
    return e / jnp.sum(e, axis=1, keepdims=True)


def route_mask(routes):
    ids = lax.broadcasted_iota(jnp.int32, (LANES, T), 0).astype(F32)
    hit = jnp.zeros((LANES, T), F32)
    for i in range(8):
        hit = hit + jnp.where(ids == routes[i : i + 1, :], 1.0, 0.0)
    return hit.T


def mid(x_ref, att_ref, wo_ref, gain_ref, h1_ref, n2_ref):
    att = jnp.concatenate([att_ref[b] for b in range(4)], axis=1)
    h1 = x_ref[...].astype(F32) + dotg(att, wo_ref[...], NT)
    h1_ref[...] = h1
    r2 = lax.rsqrt(jnp.mean(h1 * h1, axis=1, keepdims=True) + EPSILON)
    n2_ref[...] = (h1 * r2 * gain_ref[...]).astype(BF)


ROWS = 4 * T
WIDE = 2 * HALF
UNIT = 3 * HALF
TREE = [slice(t * T, (t + 1) * T) for t in range(4)]


def token_pairs(srcs, dst):
    pairs, at = [], 0
    for r in srcs:
        pairs.append((r, dst.at[at : at + r.shape[0]]))
        at += r.shape[0]
    return pairs


def chip_pairs(src, chip, dst):
    return [
        (src.at[pl.ds(pl.multiple_of((chip ^ t) * T, T), T)], dst.at[t * T : (t + 1) * T]) for t in range(4)
    ]


def tree_waits(hx, hy):
    return [hx[0:1] + hy[0:1], hx[1:2] + hy[1:2], hx[2:3] + hy[2:3], hx[3:] + hy[3:]]


def act(t, e, X, Y, W, GT, GH, DGU):
    rows = TREE[t]
    lanes = lax.broadcasted_iota(jnp.int32, (T, LANES), 1)
    gate = jnp.sum(jnp.where(lanes == e, GT[rows, :], 0.0), axis=1, keepdims=True)
    dgate = jnp.zeros((T, 1), F32)
    for u in range(2):
        gu = dot(X[rows, :], W[u, :, 0:WIDE])
        dh = dot(Y[rows, :], W[u, :, WIDE:UNIT])
        g = gu[:, :HALF]
        up = gu[:, HALF:]
        s = 0.5 * jnp.tanh(0.5 * g) + 0.5
        silu = g * s
        hid = silu * up
        GH[rows, u * HALF : (u + 1) * HALF] = (gate * hid).astype(BF)
        dgate = dgate + jnp.sum(dh * hid, axis=1, keepdims=True)
        dh = dh * gate
        base = u * WIDE
        DGU[rows, base : base + HALF] = (dh * up * (s + silu * (1.0 - s))).astype(BF)
        DGU[rows, base + HALF : base + WIDE] = (dh * silu).astype(BF)
    return jnp.where(lanes == e, dgate, 0.0)


def wgrad(X, Y, GH, DGU, DW):
    step = 256
    for r in range(MODEL_WIDTH // step):
        cols = slice(r * step, (r + 1) * step)
        dg = dotg(X[:, cols], DGU[...], TN)
        dd = dotg(Y[:, cols], GH[...], TN)
        for u in range(2):
            DW[u, cols, 0:WIDE] = dg[:, u * WIDE : (u + 1) * WIDE].astype(BF)
            DW[u, cols, WIDE:UNIT] = dd[:, u * HALF : (u + 1) * HALF].astype(BF)


def stage_scratch(n, extra, loads, stores):
    return [
        pltpu.VMEM((ROWS, MODEL_WIDTH), BF), pltpu.VMEM((ROWS, MODEL_WIDTH), BF),
        pltpu.VMEM((n, 2, MODEL_WIDTH, UNIT), BF),
        pltpu.VMEM((n, ROWS, FF), BF), pltpu.VMEM((n, ROWS, 2 * FF), BF),
        pltpu.VMEM((ROWS, LANES), F32), pltpu.VMEM((ROWS, LANES), F32),
        *extra,
        pltpu.SemaphoreType.DMA((loads,)), pltpu.SemaphoreType.DMA((stores,)),
    ]


def load_tokens(xs, dyg, chip, X, Y, head, rest, si):
    px, py = token_pairs(xs, X), chip_pairs(dyg, chip, Y)
    order = px[0:1] + head + py[0:1] + px[1:] + py[1:] + rest
    copies = fetch(order, si)
    n = 1 + len(head)
    cx = copies[0:1] + copies[n + 1 : n + 5]
    cy = copies[n : n + 1] + copies[n + 5 : n + 8]
    return copies[1:n], tree_waits(cx, cy), copies[n + 8 :]


def stage_a(e_ref, *refs):
    xs, dyg, ws = refs[0:5], refs[5], refs[6:8]
    rt_h, routes = refs[8], refs[9:13]
    gh_h, dgu_h, dwo_h, dws_h, gates_h, dgate_h = refs[13:19]
    X, Y, W, GH, DGU, GT, DG, DW, rt, si, so = refs[19:]
    head, trees, _ = load_tokens(
        xs, dyg, e_ref[4], X, Y, [(rt_h, rt)] + [(ws[i], W.at[0, i]) for i in range(2)], [], si
    )
    wait(head)
    router = rt[...].astype(BF)
    for t in range(4):
        wait(trees[t])
        GT[TREE[t], :] = soft_gates(X[TREE[t], :], router, route_mask(routes[t][...].astype(F32)))
        DG[TREE[t], :] = act(t, e_ref[1], X, Y, W.at[0], GT, GH.at[0], DGU.at[0])
    outs = fetch([(GH.at[0], gh_h), (DGU.at[0], dgu_h), (GT, gates_h), (DG, dgate_h)], so)
    wgrad(X, Y, GH.at[0], DGU.at[0], DW)
    outs += fetch([(DW.at[0], dwo_h), (DW.at[1], dws_h)], so, 4)
    wait(outs)


ACT_OUT = [((ROWS, FF), BF), ((ROWS, 2 * FF), BF)]
GATE_OUT = [((ROWS, LANES), F32)]
DW_OUT = [((MODEL_WIDTH, UNIT), BF)] * 2
DW_VMEM = pltpu.VMEM((2, MODEL_WIDTH, UNIT), BF)
EXPERT_FLOPS = 2 * ROWS * MODEL_WIDTH * 3 * FF


def run_stage_a(e, xs, dyg, pair, rt, routes):
    extra = [DW_VMEM, pltpu.VMEM((LANES, MODEL_WIDTH), F32)]
    return call(
        stage_a, ACT_OUT + DW_OUT + GATE_OUT * 2, [SM] + [HB] * 9 + [VM] * 4, [HB] * 6,
        stage_scratch(1, extra, 12, 6), (e, *xs, dyg, *pair, rt, *routes), "stage_a", 48, 2 * EXPERT_FLOPS,
    )


def stage_b(e_ref, *refs):
    xs, dyg, ws = refs[0:5], refs[5], refs[6:10]
    gates_h, dgate_i = refs[10:12]
    gh0_h, dgu0_h, gh2_h, dgu2_h, dgate_h, dwo_h, dws_h = refs[12:19]
    X, Y, W, GH, DGU, GT, DG, DW, si, so = refs[19:]
    hw = [(ws[i], W.at[i // 2, i % 2]) for i in range(4)]
    head, trees, second = load_tokens(
        xs, dyg, e_ref[4], X, Y, hw[0:2] + [(gates_h, GT), (dgate_i, DG)], hw[2:], si
    )
    wait(head)
    for t in range(4):
        wait(trees[t])
        DG[TREE[t], :] += act(t, e_ref[0], X, Y, W.at[0], GT, GH.at[0], DGU.at[0])
    outs = fetch([(GH.at[0], gh0_h), (DGU.at[0], dgu0_h)], so)
    wait(second)
    for t in range(4):
        DG[TREE[t], :] += act(t, e_ref[2], X, Y, W.at[1], GT, GH.at[1], DGU.at[1])
    outs += fetch([(GH.at[1], gh2_h), (DGU.at[1], dgu2_h), (DG, dgate_h)], so, 2)
    wgrad(X, Y, GH.at[1], DGU.at[1], DW)
    outs += fetch([(DW.at[0], dwo_h), (DW.at[1], dws_h)], so, 5)
    wait(outs)


def run_stage_b(e, xs, dyg, ws, gates, dgate):
    return call(
        stage_b, ACT_OUT * 2 + GATE_OUT + DW_OUT, [SM] + [HB] * 12, [HB] * 7,
        stage_scratch(2, [DW_VMEM], 15, 7), (e, *xs, dyg, *ws, gates, dgate), "stage_b", 48, 3 * EXPERT_FLOPS,
    )


def stage_c(e_ref, *refs):
    xs, dyg, ws = refs[0:5], refs[5], refs[6:14]
    gates_h, dgate_i = refs[14:16]
    dgus = refs[16:19]
    gh_h, dgu_h, dgate_h, parts_h = refs[19:23]
    X, Y, W, GH, DGU, GT, DG, WB, DF, OUT, si, so = refs[23:]
    late = [(ws[i].at[:, 0:WIDE], WB.at[:, i * WIDE : (i + 1) * WIDE]) for i in range(6)]
    late += [(dgus[i].at[T:ROWS], DF.at[:, 2 * i * FF : 2 * (i + 1) * FF]) for i in range(3)]
    head, trees, late = load_tokens(
        xs, dyg, e_ref[4], X, Y,
        [(ws[6 + i], W.at[0, i]) for i in range(2)] + [(gates_h, GT), (dgate_i, DG)], late, si,
    )
    wait(head)
    for t in range(4):
        wait(trees[t])
        DG[TREE[t], :] += act(t, e_ref[3], X, Y, W.at[0], GT, GH.at[0], DGU.at[0])
    outs = fetch([(GH.at[0], gh_h), (DGU.at[0], dgu_h), (DG, dgate_h)], so)
    wait(late)
    w = jnp.concatenate([WB[...]] + [W[0, i, :, 0:WIDE] for i in range(2)], axis=1)
    for i, t in enumerate((3, 1, 2)):
        a = jnp.concatenate([DF[TREE[t - 1], :], DGU[0, TREE[t], :]], axis=1)
        OUT[i, :, 0:MODEL_WIDTH] = dotg(a, w, NT).astype(BF)
        OUT[i, :, MODEL_WIDTH:] = DG[TREE[t], :].astype(BF)
        outs += fetch([(OUT.at[i], parts_h.at[e_ref[4] ^ t])], so, 3 + i)
    wait(outs)


def run_stage_c(e, xs, dyg, ws, gates, dgate, dgus):
    cols = MODEL_WIDTH + LANES
    extra = [
        pltpu.VMEM((MODEL_WIDTH, 6 * WIDE), BF), pltpu.VMEM((3 * T, 6 * FF), BF), pltpu.VMEM((3, T, cols), BF),
    ]
    return call(
        stage_c, ACT_OUT + GATE_OUT + [((4, T, cols), BF)], [SM] + [HB] * 19, [HB] * 4,
        stage_scratch(1, extra, 22, 6), (e, *xs, dyg, *ws, gates, dgate, *dgus), "stage_c", 48, 2 * EXPERT_FLOPS,
    )


def back_pairs(acts, ws, lo, m, width, first_col, A, W):
    pairs = []
    for k in range(4):
        pairs.append((acts[k].at[lo : lo + m], A.at[:, k * 2 * width : (k + 1) * 2 * width]))
        for u in range(2):
            at = (2 * k + u) * width
            pairs.append((ws[2 * k + u].at[:, first_col : first_col + width], W.at[:, at : at + width]))
    return pairs


def late_stage(n, own):
    def body(e_ref, *refs):
        xs, dyg, acts = refs[0:5], refs[5], refs[6 : 6 + 2 * n]
        refs = refs[6 + 2 * n :]
        pairs = []
        if own:
            dgus, ws, dgate_h = refs[0:4], refs[4:12], refs[12]
            refs = refs[13:]
        dws, refs = refs[: 2 * n], refs[2 * n :]
        if own:
            own_h, refs = refs[0], refs[1:]
        X, Y, GH, DGU, DW, si, so = refs[:7]
        if own:
            A, W, DG, O = refs[7:]
            pairs = back_pairs(dgus, ws, 0, T, WIDE, 0, A, W) + [(dgate_h.at[0:T], DG)]
        first = len(pairs)
        pairs += chip_pairs(dyg, e_ref[4], Y) + [(acts[0], GH.at[0])] + token_pairs(xs, X) + [(acts[1], DGU.at[0])]
        for i in range(1, n):
            pairs += [(acts[2 * i], GH.at[i]), (acts[2 * i + 1], DGU.at[i])]
        copies = fetch(pairs, si)
        outs = []
        if own:
            wait(copies[:first])
            O[:, 0:MODEL_WIDTH] = dotg(A[...], W[...], NT)
            O[:, MODEL_WIDTH:] = DG[...]
            outs += fetch([(O, own_h)], so, 2 * n)
        for i in range(n):
            wait(copies[first + (11 if i else 0) + 2 * (i - 1) * (i > 0) : first + 11 + 2 * i])
            wgrad(X, Y, GH.at[i], DGU.at[i], DW.at[i])
            outs += fetch([(DW.at[i, 0], dws[2 * i]), (DW.at[i, 1], dws[2 * i + 1])], so, 2 * i)
        wait(outs)

    return body


def run_late(e, xs, dyg, acts, back=()):
    n = len(acts) // 2
    cols = MODEL_WIDTH + LANES
    args = (e, *xs, dyg, *acts, *back)
    outs = DW_OUT * n
    scratch = [
        pltpu.VMEM((ROWS, MODEL_WIDTH), BF), pltpu.VMEM((ROWS, MODEL_WIDTH), BF),
        pltpu.VMEM((n, ROWS, FF), BF), pltpu.VMEM((n, ROWS, 2 * FF), BF),
        pltpu.VMEM((n, 2, MODEL_WIDTH, UNIT), BF),
        pltpu.SemaphoreType.DMA((22 + 2 * n,)), pltpu.SemaphoreType.DMA((2 * n + 1,)),
    ]
    if back:
        outs = outs + [((T, cols), F32)]
        scratch += [
            pltpu.VMEM((T, 8 * WIDE), BF), pltpu.VMEM((MODEL_WIDTH, 8 * WIDE), BF),
            pltpu.VMEM((T, LANES), F32), pltpu.VMEM((T, cols), F32),
        ]
    return call(
        late_stage(n, bool(back)), outs, [SM] + [HB] * (len(args) - 1), [HB] * len(outs), scratch,
        args, "late_stage", 52, 2 * EXPERT_FLOPS,
    )


def last_stage(e_ref, *refs):
    xs, dyg, gh_h, dgu_h = refs[0:5], refs[5], refs[6], refs[7]
    ghs, ws = refs[8:12], refs[12:20]
    dwo_h, dws_h, parts_h, own_h = refs[20:24]
    X, Y, GH, DGU, DW, A, W, O, OF, si, so = refs[24:]
    pairs = chip_pairs(dyg, e_ref[4], Y) + [(gh_h, GH)] + token_pairs(xs, X) + [(dgu_h, DGU)]
    pairs += back_pairs(ghs, ws, 0, ROWS, HALF, WIDE, A, W)
    copies = fetch(pairs, si)
    wait(copies[:11])
    wgrad(X, Y, GH, DGU, DW)
    outs = fetch([(DW.at[0], dwo_h), (DW.at[1], dws_h)], so)
    wait(copies[11:])
    for i, t in enumerate((3, 1, 2, 0)):
        total = dotg(A[TREE[t], :], W[...], NT)
        dst = O.at[i] if t else OF
        dst[...] = total.astype(BF) if t else total
        outs += fetch([(dst, parts_h.at[e_ref[4] ^ t] if t else own_h)], so, 2 + i)
    wait(outs)


def run_last(e, xs, dyg, acts, ghs, ws):
    args = (e, *xs, dyg, *acts, *ghs, *ws)
    return call(
        last_stage, DW_OUT + [((4, T, MODEL_WIDTH), BF), ((T, MODEL_WIDTH), F32)],
        [SM] + [HB] * (len(args) - 1), [HB] * 4,
        [
            pltpu.VMEM((ROWS, MODEL_WIDTH), BF), pltpu.VMEM((ROWS, MODEL_WIDTH), BF),
            pltpu.VMEM((ROWS, FF), BF), pltpu.VMEM((ROWS, 2 * FF), BF), DW_VMEM,
            pltpu.VMEM((ROWS, 8 * HALF), BF), pltpu.VMEM((MODEL_WIDTH, 8 * HALF), BF),
            pltpu.VMEM((3, T, MODEL_WIDTH), BF), pltpu.VMEM((T, MODEL_WIDTH), F32),
            pltpu.SemaphoreType.DMA((23,)), pltpu.SemaphoreType.DMA((6,)),
        ],
        args, "last_stage", 52, 2 * EXPERT_FLOPS,
    )


def settle(dr):
    def body(home_h, gu_ref, dn_ref, H, sem):
        c = pltpu.make_async_copy(home_h, H, sem.at[0])
        c.start()
        c.wait()
        for e in range(4):
            for h in range(2):
                part = H[2 * e + h].astype(F32)
                cols = slice(h * HALF, (h + 1) * HALF)
                gu_ref[:, e, cols] = part[:, 0:HALF]
                gu_ref[:, e, FF + h * HALF : FF + (h + 1) * HALF] = part[:, HALF:WIDE]
                dn_ref[:, e, cols] = part[:, WIDE:UNIT]

    return body


def columns_of(rowwise, lane):
    total = jnp.sum(rowwise, axis=0, keepdims=True)
    total = jnp.broadcast_to(total, (LANES, MODEL_WIDTH)).T
    lanes = lax.broadcasted_iota(jnp.int32, total.shape, 1)
    return jnp.where(lanes == lane, total, 0.0)


def join(e_ref, p_h, parts_h, gates_h, h1_h, n2_h, dy_h, wo_h, att_h, small_h,
         dh1_h, datt_h, dwo_h, P, R, GT, H1, N2, DY, WO, ATT, SMALL, DH1, DATT, DWO, si, so):
    copies = fetch(
        [(p_h, P)] + [(parts_h.at[e_ref[4] ^ t], R.at[t - 1]) for t in (1, 2, 3)]
        + [(gates_h.at[0:T], GT), (h1_h, H1), (dy_h, DY),
         (small_h, SMALL), (wo_h, WO), (att_h, ATT), (n2_h, N2)], si
    )
    wait(copies[0:8])
    gates = GT[...]
    total = P[...] + R[0].astype(F32) + R[1].astype(F32) + R[2].astype(F32)
    dg = total[:, MODEL_WIDTH:]
    dl = (gates * (dg - jnp.sum(gates * dg, axis=1, keepdims=True))).astype(BF)
    dn2 = total[:, :MODEL_WIDTH] + dot(dl, SMALL[...].astype(BF))
    h1 = H1[...]
    gain = SMALL[17:18]
    r2 = lax.rsqrt(jnp.mean(h1 * h1, axis=1, keepdims=True) + EPSILON)
    gd = gain * dn2
    inner = jnp.mean(gd * h1, axis=1, keepdims=True)
    dh1 = DY[...].astype(F32) + r2 * gd - h1 * (r2 * r2 * r2 * inner)
    DH1[...] = dh1
    db = dh1.astype(BF)
    outs = fetch([(DH1, dh1_h)], so)
    wait(copies[8:])
    for b in range(4):
        cols = slice(b * 256, (b + 1) * 256)
        DATT[b] = dot(db, WO[:, cols]).astype(BF)
        DWO[:, cols] = dotg(db, ATT[b], TN).astype(BF)
    outs += fetch([(DATT, datt_h)], so, 1)
    extra = dotg(N2[...], dl, TN) + columns_of(dn2 * h1 * r2, EXPERTS)
    DWO[:, 1024:1152] = extra.astype(BF)
    outs += fetch([(DWO, dwo_h)], so, 2)
    wait(outs)


def run_join(args):
    cols = MODEL_WIDTH + LANES
    return call(
        join,
        [((T, MODEL_WIDTH), F32), ((4, T, 256), BF), ((MODEL_WIDTH, 1152), BF)],
        [SM] + [HB] * 9, [HB] * 3,
        [
            pltpu.VMEM((T, cols), F32), pltpu.VMEM((3, T, cols), BF), pltpu.VMEM((T, LANES), F32), pltpu.VMEM((T, MODEL_WIDTH), F32),
            pltpu.VMEM((T, MODEL_WIDTH), BF), pltpu.VMEM((T, MODEL_WIDTH), BF),
            pltpu.VMEM((MODEL_WIDTH, MODEL_WIDTH), BF), pltpu.VMEM((4, T, 256), BF),
            pltpu.VMEM((LANES, MODEL_WIDTH), F32),
            pltpu.VMEM((T, MODEL_WIDTH), F32), pltpu.VMEM((4, T, 256), BF), pltpu.VMEM((MODEL_WIDTH, 1152), BF),
            pltpu.SemaphoreType.DMA((12,)), pltpu.SemaphoreType.DMA((3,)),
        ],
        args, "join", 40, 2.0e9,
    )


def attn_bwd(split, dr):
    def body(mine_ref, x_h, w_h, cos_h, sin_h, bias_h, n1_h, qkv_h, datt_h, dh1_h, small_h, *refs):
        n = 3 if split else 2
        dx_h, grads_h = refs[0], refs[1:n]
        x, w, cos, sin, bias, n1, qkv, datt, dh1, gain, dx, dw, dqkv, dk, dv, si, so = refs[n : n + 17]
        copies = fetch(
            [(bias_h, bias), (qkv_h, qkv), (datt_h, datt), (cos_h, cos), (sin_h, sin), (n1_h, n1),
             (w_h, w), (x_h, x), (dh1_h, dh1), (small_h.at[16:24], gain)], si
        )
        wait(copies[0:5])
        attn_bwd_heads(cos, sin, bias, qkv, datt, dqkv, dk, dv)
        wait(copies[5:])
        attn_bwd_body(x, gain.at[0:1], w, n1, dh1, dx, dw, dqkv)
        outs = fetch([(dx, dx_h)], so)
        if split:
            for r in range(4):
                mine = 2 * r + (mine_ref[0] & 1)
                for i, j in enumerate((mine, mine ^ 1)):
                    src = dw.at[pl.ds(pl.multiple_of(j * dr, dr), dr)]
                    outs += fetch([(src, grads_h[i].at[r * dr : (r + 1) * dr])], so, 1 + 2 * r + i)
        else:
            outs += fetch([(dw, grads_h[0])], so, 1)
        wait(outs)

    return body


def run_attn_bwd(split, dr, args):
    grads = [((4 * dr, 2176), BF)] * 2 if split else [((MODEL_WIDTH, 2176), BF)]
    tile = pltpu.VMEM((T, LANES), F32)
    return call(
        attn_bwd(split, dr),
        [((T, MODEL_WIDTH), F32)] + grads,
        [SM] + [HB] * 10, [HB] * (1 + len(grads)),
        [
            pltpu.VMEM((T, MODEL_WIDTH), BF), pltpu.VMEM((MODEL_WIDTH, 2048), BF), tile, tile,
            pltpu.VMEM((T, T), F32), pltpu.VMEM((T, MODEL_WIDTH), BF), pltpu.VMEM((4, T, 512), BF),
            pltpu.VMEM((4, T, 256), BF), pltpu.VMEM((T, MODEL_WIDTH), F32), pltpu.VMEM((8, MODEL_WIDTH), F32),
            pltpu.VMEM((T, MODEL_WIDTH), F32),
            pltpu.VMEM((MODEL_WIDTH, 2176), BF), pltpu.VMEM((4, T, 512), BF), tile, tile,
            pltpu.SemaphoreType.DMA((10,)), pltpu.SemaphoreType.DMA((9,)),
        ],
        args, "attn_bwd", 40, 6.0e9,
    )


def attn_bwd_heads(cos_ref, sin_ref, bias_ref, qkv_ref, datt_ref, dqkv, dk, dv):
    low = low_half((LANES, LANES))
    first = first_of_head((T, LANES))

    def block(b, carry):
        for c in (2, 1, 0):
            rows, seen, q, keys, p = attn_rows(qkv_ref, bias_ref, b, c, low)
            da = datt_ref[b, rows, 0:LANES]
            db = datt_ref[b, rows, LANES : 2 * LANES]
            zero = jnp.zeros_like(da)
            do = jnp.concatenate(
                [jnp.where(low, da, zero), jnp.where(low, db, zero), jnp.where(low, zero, da), jnp.where(low, zero, db)],
                axis=0,
            )
            dp = dotg(do, qkv_ref[b, :seen, 384:512], NT)
            ds = (p * (dp - jnp.sum(p * dp, axis=1, keepdims=True))).astype(BF)
            dq = dot(ds, keys) * SCALE
            dkc = dotg(ds, q, TN)
            dvc = dotg(p.astype(BF), do, TN)
            if c == 2:
                dk[...] = dkc
                dv[...] = dvc
            else:
                dk[:seen] += dkc
                dv[:seen] += dvc
            cos = cos_ref[rows, :]
            sin = -sin_ref[rows, :]
            ta = jnp.where(low, dq[0:LANES], dq[2 * LANES : 3 * LANES])
            tb = jnp.where(low, dq[LANES : 2 * LANES], dq[3 * LANES :])
            dqkv[b, rows, 0:LANES] = turn(ta, cos, sin, first[rows]).astype(BF)
            dqkv[b, rows, LANES : 2 * LANES] = turn(tb, cos, sin, first[rows]).astype(BF)
        dqkv[b, :, 256:384] = turn(dk[...] * SCALE, cos_ref[...], -sin_ref[...], first).astype(BF)
        dqkv[b, :, 384:512] = dv[...].astype(BF)
        return carry

    for b in range(4):
        block(b, 0)


def attn_bwd_body(x_ref, gain_ref, w_ref, n1_ref, dh1_ref, dx_ref, dw_ref, dqkv):
    n1 = n1_ref[...]
    cat = jnp.concatenate([dqkv[b] for b in range(4)], axis=1)
    dn1 = dotg(cat, w_ref[...], NT)
    dw_ref[:, 0:2048] = dotg(n1, cat, TN).astype(BF)
    x = x_ref[...].astype(F32)
    gain = gain_ref[...]
    r1 = lax.rsqrt(jnp.mean(x * x, axis=1, keepdims=True) + EPSILON)
    gd = gain * dn1
    inner = jnp.mean(gd * x, axis=1, keepdims=True)
    dx_ref[...] = dh1_ref[...] + r1 * gd - x * (r1 * r1 * r1 * inner)
    dw_ref[:, 2048:2176] = columns_of(dn1 * x * r1, 0).astype(BF)
def visible_bias(segment, parents):
    ids = jnp.arange(parents.shape[0], dtype=jnp.int32)
    one = jnp.sum(jnp.where(segment[:, None] == ids[None, :], parents[None, :], 0), axis=1)
    two = jnp.sum(jnp.where(one[:, None] == ids[None, :], parents[None, :], 0), axis=1)
    key = segment[None, :]
    related = (key == segment[:, None]) | (key == one[:, None]) | (key == two[:, None])
    places = jnp.arange(segment.shape[0], dtype=jnp.int32)
    return jnp.where(related & (places[None, :] <= places[:, None]), 0.0, NEG_FILL).astype(F32)


def turn_tables(positions):
    half = HEAD_SIZE // 2
    lane = jnp.arange(LANES, dtype=jnp.int32)
    frequency = ROPE_BASE ** (-((lane % half).astype(F32) * 2.0) / HEAD_SIZE)
    angle = positions.astype(F32)[:, None] * frequency[None, :]
    sign = jnp.where(lane % HEAD_SIZE < half, -1.0, 1.0).astype(F32)
    return jnp.cos(angle), jnp.sin(angle) * sign[None, :]


def make_shards(groups, fsdp):
    ring = list(range(0, groups, 1))
    if groups == 4:
        ring = [0, 1, 3, 2]
    place = [ring.index(g) for g in range(groups)]
    rest = fsdp // 8

    def shifted(k):
        return [(ring[p], ring[(p + k) % groups]) for p in range(groups)]

    def flip(bits):
        return [(i, i ^ bits) for i in range(fsdp)]

    low_groups = None if rest == 1 else [[8 * r + j for j in range(8)] for r in range(rest)]
    core_groups = [[8 * r + 2 * c + k for c in range(4)] for r in range(rest) for k in range(2)]
    rest_groups = [[8 * r + j for r in range(rest)] for j in range(8)]

    def z_next(a):
        return lax.ppermute(a, "grp", shifted(1))

    def to_x(a):
        return lax.ppermute(a, "fsdp", flip(2))

    def to_y(a):
        return lax.ppermute(a, "fsdp", flip(4))

    def to_diag(a):
        return lax.ppermute(a, "fsdp", flip(6))

    def to_core(a):
        return lax.ppermute(a, "fsdp", flip(1))

    def plane(top, bot):
        xb = to_x(bot)
        yt = to_y(top)
        xt = to_x(top)
        yb = to_y(bot)
        return (top, bot, xt, xb, yt, yb, to_x(yt), to_y(xb))

    def swap(a):
        return lax.all_to_all(a, "fsdp", 0, 0, axis_index_groups=core_groups)

    def z_sum(blocks):
        total = blocks[0].astype(F32)
        for k in range(1, groups):
            total = total + lax.ppermute(blocks[k], "grp", shifted(groups - k)).astype(F32)
        return total

    def shards(tokens, segment, positions, parents, routes, attn_gain, query_weight, key_matrix,
               value_matrix, out_weight, ffn_gain, router_weight, gate_up_weight, down_weight, cotangent):
        dr = query_weight.shape[0]
        mine = lax.axis_index("fsdp")
        spot = jnp.array(place, jnp.int32)[lax.axis_index("grp")]
        ring_ids = jnp.array(ring, jnp.int32)

        def swapped(w):
            return [w[:, 0:64], w[:, 128:192], w[:, 64:128], w[:, 192:256]]

        def z_gather(a):
            got = [a]
            for _ in range(groups - 1):
                got.append(z_next(got[-1]))
            return got

        half = T // 2
        tie = lax.optimization_barrier
        own_qkv = jnp.concatenate(swapped(query_weight) + [key_matrix, value_matrix], axis=1)
        own_out = jnp.concatenate(swapped(out_weight), axis=1)

        def z_all(a):
            return [a] + [lax.ppermute(a, "grp", shifted(k)) for k in range(1, groups)]

        route_rows = routes.T.astype(BF)
        route_rows = [route_rows, to_x(route_rows), to_y(route_rows), to_diag(route_rows)]
        blocks = z_all(jnp.concatenate([own_qkv, own_out], axis=1))

        gu = gate_up_weight.reshape(dr, 4, 2, 2, HALF)
        dn = down_weight.reshape(dr, 4, 1, 2, HALF)
        parts = jnp.concatenate([gu, dn], axis=2)
        parts = jnp.transpose(parts, (1, 3, 0, 2, 4)).reshape(8, dr, 3 * HALF)
        unit = lax.all_to_all(parts, "fsdp", 0, 0, axis_index_groups=low_groups)
        unit = unit.reshape(8 * dr, 3 * HALF)
        if rest > 1:
            unit = lax.all_gather(unit, "fsdp", axis=0, tiled=True, axis_index_groups=rest_groups)

        bias = visible_bias(segment, parents[0])
        cos, sin = turn_tables(positions)
        chip = (mine // 2) % 4
        planes = ring_ids[(spot - jnp.arange(groups, dtype=jnp.int32)) % groups]
        e = jnp.concatenate([4 * planes + chip, chip[None]]).astype(jnp.int32)
        small = jnp.concatenate(
            [router_weight, attn_gain[:, None], ffn_gain[:, None], jnp.zeros((dr, LANES - 18), BF)], axis=1
        )
        bias, cos, sin, e, small, unit, *blocks = tie((bias, cos, sin, e, small, unit, *blocks))
        cols_qkv = jnp.concatenate([b[:, :512] for b in blocks] + [small], axis=1)
        cols_out = jnp.concatenate([b[:, 512:] for b in blocks], axis=1)
        mine_s = mine.astype(jnp.int32).reshape(1)
        units_1 = z_next(unit)
        if rest == 1:
            h = dr // 2
            qx = to_x(cols_qkv)
            qy = to_y(cols_qkv)
            qc = to_core(cols_qkv)
            qx, qy, qc, units_1 = tie((qx, qy, qc, units_1))
            qa = to_x(qy[:h])
            qb = to_y(qx[h:])
            pieces = [cols_qkv, qx, qy, qa, qb, qc, to_core(qx), to_core(qy), to_core(qa), to_core(qb)]
            places = [(0, 0, dr), (2, 0, dr), (4, 0, dr), (6, 0, h), (6, h, h),
                      (1, 0, dr), (3, 0, dr), (5, 0, dr), (7, 0, h), (7, h, h)]
        else:
            pieces = [lax.all_gather(cols_qkv, "fsdp", axis=0, tiled=True)]
            places = [(None, 0, MODEL_WIDTH)]
        w_out = lax.all_gather(cols_out, "fsdp", axis=0, tiled=True)
        core_0 = to_core(after(unit, *pieces))
        dyg = lax.all_gather(after(cotangent, cols_out), "fsdp", axis=0, tiled=True, axis_index_groups=core_groups)
        tokens_f = after(tokens, *pieces)
        units_2 = z_next(units_1)
        w_qkv, n1, qkv, att, h1, n2, small = call(
            attn_fwd(places, dr),
            [((MODEL_WIDTH, 2048), BF), ((T, MODEL_WIDTH), BF), ((4, T, 512), BF), ((4, T, 256), BF),
             ((T, MODEL_WIDTH), F32), ((T, MODEL_WIDTH), BF), ((LANES, MODEL_WIDTH), F32)],
            [SM] + [HB] * (len(pieces) + 5), [HB] * 7,
            [
                pltpu.VMEM((T, MODEL_WIDTH), BF), pltpu.VMEM((T, LANES), F32), pltpu.VMEM((T, LANES), F32),
                pltpu.VMEM((T, T), F32), pltpu.VMEM((MODEL_WIDTH, MODEL_WIDTH), BF),
                pltpu.VMEM((MODEL_WIDTH, 2176), BF), pltpu.VMEM((T, MODEL_WIDTH), BF),
                pltpu.VMEM((4, T, 512), BF), pltpu.VMEM((4, T, 256), BF), pltpu.VMEM((T, MODEL_WIDTH), F32),
                pltpu.VMEM((T, MODEL_WIDTH), BF), pltpu.VMEM((LANES, MODEL_WIDTH), F32),
                pltpu.SemaphoreType.DMA((len(pieces) + 5,)), pltpu.SemaphoreType.DMA((8,)),
            ],
            (mine_s, *pieces, tokens_f, cos, sin, bias, w_out), "attn_fwd", 40, 4.0e9,
        )
        n2, core_0 = tie((n2, core_0))
        nx = to_x(n2)
        ny = to_y(n2)
        core_1 = to_core(after(units_1, n2))
        nx, ny, units_2 = tie((nx, ny, units_2))
        xs = (n2, nx, ny, to_x(ny[:half]), to_y(nx[half:]))
        core_1, *xs = tie((core_1, *xs))
        units_3 = z_next(units_2)
        core_2 = to_core(units_2)

        def chip_sum(pair, *more):
            total = pair[0].astype(F32) + pair[1].astype(F32)
            for m in more:
                total = total + m.astype(F32)
            return total.astype(BF)

        gh1, dgu1, own_1, sib_1, gates, dgate = run_stage_a(e, xs, dyg, (units_1, core_1), small, route_rows)
        core_2, gates = tie((core_2, gates))
        sib_1 = to_core(sib_1)
        gh0, dgu0, gh2, dgu2, dgate, own_2, sib_2 = run_stage_b(
            e, xs, dyg, (unit, core_0, units_2, core_2), gates, dgate
        )
        units_3, sib_1, dgate = tie((units_3, sib_1, dgate))
        core_3 = to_core(units_3)
        ws = (unit, core_0, units_1, core_1, units_2, core_2, units_3, core_3)
        sum_1, dgate = tie((chip_sum((own_1, sib_1)), dgate))
        hop = z_next(sum_1)
        sib_2 = to_core(sib_2)
        gh3, dgu3, dgate, parts = run_stage_c(e, xs, dyg, ws, gates, dgate, (dgu0, dgu1, dgu2))
        sib_2, dgate, parts = tie((sib_2, dgate, parts))
        parts = swap(parts)
        dgus = (dgu0, dgu1, dgu2, dgu3)
        own_3, sib_3, own = run_late(e, xs, dyg, (gh3, dgu3), (*dgus, *ws, dgate))
        hop, own, gh0 = tie((hop, own, gh0))
        sum_2, gh0 = tie((chip_sum((own_2, sib_2), hop), gh0))
        hop = z_next(sum_2)
        sib_3 = to_core(sib_3)
        own_0, sib_0, outs, oown = run_last(e, xs, dyg, (gh0, dgu0), (gh0, gh1, gh2, gh3), ws)
        parts, own, outs, sib_3 = tie((parts, own, outs, sib_3))
        sib_0 = to_core(sib_0)
        dh1, datt, dwo = run_join((e, own, parts, gates, h1, n2, cotangent, w_out, att, small))
        hop, dh1, sib_0 = tie((hop, dh1, sib_0))
        sum_3, dh1, outs = tie((chip_sum((own_3, sib_3), hop), dh1, outs))
        hop = z_next(sum_3)
        outs = swap(outs)
        rs_out = lax.psum_scatter(dwo, "fsdp", scatter_dimension=0, tiled=True)
        dx, *dw = run_attn_bwd(
            rest == 1, dr, (mine_s, tokens, w_qkv, cos, sin, bias, n1, qkv, datt, dh1, small)
        )
        hop, outs, *dw = tie((hop, outs, *dw))
        if rest == 1:
            sib, rs_out = tie((to_core(dw[1]), rs_out))
            total = swap(chip_sum((dw[0], sib)).reshape(4, dr, -1))
            own_0, total = tie((own_0, total))
            rs_qkv = jnp.sum(total.astype(F32), axis=0).astype(BF)
        else:
            rs_qkv = lax.psum_scatter(dw[0], "fsdp", scatter_dimension=0, tiled=True)

        acc = chip_sum((own_0, sib_0), hop)
        if rest > 1:
            acc = lax.psum_scatter(
                acc, "fsdp", scatter_dimension=0, tiled=True, axis_index_groups=rest_groups
            )
        home = lax.all_to_all(acc.reshape(8, dr, 3 * HALF), "fsdp", 0, 0, axis_index_groups=low_groups)
        gate_up_grad, down_grad = call(
            settle(dr), [((dr, 4, 2 * FF), F32), ((dr, 4, FF), F32)], [HB], [VM] * 2,
            [pltpu.VMEM((8, dr, UNIT), BF), pltpu.SemaphoreType.DMA((1,))], (home,), "settle", 48, 0,
        )

        near = [
            lax.dynamic_index_in_dim(outs, chip ^ t, 0, keepdims=False).astype(F32) for t in (1, 2, 3)
        ]
        output = (h1 + oown + near[0] + near[1] + near[2]).astype(BF)
        z_qkv = z_sum([
            jnp.concatenate(
                [rs_qkv[:, k * 512 : (k + 1) * 512], rs_out[:, k * 256 : (k + 1) * 256],
                 rs_out[:, 1024 : 1024 + 64], rs_qkv[:, 2048 : 2048 + 64]], axis=1
            )
            for k in range(groups)
        ])
        z_out = z_qkv[:, 512:]
        return (
            output,
            dx,
            z_out[:, 320],
            jnp.concatenate(swapped(z_qkv[:, :256]), axis=1),
            z_qkv[:, 256:384],
            z_qkv[:, 384:512],
            jnp.concatenate(swapped(z_out[:, :256]), axis=1),
            z_out[:, 256 + EXPERTS],
            z_out[:, 256 : 256 + EXPERTS],
            gate_up_grad,
            down_grad,
        )

    return shards


def solution(mesh):
    both = ("grp", "fsdp")
    in_specs = (
        P(both, None), P(both), P(both), P(both, None), P(both, None),
        P("fsdp"), P("fsdp", "grp"), P("fsdp", "grp"), P("fsdp", "grp"), P("fsdp", "grp"),
        P("fsdp"), P("fsdp", None), P("fsdp", "grp", None), P("fsdp", "grp", None), P(both, None),
    )
    out_specs = (
        P(both, None), P(both, None), P("fsdp"),
        P("fsdp", "grp"), P("fsdp", "grp"), P("fsdp", "grp"), P("fsdp", "grp"),
        P("fsdp"), P("fsdp", None), P("fsdp", "grp", None), P("fsdp", "grp", None),
    )
    shards = make_shards(mesh.shape["grp"], mesh.shape["fsdp"])
    return jax.shard_map(shards, mesh=mesh, in_specs=in_specs, out_specs=out_specs, check_vma=False)
```

time: 556 us -> 446 us (0.80); the launches traced: 545 us -> 441 us
  local copies, waits for them, and re-layouts: 59.4 us -> 21 us
  Pallas kernels: 173 us -> 141 us
  waiting for transfers between devices: 191 us -> 177 us
  starting transfers between devices: 68 us -> 55.1 us
  other arithmetic: 23.1 us -> 31.6 us
  blocking collectives: 8.34 us -> 0 us
  between operations: 21.7 us -> 15 us
    all_to_all x1 -> x4, waiting for transfers between devices: 0.01 us -> 41.8 us  [the longest x3 32.7 us: swap(): return lax.all_to_all(a, 'fsdp', 0, 0, axis_index_groups=core_groups)]
    ppermute x6 -> x3, waiting for transfers between devices: 35.6 us -> 3.28 us  [z_sum(): lax.ppermute(blocks[k], 'grp', shifted(groups - k)).astype(F32)]
    pallas_call x15 -> x9, Pallas kernels: 173 us -> 141 us  [call(): pl.pallas_call(body, out_shape=[jax.ShapeDtypeStruct(s, d) for s, d in ou...]
    ppermute x12 -> x6, waiting for transfers between devices: 93.1 us -> 62.2 us  [z_next(): return lax.ppermute(a, 'grp', shifted(1))]
    unnamed x156 -> x84, local copies, waits for them, and re-layouts: 40.7 us -> 10.6 us
    ppermute x12 -> x5, waiting for transfers between devices: 29.1 us -> 3.57 us  [to_y(): return lax.ppermute(a, 'fsdp', flip(4))]
    ppermute x12 -> x5, waiting for transfers between devices: 16.1 us -> 35.1 us  [to_x(): return lax.ppermute(a, 'fsdp', flip(2))]
    all_to_all x1 -> x4, starting transfers between devices: 3.58 us -> 16.9 us  [the longest x3 13.1 us: swap(): return lax.all_to_all(a, 'fsdp', 0, 0, axis_index_groups=core_groups)]
  transfers between devices with their start and end apart: 58 -> 45, of which waited for: 23 -> 20; matrix products, arithmetic and copies ran while one was open for 7% -> 7% of each run, Pallas kernels for 27% -> 31%
where the time goes in v3:
time: 446 us; the launch traced here: 441 us
  waiting for transfers between devices  177 us (40%)
  Pallas kernels  141 us (32%)
  starting transfers between devices  55.1 us (12%)
  other arithmetic  31.6 us (7%)
  local copies, waits for them, and re-layouts  21 us (5%)
  between operations  15 us (3%)
    pallas_call x9, Pallas kernels, call(): pl.pallas_call(body, out_shape=[jax.ShapeDtypeStruct(s, d) for s, d in ou...  141 us
    ppermute x6, waiting for transfers between devices, z_next(): return lax.ppermute(a, 'grp', shifted(1))  62.2 us
    ppermute x5, waiting for transfers between devices, to_x(): return lax.ppermute(a, 'fsdp', flip(2))  35.1 us
    all_to_all x3, waiting for transfers between devices, swap(): return lax.all_to_all(a, 'fsdp', 0, 0, axis_index_groups=core_groups)  32.7 us
    convert_element_type x5, other arithmetic, chip_sum(): return total.astype(BF)  18.9 us
    all_to_all x1, waiting for transfers between devices, shards(): unit = lax.all_to_all(parts, 'fsdp', 0, 0, axis_index_groups=low_groups)  15 us
    all_to_all x3, starting transfers between devices, swap(): return lax.all_to_all(a, 'fsdp', 0, 0, axis_index_groups=core_groups)  13.1 us
    reduce_scatter x1, waiting for transfers between devices, shards(): rs_out = lax.psum_scatter(dwo, 'fsdp', scatter_dimension=0, tiled=True)  12.6 us
  transfers between devices with their start and end apart: 45, of which 20 were waited for; matrix products, arithmetic and copies ran while one was open for 7% of the time, Pallas kernels for 31%

profile of v3, /device:TPU:0, one launch (start us, length us, event | category | flops | bytes accessed | tf_op | source)
XLA Modules:
  0.0 440.8 jit_solution(10932792872494755766)
XLA Ops:
  30.7 15.0 %all-to-all-done = bf16[8,128,768]{1,2,0:T(8,128)(2,1)} async-done(((bf16[8,128,768]{1,2,0:T(8,128)(2,1)}), bf16[8,128,768]{1,2,0:T(8,128)(2,1)}, u32[]{:S(2)}, u32[]{:S(2)}) %all-to-all-start) | async-done | bytes 1572896 | tf_op jit(solution)/shard_map/all_to_all | solution.py:742
  53.9 15.0 %collective-permute-done.3.refs_1_ = bf16[128,2176]{1,0:T(8,128)(2,1)S(1)} collective-permute-done((bf16[128,2176]{1,0:T(8,128)(2,1)S(1)}, bf16[128,2176]{1,0:T(8,128)(2,1)S(1)}, u32[]{:S(2)}, u32[]{:S(2)}) %collective-permute-start.3) | collective-permute-done | bytes 557088 | tf_op jit(solution)/shard_map/ppermute | solution.py:683
  71.2 13.1 %collective-permute-done.6.refs_6_.refs_8_.refs_14_ = bf16[1024,768]{1,0:T(8,128)(2,1)} collective-permute-done((bf16[1024,768]{1,0:T(8,128)(2,1)S(1)}, bf16[1024,768]{1,0:T(8,128)(2,1)}, u32[]{:S(2)}, u32[]{:S(2)}) %collective-permute-start.6) | collective-permute-done | bytes 1572896 | tf_op jit(solution)/shard_map/ppermute | solution.py:680
  88.7 12.6 %collective-permute-done.7.refs_3_ = bf16[64,2176]{1,0:T(8,128)(2,1)S(1)} collective-permute-done((bf16[64,2176]{1,0:T(8,128)(2,1)S(1)}, bf16[64,2176]{1,0:T(8,128)(2,1)S(1)}, u32[]{:S(2)}, u32[]{:S(2)}) %collective-permute-start.7) | collective-permute-done | bytes 278560 | tf_op jit(solution)/shard_map/ppermute | solution.py:683
  105.9 12.2 %attn_fwd.1 = (bf16[1024,2048]{1,0:T(8,128)(2,1)}, bf16[384,1024]{1,0:T(8,128)(2,1)}, bf16[4,384,512]{2,1,0:T(8,128)(2,1)}, bf16[4,384,256]{2,1,0:T(8,128)(2,1)}...) custom-call(s32[1]{0:T(128)} %bitcast.mine_ref, bf16[128,2176]{1,0:T(8,128)(2,1)} %copy-done.18, ...), custom_call_target="tpu_custom_call" | custom-call | flops 80000000 | bytes 370933 | tf_op jit(solution)/shard_map/attn_fwd/pallas_call | solution.py:45
  118.4 25.1 %collective-permute-done.17.refs_8_.refs_10_.refs_16_ = bf16[1024,768]{1,0:T(8,128)(2,1)} collective-permute-done((bf16[1024,768]{1,0:T(8,128)(2,1)}, bf16[1024,768]{1,0:T(8,128)(2,1)}, u32[]{:S(2)}, u32[]{:S(2)}) %collective-permute-start.17) | collective-permute-done | bytes 1572896 | tf_op jit(solution)/shard_map/ppermute | solution.py:680
  147.5 7.4 %collective-permute-done.18.refs_3_ = bf16[192,1024]{1,0:T(8,128)(2,1)S(1)} collective-permute-done((bf16[192,1024]{1,0:T(8,128)(2,1)S(1)}, bf16[192,1024]{1,0:T(8,128)(2,1)S(1)}, u32[]{:S(2)}, u32[]{:S(2)}) %collective-permute-start.18) | collective-permute-done | bytes 393248 | tf_op jit(solution)/shard_map/ppermute | solution.py:683
  161.4 18.4 %stage_a.1 = (bf16[1536,512]{1,0:T(8,128)(2,1)}, bf16[1536,1024]{1,0:T(8,128)(2,1)}, bf16[1024,768]{1,0:T(8,128)(2,1)}, bf16[1024,768]{1,0:T(8,128)(2,1)}, f32[1536,128]{1,0:T(8,128)}, /*index=5*/f32[1536,128]{1,0:T(8,128)}) custom-call(s32[5]{0:T(128)} %pad_add_fusion.e_ref, bf16[384,1024]{1,0:T(8,128)(2,1)} %get-tuple-element.134.refs_0_.n2_h, ...), custom_call_target="tpu_custom_call" | custom-call | flops 193273536 | bytes 388465 | tf_op jit(solution)/shard_map/stage_a/pallas_call | solution.py:45
  179.9 23.0 %stage_b.1 = (bf16[1536,512]{1,0:T(8,128)(2,1)}, bf16[1536,1024]{1,0:T(8,128)(2,1)}, bf16[1536,512]{1,0:T(8,128)(2,1)}, bf16[1536,1024]{1,0:T(8,128)(2,1)}, f32[...) custom-call(s32[5]{0:T(128)} %pad_add_fusion.e_ref, ...), custom_call_target="tpu_custom_call" | custom-call | flops 289910304 | bytes 550502 | tf_op jit(solution)/shard_map/stage_b/pallas_call | solution.py:45
  210.9 21.4 %stage_c.1 = (bf16[1536,512]{1,0:T(8,128)(2,1)}, bf16[1536,1024]{1,0:T(8,128)(2,1)}, f32[1536,128]{1,0:T(8,128)}, bf16[4,384,1152]{2,1,0:T(8,128)(2,1)}) custom-call(s32[5]{0:T(128)} %pad_add_fusion.e_ref, bf16[384,1024]{1,0:T(8,128)(2,1)} %get-tuple-element.134.refs_0_.n2_h, bf16[384,1024]{1,0:T(8,128)(2,1)} %copy-done.3, bf16[384,1024]{1,0:T(8,128)(2,1)} %copy-done.4, ...), custom_call_target="tpu_custom_call" | custom-call | flops 193273536 | bytes 778568 | tf_op jit(solution)/shard_map/stage_c/pallas_call | solution.py:45
  232.3 4.7 %all-to-all-start.1 = ((bf16[4,384,1152]{2,1,0:T(8,128)(2,1)}), bf16[4,384,1152]{2,1,0:T(8,128)(2,1)}, u32[]{:S(2)}, u32[]{:S(2)}) async-start(bf16[4,384,1152]{2,1,0:T(8,128)(2,1)} %get-tuple-element.176), calls=%async_computation.1 | async-start | bytes 7077888 | tf_op jit(solution)/shard_map/all_to_all | solution.py:702
  237.1 15.7 %late_stage.1 = (bf16[1024,768]{1,0:T(8,128)(2,1)}, bf16[1024,768]{1,0:T(8,128)(2,1)}, f32[384,1152]{1,0:T(8,128)}) custom-call(s32[5]{0:T(128)} %pad_add_fusion.e_ref, bf16[384,1024]{1,0:T(8,128)(2,1)} %get-tuple-element.134.refs_0_.n2_h, bf16[384,1024]{1,0:T(8,128)(2,1)} %copy-done.3, bf16[384,1024]{1,0:T(8,128)(2,1)} %copy-done.4, ...), custom_call_target="tpu_custom_call" | custom-call | flops 193273536 | bytes 837550 | tf_op jit(solution)/shard_map/late_stage/pallas_call | solution.py:45
  258.7 18.1 %last_stage.1 = (bf16[1024,768]{1,0:T(8,128)(2,1)}, bf16[1024,768]{1,0:T(8,128)(2,1)}, bf16[4,384,1024]{2,1,0:T(8,128)(2,1)}, f32[384,1024]{1,0:T(8,128)}) custom-call(s32[5]{0:T(128)} %pad_add_fusion.e_ref, bf16[384,1024]{1,0:T(8,128)(2,1)} %get-tuple-element.134.refs_0_.n2_h, bf16[384,1024]{1,0:T(8,128)(2,1)} %copy-done.3, bf16[384,1024]{1,0:T(8,128)(2,1)} %copy-done.4, ...), custom_call_target="tpu_custom_call" | custom-call | flops 193273536 | bytes 754975 | tf_op jit(solution)/shard_map/last_stage/pallas_call | solution.py:45
  278.2 9.0 %join.1 = (f32[384,1024]{1,0:T(8,128)}, bf16[4,384,256]{2,1,0:T(8,128)(2,1)}, bf16[1024,1152]{1,0:T(8,128)(2,1)}) custom-call(s32[5]{0:T(128)} %pad_add_fusion.e_ref, f32[384,1152]{1,0:T(8,128)} %get-tuple-element.182.p_h, bf16[4,384,1152]{2,1,0:T(8,128)(2,1)} %all-to-all-done.1.parts_h, f32[1536,128]{1,0:T(8,128)} %get-tuple-element.146.refs_10_.refs_14_.gates_h, ...), custom_call_target="tpu_custom_call" | custom-call | flops 40000000 | bytes 347341 | tf_op jit(solution)/shard_map/join/pallas_call | solution.py:45
  287.2 7.2 %collective-permute-done.30 = bf16[1024,768]{1,0:T(8,128)(2,1)} collective-permute-done((bf16[1024,768]{1,0:T(8,128)(2,1)}, bf16[1024,768]{1,0:T(8,128)(2,1)}, u32[]{:S(2)}, u32[]{:S(2)}) %collective-permute-start.30) | collective-permute-done | bytes 1572896 | tf_op jit(solution)/shard_map/ppermute | solution.py:680
  294.4 4.6 %add_convert_fusion.2 = bf16[1024,768]{1,0:T(8,128)(2,1)} fusion(bf16[1024,768]{1,0:T(8,128)(2,1)} %collective-permute-done.30, bf16[1024,768]{1,0:T(8,128)(2,1)} %collective-permute-done.29, bf16[1024,768]{1,0:T(8,128)(2,1)} %get-tuple-element.175), kind=kLoop, calls=%fused_computation.3 | loop fusion | flops 4718592 | bytes 6291456 | tf_op jit(solution)/shard_map/convert_element_type | solution.py:808
  299.0 4.7 %all-to-all-start.2 = ((bf16[4,384,1024]{2,1,0:T(8,128)(2,1)}), bf16[4,384,1024]{2,1,0:T(8,128)(2,1)}, u32[]{:S(2)}, u32[]{:S(2)}) async-start(bf16[4,384,1024]{2,1,0:T(8,128)(2,1)} %get-tuple-element.191), calls=%async_computation.2 | async-start | bytes 6291456 | tf_op jit(solution)/shard_map/all_to_all | solution.py:702
  304.9 19.1 %attn_bwd.1 = (f32[384,1024]{1,0:T(8,128)}, bf16[512,2176]{1,0:T(8,128)(2,1)}, bf16[512,2176]{1,0:T(8,128)(2,1)}) custom-call(s32[1]{0:T(128)} %bitcast.mine_ref, bf16[384,1024]{1,0:T(8,128)(2,1)} %x_h.1, bf16[1024,2048]{1,0:T(8,128)(2,1)} %get-tuple-element.192.w_h, f32[384,128]{1,0:T(8,128)} %get-tuple-element.122.refs_11_.cos_h, ...), custom_call_target="tpu_custom_call" | custom-call | flops 120000000 | bytes 344719 | tf_op jit(solution)/shard_map/attn_bwd/pallas_call | solution.py:45
  324.0 16.8 %collective-permute-done.32 = bf16[1024,768]{1,0:T(8,128)(2,1)S(1)} collective-permute-done((bf16[1024,768]{1,0:T(8,128)(2,1)}, bf16[1024,768]{1,0:T(8,128)(2,1)S(1)}, u32[]{:S(2)}, u32[]{:S(2)}) %collective-permute-start.32) | collective-permute-done | bytes 1572896 | tf_op jit(solution)/shard_map/ppermute | solution.py:680
  340.8 5.4 %all-to-all-done.2 = bf16[4,384,1024]{2,1,0:T(8,128)(2,1)} async-done(((bf16[4,384,1024]{2,1,0:T(8,128)(2,1)}), bf16[4,384,1024]{2,1,0:T(8,128)(2,1)}, u32[]{:S(2)}, u32[]{:S(2)}) %all-to-all-start.2) | async-done | bytes 3145760 | tf_op jit(solution)/shard_map/all_to_all | solution.py:702
  346.2 12.6 %reduce-scatter.2.cloned.1.call-done = bf16[128,1152]{1,0:T(8,128)(2,1)} async-done(((bf16[1024,1152]{1,0:T(8,128)(2,1)}), bf16[128,1152]{1,0:T(8,128)(2,1)}) %reduce-scatter.2.cloned.1.call-update) | async-done | bytes 294928 | tf_op jit(solution)/shard_map/reduce_scatter | solution.py:839
  366.2 26.5 %all-to-all-done.3 = bf16[4,128,2176]{2,1,0:T(8,128)(2,1)S(1)} async-done(((bf16[4,128,2176]{2,1,0:T(8,128)(2,1)}), bf16[4,128,2176]{2,1,0:T(8,128)(2,1)S(1)}, u32[]{:S(2)}, u32[]{:S(2)}) %all-to-all-start.3) | async-done | bytes 2228256 | tf_op jit(solution)/shard_map/all_to_all | solution.py:702
  419.1 9.1 %all-to-all-done.4.home_h = bf16[8,128,768]{2,1,0:T(8,128)(2,1)S(1)} async-done(((bf16[8,128,768]{2,1,0:T(8,128)(2,1)}), bf16[8,128,768]{2,1,0:T(8,128)(2,1)S(1)}, u32[]{:S(2)}, u32[]{:S(2)}) %all-to-all-start.4) | async-done | bytes 1572896 | tf_op jit(solution)/shard_map/all_to_all | solution.py:857
  429.3 4.5 %settle.1 = (f32[128,4,1024]{2,1,0:T(4,128)}, f32[128,4,512]{2,1,0:T(4,128)}) custom-call(bf16[8,128,768]{2,1,0:T(8,128)(2,1)} %copy-done.9), custom_call_target="tpu_custom_call" | custom-call | bytes 94371 | tf_op jit(solution)/shard_map/settle/pallas_call | solution.py:45
  (216 shorter events, 104.8 us)
Async XLA Ops:
  9.2 38.3 %collective-permute-start = (bf16[128,768]{1,0:T(8,128)(2,1)S(1)}, bf16[128,768]{1,0:T(8,128)(2,1)S(1)}, u32[]{:S(2)}, u32[]{:S(2)}) collective-permute-start(bf16[128,768]{1,0:T(8,128)(2,1)S(1)} %concatenate.40), channel_id=1, source_target_pairs={{0,8},{8,24},{24,16},{16,0},{1,9},{9,25},{25,17},{17,1},{2,10},{10... | collective-permute-start | bytes 589832 | tf_op jit(solution)/shard_map/ppermute | solution.py:732
  12.2 35.2 %collective-permute-start.1 = (bf16[128,768]{1,0:T(8,128)(2,1)S(1)}, bf16[128,768]{1,0:T(8,128)(2,1)}, u32[]{:S(2)}, u32[]{:S(2)}) collective-permute-start(bf16[128,768]{1,0:T(8,128)(2,1)S(1)} %concatenate.40), channel_id=1, source_target_pairs={{0,24},{8,16},{24,0},{16,8},{1,25},{9,17},{25,1},{17,9},{2,26},{10... | collective-permute-start | bytes 589832 | tf_op jit(solution)/shard_map/ppermute | solution.py:732
  14.7 32.7 %collective-permute-start.2 = (bf16[128,768]{1,0:T(8,128)(2,1)S(1)}, bf16[128,768]{1,0:T(8,128)(2,1)}, u32[]{:S(2)}, u32[]{:S(2)}) collective-permute-start(bf16[128,768]{1,0:T(8,128)(2,1)S(1)} %concatenate.40), channel_id=1, source_target_pairs={{0,16},{8,0},{24,8},{16,24},{1,17},{9,1},{25,9},{17,25},{2,18},{10... | collective-permute-start | bytes 589832 | tf_op jit(solution)/shard_map/ppermute | solution.py:732
  20.2 25.5 %all-to-all-start = ((bf16[8,128,768]{1,2,0:T(8,128)(2,1)}), bf16[8,128,768]{1,2,0:T(8,128)(2,1)}, u32[]{:S(2)}, u32[]{:S(2)}) async-start(bf16[8,128,768]{1,2,0:T(8,128)(2,1)} %bitcast.10), calls=%async_computation | async-start | bytes 3145728 | tf_op jit(solution)/shard_map/all_to_all | solution.py:742
  24.7 81.3 %all-gather.3.cloned.1.call-start = ((), (), s32[]{:S(2)}) async-start(), calls=%async_computation.6 | async-start | bytes 2359296 | tf_op jit(solution)/shard_map/all_gather | solution.py:774
  50.0 110.8 %all-gather.5.cloned.1.call-start = ((), (), s32[]{:S(2)}) async-start(), calls=%async_computation.7 | async-start | bytes 3932160 | tf_op jit(solution)/shard_map/all_gather | solution.py:776
  50.0 34.2 %collective-permute-start.6 = (bf16[1024,768]{1,0:T(8,128)(2,1)S(1)}, bf16[1024,768]{1,0:T(8,128)(2,1)}, u32[]{:S(2)}, u32[]{:S(2)}) collective-permute-start(bf16[1024,768]{1,0:T(8,128)(2,1)S(1)} %bitcast.27), channel_id=1, source_target_pairs={{0,8},{8,24},{24,16},{16,0},{1,9},{9,25},{25,17},{17,1},{2,10},{10... | collective-permute-start | bytes 4718600 | tf_op jit(solution)/shard_map/ppermute | solution.py:680
  105.7 37.8 %collective-permute-start.17 = (bf16[1024,768]{1,0:T(8,128)(2,1)}, bf16[1024,768]{1,0:T(8,128)(2,1)}, u32[]{:S(2)}, u32[]{:S(2)}) collective-permute-start(bf16[1024,768]{1,0:T(8,128)(2,1)} %collective-permute-done.6.refs_6_.refs_8_.refs_14_), channel_id=1, source_target_pairs={{0,8},{8,24},{24,16},{16,0},{1,9},{9,25},{25,17},{17,1},{2,10},{10... | collective-permute-start | bytes 4718600 | tf_op jit(solution)/shard_map/ppermute | solution.py:680
  118.2 39.5 %collective-permute-start.14 = (bf16[1024,768]{1,0:T(8,128)(2,1)}, bf16[1024,768]{1,0:T(8,128)(2,1)S(1)}, u32[]{:S(2)}, u32[]{:S(2)}) collective-permute-start(bf16[1024,768]{1,0:T(8,128)(2,1)} %collective-permute-done.6.refs_6_.refs_8_.refs_14_), channel_id=1, source_target_pairs={{0,1},{1,0},{2,3},{3,2},{4,5},{5,4},{6,7},{7,6},{8,9},{9,8},{10,11... | collective-permute-start | bytes 4718600 | tf_op jit(solution)/shard_map/ppermute | solution.py:692
  118.3 25.4 %collective-permute-start.15 = (bf16[384,1024]{1,0:T(8,128)(2,1)}, bf16[384,1024]{1,0:T(8,128)(2,1)S(1)}, u32[]{:S(2)}, u32[]{:S(2)}) collective-permute-start(bf16[384,1024]{1,0:T(8,128)(2,1)} %get-tuple-element.134.refs_0_.n2_h), channel_id=1, source_target_pairs={{0,2},{1,3},{2,0},{3,1},{4,6},{5,7},{6,4},{7,5},{8,10},{9,11},{10,... | collective-permute-start | bytes 2359304 | tf_op jit(solution)/shard_map/ppermute | solution.py:683
  118.3 25.4 %collective-permute-start.16 = (bf16[384,1024]{1,0:T(8,128)(2,1)}, bf16[384,1024]{1,0:T(8,128)(2,1)S(1)}, u32[]{:S(2)}, u32[]{:S(2)}) collective-permute-start(bf16[384,1024]{1,0:T(8,128)(2,1)} %get-tuple-element.134.refs_0_.n2_h), channel_id=1, source_target_pairs={{0,4},{1,5},{2,6},{3,7},{4,0},{5,1},{6,2},{7,3},{8,12},{9,13},{10,... | collective-permute-start | bytes 2359304 | tf_op jit(solution)/shard_map/ppermute | solution.py:686
  145.9 34.0 %collective-permute-start.20 = (bf16[1024,768]{1,0:T(8,128)(2,1)}, bf16[1024,768]{1,0:T(8,128)(2,1)}, u32[]{:S(2)}, u32[]{:S(2)}) collective-permute-start(bf16[1024,768]{1,0:T(8,128)(2,1)} %collective-permute-done.17.refs_8_.refs_10_.refs_16_), channel_id=1, source_target_pairs={{0,1},{1,0},{2,3},{3,2},{4,5},{5,4},{6,7},{7,6},{8,9},{9,8},{10,11... | collective-permute-start | bytes 4718600 | tf_op jit(solution)/shard_map/ppermute | solution.py:692
  157.7 45.3 %collective-permute-start.25 = (bf16[1024,768]{1,0:T(8,128)(2,1)}, bf16[1024,768]{1,0:T(8,128)(2,1)}, u32[]{:S(2)}, u32[]{:S(2)}) collective-permute-start(bf16[1024,768]{1,0:T(8,128)(2,1)} %collective-permute-done.17.refs_8_.refs_10_.refs_16_), channel_id=1, source_target_pairs={{0,8},{8,24},{24,16},{16,0},{1,9},{9,25},{25,17},{17,1},{2,10},{10... | collective-permute-start | bytes 4718600 | tf_op jit(solution)/shard_map/ppermute | solution.py:680
  179.9 23.1 %collective-permute-start.26 = (bf16[1024,768]{1,0:T(8,128)(2,1)}, bf16[1024,768]{1,0:T(8,128)(2,1)S(1)}, u32[]{:S(2)}, u32[]{:S(2)}) collective-permute-start(bf16[1024,768]{1,0:T(8,128)(2,1)} %get-tuple-element.150), channel_id=1, source_target_pairs={{0,1},{1,0},{2,3},{3,2},{4,5},{5,4},{6,7},{7,6},{8,9},{9,8},{10,11... | collective-permute-start | bytes 4718600 | tf_op jit(solution)/shard_map/ppermute | solution.py:692
  204.5 27.7 %collective-permute-start.24 = (bf16[1024,768]{1,0:T(8,128)(2,1)}, bf16[1024,768]{1,0:T(8,128)(2,1)}, u32[]{:S(2)}, u32[]{:S(2)}) collective-permute-start(bf16[1024,768]{1,0:T(8,128)(2,1)} %get-tuple-element.149), channel_id=1, source_target_pairs={{0,1},{1,0},{2,3},{3,2},{4,5},{5,4},{6,7},{7,6},{8,9},{9,8},{10,11... | collective-permute-start | bytes 4718600 | tf_op jit(solution)/shard_map/ppermute | solution.py:692
  208.0 44.7 %collective-permute-start.28 = (bf16[1024,768]{1,0:T(8,128)(2,1)}, bf16[1024,768]{1,0:T(8,128)(2,1)}, u32[]{:S(2)}, u32[]{:S(2)}) collective-permute-start(bf16[1024,768]{1,0:T(8,128)(2,1)} %add_convert_fusion.4), channel_id=1, source_target_pairs={{0,8},{8,24},{24,16},{16,0},{1,9},{9,25},{25,17},{17,1},{2,10},{10... | collective-permute-start | bytes 4718600 | tf_op jit(solution)/shard_map/ppermute | solution.py:680
  232.3 45.9 %all-to-all-start.1 = ((bf16[4,384,1152]{2,1,0:T(8,128)(2,1)}), bf16[4,384,1152]{2,1,0:T(8,128)(2,1)}, u32[]{:S(2)}, u32[]{:S(2)}) async-start(bf16[4,384,1152]{2,1,0:T(8,128)(2,1)} %get-tuple-element.176), calls=%async_computation.1 | async-start | bytes 7077888 | tf_op jit(solution)/shard_map/all_to_all | solution.py:702
  256.4 38.0 %collective-permute-start.30 = (bf16[1024,768]{1,0:T(8,128)(2,1)}, bf16[1024,768]{1,0:T(8,128)(2,1)}, u32[]{:S(2)}, u32[]{:S(2)}) collective-permute-start(bf16[1024,768]{1,0:T(8,128)(2,1)} %add_convert_fusion.3), channel_id=1, source_target_pairs={{0,8},{8,24},{24,16},{16,0},{1,9},{9,25},{25,17},{17,1},{2,10},{10... | collective-permute-start | bytes 4718600 | tf_op jit(solution)/shard_map/ppermute | solution.py:680
  299.0 47.2 %all-to-all-start.2 = ((bf16[4,384,1024]{2,1,0:T(8,128)(2,1)}), bf16[4,384,1024]{2,1,0:T(8,128)(2,1)}, u32[]{:S(2)}, u32[]{:S(2)}) async-start(bf16[4,384,1024]{2,1,0:T(8,128)(2,1)} %get-tuple-element.191), calls=%async_computation.2 | async-start | bytes 6291456 | tf_op jit(solution)/shard_map/all_to_all | solution.py:702
  303.7 55.1 %reduce-scatter.2.cloned.1.call-start = ((), (), s32[]{:S(2)}) async-start(), calls=%async_computation.8 | async-start | bytes 2654208 | tf_op jit(solution)/shard_map/reduce_scatter | solution.py:839
  303.8 37.0 %collective-permute-start.32 = (bf16[1024,768]{1,0:T(8,128)(2,1)}, bf16[1024,768]{1,0:T(8,128)(2,1)S(1)}, u32[]{:S(2)}, u32[]{:S(2)}) collective-permute-start(bf16[1024,768]{1,0:T(8,128)(2,1)} %add_convert_fusion.2), channel_id=1, source_target_pairs={{0,8},{8,24},{24,16},{16,0},{1,9},{9,25},{25,17},{17,1},{2,10},{10... | collective-permute-start | bytes 4718600 | tf_op jit(solution)/shard_map/ppermute | solution.py:680
  362.4 30.3 %all-to-all-start.3 = ((bf16[4,128,2176]{2,1,0:T(8,128)(2,1)}), bf16[4,128,2176]{2,1,0:T(8,128)(2,1)S(1)}, u32[]{:S(2)}, u32[]{:S(2)}) async-start(bf16[4,128,2176]{2,1,0:T(8,128)(2,1)} %bitcast.33), calls=%async_computation.4 | async-start | bytes 4456448 | tf_op jit(solution)/shard_map/all_to_all | solution.py:702
  394.5 19.6 %collective-permute-start.36 = (bf16[128,896]{1,0:T(8,128)(2,1)}, bf16[128,896]{1,0:T(8,128)(2,1)}, u32[]{:S(2)}, u32[]{:S(2)}) collective-permute-start(bf16[128,896]{1,0:T(8,128)(2,1)} %get-tuple-element.308), channel_id=1, source_target_pairs={{0,8},{8,24},{24,16},{16,0},{1,9},{9,25},{25,17},{17,1},{2,10},{10... | collective-permute-start | bytes 688136 | tf_op jit(solution)/shard_map/ppermute | solution.py:707
  403.5 24.7 %all-to-all-start.4 = ((bf16[8,128,768]{2,1,0:T(8,128)(2,1)}), bf16[8,128,768]{2,1,0:T(8,128)(2,1)S(1)}, u32[]{:S(2)}, u32[]{:S(2)}) async-start(bf16[8,128,768]{2,1,0:T(8,128)(2,1)} %bitcast.34), calls=%async_computation.5 | async-start | bytes 3145728 | tf_op jit(solution)/shard_map/all_to_all | solution.py:857
  (60 other events, 614.4 us)
Sparse Core Ops, SparseCore 0:
  50.1 27.5 all-gather.2
  79.5 52.9 all-gather.4
  307.9 50.8 reduce-scatter.1

commit v4 on v3

--- a/solution.py
+++ b/solution.py
@@ -20,7 +20,7 @@
 SCALE = 1.0 / math.sqrt(HEAD_SIZE)
 BF = jnp.bfloat16
 F32 = jnp.float32
-COST = 0.02
+COST = 1.0
 VMEM_MIB = 62
 
 NT = (((1,), (1,)), ((), ()))
@@ -203,10 +203,6 @@
     ]
 
 
-def tree_waits(hx, hy):
-    return [hx[0:1] + hy[0:1], hx[1:2] + hy[1:2], hx[2:3] + hy[2:3], hx[3:] + hy[3:]]
-
-
 def act(t, e, X, Y, W, GT, GH, DGU):
     rows = TREE[t]
     lanes = lax.broadcasted_iota(jnp.int32, (T, LANES), 1)
@@ -229,15 +225,27 @@
     return jnp.where(lanes == e, dgate, 0.0)
 
 
-def wgrad(X, Y, GH, DGU, DW):
+def wgrad_down(Y, GH, DW):
+    step = 256
+    for r in range(MODEL_WIDTH // step):
+        cols = slice(r * step, (r + 1) * step)
+        dd = dotg(Y[:, cols], GH[...], TN)
+        for u in range(2):
+            DW[u, cols, WIDE:UNIT] = dd[:, u * HALF : (u + 1) * HALF].astype(BF)
+
+
+def wgrad_up(X, DGU, DW):
     step = 256
     for r in range(MODEL_WIDTH // step):
         cols = slice(r * step, (r + 1) * step)
         dg = dotg(X[:, cols], DGU[...], TN)
-        dd = dotg(Y[:, cols], GH[...], TN)
         for u in range(2):
             DW[u, cols, 0:WIDE] = dg[:, u * WIDE : (u + 1) * WIDE].astype(BF)
-            DW[u, cols, WIDE:UNIT] = dd[:, u * HALF : (u + 1) * HALF].astype(BF)
+
+
+def wgrad(X, Y, GH, DGU, DW):
+    wgrad_down(Y, GH, DW)
+    wgrad_up(X, DGU, DW)
 
 
 def stage_scratch(n, extra, loads, stores):
@@ -253,12 +261,11 @@
 
 def load_tokens(xs, dyg, chip, X, Y, head, rest, si):
     px, py = token_pairs(xs, X), chip_pairs(dyg, chip, Y)
-    order = px[0:1] + head + py[0:1] + px[1:] + py[1:] + rest
-    copies = fetch(order, si)
-    n = 1 + len(head)
-    cx = copies[0:1] + copies[n + 1 : n + 5]
-    cy = copies[n : n + 1] + copies[n + 5 : n + 8]
-    return copies[1:n], tree_waits(cx, cy), copies[n + 8 :]
+    urgent = fetch(px[0:1] + head + py[0:1], si)
+    wait(urgent)
+    n = len(urgent)
+    more = fetch([px[1], py[1], px[2], py[2], px[3], px[4], py[3]] + rest, si, n)
+    return [[], more[0:2], more[2:4], more[4:7]], more[7:]
 
 
 def stage_a(e_ref, *refs):
@@ -266,10 +273,9 @@
     rt_h, routes = refs[8], refs[9:13]
     gh_h, dgu_h, dwo_h, dws_h, gates_h, dgate_h = refs[13:19]
     X, Y, W, GH, DGU, GT, DG, DW, rt, si, so = refs[19:]
-    head, trees, _ = load_tokens(
+    trees, _ = load_tokens(
         xs, dyg, e_ref[4], X, Y, [(rt_h, rt)] + [(ws[i], W.at[0, i]) for i in range(2)], [], si
     )
-    wait(head)
     router = rt[...].astype(BF)
     for t in range(4):
         wait(trees[t])
@@ -302,10 +308,9 @@
     gh0_h, dgu0_h, gh2_h, dgu2_h, dgate_h, dwo_h, dws_h = refs[12:19]
     X, Y, W, GH, DGU, GT, DG, DW, si, so = refs[19:]
     hw = [(ws[i], W.at[i // 2, i % 2]) for i in range(4)]
-    head, trees, second = load_tokens(
+    trees, second = load_tokens(
         xs, dyg, e_ref[4], X, Y, hw[0:2] + [(gates_h, GT), (dgate_i, DG)], hw[2:], si
     )
-    wait(head)
     for t in range(4):
         wait(trees[t])
         DG[TREE[t], :] += act(t, e_ref[0], X, Y, W.at[0], GT, GH.at[0], DGU.at[0])
@@ -334,11 +339,10 @@
     X, Y, W, GH, DGU, GT, DG, WB, DF, OUT, si, so = refs[23:]
     late = [(ws[i].at[:, 0:WIDE], WB.at[:, i * WIDE : (i + 1) * WIDE]) for i in range(6)]
     late += [(dgus[i].at[T:ROWS], DF.at[:, 2 * i * FF : 2 * (i + 1) * FF]) for i in range(3)]
-    head, trees, late = load_tokens(
+    trees, late = load_tokens(
         xs, dyg, e_ref[4], X, Y,
         [(ws[6 + i], W.at[0, i]) for i in range(2)] + [(gates_h, GT), (dgate_i, DG)], late, si,
     )
-    wait(head)
     for t in range(4):
         wait(trees[t])
         DG[TREE[t], :] += act(t, e_ref[3], X, Y, W.at[0], GT, GH.at[0], DGU.at[0])
@@ -374,60 +378,38 @@
     return pairs
 
 
-def late_stage(n, own):
-    def body(e_ref, *refs):
-        xs, dyg, acts = refs[0:5], refs[5], refs[6 : 6 + 2 * n]
-        refs = refs[6 + 2 * n :]
-        pairs = []
-        if own:
-            dgus, ws, dgate_h = refs[0:4], refs[4:12], refs[12]
-            refs = refs[13:]
-        dws, refs = refs[: 2 * n], refs[2 * n :]
-        if own:
-            own_h, refs = refs[0], refs[1:]
-        X, Y, GH, DGU, DW, si, so = refs[:7]
-        if own:
-            A, W, DG, O = refs[7:]
-            pairs = back_pairs(dgus, ws, 0, T, WIDE, 0, A, W) + [(dgate_h.at[0:T], DG)]
-        first = len(pairs)
-        pairs += chip_pairs(dyg, e_ref[4], Y) + [(acts[0], GH.at[0])] + token_pairs(xs, X) + [(acts[1], DGU.at[0])]
-        for i in range(1, n):
-            pairs += [(acts[2 * i], GH.at[i]), (acts[2 * i + 1], DGU.at[i])]
-        copies = fetch(pairs, si)
-        outs = []
-        if own:
-            wait(copies[:first])
-            O[:, 0:MODEL_WIDTH] = dotg(A[...], W[...], NT)
-            O[:, MODEL_WIDTH:] = DG[...]
-            outs += fetch([(O, own_h)], so, 2 * n)
-        for i in range(n):
-            wait(copies[first + (11 if i else 0) + 2 * (i - 1) * (i > 0) : first + 11 + 2 * i])
-            wgrad(X, Y, GH.at[i], DGU.at[i], DW.at[i])
-            outs += fetch([(DW.at[i, 0], dws[2 * i]), (DW.at[i, 1], dws[2 * i + 1])], so, 2 * i)
-        wait(outs)
-
-    return body
-
-
-def run_late(e, xs, dyg, acts, back=()):
-    n = len(acts) // 2
+def late_stage(e_ref, *refs):
+    xs, dyg, gh_h, dgu_h = refs[0:5], refs[5], refs[6], refs[7]
+    dgus, ws, dgate_h = refs[8:12], refs[12:20], refs[20]
+    dwo_h, dws_h, own_h = refs[21:24]
+    X, Y, GH, DGU, DW, A, W, DG, O, si, so = refs[24:]
+    first = fetch(chip_pairs(dyg, e_ref[4], Y) + [(gh_h, GH)], si)
+    wait(first)
+    second = fetch(token_pairs(xs, X) + [(dgu_h, DGU)], si, 5)
+    third = fetch(back_pairs(dgus, ws, 0, T, WIDE, 0, A, W) + [(dgate_h.at[0:T], DG)], si, 11)
+    wgrad_down(Y, GH, DW)
+    wait(second)
+    wgrad_up(X, DGU, DW)
+    outs = fetch([(DW.at[0], dwo_h), (DW.at[1], dws_h)], so)
+    wait(third)
+    O[:, 0:MODEL_WIDTH] = dotg(A[...], W[...], NT)
+    O[:, MODEL_WIDTH:] = DG[...]
+    outs += fetch([(O, own_h)], so, 2)
+    wait(outs)
+
+
+def run_late(e, xs, dyg, acts, back):
     cols = MODEL_WIDTH + LANES
     args = (e, *xs, dyg, *acts, *back)
-    outs = DW_OUT * n
-    scratch = [
-        pltpu.VMEM((ROWS, MODEL_WIDTH), BF), pltpu.VMEM((ROWS, MODEL_WIDTH), BF),
-        pltpu.VMEM((n, ROWS, FF), BF), pltpu.VMEM((n, ROWS, 2 * FF), BF),
-        pltpu.VMEM((n, 2, MODEL_WIDTH, UNIT), BF),
-        pltpu.SemaphoreType.DMA((22 + 2 * n,)), pltpu.SemaphoreType.DMA((2 * n + 1,)),
-    ]
-    if back:
-        outs = outs + [((T, cols), F32)]
-        scratch += [
+    return call(
+        late_stage, DW_OUT + [((T, cols), F32)], [SM] + [HB] * (len(args) - 1), [HB] * 3,
+        [
+            pltpu.VMEM((ROWS, MODEL_WIDTH), BF), pltpu.VMEM((ROWS, MODEL_WIDTH), BF),
+            pltpu.VMEM((ROWS, FF), BF), pltpu.VMEM((ROWS, 2 * FF), BF), DW_VMEM,
             pltpu.VMEM((T, 8 * WIDE), BF), pltpu.VMEM((MODEL_WIDTH, 8 * WIDE), BF),
             pltpu.VMEM((T, LANES), F32), pltpu.VMEM((T, cols), F32),
-        ]
-    return call(
-        late_stage(n, bool(back)), outs, [SM] + [HB] * (len(args) - 1), [HB] * len(outs), scratch,
+            pltpu.SemaphoreType.DMA((24,)), pltpu.SemaphoreType.DMA((3,)),
+        ],
         args, "late_stage", 52, 2 * EXPERT_FLOPS,
     )
 
@@ -437,13 +419,15 @@
     ghs, ws = refs[8:12], refs[12:20]
     dwo_h, dws_h, parts_h, own_h = refs[20:24]
     X, Y, GH, DGU, DW, A, W, O, OF, si, so = refs[24:]
-    pairs = chip_pairs(dyg, e_ref[4], Y) + [(gh_h, GH)] + token_pairs(xs, X) + [(dgu_h, DGU)]
-    pairs += back_pairs(ghs, ws, 0, ROWS, HALF, WIDE, A, W)
-    copies = fetch(pairs, si)
-    wait(copies[:11])
-    wgrad(X, Y, GH, DGU, DW)
+    first = fetch(chip_pairs(dyg, e_ref[4], Y) + [(gh_h, GH)], si)
+    wait(first)
+    second = fetch(token_pairs(xs, X) + [(dgu_h, DGU)], si, 5)
+    third = fetch(back_pairs(ghs, ws, 0, ROWS, HALF, WIDE, A, W), si, 11)
+    wgrad_down(Y, GH, DW)
+    wait(second)
+    wgrad_up(X, DGU, DW)
     outs = fetch([(DW.at[0], dwo_h), (DW.at[1], dws_h)], so)
-    wait(copies[11:])
+    wait(third)
     for i, t in enumerate((3, 1, 2, 0)):
         total = dotg(A[TREE[t], :], W[...], NT)
         dst = O.at[i] if t else OF
@@ -545,7 +529,7 @@
 
 def attn_bwd(split, dr):
     def body(mine_ref, x_h, w_h, cos_h, sin_h, bias_h, n1_h, qkv_h, datt_h, dh1_h, small_h, *refs):
-        n = 3 if split else 2
+        n = 5 if split else 2
         dx_h, grads_h = refs[0], refs[1:n]
         x, w, cos, sin, bias, n1, qkv, datt, dh1, gain, dx, dw, dqkv, dk, dv, si, so = refs[n : n + 17]
         copies = fetch(
@@ -562,7 +546,8 @@
                 mine = 2 * r + (mine_ref[0] & 1)
                 for i, j in enumerate((mine, mine ^ 1)):
                     src = dw.at[pl.ds(pl.multiple_of(j * dr, dr), dr)]
-                    outs += fetch([(src, grads_h[i].at[r * dr : (r + 1) * dr])], so, 1 + 2 * r + i)
+                    at = (r % 2) * dr
+                    outs += fetch([(src, grads_h[2 * i + r // 2].at[at : at + dr])], so, 1 + 2 * r + i)
         else:
             outs += fetch([(dw, grads_h[0])], so, 1)
         wait(outs)
@@ -571,7 +556,7 @@
 
 
 def run_attn_bwd(split, dr, args):
-    grads = [((4 * dr, 2176), BF)] * 2 if split else [((MODEL_WIDTH, 2176), BF)]
+    grads = [((2 * dr, 2176), BF)] * 4 if split else [((MODEL_WIDTH, 2176), BF)]
     tile = pltpu.VMEM((T, LANES), F32)
     return call(
         attn_bwd(split, dr),
@@ -701,6 +686,9 @@
     def swap(a):
         return lax.all_to_all(a, "fsdp", 0, 0, axis_index_groups=core_groups)
 
+    def swap_all(a):
+        return lax.all_to_all(a, "fsdp", 0, 0, axis_index_groups=low_groups)
+
     def z_sum(blocks):
         total = blocks[0].astype(F32)
         for k in range(1, groups):
@@ -733,12 +721,13 @@
 
         route_rows = routes.T.astype(BF)
         route_rows = [route_rows, to_x(route_rows), to_y(route_rows), to_diag(route_rows)]
-        blocks = z_all(jnp.concatenate([own_qkv, own_out], axis=1))
 
         gu = gate_up_weight.reshape(dr, 4, 2, 2, HALF)
         dn = down_weight.reshape(dr, 4, 1, 2, HALF)
         parts = jnp.concatenate([gu, dn], axis=2)
         parts = jnp.transpose(parts, (1, 3, 0, 2, 4)).reshape(8, dr, 3 * HALF)
+        parts, own_qkv, own_out = tie((parts, own_qkv, own_out))
+        blocks = z_all(jnp.concatenate([own_qkv, own_out], axis=1))
         unit = lax.all_to_all(parts, "fsdp", 0, 0, axis_index_groups=low_groups)
         unit = unit.reshape(8 * dr, 3 * HALF)
         if rest > 1:
@@ -762,10 +751,12 @@
             qx = to_x(cols_qkv)
             qy = to_y(cols_qkv)
             qc = to_core(cols_qkv)
-            qx, qy, qc, units_1 = tie((qx, qy, qc, units_1))
+            qx, qy, qc = tie((qx, qy, qc))
             qa = to_x(qy[:h])
             qb = to_y(qx[h:])
-            pieces = [cols_qkv, qx, qy, qa, qb, qc, to_core(qx), to_core(qy), to_core(qa), to_core(qb)]
+            cx, cy = to_core(qx), to_core(qy)
+            qa, qb, units_1 = tie((qa, qb, units_1))
+            pieces = [cols_qkv, qx, qy, qa, qb, qc, cx, cy, to_core(qa), to_core(qb)]
             places = [(0, 0, dr), (2, 0, dr), (4, 0, dr), (6, 0, h), (6, h, h),
                       (1, 0, dr), (3, 0, dr), (5, 0, dr), (7, 0, h), (7, h, h)]
         else:
@@ -774,7 +765,7 @@
         w_out = lax.all_gather(cols_out, "fsdp", axis=0, tiled=True)
         core_0 = to_core(after(unit, *pieces))
         dyg = lax.all_gather(after(cotangent, cols_out), "fsdp", axis=0, tiled=True, axis_index_groups=core_groups)
-        tokens_f = after(tokens, *pieces)
+        tokens_f = after(tokens, *pieces, *route_rows)
         units_2 = z_next(units_1)
         w_qkv, n1, qkv, att, h1, n2, small = call(
             attn_fwd(places, dr),
@@ -831,30 +822,32 @@
         own_0, sib_0, outs, oown = run_last(e, xs, dyg, (gh0, dgu0), (gh0, gh1, gh2, gh3), ws)
         parts, own, outs, sib_3 = tie((parts, own, outs, sib_3))
         sib_0 = to_core(sib_0)
+        outs = swap(outs)
         dh1, datt, dwo = run_join((e, own, parts, gates, h1, n2, cotangent, w_out, att, small))
         hop, dh1, sib_0 = tie((hop, dh1, sib_0))
-        sum_3, dh1, outs = tie((chip_sum((own_3, sib_3), hop), dh1, outs))
+        sum_3, dh1 = tie((chip_sum((own_3, sib_3), hop), dh1))
         hop = z_next(sum_3)
-        outs = swap(outs)
         rs_out = lax.psum_scatter(dwo, "fsdp", scatter_dimension=0, tiled=True)
         dx, *dw = run_attn_bwd(
             rest == 1, dr, (mine_s, tokens, w_qkv, cos, sin, bias, n1, qkv, datt, dh1, small)
         )
-        hop, outs, *dw = tie((hop, outs, *dw))
         if rest == 1:
-            sib, rs_out = tie((to_core(dw[1]), rs_out))
-            total = swap(chip_sum((dw[0], sib)).reshape(4, dr, -1))
-            own_0, total = tie((own_0, total))
+            sib_a, sib_b, hop, rs_out, outs = tie((to_core(dw[2]), to_core(dw[3]), hop, rs_out, outs))
+            total = jnp.concatenate([dw[0].astype(F32) + sib_a.astype(F32), dw[1].astype(F32) + sib_b.astype(F32)])
+            total = swap(total.astype(BF).reshape(4, dr, -1))
+            acc = chip_sum((own_0, sib_0), hop)
+            acc, total = tie((acc, total))
+            home = swap_all(acc.reshape(8, dr, UNIT))
             rs_qkv = jnp.sum(total.astype(F32), axis=0).astype(BF)
         else:
             rs_qkv = lax.psum_scatter(dw[0], "fsdp", scatter_dimension=0, tiled=True)
 
-        acc = chip_sum((own_0, sib_0), hop)
         if rest > 1:
             acc = lax.psum_scatter(
-                acc, "fsdp", scatter_dimension=0, tiled=True, axis_index_groups=rest_groups
+                chip_sum((own_0, sib_0), hop), "fsdp", scatter_dimension=0, tiled=True,
+                axis_index_groups=rest_groups,
             )
-        home = lax.all_to_all(acc.reshape(8, dr, 3 * HALF), "fsdp", 0, 0, axis_index_groups=low_groups)
+            home = swap_all(acc.reshape(8, dr, UNIT))
         gate_up_grad, down_grad = call(
             settle(dr), [((dr, 4, 2 * FF), F32), ((dr, 4, FF), F32)], [HB], [VM] * 2,
             [pltpu.VMEM((8, dr, UNIT), BF), pltpu.SemaphoreType.DMA((1,))], (home,), "settle", 48, 0,

time: 446 us -> 422 us (0.946)
  waiting for transfers between devices: 177 us -> 159 us
    ppermute x6, waiting for transfers between devices: 62.2 us -> 31.1 us  [z_next(): return lax.ppermute(a, 'grp', shifted(1))]
    ppermute x5, waiting for transfers between devices: 35.1 us -> 50.5 us  [to_x(): return lax.ppermute(a, 'fsdp', flip(2))]
    all_to_all x3, waiting for transfers between devices: 32.7 us -> 25.4 us  [swap(): return lax.all_to_all(a, 'fsdp', 0, 0, axis_index_groups=core_groups)]
    convert_element_type x5 -> x4, other arithmetic: 18.9 us -> 16 us  [chip_sum(): return total.astype(BF)]
    unnamed x84 -> x85, local copies, waits for them, and re-layouts: 10.6 us -> 10.2 us
  transfers between devices with their start and end apart: 45 -> 46, of which waited for: 20 -> 25; matrix products, arithmetic and copies ran while one was open for 7% -> 9% of each run, Pallas kernels for 31% -> 32%
where the time goes in v4:
time: 422 us; the launch traced here: 417 us
  waiting for transfers between devices  159 us (38%)
  Pallas kernels  139 us (33%)
  starting transfers between devices  54.2 us (13%)
  other arithmetic  32.5 us (8%)
  local copies, waits for them, and re-layouts  17.3 us (4%)
  between operations  15.1 us (4%)
    pallas_call x9, Pallas kernels, call(): pl.pallas_call(body, out_shape=[jax.ShapeDtypeStruct(s, d) for s, d in ou...  139 us
    ppermute x5, waiting for transfers between devices, to_x(): return lax.ppermute(a, 'fsdp', flip(2))  50.5 us
    ppermute x6, waiting for transfers between devices, z_next(): return lax.ppermute(a, 'grp', shifted(1))  31.1 us
    all_to_all x3, waiting for transfers between devices, swap(): return lax.all_to_all(a, 'fsdp', 0, 0, axis_index_groups=core_groups)  25.4 us
    convert_element_type x4, other arithmetic, chip_sum(): return total.astype(BF)  16 us
    all_to_all x1, waiting for transfers between devices, shards(): unit = lax.all_to_all(parts, 'fsdp', 0, 0, axis_index_groups=low_groups)  15 us
    all_to_all x3, starting transfers between devices, swap(): return lax.all_to_all(a, 'fsdp', 0, 0, axis_index_groups=core_groups)  13.2 us
    reduce_scatter x1, waiting for transfers between devices, shards(): rs_out = lax.psum_scatter(dwo, 'fsdp', scatter_dimension=0, tiled=True)  10.4 us
  transfers between devices with their start and end apart: 46, of which 25 were waited for; matrix products, arithmetic and copies ran while one was open for 9% of the time, Pallas kernels for 32%

profile of v4, /device:TPU:0, one launch (start us, length us, event | category | flops | bytes accessed | tf_op | source)
XLA Modules:
  0.0 417.0 jit_solution(16646541590789411707)
XLA Ops:
  18.9 4.3 %all-to-all-start = ((bf16[8,128,768]{1,2,0:T(8,128)(2,1)}), bf16[8,128,768]{1,2,0:T(8,128)(2,1)}, u32[]{:S(2)}, u32[]{:S(2)}) async-start(bf16[8,128,768]{1,2,0:T(8,128)(2,1)} %bitcast.10), calls=%async_computation | async-start | bytes 3145728 | tf_op jit(solution)/shard_map/all_to_all | solution.py:731
  29.2 15.0 %all-to-all-done = bf16[8,128,768]{1,2,0:T(8,128)(2,1)} async-done(((bf16[8,128,768]{1,2,0:T(8,128)(2,1)}), bf16[8,128,768]{1,2,0:T(8,128)(2,1)}, u32[]{:S(2)}, u32[]{:S(2)}) %all-to-all-start) | async-done | bytes 1572896 | tf_op jit(solution)/shard_map/all_to_all | solution.py:731
  52.0 15.6 %collective-permute-done.3.refs_1_ = bf16[128,2176]{1,0:T(8,128)(2,1)S(1)} collective-permute-done((bf16[128,2176]{1,0:T(8,128)(2,1)}, bf16[128,2176]{1,0:T(8,128)(2,1)S(1)}, u32[]{:S(2)}, u32[]{:S(2)}) %collective-permute-start.3) | collective-permute-done | bytes 557088 | tf_op jit(solution)/shard_map/ppermute | solution.py:668
  71.2 7.7 %collective-permute-done.6.refs_3_ = bf16[64,2176]{1,0:T(8,128)(2,1)S(1)} collective-permute-done((bf16[64,2176]{1,0:T(8,128)(2,1)S(1)}, bf16[64,2176]{1,0:T(8,128)(2,1)S(1)}, u32[]{:S(2)}, u32[]{:S(2)}) %collective-permute-start.6) | collective-permute-done | bytes 278560 | tf_op jit(solution)/shard_map/ppermute | solution.py:668
  92.9 11.7 %attn_fwd.1 = (bf16[1024,2048]{1,0:T(8,128)(2,1)}, bf16[384,1024]{1,0:T(8,128)(2,1)}, bf16[4,384,512]{2,1,0:T(8,128)(2,1)}, bf16[4,384,256]{2,1,0:T(8,128)(2,1)}...) custom-call(s32[1]{0:T(128)} %bitcast.mine_ref, ...), custom_call_target="tpu_custom_call" | custom-call | flops 4000000000 | bytes 18546692 | tf_op jit(solution)/shard_map/attn_fwd/pallas_call | solution.py:45
  106.6 15.2 %collective-permute-done.20.refs_8_.refs_10_.refs_16_ = bf16[1024,768]{1,0:T(8,128)(2,1)} collective-permute-done((bf16[1024,768]{1,0:T(8,128)(2,1)}, bf16[1024,768]{1,0:T(8,128)(2,1)}, u32[]{:S(2)}, u32[]{:S(2)}) %collective-permute-start.20) | collective-permute-done | bytes 1572896 | tf_op jit(solution)/shard_map/ppermute | solution.py:665
  121.7 19.7 %collective-permute-done.18.refs_1_ = bf16[384,1024]{1,0:T(8,128)(2,1)S(1)} collective-permute-done((bf16[384,1024]{1,0:T(8,128)(2,1)}, bf16[384,1024]{1,0:T(8,128)(2,1)S(1)}, u32[]{:S(2)}, u32[]{:S(2)}) %collective-permute-start.18) | collective-permute-done | bytes 786464 | tf_op jit(solution)/shard_map/ppermute | solution.py:668
  145.8 7.4 %collective-permute-done.21.refs_3_ = bf16[192,1024]{1,0:T(8,128)(2,1)S(1)} collective-permute-done((bf16[192,1024]{1,0:T(8,128)(2,1)S(1)}, bf16[192,1024]{1,0:T(8,128)(2,1)S(1)}, u32[]{:S(2)}, u32[]{:S(2)}) %collective-permute-start.21) | collective-permute-done | bytes 393248 | tf_op jit(solution)/shard_map/ppermute | solution.py:668
  154.5 18.4 %stage_a.1 = (bf16[1536,512]{1,0:T(8,128)(2,1)}, bf16[1536,1024]{1,0:T(8,128)(2,1)}, bf16[1024,768]{1,0:T(8,128)(2,1)}, bf16[1024,768]{1,0:T(8,128)(2,1)}, f32[1536,128]{1,0:T(8,128)}, /*index=5*/f32[1536,128]{1,0:T(8,128)}) custom-call(s32[5]{0:T(128)} %pad_add_fusion.e_ref, bf16[384,1024]{1,0:T(8,128)(2,1)} %get-tuple-element.144.refs_0_.n2_h, ...), custom_call_target="tpu_custom_call" | custom-call | flops 9663676416 | bytes 19423252 | tf_op jit(solution)/shard_map/stage_a/pallas_call | solution.py:45
  173.1 23.0 %stage_b.1 = (bf16[1536,512]{1,0:T(8,128)(2,1)}, bf16[1536,1024]{1,0:T(8,128)(2,1)}, bf16[1536,512]{1,0:T(8,128)(2,1)}, bf16[1536,1024]{1,0:T(8,128)(2,1)}, f32[...) custom-call(s32[5]{0:T(128)} %pad_add_fusion.e_ref, ...), custom_call_target="tpu_custom_call" | custom-call | flops 14495514624 | bytes 27525140 | tf_op jit(solution)/shard_map/stage_b/pallas_call | solution.py:45
  204.1 21.4 %stage_c.1 = (bf16[1536,512]{1,0:T(8,128)(2,1)}, bf16[1536,1024]{1,0:T(8,128)(2,1)}, f32[1536,128]{1,0:T(8,128)}, bf16[4,384,1152]{2,1,0:T(8,128)(2,1)}) custom-call(s32[5]{0:T(128)} %pad_add_fusion.e_ref, bf16[384,1024]{1,0:T(8,128)(2,1)} %get-tuple-element.144.refs_0_.n2_h, bf16[384,1024]{1,0:T(8,128)(2,1)} %copy-done.4, bf16[384,1024]{1,0:T(8,128)(2,1)} %copy-done.5, ...), custom_call_target="tpu_custom_call" | custom-call | flops 9663676416 | bytes 38928404 | tf_op jit(solution)/shard_map/stage_c/pallas_call | solution.py:45
  225.5 4.7 %all-to-all-start.1 = ((bf16[4,384,1152]{2,1,0:T(8,128)(2,1)}), bf16[4,384,1152]{2,1,0:T(8,128)(2,1)}, u32[]{:S(2)}, u32[]{:S(2)}) async-start(bf16[4,384,1152]{2,1,0:T(8,128)(2,1)} %get-tuple-element.188), calls=%async_computation.1 | async-start | bytes 7077888 | tf_op jit(solution)/shard_map/all_to_all | solution.py:687
  230.3 14.9 %late_stage.1 = (bf16[1024,768]{1,0:T(8,128)(2,1)}, bf16[1024,768]{1,0:T(8,128)(2,1)}, f32[384,1152]{1,0:T(8,128)}) custom-call(s32[5]{0:T(128)} %pad_add_fusion.e_ref, bf16[384,1024]{1,0:T(8,128)(2,1)} %get-tuple-element.144.refs_0_.n2_h, bf16[384,1024]{1,0:T(8,128)(2,1)} %copy-done.4, bf16[384,1024]{1,0:T(8,128)(2,1)} %copy-done.5, ...), custom_call_target="tpu_custom_call" | custom-call | flops 9663676416 | bytes 41877524 | tf_op jit(solution)/shard_map/late_stage/pallas_call | solution.py:45
  250.8 17.5 %last_stage.1 = (bf16[1024,768]{1,0:T(8,128)(2,1)}, bf16[1024,768]{1,0:T(8,128)(2,1)}, bf16[4,384,1024]{2,1,0:T(8,128)(2,1)}, f32[384,1024]{1,0:T(8,128)}) custom-call(s32[5]{0:T(128)} %pad_add_fusion.e_ref, bf16[384,1024]{1,0:T(8,128)(2,1)} %get-tuple-element.144.refs_0_.n2_h, bf16[384,1024]{1,0:T(8,128)(2,1)} %copy-done.4, bf16[384,1024]{1,0:T(8,128)(2,1)} %copy-done.5, ...), custom_call_target="tpu_custom_call" | custom-call | flops 9663676416 | bytes 37748756 | tf_op jit(solution)/shard_map/last_stage/pallas_call | solution.py:45
  271.4 8.9 %join.1 = (f32[384,1024]{1,0:T(8,128)}, bf16[4,384,256]{2,1,0:T(8,128)(2,1)}, bf16[1024,1152]{1,0:T(8,128)(2,1)}) custom-call(s32[5]{0:T(128)} %pad_add_fusion.e_ref, f32[384,1152]{1,0:T(8,128)} %get-tuple-element.192.p_h, bf16[4,384,1152]{2,1,0:T(8,128)(2,1)} %all-to-all-done.1.parts_h, f32[1536,128]{1,0:T(8,128)} %get-tuple-element.156.refs_10_.refs_14_.gates_h, ...), custom_call_target="tpu_custom_call" | custom-call | flops 2000000000 | bytes 17367060 | tf_op jit(solution)/shard_map/join/pallas_call | solution.py:45
  280.4 4.7 %all-to-all-start.2 = ((bf16[4,384,1024]{2,1,0:T(8,128)(2,1)}), bf16[4,384,1024]{2,1,0:T(8,128)(2,1)}, u32[]{:S(2)}, u32[]{:S(2)}) async-start(bf16[4,384,1024]{2,1,0:T(8,128)(2,1)} %get-tuple-element.208), calls=%async_computation.3 | async-start | bytes 6291456 | tf_op jit(solution)/shard_map/all_to_all | solution.py:687
  287.1 4.9 %add_convert_fusion.1 = bf16[1024,768]{1,0:T(8,128)(2,1)} fusion(bf16[1024,768]{1,0:T(8,128)(2,1)} %collective-permute-done.30, bf16[1024,768]{1,0:T(8,128)(2,1)} %collective-permute-done.29, bf16[1024,768]{1,0:T(8,128)(2,1)} %get-tuple-element.196), kind=kLoop, calls=%fused_computation.2 | loop fusion | flops 4718592 | bytes 6291456 | tf_op jit(solution)/shard_map/convert_element_type | solution.py:799
  292.5 19.0 %attn_bwd.1 = (f32[384,1024]{1,0:T(8,128)}, bf16[256,2176]{1,0:T(8,128)(2,1)}, bf16[256,2176]{1,0:T(8,128)(2,1)}, bf16[256,2176]{1,0:T(8,128)(2,1)}, bf16[256,2176]{1,0:T(8,128)(2,1)}) custom-call(s32[1]{0:T(128)} %bitcast.mine_ref, bf16[384,1024]{1,0:T(8,128)(2,1)} %x_h.1, bf16[1024,2048]{1,0:T(8,128)(2,1)} %get-tuple-element.185.w_h, ...), custom_call_target="tpu_custom_call" | custom-call | flops 6000000000 | bytes 17235972 | tf_op jit(solution)/shard_map/attn_bwd/pallas_call | solution.py:45
  316.1 12.7 %collective-permute-done.34 = bf16[1024,768]{1,0:T(8,128)(2,1)} collective-permute-done((bf16[1024,768]{1,0:T(8,128)(2,1)}, bf16[1024,768]{1,0:T(8,128)(2,1)}, u32[]{:S(2)}, u32[]{:S(2)}) %collective-permute-start.34) | collective-permute-done | bytes 1572896 | tf_op jit(solution)/shard_map/ppermute | solution.py:665
  328.8 10.4 %reduce-scatter.2.cloned.1.call-done = bf16[128,1152]{1,0:T(8,128)(2,1)} async-done(((bf16[1024,1152]{1,0:T(8,128)(2,1)}), bf16[128,1152]{1,0:T(8,128)(2,1)}) %reduce-scatter.2.cloned.1.call-update) | async-done | bytes 294928 | tf_op jit(solution)/shard_map/reduce_scatter | solution.py:830
  350.5 22.4 %all-to-all-done.3 = bf16[4,128,2176]{2,1,0:T(8,128)(2,1)S(1)} async-done(((bf16[4,128,2176]{2,1,0:T(8,128)(2,1)}), bf16[4,128,2176]{2,1,0:T(8,128)(2,1)S(1)}, u32[]{:S(2)}, u32[]{:S(2)}) %all-to-all-start.3) | async-done | bytes 2228256 | tf_op jit(solution)/shard_map/all_to_all | solution.py:687
  387.0 6.9 %collective-permute-done.37 = bf16[128,896]{1,0:T(8,128)(2,1)} collective-permute-done((bf16[128,896]{1,0:T(8,128)(2,1)}, bf16[128,896]{1,0:T(8,128)(2,1)}, u32[]{:S(2)}, u32[]{:S(2)}) %collective-permute-start.37) | collective-permute-done | bytes 229408 | tf_op jit(solution)/shard_map/ppermute | solution.py:695
  398.9 5.4 %all-to-all-done.4.home_h = bf16[8,128,768]{2,1,0:T(8,128)(2,1)S(1)} async-done(((bf16[8,128,768]{2,1,0:T(8,128)(2,1)}), bf16[8,128,768]{2,1,0:T(8,128)(2,1)S(1)}, u32[]{:S(2)}, u32[]{:S(2)}) %all-to-all-start.4) | async-done | bytes 1572896 | tf_op jit(solution)/shard_map/all_to_all | solution.py:690
  405.5 4.5 %settle.1 = (f32[128,4,1024]{2,1,0:T(4,128)}, f32[128,4,512]{2,1,0:T(4,128)}) custom-call(bf16[8,128,768]{2,1,0:T(8,128)(2,1)} %copy-done.3), custom_call_target="tpu_custom_call" | custom-call | bytes 4718592 | tf_op jit(solution)/shard_map/settle/pallas_call | solution.py:45
  (224 shorter events, 105.7 us)
Async XLA Ops:
  11.7 34.2 %collective-permute-start = (bf16[128,768]{1,0:T(8,128)(2,1)S(1)}, bf16[128,768]{1,0:T(8,128)(2,1)S(1)}, u32[]{:S(2)}, u32[]{:S(2)}) collective-permute-start(bf16[128,768]{1,0:T(8,128)(2,1)S(1)} %constant_dynamic-update-slice_fusion), channel_id=1, source_target_pairs={{0,8},{8,24},{24,16},{16,0},{1,9},{9,25},{25,17},{17,1},{2,10},{10... | collective-permute-start | bytes 589832 | tf_op jit(solution)/shard_map/ppermute | solution.py:720
  14.8 31.1 %collective-permute-start.1 = (bf16[128,768]{1,0:T(8,128)(2,1)S(1)}, bf16[128,768]{1,0:T(8,128)(2,1)S(1)}, u32[]{:S(2)}, u32[]{:S(2)}) collective-permute-start(bf16[128,768]{1,0:T(8,128)(2,1)S(1)} %constant_dynamic-update-slice_fusion), channel_id=1, source_target_pairs={{0,24},{8,16},{24,0},{16,8},{1,25},{9,17},{25,1},{17,9},{2,26},{10... | collective-permute-start | bytes 589832 | tf_op jit(solution)/shard_map/ppermute | solution.py:720
  17.3 28.7 %collective-permute-start.2 = (bf16[128,768]{1,0:T(8,128)(2,1)S(1)}, bf16[128,768]{1,0:T(8,128)(2,1)S(1)}, u32[]{:S(2)}, u32[]{:S(2)}) collective-permute-start(bf16[128,768]{1,0:T(8,128)(2,1)S(1)} %constant_dynamic-update-slice_fusion), channel_id=1, source_target_pairs={{0,16},{8,0},{24,8},{16,24},{1,17},{9,1},{25,9},{17,25},{2,18},{10... | collective-permute-start | bytes 589832 | tf_op jit(solution)/shard_map/ppermute | solution.py:720
  18.9 25.4 %all-to-all-start = ((bf16[8,128,768]{1,2,0:T(8,128)(2,1)}), bf16[8,128,768]{1,2,0:T(8,128)(2,1)}, u32[]{:S(2)}, u32[]{:S(2)}) async-start(bf16[8,128,768]{1,2,0:T(8,128)(2,1)} %bitcast.10), calls=%async_computation | async-start | bytes 3145728 | tf_op jit(solution)/shard_map/all_to_all | solution.py:731
  23.2 69.7 %all-gather.3.cloned.1.call-start = ((), (), s32[]{:S(2)}) async-start(), calls=%async_computation.6 | async-start | bytes 2359296 | tf_op jit(solution)/shard_map/all_gather | solution.py:765
  47.0 107.6 %all-gather.5.cloned.1.call-start = ((), (), s32[]{:S(2)}) async-start(), calls=%async_computation.7 | async-start | bytes 3932160 | tf_op jit(solution)/shard_map/all_gather | solution.py:767
  47.0 34.2 %collective-permute-start.8 = (bf16[1024,768]{1,0:T(8,128)(2,1)S(1)}, bf16[1024,768]{1,0:T(8,128)(2,1)}, u32[]{:S(2)}, u32[]{:S(2)}) collective-permute-start(bf16[1024,768]{1,0:T(8,128)(2,1)S(1)} %bitcast.28), channel_id=1, source_target_pairs={{0,8},{8,24},{24,16},{16,0},{1,9},{9,25},{25,17},{17,1},{2,10},{10... | collective-permute-start | bytes 4718600 | tf_op jit(solution)/shard_map/ppermute | solution.py:665
  83.9 37.8 %collective-permute-start.20 = (bf16[1024,768]{1,0:T(8,128)(2,1)}, bf16[1024,768]{1,0:T(8,128)(2,1)}, u32[]{:S(2)}, u32[]{:S(2)}) collective-permute-start(bf16[1024,768]{1,0:T(8,128)(2,1)} %collective-permute-done.8.refs_6_.refs_8_.refs_14_), channel_id=1, source_target_pairs={{0,8},{8,24},{24,16},{16,0},{1,9},{9,25},{25,17},{17,1},{2,10},{10... | collective-permute-start | bytes 4718600 | tf_op jit(solution)/shard_map/ppermute | solution.py:665
  104.7 49.9 %collective-permute-start.17 = (bf16[1024,768]{1,0:T(8,128)(2,1)}, bf16[1024,768]{1,0:T(8,128)(2,1)}, u32[]{:S(2)}, u32[]{:S(2)}) collective-permute-start(bf16[1024,768]{1,0:T(8,128)(2,1)} %collective-permute-done.8.refs_6_.refs_8_.refs_14_), channel_id=1, source_target_pairs={{0,1},{1,0},{2,3},{3,2},{4,5},{5,4},{6,7},{7,6},{8,9},{9,8},{10,11... | collective-permute-start | bytes 4718600 | tf_op jit(solution)/shard_map/ppermute | solution.py:677
  104.7 36.8 %collective-permute-start.18 = (bf16[384,1024]{1,0:T(8,128)(2,1)}, bf16[384,1024]{1,0:T(8,128)(2,1)S(1)}, u32[]{:S(2)}, u32[]{:S(2)}) collective-permute-start(bf16[384,1024]{1,0:T(8,128)(2,1)} %get-tuple-element.144.refs_0_.n2_h), channel_id=1, source_target_pairs={{0,2},{1,3},{2,0},{3,1},{4,6},{5,7},{6,4},{7,5},{8,10},{9,11},{10,... | collective-permute-start | bytes 2359304 | tf_op jit(solution)/shard_map/ppermute | solution.py:668
  104.9 36.6 %collective-permute-start.19 = (bf16[384,1024]{1,0:T(8,128)(2,1)}, bf16[384,1024]{1,0:T(8,128)(2,1)S(1)}, u32[]{:S(2)}, u32[]{:S(2)}) collective-permute-start(bf16[384,1024]{1,0:T(8,128)(2,1)} %get-tuple-element.144.refs_0_.n2_h), channel_id=1, source_target_pairs={{0,4},{1,5},{2,6},{3,7},{4,0},{5,1},{6,2},{7,3},{8,12},{9,13},{10,... | collective-permute-start | bytes 2359304 | tf_op jit(solution)/shard_map/ppermute | solution.py:671
  141.5 31.6 %collective-permute-start.23 = (bf16[1024,768]{1,0:T(8,128)(2,1)}, bf16[1024,768]{1,0:T(8,128)(2,1)}, u32[]{:S(2)}, u32[]{:S(2)}) collective-permute-start(bf16[1024,768]{1,0:T(8,128)(2,1)} %collective-permute-done.20.refs_8_.refs_10_.refs_16_), channel_id=1, source_target_pairs={{0,1},{1,0},{2,3},{3,2},{4,5},{5,4},{6,7},{7,6},{8,9},{9,8},{10,11... | collective-permute-start | bytes 4718600 | tf_op jit(solution)/shard_map/ppermute | solution.py:677
  143.9 52.1 %collective-permute-start.25 = (bf16[1024,768]{1,0:T(8,128)(2,1)}, bf16[1024,768]{1,0:T(8,128)(2,1)}, u32[]{:S(2)}, u32[]{:S(2)}) collective-permute-start(bf16[1024,768]{1,0:T(8,128)(2,1)} %collective-permute-done.20.refs_8_.refs_10_.refs_16_), channel_id=1, source_target_pairs={{0,8},{8,24},{24,16},{16,0},{1,9},{9,25},{25,17},{17,1},{2,10},{10... | collective-permute-start | bytes 4718600 | tf_op jit(solution)/shard_map/ppermute | solution.py:665
  173.0 23.1 %collective-permute-start.26 = (bf16[1024,768]{1,0:T(8,128)(2,1)}, bf16[1024,768]{1,0:T(8,128)(2,1)S(1)}, u32[]{:S(2)}, u32[]{:S(2)}) collective-permute-start(bf16[1024,768]{1,0:T(8,128)(2,1)} %get-tuple-element.160), channel_id=1, source_target_pairs={{0,1},{1,0},{2,3},{3,2},{4,5},{5,4},{6,7},{7,6},{8,9},{9,8},{10,11... | collective-permute-start | bytes 4718600 | tf_op jit(solution)/shard_map/ppermute | solution.py:677
  197.7 27.8 %collective-permute-start.24 = (bf16[1024,768]{1,0:T(8,128)(2,1)}, bf16[1024,768]{1,0:T(8,128)(2,1)}, u32[]{:S(2)}, u32[]{:S(2)}) collective-permute-start(bf16[1024,768]{1,0:T(8,128)(2,1)} %get-tuple-element.159), channel_id=1, source_target_pairs={{0,1},{1,0},{2,3},{3,2},{4,5},{5,4},{6,7},{7,6},{8,9},{9,8},{10,11... | collective-permute-start | bytes 4718600 | tf_op jit(solution)/shard_map/ppermute | solution.py:677
  201.2 44.5 %collective-permute-start.28 = (bf16[1024,768]{1,0:T(8,128)(2,1)}, bf16[1024,768]{1,0:T(8,128)(2,1)}, u32[]{:S(2)}, u32[]{:S(2)}) collective-permute-start(bf16[1024,768]{1,0:T(8,128)(2,1)} %add_convert_fusion.3), channel_id=1, source_target_pairs={{0,8},{8,24},{24,16},{16,0},{1,9},{9,25},{25,17},{17,1},{2,10},{10... | collective-permute-start | bytes 4718600 | tf_op jit(solution)/shard_map/ppermute | solution.py:665
  225.5 45.9 %all-to-all-start.1 = ((bf16[4,384,1152]{2,1,0:T(8,128)(2,1)}), bf16[4,384,1152]{2,1,0:T(8,128)(2,1)}, u32[]{:S(2)}, u32[]{:S(2)}) async-start(bf16[4,384,1152]{2,1,0:T(8,128)(2,1)} %get-tuple-element.188), calls=%async_computation.1 | async-start | bytes 7077888 | tf_op jit(solution)/shard_map/all_to_all | solution.py:687
  230.3 108.9 %reduce-scatter.2.cloned.1.call-start = ((), (), s32[]{:S(2)}) async-start(), calls=%async_computation.8 | async-start | bytes 2654208 | tf_op jit(solution)/shard_map/reduce_scatter | solution.py:830
  245.2 23.2 %collective-permute-start.29 = (bf16[1024,768]{1,0:T(8,128)(2,1)}, bf16[1024,768]{1,0:T(8,128)(2,1)}, u32[]{:S(2)}, u32[]{:S(2)}) collective-permute-start(bf16[1024,768]{1,0:T(8,128)(2,1)} %get-tuple-element.191), channel_id=1, source_target_pairs={{0,1},{1,0},{2,3},{3,2},{4,5},{5,4},{6,7},{7,6},{8,9},{9,8},{10,11... | collective-permute-start | bytes 4718600 | tf_op jit(solution)/shard_map/ppermute | solution.py:677
  249.3 37.8 %collective-permute-start.30 = (bf16[1024,768]{1,0:T(8,128)(2,1)}, bf16[1024,768]{1,0:T(8,128)(2,1)}, u32[]{:S(2)}, u32[]{:S(2)}) collective-permute-start(bf16[1024,768]{1,0:T(8,128)(2,1)} %add_convert_fusion.2), channel_id=1, source_target_pairs={{0,8},{8,24},{24,16},{16,0},{1,9},{9,25},{25,17},{17,1},{2,10},{10... | collective-permute-start | bytes 4718600 | tf_op jit(solution)/shard_map/ppermute | solution.py:665
  280.4 48.4 %all-to-all-start.2 = ((bf16[4,384,1024]{2,1,0:T(8,128)(2,1)}), bf16[4,384,1024]{2,1,0:T(8,128)(2,1)}, u32[]{:S(2)}, u32[]{:S(2)}) async-start(bf16[4,384,1024]{2,1,0:T(8,128)(2,1)} %get-tuple-element.208), calls=%async_computation.3 | async-start | bytes 6291456 | tf_op jit(solution)/shard_map/all_to_all | solution.py:687
  292.0 36.8 %collective-permute-start.34 = (bf16[1024,768]{1,0:T(8,128)(2,1)}, bf16[1024,768]{1,0:T(8,128)(2,1)}, u32[]{:S(2)}, u32[]{:S(2)}) collective-permute-start(bf16[1024,768]{1,0:T(8,128)(2,1)} %add_convert_fusion.1), channel_id=1, source_target_pairs={{0,8},{8,24},{24,16},{16,0},{1,9},{9,25},{25,17},{17,1},{2,10},{10... | collective-permute-start | bytes 4718600 | tf_op jit(solution)/shard_map/ppermute | solution.py:665
  342.6 30.3 %all-to-all-start.3 = ((bf16[4,128,2176]{2,1,0:T(8,128)(2,1)}), bf16[4,128,2176]{2,1,0:T(8,128)(2,1)S(1)}, u32[]{:S(2)}, u32[]{:S(2)}) async-start(bf16[4,128,2176]{2,1,0:T(8,128)(2,1)} %bitcast.27), calls=%async_computation.4 | async-start | bytes 4456448 | tf_op jit(solution)/shard_map/all_to_all | solution.py:687
  379.7 24.7 %all-to-all-start.4 = ((bf16[8,128,768]{2,1,0:T(8,128)(2,1)}), bf16[8,128,768]{2,1,0:T(8,128)(2,1)S(1)}, u32[]{:S(2)}, u32[]{:S(2)}) async-start(bf16[8,128,768]{2,1,0:T(8,128)(2,1)} %bitcast.34), calls=%async_computation.5 | async-start | bytes 3145728 | tf_op jit(solution)/shard_map/all_to_all | solution.py:690
  (61 other events, 645.6 us)
Sparse Core Ops, SparseCore 0:
  47.1 30.2 all-gather.2
  79.2 62.4 all-gather.4
  280.5 58.6 reduce-scatter.1

commit v5 on v4

--- a/solution.py
+++ b/solution.py
@@ -1,3 +1,4 @@
+import functools
 import math
 
 import jax
@@ -305,8 +306,8 @@
 def stage_b(e_ref, *refs):
     xs, dyg, ws = refs[0:5], refs[5], refs[6:10]
     gates_h, dgate_i = refs[10:12]
-    gh0_h, dgu0_h, gh2_h, dgu2_h, dgate_h, dwo_h, dws_h = refs[12:19]
-    X, Y, W, GH, DGU, GT, DG, DW, si, so = refs[19:]
+    gh0_h, dgu0_h, gh2_h, dgu2_h, dgate_h = refs[12:17]
+    X, Y, W, GH, DGU, GT, DG, si, so = refs[17:]
     hw = [(ws[i], W.at[i // 2, i % 2]) for i in range(4)]
     trees, second = load_tokens(
         xs, dyg, e_ref[4], X, Y, hw[0:2] + [(gates_h, GT), (dgate_i, DG)], hw[2:], si
@@ -319,15 +320,13 @@
     for t in range(4):
         DG[TREE[t], :] += act(t, e_ref[2], X, Y, W.at[1], GT, GH.at[1], DGU.at[1])
     outs += fetch([(GH.at[1], gh2_h), (DGU.at[1], dgu2_h), (DG, dgate_h)], so, 2)
-    wgrad(X, Y, GH.at[1], DGU.at[1], DW)
-    outs += fetch([(DW.at[0], dwo_h), (DW.at[1], dws_h)], so, 5)
     wait(outs)
 
 
 def run_stage_b(e, xs, dyg, ws, gates, dgate):
     return call(
-        stage_b, ACT_OUT * 2 + GATE_OUT + DW_OUT, [SM] + [HB] * 12, [HB] * 7,
-        stage_scratch(2, [DW_VMEM], 15, 7), (e, *xs, dyg, *ws, gates, dgate), "stage_b", 48, 3 * EXPERT_FLOPS,
+        stage_b, ACT_OUT * 2 + GATE_OUT, [SM] + [HB] * 12, [HB] * 5,
+        stage_scratch(2, [], 15, 5), (e, *xs, dyg, *ws, gates, dgate), "stage_b", 48, 2 * EXPERT_FLOPS,
     )
 
 
@@ -414,41 +413,82 @@
     )
 
 
-def last_stage(e_ref, *refs):
-    xs, dyg, gh_h, dgu_h = refs[0:5], refs[5], refs[6], refs[7]
-    ghs, ws = refs[8:12], refs[12:20]
-    dwo_h, dws_h, parts_h, own_h = refs[20:24]
-    X, Y, GH, DGU, DW, A, W, O, OF, si, so = refs[24:]
-    first = fetch(chip_pairs(dyg, e_ref[4], Y) + [(gh_h, GH)], si)
+def grads_stage(e_ref, *refs):
+    xs, dyg, acts = refs[0:5], refs[5], refs[6:10]
+    dws = refs[10:14]
+    X, Y, GH, DGU, DW, si, so = refs[14:]
+    first = fetch(chip_pairs(dyg, e_ref[4], Y) + [(acts[0], GH.at[0])], si)
     wait(first)
-    second = fetch(token_pairs(xs, X) + [(dgu_h, DGU)], si, 5)
-    third = fetch(back_pairs(ghs, ws, 0, ROWS, HALF, WIDE, A, W), si, 11)
-    wgrad_down(Y, GH, DW)
-    wait(second)
-    wgrad_up(X, DGU, DW)
-    outs = fetch([(DW.at[0], dwo_h), (DW.at[1], dws_h)], so)
-    wait(third)
+    second = fetch(token_pairs(xs, X) + [(acts[1], DGU.at[0])], si, 5)
+    third = fetch([(acts[2], GH.at[1]), (acts[3], DGU.at[1])], si, 11)
+    outs = []
+    for i in range(2):
+        wgrad_down(Y, GH.at[i], DW.at[i])
+        if i == 0:
+            wait(second)
+        wgrad_up(X, DGU.at[i], DW.at[i])
+        outs += fetch([(DW.at[i, 0], dws[2 * i]), (DW.at[i, 1], dws[2 * i + 1])], so, 2 * i)
+        if i == 0:
+            wait(third)
+    wait(outs)
+
+
+def run_grads(e, xs, dyg, acts):
+    args = (e, *xs, dyg, *acts)
+    return call(
+        grads_stage, DW_OUT * 2, [SM] + [HB] * (len(args) - 1), [HB] * 4,
+        [
+            pltpu.VMEM((ROWS, MODEL_WIDTH), BF), pltpu.VMEM((ROWS, MODEL_WIDTH), BF),
+            pltpu.VMEM((2, ROWS, FF), BF), pltpu.VMEM((2, ROWS, 2 * FF), BF),
+            pltpu.VMEM((2, 2, MODEL_WIDTH, UNIT), BF),
+            pltpu.SemaphoreType.DMA((13,)), pltpu.SemaphoreType.DMA((4,)),
+        ],
+        args, "grads_stage", 52, 2 * EXPERT_FLOPS,
+    )
+
+
+def out_stage(e_ref, *refs):
+    ghs, ws = refs[0:4], refs[4:12]
+    parts_h, own_h = refs[12:14]
+    A, W, O, OF, si, so = refs[14:]
+    wait(fetch(back_pairs(ghs, ws, 0, ROWS, HALF, WIDE, A, W), si))
+    outs = []
     for i, t in enumerate((3, 1, 2, 0)):
         total = dotg(A[TREE[t], :], W[...], NT)
         dst = O.at[i] if t else OF
         dst[...] = total.astype(BF) if t else total
-        outs += fetch([(dst, parts_h.at[e_ref[4] ^ t] if t else own_h)], so, 2 + i)
+        outs += fetch([(dst, parts_h.at[e_ref[4] ^ t] if t else own_h)], so, i)
     wait(outs)
 
 
-def run_last(e, xs, dyg, acts, ghs, ws):
-    args = (e, *xs, dyg, *acts, *ghs, *ws)
+def run_out(e, ghs, ws):
     return call(
-        last_stage, DW_OUT + [((4, T, MODEL_WIDTH), BF), ((T, MODEL_WIDTH), F32)],
-        [SM] + [HB] * (len(args) - 1), [HB] * 4,
+        out_stage, [((4, T, MODEL_WIDTH), BF), ((T, MODEL_WIDTH), F32)], [SM] + [HB] * 12, [HB] * 2,
         [
-            pltpu.VMEM((ROWS, MODEL_WIDTH), BF), pltpu.VMEM((ROWS, MODEL_WIDTH), BF),
-            pltpu.VMEM((ROWS, FF), BF), pltpu.VMEM((ROWS, 2 * FF), BF), DW_VMEM,
             pltpu.VMEM((ROWS, 8 * HALF), BF), pltpu.VMEM((MODEL_WIDTH, 8 * HALF), BF),
             pltpu.VMEM((3, T, MODEL_WIDTH), BF), pltpu.VMEM((T, MODEL_WIDTH), F32),
-            pltpu.SemaphoreType.DMA((23,)), pltpu.SemaphoreType.DMA((6,)),
+            pltpu.SemaphoreType.DMA((12,)), pltpu.SemaphoreType.DMA((4,)),
         ],
-        args, "last_stage", 52, 2 * EXPERT_FLOPS,
+        (e, *ghs, *ws), "out_stage", 32, 2 * ROWS * MODEL_WIDTH * 8 * HALF,
+    )
+
+
+def fold(*refs):
+    totals, outs, H, sem = refs[0:4], refs[4:8], refs[8], refs[9]
+    wait(fetch([(t, H.at[i]) for i, t in enumerate(totals)], sem))
+    for k, o in enumerate(outs):
+        for at, first, width in ((0, k * 512, 512), (512, 2176 + k * 256, 256), (768, 2048, LANES), (896, 3200, LANES)):
+            cols = slice(first, first + width)
+            part = H[0, :, cols].astype(F32) + H[1, :, cols].astype(F32)
+            part = part + (H[2, :, cols].astype(F32) + H[3, :, cols].astype(F32))
+            o[:, at : at + width] = part.astype(BF)
+
+
+def run_fold(total):
+    dr, cols = total[0].shape
+    return call(
+        fold, [((dr, 1024), BF)] * 4, [HB] * 4, [VM] * 4,
+        [pltpu.VMEM((4, dr, cols), BF), pltpu.SemaphoreType.DMA((4,))], total, "fold", 48, 0,
     )
 
 
@@ -475,8 +515,11 @@
     return jnp.where(lanes == lane, total, 0.0)
 
 
-def join(e_ref, p_h, parts_h, gates_h, h1_h, n2_h, dy_h, wo_h, att_h, small_h,
-         dh1_h, datt_h, dwo_h, P, R, GT, H1, N2, DY, WO, ATT, SMALL, DH1, DATT, DWO, si, so):
+def join(split, dr, e_ref, p_h, parts_h, gates_h, h1_h, n2_h, dy_h, wo_h, att_h, small_h,
+         dh1_h, datt_h, *refs):
+    n = 2 if split else 1
+    dwo_h = refs[:n]
+    P, R, GT, H1, N2, DY, WO, ATT, SMALL, DH1, DATT, DWO, si, so = refs[n:]
     copies = fetch(
         [(p_h, P)] + [(parts_h.at[e_ref[4] ^ t], R.at[t - 1]) for t in (1, 2, 3)]
         + [(gates_h.at[0:T], GT), (h1_h, H1), (dy_h, DY),
@@ -505,23 +548,31 @@
     outs += fetch([(DATT, datt_h)], so, 1)
     extra = dotg(N2[...], dl, TN) + columns_of(dn2 * h1 * r2, EXPERTS)
     DWO[:, 1024:1152] = extra.astype(BF)
-    outs += fetch([(DWO, dwo_h)], so, 2)
+    if split:
+        for r in range(4):
+            mine = 2 * (e_ref[4] ^ r) + e_ref[5]
+            for i, at in enumerate((mine, mine ^ 1)):
+                src = DWO.at[pl.ds(pl.multiple_of(at * dr, dr), dr)]
+                outs += fetch([(src, dwo_h[i].at[r * dr : (r + 1) * dr])], so, 2 + 2 * r + i)
+    else:
+        outs += fetch([(DWO, dwo_h[0])], so, 2)
     wait(outs)
 
 
-def run_join(args):
+def run_join(split, dr, args):
     cols = MODEL_WIDTH + LANES
+    grads = [((4 * dr, 1152), BF)] * 2 if split else [((MODEL_WIDTH, 1152), BF)]
     return call(
-        join,
-        [((T, MODEL_WIDTH), F32), ((4, T, 256), BF), ((MODEL_WIDTH, 1152), BF)],
-        [SM] + [HB] * 9, [HB] * 3,
+        functools.partial(join, split, dr),
+        [((T, MODEL_WIDTH), F32), ((4, T, 256), BF)] + grads,
+        [SM] + [HB] * 9, [HB] * (2 + len(grads)),
         [
             pltpu.VMEM((T, cols), F32), pltpu.VMEM((3, T, cols), BF), pltpu.VMEM((T, LANES), F32), pltpu.VMEM((T, MODEL_WIDTH), F32),
             pltpu.VMEM((T, MODEL_WIDTH), BF), pltpu.VMEM((T, MODEL_WIDTH), BF),
             pltpu.VMEM((MODEL_WIDTH, MODEL_WIDTH), BF), pltpu.VMEM((4, T, 256), BF),
             pltpu.VMEM((LANES, MODEL_WIDTH), F32),
             pltpu.VMEM((T, MODEL_WIDTH), F32), pltpu.VMEM((4, T, 256), BF), pltpu.VMEM((MODEL_WIDTH, 1152), BF),
-            pltpu.SemaphoreType.DMA((12,)), pltpu.SemaphoreType.DMA((3,)),
+            pltpu.SemaphoreType.DMA((12,)), pltpu.SemaphoreType.DMA((10,)),
         ],
         args, "join", 40, 2.0e9,
     )
@@ -543,7 +594,7 @@
         outs = fetch([(dx, dx_h)], so)
         if split:
             for r in range(4):
-                mine = 2 * r + (mine_ref[0] & 1)
+                mine = mine_ref[0] ^ (2 * r)
                 for i, j in enumerate((mine, mine ^ 1)):
                     src = dw.at[pl.ds(pl.multiple_of(j * dr, dr), dr)]
                     at = (r % 2) * dr
@@ -737,7 +788,7 @@
         cos, sin = turn_tables(positions)
         chip = (mine // 2) % 4
         planes = ring_ids[(spot - jnp.arange(groups, dtype=jnp.int32)) % groups]
-        e = jnp.concatenate([4 * planes + chip, chip[None]]).astype(jnp.int32)
+        e = jnp.concatenate([4 * planes + chip, chip[None], (mine % 2)[None]]).astype(jnp.int32)
         small = jnp.concatenate(
             [router_weight, attn_gain[:, None], ffn_gain[:, None], jnp.zeros((dr, LANES - 18), BF)], axis=1
         )
@@ -765,7 +816,7 @@
         w_out = lax.all_gather(cols_out, "fsdp", axis=0, tiled=True)
         core_0 = to_core(after(unit, *pieces))
         dyg = lax.all_gather(after(cotangent, cols_out), "fsdp", axis=0, tiled=True, axis_index_groups=core_groups)
-        tokens_f = after(tokens, *pieces, *route_rows)
+        tokens_f = after(tokens, *pieces)
         units_2 = z_next(units_1)
         w_qkv, n1, qkv, att, h1, n2, small = call(
             attn_fwd(places, dr),
@@ -801,44 +852,56 @@
         gh1, dgu1, own_1, sib_1, gates, dgate = run_stage_a(e, xs, dyg, (units_1, core_1), small, route_rows)
         core_2, gates = tie((core_2, gates))
         sib_1 = to_core(sib_1)
-        gh0, dgu0, gh2, dgu2, dgate, own_2, sib_2 = run_stage_b(
-            e, xs, dyg, (unit, core_0, units_2, core_2), gates, dgate
-        )
+        gh0, dgu0, gh2, dgu2, dgate = run_stage_b(e, xs, dyg, (unit, core_0, units_2, core_2), gates, dgate)
         units_3, sib_1, dgate = tie((units_3, sib_1, dgate))
         core_3 = to_core(units_3)
         ws = (unit, core_0, units_1, core_1, units_2, core_2, units_3, core_3)
         sum_1, dgate = tie((chip_sum((own_1, sib_1)), dgate))
         hop = z_next(sum_1)
-        sib_2 = to_core(sib_2)
         gh3, dgu3, dgate, parts = run_stage_c(e, xs, dyg, ws, gates, dgate, (dgu0, dgu1, dgu2))
-        sib_2, dgate, parts = tie((sib_2, dgate, parts))
+        dgate, parts = tie((dgate, parts))
         parts = swap(parts)
         dgus = (dgu0, dgu1, dgu2, dgu3)
-        own_3, sib_3, own = run_late(e, xs, dyg, (gh3, dgu3), (*dgus, *ws, dgate))
-        hop, own, gh0 = tie((hop, own, gh0))
+        own_2, sib_2, own = run_late(e, xs, dyg, (gh2, dgu2), (*dgus, *ws, dgate))
+        sib_2 = to_core(sib_2)
+        hop, own, gh3 = tie((hop, own, gh3))
+        own_3, sib_3, own_0, sib_0 = run_grads(e, xs, dyg, (gh3, dgu3, gh0, dgu0))
+        sib_2, gh0, own_3 = tie((sib_2, gh0, own_3))
         sum_2, gh0 = tie((chip_sum((own_2, sib_2), hop), gh0))
         hop = z_next(sum_2)
         sib_3 = to_core(sib_3)
-        own_0, sib_0, outs, oown = run_last(e, xs, dyg, (gh0, dgu0), (gh0, gh1, gh2, gh3), ws)
-        parts, own, outs, sib_3 = tie((parts, own, outs, sib_3))
         sib_0 = to_core(sib_0)
+        outs, oown = run_out(e, (gh0, gh1, gh2, gh3), ws)
+        parts, own, outs, sib_3, sib_0 = tie((parts, own, outs, sib_3, sib_0))
         outs = swap(outs)
-        dh1, datt, dwo = run_join((e, own, parts, gates, h1, n2, cotangent, w_out, att, small))
-        hop, dh1, sib_0 = tie((hop, dh1, sib_0))
-        sum_3, dh1 = tie((chip_sum((own_3, sib_3), hop), dh1))
-        hop = z_next(sum_3)
-        rs_out = lax.psum_scatter(dwo, "fsdp", scatter_dimension=0, tiled=True)
+        dh1, datt, *dwo = run_join(
+            rest == 1, dr, (e, own, parts, gates, h1, n2, cotangent, w_out, att, small)
+        )
+        if rest == 1:
+            sib_o = to_core(dwo[1])
+        else:
+            rs_out = lax.psum_scatter(dwo[0], "fsdp", scatter_dimension=0, tiled=True)
         dx, *dw = run_attn_bwd(
             rest == 1, dr, (mine_s, tokens, w_qkv, cos, sin, bias, n1, qkv, datt, dh1, small)
         )
+        hop, *dw = tie((hop, *dw))
+        hop = z_next(chip_sum((own_3, sib_3), hop))
         if rest == 1:
-            sib_a, sib_b, hop, rs_out, outs = tie((to_core(dw[2]), to_core(dw[3]), hop, rs_out, outs))
-            total = jnp.concatenate([dw[0].astype(F32) + sib_a.astype(F32), dw[1].astype(F32) + sib_b.astype(F32)])
-            total = swap(total.astype(BF).reshape(4, dr, -1))
+            sib_a, sib_b, sib_o, outs = tie((to_core(dw[2]), to_core(dw[3]), sib_o, outs))
+            def chip_part(r):
+                pair = (dw[r // 2], sib_a if r < 2 else sib_b)
+                here = slice((r % 2) * dr, (r % 2 + 1) * dr)
+                there = slice(r * dr, (r + 1) * dr)
+                return jnp.concatenate([
+                    pair[0][here].astype(F32) + pair[1][here].astype(F32),
+                    dwo[0][there].astype(F32) + sib_o[there].astype(F32),
+                ], axis=1).astype(BF)
+
+            total = (chip_part(0), to_x(chip_part(1)), to_y(chip_part(2)), to_diag(chip_part(3)))
             acc = chip_sum((own_0, sib_0), hop)
-            acc, total = tie((acc, total))
+            acc, *total = tie((acc, *total))
             home = swap_all(acc.reshape(8, dr, UNIT))
-            rs_qkv = jnp.sum(total.astype(F32), axis=0).astype(BF)
+            blocks = run_fold(total)
         else:
             rs_qkv = lax.psum_scatter(dw[0], "fsdp", scatter_dimension=0, tiled=True)
 
@@ -857,24 +920,26 @@
             lax.dynamic_index_in_dim(outs, chip ^ t, 0, keepdims=False).astype(F32) for t in (1, 2, 3)
         ]
         output = (h1 + oown + near[0] + near[1] + near[2]).astype(BF)
-        z_qkv = z_sum([
-            jnp.concatenate(
-                [rs_qkv[:, k * 512 : (k + 1) * 512], rs_out[:, k * 256 : (k + 1) * 256],
-                 rs_out[:, 1024 : 1024 + 64], rs_qkv[:, 2048 : 2048 + 64]], axis=1
-            )
-            for k in range(groups)
-        ])
+        if rest > 1:
+            blocks = [
+                jnp.concatenate(
+                    [rs_qkv[:, k * 512 : (k + 1) * 512], rs_out[:, k * 256 : (k + 1) * 256],
+                     rs_qkv[:, 2048:], rs_out[:, 1024:]], axis=1
+                )
+                for k in range(groups)
+            ]
+        z_qkv = z_sum(blocks)
         z_out = z_qkv[:, 512:]
         return (
             output,
             dx,
-            z_out[:, 320],
+            z_out[:, 256],
             jnp.concatenate(swapped(z_qkv[:, :256]), axis=1),
             z_qkv[:, 256:384],
             z_qkv[:, 384:512],
             jnp.concatenate(swapped(z_out[:, :256]), axis=1),
-            z_out[:, 256 + EXPERTS],
-            z_out[:, 256 : 256 + EXPERTS],
+            z_out[:, 384 + EXPERTS],
+            z_out[:, 384 : 384 + EXPERTS],
             gate_up_grad,
             down_grad,
         )

time: 422 us -> 408 us (0.967)
  waiting for transfers between devices: 159 us -> 130 us
  Pallas kernels: 139 us -> 149 us
    all_to_all x3 -> x2, waiting for transfers between devices: 25.4 us -> 1.43 us  [swap(): return lax.all_to_all(a, 'fsdp', 0, 0, axis_index_groups=core_groups)]
    ppermute x6, waiting for transfers between devices: 31.1 us -> 47.9 us  [z_next(): return lax.ppermute(a, 'grp', shifted(1))]
    ppermute x5 -> x6, waiting for transfers between devices: 50.5 us -> 38.8 us  [to_x(): return lax.ppermute(a, 'fsdp', flip(2))]
    reduce_scatter x1 -> x0, waiting for transfers between devices: 10.4 us -> none  [shards(): rs_out = lax.psum_scatter(dwo, 'fsdp', scatter_dimension=0, tiled=True)]
    pallas_call x9 -> x11, Pallas kernels: 139 us -> 149 us  [call(): pl.pallas_call(body, out_shape=[jax.ShapeDtypeStruct(s, d) for s, d in ou...]
    ppermute x5 -> x6, waiting for transfers between devices: 6.68 us -> 12.5 us  [to_y(): return lax.ppermute(a, 'fsdp', flip(4))]
    ppermute x15 -> x16, waiting for transfers between devices: 5.78 us -> 1.46 us  [to_core(): return lax.ppermute(a, 'fsdp', flip(1))]
    all_to_all x3 -> x2, starting transfers between devices: 13.2 us -> 9.63 us  [swap(): return lax.all_to_all(a, 'fsdp', 0, 0, axis_index_groups=core_groups)]
  transfers between devices with their start and end apart: 46 -> 48, of which waited for: 25 -> 19; matrix products, arithmetic and copies ran while one was open for 9% -> 10% of each run, Pallas kernels for 32% -> 35%
where the time goes in v5:
time: 408 us; the launch traced here: 403 us
  Pallas kernels  149 us (37%)
  waiting for transfers between devices  130 us (32%)
  starting transfers between devices  56.3 us (14%)
  other arithmetic  32.4 us (8%)
  local copies, waits for them, and re-layouts  18.7 us (5%)
  between operations  15.4 us (4%)
    pallas_call x11, Pallas kernels, call(): pl.pallas_call(body, out_shape=[jax.ShapeDtypeStruct(s, d) for s, d in ou...  149 us
    ppermute x6, waiting for transfers between devices, z_next(): return lax.ppermute(a, 'grp', shifted(1))  47.9 us
    ppermute x6, waiting for transfers between devices, to_x(): return lax.ppermute(a, 'fsdp', flip(2))  38.8 us
    all_to_all x1, waiting for transfers between devices, shards(): unit = lax.all_to_all(parts, 'fsdp', 0, 0, axis_index_groups=low_groups)  15 us
    convert_element_type x4, other arithmetic, chip_sum(): return total.astype(BF)  14.9 us
    ppermute x6, waiting for transfers between devices, to_y(): return lax.ppermute(a, 'fsdp', flip(4))  12.5 us
    unnamed x89, local copies, waits for them, and re-layouts  11.6 us
    all_to_all x2, starting transfers between devices, swap(): return lax.all_to_all(a, 'fsdp', 0, 0, axis_index_groups=core_groups)  9.63 us
  transfers between devices with their start and end apart: 48, of which 19 were waited for; matrix products, arithmetic and copies ran while one was open for 10% of the time, Pallas kernels for 35%

profile of v5, /device:TPU:0, one launch (start us, length us, event | category | flops | bytes accessed | tf_op | source)
XLA Modules:
  0.0 402.8 jit_solution(12828287998354792670)
XLA Ops:
  18.9 4.3 %all-to-all-start = ((bf16[8,128,768]{1,2,0:T(8,128)(2,1)}), bf16[8,128,768]{1,2,0:T(8,128)(2,1)}, u32[]{:S(2)}, u32[]{:S(2)}) async-start(bf16[8,128,768]{1,2,0:T(8,128)(2,1)} %bitcast.11), calls=%async_computation | async-start | bytes 3145728 | tf_op jit(solution)/shard_map/all_to_all | solution.py:782
  29.2 15.0 %all-to-all-done = bf16[8,128,768]{1,2,0:T(8,128)(2,1)} async-done(((bf16[8,128,768]{1,2,0:T(8,128)(2,1)}), bf16[8,128,768]{1,2,0:T(8,128)(2,1)}, u32[]{:S(2)}, u32[]{:S(2)}) %all-to-all-start) | async-done | bytes 1572896 | tf_op jit(solution)/shard_map/all_to_all | solution.py:782
  52.0 15.6 %collective-permute-done.3.refs_1_ = bf16[128,2176]{1,0:T(8,128)(2,1)S(1)} collective-permute-done((bf16[128,2176]{1,0:T(8,128)(2,1)}, bf16[128,2176]{1,0:T(8,128)(2,1)S(1)}, u32[]{:S(2)}, u32[]{:S(2)}) %collective-permute-start.3) | collective-permute-done | bytes 557088 | tf_op jit(solution)/shard_map/ppermute | solution.py:719
  71.1 7.8 %collective-permute-done.6.refs_3_ = bf16[64,2176]{1,0:T(8,128)(2,1)S(1)} collective-permute-done((bf16[64,2176]{1,0:T(8,128)(2,1)S(1)}, bf16[64,2176]{1,0:T(8,128)(2,1)S(1)}, u32[]{:S(2)}, u32[]{:S(2)}) %collective-permute-start.6) | collective-permute-done | bytes 278560 | tf_op jit(solution)/shard_map/ppermute | solution.py:719
  84.2 11.7 %attn_fwd.1 = (bf16[1024,2048]{1,0:T(8,128)(2,1)}, bf16[384,1024]{1,0:T(8,128)(2,1)}, bf16[4,384,512]{2,1,0:T(8,128)(2,1)}, bf16[4,384,256]{2,1,0:T(8,128)(2,1)}...) custom-call(s32[1]{0:T(128)} %bitcast.mine_ref, ...), custom_call_target="tpu_custom_call" | custom-call | flops 4000000000 | bytes 18546692 | tf_op jit(solution)/shard_map/attn_fwd/pallas_call | solution.py:46
  96.1 4.2 %collective-permute-start.15 = (bf16[384,1024]{1,0:T(8,128)(2,1)}, bf16[384,1024]{1,0:T(8,128)(2,1)S(1)}, u32[]{:S(2)}, u32[]{:S(2)}) collective-permute-start(bf16[384,1024]{1,0:T(8,128)(2,1)} %get-tuple-element.154.refs_0_.n2_h), channel_id=1, source_target_pairs={{0,2},{1,3},{2,0},{3,1},{4,6},{5,7},{6,4},{7,5},{8,10},{9,11},{10,... | collective-permute-start | bytes 2359304 | tf_op jit(solution)/shard_map/ppermute | solution.py:719
  100.3 21.5 %collective-permute-done.17.refs_8_.refs_10_.refs_16_ = bf16[1024,768]{1,0:T(8,128)(2,1)} collective-permute-done((bf16[1024,768]{1,0:T(8,128)(2,1)}, bf16[1024,768]{1,0:T(8,128)(2,1)}, u32[]{:S(2)}, u32[]{:S(2)}) %collective-permute-start.17) | collective-permute-done | bytes 1572896 | tf_op jit(solution)/shard_map/ppermute | solution.py:716
  121.8 7.0 %collective-permute-done.15.refs_1_ = bf16[384,1024]{1,0:T(8,128)(2,1)S(1)} collective-permute-done((bf16[384,1024]{1,0:T(8,128)(2,1)}, bf16[384,1024]{1,0:T(8,128)(2,1)S(1)}, u32[]{:S(2)}, u32[]{:S(2)}) %collective-permute-start.15) | collective-permute-done | bytes 786464 | tf_op jit(solution)/shard_map/ppermute | solution.py:719
  135.6 8.3 %collective-permute-done.18.refs_3_ = bf16[192,1024]{1,0:T(8,128)(2,1)S(1)} collective-permute-done((bf16[192,1024]{1,0:T(8,128)(2,1)S(1)}, bf16[192,1024]{1,0:T(8,128)(2,1)S(1)}, u32[]{:S(2)}, u32[]{:S(2)}) %collective-permute-start.18) | collective-permute-done | bytes 393248 | tf_op jit(solution)/shard_map/ppermute | solution.py:719
  149.1 18.4 %stage_a.1 = (bf16[1536,512]{1,0:T(8,128)(2,1)}, bf16[1536,1024]{1,0:T(8,128)(2,1)}, bf16[1024,768]{1,0:T(8,128)(2,1)}, bf16[1024,768]{1,0:T(8,128)(2,1)}, f32[1536,128]{1,0:T(8,128)}, /*index=5*/f32[1536,128]{1,0:T(8,128)}) custom-call(s32[6]{0:T(128)} %pad_add_fusion.e_ref, bf16[384,1024]{1,0:T(8,128)(2,1)} %get-tuple-element.154.refs_0_.n2_h, ...), custom_call_target="tpu_custom_call" | custom-call | flops 9663676416 | bytes 19423256 | tf_op jit(solution)/shard_map/stage_a/pallas_call | solution.py:46
  167.7 17.9 %stage_b.1 = (bf16[1536,512]{1,0:T(8,128)(2,1)}, bf16[1536,1024]{1,0:T(8,128)(2,1)}, bf16[1536,512]{1,0:T(8,128)(2,1)}, bf16[1536,1024]{1,0:T(8,128)(2,1)}, f32[1536,128]{1,0:T(8,128)}) custom-call(s32[6]{0:T(128)} %pad_add_fusion.e_ref, bf16[384,1024]{1,0:T(8,128)(2,1)} %get-tuple-element.154.refs_0_.n2_h, bf16[384,1024]{1,0:T(8,128)(2,1)} %copy-done.4, ...), custom_call_target="tpu_custom_call" | custom-call | flops 9663676416 | bytes 24379416 | tf_op jit(solution)/shard_map/stage_b/pallas_call | solution.py:46
  193.5 21.3 %stage_c.1 = (bf16[1536,512]{1,0:T(8,128)(2,1)}, bf16[1536,1024]{1,0:T(8,128)(2,1)}, f32[1536,128]{1,0:T(8,128)}, bf16[4,384,1152]{2,1,0:T(8,128)(2,1)}) custom-call(s32[6]{0:T(128)} %pad_add_fusion.e_ref, bf16[384,1024]{1,0:T(8,128)(2,1)} %get-tuple-element.154.refs_0_.n2_h, bf16[384,1024]{1,0:T(8,128)(2,1)} %copy-done.4, bf16[384,1024]{1,0:T(8,128)(2,1)} %copy-done.5, ...), custom_call_target="tpu_custom_call" | custom-call | flops 9663676416 | bytes 38928408 | tf_op jit(solution)/shard_map/stage_c/pallas_call | solution.py:46
  214.9 4.8 %all-to-all-start.1 = ((bf16[4,384,1152]{2,1,0:T(8,128)(2,1)}), bf16[4,384,1152]{2,1,0:T(8,128)(2,1)}, u32[]{:S(2)}, u32[]{:S(2)}) async-start(bf16[4,384,1152]{2,1,0:T(8,128)(2,1)} %get-tuple-element.201), calls=%async_computation.1 | async-start | bytes 7077888 | tf_op jit(solution)/shard_map/all_to_all | solution.py:738
  219.6 15.5 %late_stage.1 = (bf16[1024,768]{1,0:T(8,128)(2,1)}, bf16[1024,768]{1,0:T(8,128)(2,1)}, f32[384,1152]{1,0:T(8,128)}) custom-call(s32[6]{0:T(128)} %pad_add_fusion.e_ref, bf16[384,1024]{1,0:T(8,128)(2,1)} %get-tuple-element.154.refs_0_.n2_h, bf16[384,1024]{1,0:T(8,128)(2,1)} %copy-done.4, bf16[384,1024]{1,0:T(8,128)(2,1)} %copy-done.5, ...), custom_call_target="tpu_custom_call" | custom-call | flops 9663676416 | bytes 41877528 | tf_op jit(solution)/shard_map/late_stage/pallas_call | solution.py:46
  235.2 16.4 %grads_stage.1 = (bf16[1024,768]{1,0:T(8,128)(2,1)}, bf16[1024,768]{1,0:T(8,128)(2,1)}, bf16[1024,768]{1,0:T(8,128)(2,1)}, bf16[1024,768]{1,0:T(8,128)(2,1)}) custom-call(s32[6]{0:T(128)} %pad_add_fusion.e_ref, bf16[384,1024]{1,0:T(8,128)(2,1)} %get-tuple-element.154.refs_0_.n2_h, bf16[384,1024]{1,0:T(8,128)(2,1)} %copy-done.4, bf16[384,1024]{1,0:T(8,128)(2,1)} %copy-done.5, ...), custom_call_target="tpu_custom_call" | custom-call | flops 9663676416 | bytes 22020120 | tf_op jit(solution)/shard_map/grads_stage/pallas_call | solution.py:46
  257.7 12.7 %out_stage.1 = (bf16[4,384,1024]{2,1,0:T(8,128)(2,1)}, f32[384,1024]{1,0:T(8,128)}) custom-call(s32[6]{0:T(128)} %pad_add_fusion.e_ref, bf16[1536,512]{1,0:T(8,128)(2,1)} %get-tuple-element.194.refs_8_.refs_0_, bf16[1536,512]{1,0:T(8,128)(2,1)} %get-tuple-element.195.refs_1_, bf16[1536,512]{1,0:T(8,128)(2,1)} %get-tuple-element.168.refs_6_.refs_2_, ...), custom_call_target="tpu_custom_call" | custom-call | flops 6442450944 | bytes 23592984 | tf_op jit(solution)/shard_map/out_stage/pallas_call | solution.py:46
  270.4 4.9 %all-to-all-start.2 = ((bf16[4,384,1024]{2,1,0:T(8,128)(2,1)}), bf16[4,384,1024]{2,1,0:T(8,128)(2,1)}, u32[]{:S(2)}, u32[]{:S(2)}) async-start(bf16[4,384,1024]{2,1,0:T(8,128)(2,1)} %get-tuple-element.218), calls=%async_computation.2 | async-start | bytes 6291456 | tf_op jit(solution)/shard_map/all_to_all | solution.py:738
  275.2 9.0 %join.1 = (f32[384,1024]{1,0:T(8,128)}, bf16[4,384,256]{2,1,0:T(8,128)(2,1)}, bf16[512,1152]{1,0:T(8,128)(2,1)}, bf16[512,1152]{1,0:T(8,128)(2,1)}) custom-call(s32[6]{0:T(128)} %pad_add_fusion.e_ref, f32[384,1152]{1,0:T(8,128)} %get-tuple-element.206.p_h, bf16[4,384,1152]{2,1,0:T(8,128)(2,1)} %all-to-all-done.1.parts_h, ...), custom_call_target="tpu_custom_call" | custom-call | flops 2000000000 | bytes 17367064 | tf_op jit(solution)/shard_map/join/pallas_call | solution.py:46
  284.3 19.0 %attn_bwd.1 = (f32[384,1024]{1,0:T(8,128)}, bf16[256,2176]{1,0:T(8,128)(2,1)}, bf16[256,2176]{1,0:T(8,128)(2,1)}, bf16[256,2176]{1,0:T(8,128)(2,1)}, bf16[256,2176]{1,0:T(8,128)(2,1)}) custom-call(s32[1]{0:T(128)} %bitcast.mine_ref, bf16[384,1024]{1,0:T(8,128)(2,1)} %x_h.1, bf16[1024,2048]{1,0:T(8,128)(2,1)} %get-tuple-element.198.w_h, ...), custom_call_target="tpu_custom_call" | custom-call | flops 6000000000 | bytes 17235972 | tf_op jit(solution)/shard_map/attn_bwd/pallas_call | solution.py:46
  304.0 4.2 %add_convert_fusion.1 = bf16[1024,768]{1,0:T(8,128)(2,1)} fusion(bf16[1024,768]{1,0:T(8,128)(2,1)} %collective-permute-done.29, bf16[1024,768]{1,0:T(8,128)(2,1)} %collective-permute-done.30, bf16[1024,768]{1,0:T(8,128)(2,1)} %get-tuple-element.223), kind=kLoop, calls=%fused_computation.2 | loop fusion | flops 4718592 | bytes 6291456 | tf_op jit(solution)/shard_map/convert_element_type | solution.py:850
  321.0 25.1 %collective-permute-done.35 = bf16[1024,768]{1,0:T(8,128)(2,1)} collective-permute-done((bf16[1024,768]{1,0:T(8,128)(2,1)}, bf16[1024,768]{1,0:T(8,128)(2,1)}, u32[]{:S(2)}, u32[]{:S(2)}) %collective-permute-start.35) | collective-permute-done | bytes 1572896 | tf_op jit(solution)/shard_map/ppermute | solution.py:716
  350.3 6.3 %collective-permute-done.37.refs_2_ = bf16[128,3328]{1,0:T(8,128)(2,1)S(1)} collective-permute-done((bf16[128,3328]{1,0:T(8,128)(2,1)S(1)}, bf16[128,3328]{1,0:T(8,128)(2,1)S(1)}, u32[]{:S(2)}, u32[]{:S(2)}) %collective-permute-start.37) | collective-permute-done | bytes 852000 | tf_op jit(solution)/shard_map/ppermute | solution.py:722
  372.5 9.2 %collective-permute-done.41 = bf16[128,1024]{1,0:T(8,128)(2,1)S(1)} collective-permute-done((bf16[128,1024]{1,0:T(8,128)(2,1)}, bf16[128,1024]{1,0:T(8,128)(2,1)S(1)}, u32[]{:S(2)}, u32[]{:S(2)}) %collective-permute-start.41) | collective-permute-done | bytes 262176 | tf_op jit(solution)/shard_map/ppermute | solution.py:746
  391.0 4.5 %settle.1 = (f32[128,4,1024]{2,1,0:T(4,128)}, f32[128,4,512]{2,1,0:T(4,128)}) custom-call(bf16[8,128,768]{2,1,0:T(8,128)(2,1)} %copy-done.3), custom_call_target="tpu_custom_call" | custom-call | bytes 4718592 | tf_op jit(solution)/shard_map/settle/pallas_call | solution.py:46
  (229 shorter events, 103.0 us)
Async XLA Ops:
  11.7 34.2 %collective-permute-start = (bf16[128,768]{1,0:T(8,128)(2,1)S(1)}, bf16[128,768]{1,0:T(8,128)(2,1)S(1)}, u32[]{:S(2)}, u32[]{:S(2)}) collective-permute-start(bf16[128,768]{1,0:T(8,128)(2,1)S(1)} %constant_dynamic-update-slice_fusion), channel_id=1, source_target_pairs={{0,8},{8,24},{24,16},{16,0},{1,9},{9,25},{25,17},{17,1},{2,10},{10... | collective-permute-start | bytes 589832 | tf_op jit(solution)/shard_map/ppermute | solution.py:771
  14.8 31.1 %collective-permute-start.1 = (bf16[128,768]{1,0:T(8,128)(2,1)S(1)}, bf16[128,768]{1,0:T(8,128)(2,1)S(1)}, u32[]{:S(2)}, u32[]{:S(2)}) collective-permute-start(bf16[128,768]{1,0:T(8,128)(2,1)S(1)} %constant_dynamic-update-slice_fusion), channel_id=1, source_target_pairs={{0,24},{8,16},{24,0},{16,8},{1,25},{9,17},{25,1},{17,9},{2,26},{10... | collective-permute-start | bytes 589832 | tf_op jit(solution)/shard_map/ppermute | solution.py:771
  17.3 28.7 %collective-permute-start.2 = (bf16[128,768]{1,0:T(8,128)(2,1)S(1)}, bf16[128,768]{1,0:T(8,128)(2,1)S(1)}, u32[]{:S(2)}, u32[]{:S(2)}) collective-permute-start(bf16[128,768]{1,0:T(8,128)(2,1)S(1)} %constant_dynamic-update-slice_fusion), channel_id=1, source_target_pairs={{0,16},{8,0},{24,8},{16,24},{1,17},{9,1},{25,9},{17,25},{2,18},{10... | collective-permute-start | bytes 589832 | tf_op jit(solution)/shard_map/ppermute | solution.py:771
  18.9 25.3 %all-to-all-start = ((bf16[8,128,768]{1,2,0:T(8,128)(2,1)}), bf16[8,128,768]{1,2,0:T(8,128)(2,1)}, u32[]{:S(2)}, u32[]{:S(2)}) async-start(bf16[8,128,768]{1,2,0:T(8,128)(2,1)} %bitcast.11), calls=%async_computation | async-start | bytes 3145728 | tf_op jit(solution)/shard_map/all_to_all | solution.py:782
  23.2 61.0 %all-gather.3.cloned.1.call-start = ((), (), s32[]{:S(2)}) async-start(), calls=%async_computation.4 | async-start | bytes 2359296 | tf_op jit(solution)/shard_map/all_gather | solution.py:816
  47.0 101.5 %all-gather.5.cloned.1.call-start = ((), (), s32[]{:S(2)}) async-start(), calls=%async_computation.5 | async-start | bytes 3932160 | tf_op jit(solution)/shard_map/all_gather | solution.py:818
  47.0 34.2 %collective-permute-start.8 = (bf16[1024,768]{1,0:T(8,128)(2,1)S(1)}, bf16[1024,768]{1,0:T(8,128)(2,1)}, u32[]{:S(2)}, u32[]{:S(2)}) collective-permute-start(bf16[1024,768]{1,0:T(8,128)(2,1)S(1)} %bitcast.27), channel_id=1, source_target_pairs={{0,8},{8,24},{24,16},{16,0},{1,9},{9,25},{25,17},{17,1},{2,10},{10... | collective-permute-start | bytes 4718600 | tf_op jit(solution)/shard_map/ppermute | solution.py:716
  83.9 37.9 %collective-permute-start.17 = (bf16[1024,768]{1,0:T(8,128)(2,1)}, bf16[1024,768]{1,0:T(8,128)(2,1)}, u32[]{:S(2)}, u32[]{:S(2)}) collective-permute-start(bf16[1024,768]{1,0:T(8,128)(2,1)} %collective-permute-done.8.refs_6_.refs_8_.refs_14_), channel_id=1, source_target_pairs={{0,8},{8,24},{24,16},{16,0},{1,9},{9,25},{25,17},{17,1},{2,10},{10... | collective-permute-start | bytes 4718600 | tf_op jit(solution)/shard_map/ppermute | solution.py:716
  95.9 51.5 %collective-permute-start.14 = (bf16[1024,768]{1,0:T(8,128)(2,1)}, bf16[1024,768]{1,0:T(8,128)(2,1)}, u32[]{:S(2)}, u32[]{:S(2)}) collective-permute-start(bf16[1024,768]{1,0:T(8,128)(2,1)} %collective-permute-done.8.refs_6_.refs_8_.refs_14_), channel_id=1, source_target_pairs={{0,1},{1,0},{2,3},{3,2},{4,5},{5,4},{6,7},{7,6},{8,9},{9,8},{10,11... | collective-permute-start | bytes 4718600 | tf_op jit(solution)/shard_map/ppermute | solution.py:728
  96.1 32.7 %collective-permute-start.15 = (bf16[384,1024]{1,0:T(8,128)(2,1)}, bf16[384,1024]{1,0:T(8,128)(2,1)S(1)}, u32[]{:S(2)}, u32[]{:S(2)}) collective-permute-start(bf16[384,1024]{1,0:T(8,128)(2,1)} %get-tuple-element.154.refs_0_.n2_h), channel_id=1, source_target_pairs={{0,2},{1,3},{2,0},{3,1},{4,6},{5,7},{6,4},{7,5},{8,10},{9,11},{10,... | collective-permute-start | bytes 2359304 | tf_op jit(solution)/shard_map/ppermute | solution.py:719
  100.3 31.0 %collective-permute-start.16 = (bf16[384,1024]{1,0:T(8,128)(2,1)}, bf16[384,1024]{1,0:T(8,128)(2,1)S(1)}, u32[]{:S(2)}, u32[]{:S(2)}) collective-permute-start(bf16[384,1024]{1,0:T(8,128)(2,1)} %get-tuple-element.154.refs_0_.n2_h), channel_id=1, source_target_pairs={{0,4},{1,5},{2,6},{3,7},{4,0},{5,1},{6,2},{7,3},{8,12},{9,13},{10,... | collective-permute-start | bytes 2359304 | tf_op jit(solution)/shard_map/ppermute | solution.py:722
  145.5 40.1 %collective-permute-start.24 = (bf16[1024,768]{1,0:T(8,128)(2,1)}, bf16[1024,768]{1,0:T(8,128)(2,1)}, u32[]{:S(2)}, u32[]{:S(2)}) collective-permute-start(bf16[1024,768]{1,0:T(8,128)(2,1)} %collective-permute-done.17.refs_8_.refs_10_.refs_16_), channel_id=1, source_target_pairs={{0,8},{8,24},{24,16},{16,0},{1,9},{9,25},{25,17},{17,1},{2,10},{10... | collective-permute-start | bytes 4718600 | tf_op jit(solution)/shard_map/ppermute | solution.py:716
  147.4 20.3 %collective-permute-start.20 = (bf16[1024,768]{1,0:T(8,128)(2,1)}, bf16[1024,768]{1,0:T(8,128)(2,1)}, u32[]{:S(2)}, u32[]{:S(2)}) collective-permute-start(bf16[1024,768]{1,0:T(8,128)(2,1)} %collective-permute-done.17.refs_8_.refs_10_.refs_16_), channel_id=1, source_target_pairs={{0,1},{1,0},{2,3},{3,2},{4,5},{5,4},{6,7},{7,6},{8,9},{9,8},{10,11... | collective-permute-start | bytes 4718600 | tf_op jit(solution)/shard_map/ppermute | solution.py:728
  190.8 44.4 %collective-permute-start.28 = (bf16[1024,768]{1,0:T(8,128)(2,1)}, bf16[1024,768]{1,0:T(8,128)(2,1)}, u32[]{:S(2)}, u32[]{:S(2)}) collective-permute-start(bf16[1024,768]{1,0:T(8,128)(2,1)} %add_convert_fusion.3), channel_id=1, source_target_pairs={{0,8},{8,24},{24,16},{16,0},{1,9},{9,25},{25,17},{17,1},{2,10},{10... | collective-permute-start | bytes 4718600 | tf_op jit(solution)/shard_map/ppermute | solution.py:716
  214.9 55.5 %all-to-all-start.1 = ((bf16[4,384,1152]{2,1,0:T(8,128)(2,1)}), bf16[4,384,1152]{2,1,0:T(8,128)(2,1)}, u32[]{:S(2)}, u32[]{:S(2)}) async-start(bf16[4,384,1152]{2,1,0:T(8,128)(2,1)} %get-tuple-element.201), calls=%async_computation.1 | async-start | bytes 7077888 | tf_op jit(solution)/shard_map/all_to_all | solution.py:738
  256.4 47.0 %collective-permute-start.29 = (bf16[1024,768]{1,0:T(8,128)(2,1)}, bf16[1024,768]{1,0:T(8,128)(2,1)}, u32[]{:S(2)}, u32[]{:S(2)}) collective-permute-start(bf16[1024,768]{1,0:T(8,128)(2,1)} %add_convert_fusion.2), channel_id=1, source_target_pairs={{0,8},{8,24},{24,16},{16,0},{1,9},{9,25},{25,17},{17,1},{2,10},{10... | collective-permute-start | bytes 4718600 | tf_op jit(solution)/shard_map/ppermute | solution.py:716
  270.4 41.6 %all-to-all-start.2 = ((bf16[4,384,1024]{2,1,0:T(8,128)(2,1)}), bf16[4,384,1024]{2,1,0:T(8,128)(2,1)}, u32[]{:S(2)}, u32[]{:S(2)}) async-start(bf16[4,384,1024]{2,1,0:T(8,128)(2,1)} %get-tuple-element.218), calls=%async_computation.2 | async-start | bytes 6291456 | tf_op jit(solution)/shard_map/all_to_all | solution.py:738
  284.2 26.3 %collective-permute-start.34 = (bf16[512,1152]{1,0:T(8,128)(2,1)}, bf16[512,1152]{1,0:T(8,128)(2,1)}, u32[]{:S(2)}, u32[]{:S(2)}) collective-permute-start(bf16[512,1152]{1,0:T(8,128)(2,1)} %get-tuple-element.217), channel_id=1, source_target_pairs={{0,1},{1,0},{2,3},{3,2},{4,5},{5,4},{6,7},{7,6},{8,9},{9,8},{10,11... | collective-permute-start | bytes 3538952 | tf_op jit(solution)/shard_map/ppermute | solution.py:728
  308.2 38.0 %collective-permute-start.35 = (bf16[1024,768]{1,0:T(8,128)(2,1)}, bf16[1024,768]{1,0:T(8,128)(2,1)}, u32[]{:S(2)}, u32[]{:S(2)}) collective-permute-start(bf16[1024,768]{1,0:T(8,128)(2,1)} %add_convert_fusion.1), channel_id=1, source_target_pairs={{0,8},{8,24},{24,16},{16,0},{1,9},{9,25},{25,17},{17,1},{2,10},{10... | collective-permute-start | bytes 4718600 | tf_op jit(solution)/shard_map/ppermute | solution.py:716
  315.1 35.1 %collective-permute-start.36 = (bf16[128,3328]{1,0:T(8,128)(2,1)S(1)}, bf16[128,3328]{1,0:T(8,128)(2,1)S(1)}, u32[]{:S(2)}, u32[]{:S(2)}) collective-permute-start(bf16[128,3328]{1,0:T(8,128)(2,1)S(1)} %pad_maximum_fusion.1), channel_id=1, source_target_pairs={{0,2},{1,3},{2,0},{3,1},{4,6},{5,7},{6,4},{7,5},{8,10},{9,11},{10,... | collective-permute-start | bytes 2555912 | tf_op jit(solution)/shard_map/ppermute | solution.py:719
  318.2 38.3 %collective-permute-start.37 = (bf16[128,3328]{1,0:T(8,128)(2,1)S(1)}, bf16[128,3328]{1,0:T(8,128)(2,1)S(1)}, u32[]{:S(2)}, u32[]{:S(2)}) collective-permute-start(bf16[128,3328]{1,0:T(8,128)(2,1)S(1)} %pad_maximum_fusion.2), channel_id=1, source_target_pairs={{0,4},{1,5},{2,6},{3,7},{4,0},{5,1},{6,2},{7,3},{8,12},{9,13},{10,... | collective-permute-start | bytes 2555912 | tf_op jit(solution)/shard_map/ppermute | solution.py:722
  319.5 38.0 %collective-permute-start.38 = (bf16[128,3328]{1,0:T(8,128)(2,1)S(1)}, bf16[128,3328]{1,0:T(8,128)(2,1)}, u32[]{:S(2)}, u32[]{:S(2)}) collective-permute-start(bf16[128,3328]{1,0:T(8,128)(2,1)S(1)} %pad_maximum_fusion.3), channel_id=1, source_target_pairs={{0,6},{1,7},{2,4},{3,5},{4,2},{5,3},{6,0},{7,1},{8,14},{9,15},{10,... | collective-permute-start | bytes 2555912 | tf_op jit(solution)/shard_map/ppermute | solution.py:725
  360.6 21.0 %collective-permute-start.41 = (bf16[128,1024]{1,0:T(8,128)(2,1)}, bf16[128,1024]{1,0:T(8,128)(2,1)S(1)}, u32[]{:S(2)}, u32[]{:S(2)}) collective-permute-start(bf16[128,1024]{1,0:T(8,128)(2,1)} %get-tuple-element.239), channel_id=1, source_target_pairs={{0,8},{8,24},{24,16},{16,0},{1,9},{9,25},{25,17},{17,1},{2,10},{10... | collective-permute-start | bytes 786440 | tf_op jit(solution)/shard_map/ppermute | solution.py:746
  365.2 24.7 %all-to-all-start.3 = ((bf16[8,128,768]{2,1,0:T(8,128)(2,1)}), bf16[8,128,768]{2,1,0:T(8,128)(2,1)S(1)}, u32[]{:S(2)}, u32[]{:S(2)}) async-start(bf16[8,128,768]{2,1,0:T(8,128)(2,1)} %bitcast.33), calls=%async_computation.3 | async-start | bytes 3145728 | tf_op jit(solution)/shard_map/all_to_all | solution.py:741
  (64 other events, 643.9 us)
Sparse Core Ops, SparseCore 0:
  47.1 30.3 all-gather.2
  79.3 61.6 all-gather.4

commit v6 on v5

--- a/solution.py
+++ b/solution.py
@@ -451,9 +451,17 @@
     ghs, ws = refs[0:4], refs[4:12]
     parts_h, own_h = refs[12:14]
     A, W, O, OF, si, so = refs[14:]
-    wait(fetch(back_pairs(ghs, ws, 0, ROWS, HALF, WIDE, A, W), si))
+    order = (3, 1, 2, 0)
+    pairs = [
+        (ws[i].at[:, WIDE:UNIT], W.at[:, i * HALF : (i + 1) * HALF]) for i in range(8)
+    ]
+    for t in order:
+        pairs += [(ghs[k].at[TREE[t]], A.at[TREE[t], k * FF : (k + 1) * FF]) for k in range(4)]
+    copies = fetch(pairs, si)
+    wait(copies[:8])
     outs = []
-    for i, t in enumerate((3, 1, 2, 0)):
+    for i, t in enumerate(order):
+        wait(copies[8 + 4 * i : 12 + 4 * i])
         total = dotg(A[TREE[t], :], W[...], NT)
         dst = O.at[i] if t else OF
         dst[...] = total.astype(BF) if t else total
@@ -467,7 +475,7 @@
         [
             pltpu.VMEM((ROWS, 8 * HALF), BF), pltpu.VMEM((MODEL_WIDTH, 8 * HALF), BF),
             pltpu.VMEM((3, T, MODEL_WIDTH), BF), pltpu.VMEM((T, MODEL_WIDTH), F32),
-            pltpu.SemaphoreType.DMA((12,)), pltpu.SemaphoreType.DMA((4,)),
+            pltpu.SemaphoreType.DMA((24,)), pltpu.SemaphoreType.DMA((4,)),
         ],
         (e, *ghs, *ws), "out_stage", 32, 2 * ROWS * MODEL_WIDTH * 8 * HALF,
     )
@@ -477,7 +485,7 @@
     totals, outs, H, sem = refs[0:4], refs[4:8], refs[8], refs[9]
     wait(fetch([(t, H.at[i]) for i, t in enumerate(totals)], sem))
     for k, o in enumerate(outs):
-        for at, first, width in ((0, k * 512, 512), (512, 2176 + k * 256, 256), (768, 2048, LANES), (896, 3200, LANES)):
+        for at, first, width in ((0, k * 512, 512), (512, 2048 + k * 256, 256), (768, 3072, LANES)):
             cols = slice(first, first + width)
             part = H[0, :, cols].astype(F32) + H[1, :, cols].astype(F32)
             part = part + (H[2, :, cols].astype(F32) + H[3, :, cols].astype(F32))
@@ -487,7 +495,7 @@
 def run_fold(total):
     dr, cols = total[0].shape
     return call(
-        fold, [((dr, 1024), BF)] * 4, [HB] * 4, [VM] * 4,
+        fold, [((dr, 896), BF)] * 4, [HB] * 4, [VM] * 4,
         [pltpu.VMEM((4, dr, cols), BF), pltpu.SemaphoreType.DMA((4,))], total, "fold", 48, 0,
     )
 
@@ -675,7 +683,7 @@
     gd = gain * dn1
     inner = jnp.mean(gd * x, axis=1, keepdims=True)
     dx_ref[...] = dh1_ref[...] + r1 * gd - x * (r1 * r1 * r1 * inner)
-    dw_ref[:, 2048:2176] = columns_of(dn1 * x * r1, 0).astype(BF)
+    dw_ref[:, 2048:2176] = columns_of(dn1 * x * r1, 32).astype(BF)
 def visible_bias(segment, parents):
     ids = jnp.arange(parents.shape[0], dtype=jnp.int32)
     one = jnp.sum(jnp.where(segment[:, None] == ids[None, :], parents[None, :], 0), axis=1)
@@ -892,10 +900,11 @@
                 pair = (dw[r // 2], sib_a if r < 2 else sib_b)
                 here = slice((r % 2) * dr, (r % 2 + 1) * dr)
                 there = slice(r * dr, (r + 1) * dr)
-                return jnp.concatenate([
-                    pair[0][here].astype(F32) + pair[1][here].astype(F32),
-                    dwo[0][there].astype(F32) + sib_o[there].astype(F32),
-                ], axis=1).astype(BF)
+                mine_q = pair[0][here].astype(F32) + pair[1][here].astype(F32)
+                mine_o = dwo[0][there].astype(F32) + sib_o[there].astype(F32)
+                return jnp.concatenate(
+                    [mine_q[:, :2048], mine_o[:, :1024], mine_q[:, 2048:] + mine_o[:, 1024:]], axis=1
+                ).astype(BF)
 
             total = (chip_part(0), to_x(chip_part(1)), to_y(chip_part(2)), to_diag(chip_part(3)))
             acc = chip_sum((own_0, sib_0), hop)
@@ -924,7 +933,7 @@
             blocks = [
                 jnp.concatenate(
                     [rs_qkv[:, k * 512 : (k + 1) * 512], rs_out[:, k * 256 : (k + 1) * 256],
-                     rs_qkv[:, 2048:], rs_out[:, 1024:]], axis=1
+                     rs_qkv[:, 2048:] + rs_out[:, 1024:]], axis=1
                 )
                 for k in range(groups)
             ]
@@ -933,13 +942,13 @@
         return (
             output,
             dx,
-            z_out[:, 256],
+            z_out[:, 256 + 32],
             jnp.concatenate(swapped(z_qkv[:, :256]), axis=1),
             z_qkv[:, 256:384],
             z_qkv[:, 384:512],
             jnp.concatenate(swapped(z_out[:, :256]), axis=1),
-            z_out[:, 384 + EXPERTS],
-            z_out[:, 384 : 384 + EXPERTS],
+            z_out[:, 256 + EXPERTS],
+            z_out[:, 256 : 256 + EXPERTS],
             gate_up_grad,
             down_grad,
         )

time: 408 us -> 405 us (level)
    another operation x3 -> x4, other arithmetic: 4.63 us -> 0.05 us
    add x0 -> x3, other arithmetic: none -> 4.54 us  [the longest x2 2.99 us: chip_part(): mine_q = pair[0][here].astype(F32) + pair[1][here].astype(F32)]
    unnamed x89 -> x85, local copies, waits for them, and re-layouts: 11.6 us -> 10.7 us
where the time goes in v6:
time: 405 us; the launch traced here: 400 us
  Pallas kernels  149 us (37%)
  waiting for transfers between devices  129 us (32%)
  starting transfers between devices  56.2 us (14%)
  other arithmetic  32.3 us (8%)
  local copies, waits for them, and re-layouts  18.1 us (4%)
  between operations  15.5 us (4%)
    pallas_call x11, Pallas kernels, call(): pl.pallas_call(body, out_shape=[jax.ShapeDtypeStruct(s, d) for s, d in ou...  149 us
    ppermute x6, waiting for transfers between devices, z_next(): return lax.ppermute(a, 'grp', shifted(1))  47.7 us
    ppermute x6, waiting for transfers between devices, to_x(): return lax.ppermute(a, 'fsdp', flip(2))  38.8 us
    all_to_all x1, waiting for transfers between devices, shards(): unit = lax.all_to_all(parts, 'fsdp', 0, 0, axis_index_groups=low_groups)  15 us
    convert_element_type x4, other arithmetic, chip_sum(): return total.astype(BF)  14.9 us
    ppermute x6, waiting for transfers between devices, to_y(): return lax.ppermute(a, 'fsdp', flip(4))  11.3 us
    unnamed x85, local copies, waits for them, and re-layouts  10.7 us
    all_to_all x2, starting transfers between devices, swap(): return lax.all_to_all(a, 'fsdp', 0, 0, axis_index_groups=core_groups)  9.61 us
  transfers between devices with their start and end apart: 48, of which 19 were waited for; matrix products, arithmetic and copies ran while one was open for 10% of the time, Pallas kernels for 35%

profile of v6, /device:TPU:0, one launch (start us, length us, event | category | flops | bytes accessed | tf_op | source)
XLA Modules:
  0.0 399.9 jit_solution(14479744927046136387)
XLA Ops:
  18.9 4.3 %all-to-all-start = ((bf16[8,128,768]{1,2,0:T(8,128)(2,1)}), bf16[8,128,768]{1,2,0:T(8,128)(2,1)}, u32[]{:S(2)}, u32[]{:S(2)}) async-start(bf16[8,128,768]{1,2,0:T(8,128)(2,1)} %bitcast.11), calls=%async_computation | async-start | bytes 3145728 | tf_op jit(solution)/shard_map/all_to_all | solution.py:790
  29.2 15.0 %all-to-all-done = bf16[8,128,768]{1,2,0:T(8,128)(2,1)} async-done(((bf16[8,128,768]{1,2,0:T(8,128)(2,1)}), bf16[8,128,768]{1,2,0:T(8,128)(2,1)}, u32[]{:S(2)}, u32[]{:S(2)}) %all-to-all-start) | async-done | bytes 1572896 | tf_op jit(solution)/shard_map/all_to_all | solution.py:790
  52.0 15.6 %collective-permute-done.3.refs_1_ = bf16[128,2176]{1,0:T(8,128)(2,1)S(1)} collective-permute-done((bf16[128,2176]{1,0:T(8,128)(2,1)}, bf16[128,2176]{1,0:T(8,128)(2,1)S(1)}, u32[]{:S(2)}, u32[]{:S(2)}) %collective-permute-start.3) | collective-permute-done | bytes 557088 | tf_op jit(solution)/shard_map/ppermute | solution.py:727
  71.1 7.8 %collective-permute-done.6.refs_3_ = bf16[64,2176]{1,0:T(8,128)(2,1)S(1)} collective-permute-done((bf16[64,2176]{1,0:T(8,128)(2,1)S(1)}, bf16[64,2176]{1,0:T(8,128)(2,1)S(1)}, u32[]{:S(2)}, u32[]{:S(2)}) %collective-permute-start.6) | collective-permute-done | bytes 278560 | tf_op jit(solution)/shard_map/ppermute | solution.py:727
  84.2 11.7 %attn_fwd.1 = (bf16[1024,2048]{1,0:T(8,128)(2,1)}, bf16[384,1024]{1,0:T(8,128)(2,1)}, bf16[4,384,512]{2,1,0:T(8,128)(2,1)}, bf16[4,384,256]{2,1,0:T(8,128)(2,1)}...) custom-call(s32[1]{0:T(128)} %bitcast.mine_ref, ...), custom_call_target="tpu_custom_call" | custom-call | flops 4000000000 | bytes 18546692 | tf_op jit(solution)/shard_map/attn_fwd/pallas_call | solution.py:46
  96.1 4.2 %collective-permute-start.15 = (bf16[384,1024]{1,0:T(8,128)(2,1)}, bf16[384,1024]{1,0:T(8,128)(2,1)S(1)}, u32[]{:S(2)}, u32[]{:S(2)}) collective-permute-start(bf16[384,1024]{1,0:T(8,128)(2,1)} %get-tuple-element.154.refs_0_.n2_h), channel_id=1, source_target_pairs={{0,2},{1,3},{2,0},{3,1},{4,6},{5,7},{6,4},{7,5},{8,10},{9,11},{10,... | collective-permute-start | bytes 2359304 | tf_op jit(solution)/shard_map/ppermute | solution.py:727
  100.3 21.5 %collective-permute-done.17.refs_8_.refs_10_.refs_16_ = bf16[1024,768]{1,0:T(8,128)(2,1)} collective-permute-done((bf16[1024,768]{1,0:T(8,128)(2,1)}, bf16[1024,768]{1,0:T(8,128)(2,1)}, u32[]{:S(2)}, u32[]{:S(2)}) %collective-permute-start.17) | collective-permute-done | bytes 1572896 | tf_op jit(solution)/shard_map/ppermute | solution.py:724
  121.8 7.0 %collective-permute-done.15.refs_1_ = bf16[384,1024]{1,0:T(8,128)(2,1)S(1)} collective-permute-done((bf16[384,1024]{1,0:T(8,128)(2,1)}, bf16[384,1024]{1,0:T(8,128)(2,1)S(1)}, u32[]{:S(2)}, u32[]{:S(2)}) %collective-permute-start.15) | collective-permute-done | bytes 786464 | tf_op jit(solution)/shard_map/ppermute | solution.py:727
  135.7 8.3 %collective-permute-done.18.refs_3_ = bf16[192,1024]{1,0:T(8,128)(2,1)S(1)} collective-permute-done((bf16[192,1024]{1,0:T(8,128)(2,1)S(1)}, bf16[192,1024]{1,0:T(8,128)(2,1)S(1)}, u32[]{:S(2)}, u32[]{:S(2)}) %collective-permute-start.18) | collective-permute-done | bytes 393248 | tf_op jit(solution)/shard_map/ppermute | solution.py:727
  149.1 18.4 %stage_a.1 = (bf16[1536,512]{1,0:T(8,128)(2,1)}, bf16[1536,1024]{1,0:T(8,128)(2,1)}, bf16[1024,768]{1,0:T(8,128)(2,1)}, bf16[1024,768]{1,0:T(8,128)(2,1)}, f32[1536,128]{1,0:T(8,128)}, /*index=5*/f32[1536,128]{1,0:T(8,128)}) custom-call(s32[6]{0:T(128)} %pad_add_fusion.e_ref, bf16[384,1024]{1,0:T(8,128)(2,1)} %get-tuple-element.154.refs_0_.n2_h, ...), custom_call_target="tpu_custom_call" | custom-call | flops 9663676416 | bytes 19423256 | tf_op jit(solution)/shard_map/stage_a/pallas_call | solution.py:46
  167.7 17.9 %stage_b.1 = (bf16[1536,512]{1,0:T(8,128)(2,1)}, bf16[1536,1024]{1,0:T(8,128)(2,1)}, bf16[1536,512]{1,0:T(8,128)(2,1)}, bf16[1536,1024]{1,0:T(8,128)(2,1)}, f32[1536,128]{1,0:T(8,128)}) custom-call(s32[6]{0:T(128)} %pad_add_fusion.e_ref, bf16[384,1024]{1,0:T(8,128)(2,1)} %get-tuple-element.154.refs_0_.n2_h, bf16[384,1024]{1,0:T(8,128)(2,1)} %copy-done.4, ...), custom_call_target="tpu_custom_call" | custom-call | flops 9663676416 | bytes 24379416 | tf_op jit(solution)/shard_map/stage_b/pallas_call | solution.py:46
  193.5 21.3 %stage_c.1 = (bf16[1536,512]{1,0:T(8,128)(2,1)}, bf16[1536,1024]{1,0:T(8,128)(2,1)}, f32[1536,128]{1,0:T(8,128)}, bf16[4,384,1152]{2,1,0:T(8,128)(2,1)}) custom-call(s32[6]{0:T(128)} %pad_add_fusion.e_ref, bf16[384,1024]{1,0:T(8,128)(2,1)} %get-tuple-element.154.refs_0_.n2_h, bf16[384,1024]{1,0:T(8,128)(2,1)} %copy-done.4, bf16[384,1024]{1,0:T(8,128)(2,1)} %copy-done.5, ...), custom_call_target="tpu_custom_call" | custom-call | flops 9663676416 | bytes 38928408 | tf_op jit(solution)/shard_map/stage_c/pallas_call | solution.py:46
  214.8 4.7 %all-to-all-start.1 = ((bf16[4,384,1152]{2,1,0:T(8,128)(2,1)}), bf16[4,384,1152]{2,1,0:T(8,128)(2,1)}, u32[]{:S(2)}, u32[]{:S(2)}) async-start(bf16[4,384,1152]{2,1,0:T(8,128)(2,1)} %get-tuple-element.201), calls=%async_computation.1 | async-start | bytes 7077888 | tf_op jit(solution)/shard_map/all_to_all | solution.py:746
  219.6 15.5 %late_stage.1 = (bf16[1024,768]{1,0:T(8,128)(2,1)}, bf16[1024,768]{1,0:T(8,128)(2,1)}, f32[384,1152]{1,0:T(8,128)}) custom-call(s32[6]{0:T(128)} %pad_add_fusion.e_ref, bf16[384,1024]{1,0:T(8,128)(2,1)} %get-tuple-element.154.refs_0_.n2_h, bf16[384,1024]{1,0:T(8,128)(2,1)} %copy-done.4, bf16[384,1024]{1,0:T(8,128)(2,1)} %copy-done.5, ...), custom_call_target="tpu_custom_call" | custom-call | flops 9663676416 | bytes 41877528 | tf_op jit(solution)/shard_map/late_stage/pallas_call | solution.py:46
  235.2 16.4 %grads_stage.1 = (bf16[1024,768]{1,0:T(8,128)(2,1)}, bf16[1024,768]{1,0:T(8,128)(2,1)}, bf16[1024,768]{1,0:T(8,128)(2,1)}, bf16[1024,768]{1,0:T(8,128)(2,1)}) custom-call(s32[6]{0:T(128)} %pad_add_fusion.e_ref, bf16[384,1024]{1,0:T(8,128)(2,1)} %get-tuple-element.154.refs_0_.n2_h, bf16[384,1024]{1,0:T(8,128)(2,1)} %copy-done.4, bf16[384,1024]{1,0:T(8,128)(2,1)} %copy-done.5, ...), custom_call_target="tpu_custom_call" | custom-call | flops 9663676416 | bytes 22020120 | tf_op jit(solution)/shard_map/grads_stage/pallas_call | solution.py:46
  257.6 12.0 %out_stage.1 = (bf16[4,384,1024]{2,1,0:T(8,128)(2,1)}, f32[384,1024]{1,0:T(8,128)}) custom-call(s32[6]{0:T(128)} %pad_add_fusion.e_ref, bf16[1536,512]{1,0:T(8,128)(2,1)} %get-tuple-element.194.refs_8_.refs_0_, bf16[1536,512]{1,0:T(8,128)(2,1)} %get-tuple-element.195.refs_1_, bf16[1536,512]{1,0:T(8,128)(2,1)} %get-tuple-element.168.refs_6_.refs_2_, ...), custom_call_target="tpu_custom_call" | custom-call | flops 6442450944 | bytes 23592984 | tf_op jit(solution)/shard_map/out_stage/pallas_call | solution.py:46
  269.7 4.9 %all-to-all-start.2 = ((bf16[4,384,1024]{2,1,0:T(8,128)(2,1)}), bf16[4,384,1024]{2,1,0:T(8,128)(2,1)}, u32[]{:S(2)}, u32[]{:S(2)}) async-start(bf16[4,384,1024]{2,1,0:T(8,128)(2,1)} %get-tuple-element.218), calls=%async_computation.2 | async-start | bytes 6291456 | tf_op jit(solution)/shard_map/all_to_all | solution.py:746
  274.6 8.9 %join.1 = (f32[384,1024]{1,0:T(8,128)}, bf16[4,384,256]{2,1,0:T(8,128)(2,1)}, bf16[512,1152]{1,0:T(8,128)(2,1)}, bf16[512,1152]{1,0:T(8,128)(2,1)}) custom-call(s32[6]{0:T(128)} %pad_add_fusion.e_ref, f32[384,1152]{1,0:T(8,128)} %get-tuple-element.206.p_h, bf16[4,384,1152]{2,1,0:T(8,128)(2,1)} %all-to-all-done.1.parts_h, ...), custom_call_target="tpu_custom_call" | custom-call | flops 2000000000 | bytes 17367064 | tf_op jit(solution)/shard_map/join/pallas_call | solution.py:46
  283.6 19.0 %attn_bwd.1 = (f32[384,1024]{1,0:T(8,128)}, bf16[256,2176]{1,0:T(8,128)(2,1)}, bf16[256,2176]{1,0:T(8,128)(2,1)}, bf16[256,2176]{1,0:T(8,128)(2,1)}, bf16[256,2176]{1,0:T(8,128)(2,1)}) custom-call(s32[1]{0:T(128)} %bitcast.mine_ref, bf16[384,1024]{1,0:T(8,128)(2,1)} %x_h.1, bf16[1024,2048]{1,0:T(8,128)(2,1)} %get-tuple-element.198.w_h, ...), custom_call_target="tpu_custom_call" | custom-call | flops 6000000000 | bytes 17235972 | tf_op jit(solution)/shard_map/attn_bwd/pallas_call | solution.py:46
  320.5 24.9 %collective-permute-done.35 = bf16[1024,768]{1,0:T(8,128)(2,1)} collective-permute-done((bf16[1024,768]{1,0:T(8,128)(2,1)}, bf16[1024,768]{1,0:T(8,128)(2,1)}, u32[]{:S(2)}, u32[]{:S(2)}) %collective-permute-start.35) | collective-permute-done | bytes 1572896 | tf_op jit(solution)/shard_map/ppermute | solution.py:724
  349.7 5.1 %collective-permute-done.37.refs_2_ = bf16[128,3200]{1,0:T(8,128)(2,1)} collective-permute-done((bf16[128,3200]{1,0:T(8,128)(2,1)S(1)}, bf16[128,3200]{1,0:T(8,128)(2,1)}, u32[]{:S(2)}, u32[]{:S(2)}) %collective-permute-start.37) | collective-permute-done | bytes 819232 | tf_op jit(solution)/shard_map/ppermute | solution.py:730
  369.7 7.4 %collective-permute-done.41 = bf16[128,896]{1,0:T(8,128)(2,1)S(1)} collective-permute-done((bf16[128,896]{1,0:T(8,128)(2,1)}, bf16[128,896]{1,0:T(8,128)(2,1)S(1)}, u32[]{:S(2)}, u32[]{:S(2)}) %collective-permute-start.41) | collective-permute-done | bytes 229408 | tf_op jit(solution)/shard_map/ppermute | solution.py:754
  382.0 5.0 %all-to-all-done.3.home_h = bf16[8,128,768]{2,1,0:T(8,128)(2,1)S(1)} async-done(((bf16[8,128,768]{2,1,0:T(8,128)(2,1)}), bf16[8,128,768]{2,1,0:T(8,128)(2,1)S(1)}, u32[]{:S(2)}, u32[]{:S(2)}) %all-to-all-start.3) | async-done | bytes 1572896 | tf_op jit(solution)/shard_map/all_to_all | solution.py:749
  388.2 4.5 %settle.1 = (f32[128,4,1024]{2,1,0:T(4,128)}, f32[128,4,512]{2,1,0:T(4,128)}) custom-call(bf16[8,128,768]{2,1,0:T(8,128)(2,1)} %copy-done.3), custom_call_target="tpu_custom_call" | custom-call | bytes 4718592 | tf_op jit(solution)/shard_map/settle/pallas_call | solution.py:46
  (237 shorter events, 103.1 us)
Async XLA Ops:
  11.7 34.2 %collective-permute-start = (bf16[128,768]{1,0:T(8,128)(2,1)S(1)}, bf16[128,768]{1,0:T(8,128)(2,1)S(1)}, u32[]{:S(2)}, u32[]{:S(2)}) collective-permute-start(bf16[128,768]{1,0:T(8,128)(2,1)S(1)} %constant_dynamic-update-slice_fusion), channel_id=1, source_target_pairs={{0,8},{8,24},{24,16},{16,0},{1,9},{9,25},{25,17},{17,1},{2,10},{10... | collective-permute-start | bytes 589832 | tf_op jit(solution)/shard_map/ppermute | solution.py:779
  14.8 31.1 %collective-permute-start.1 = (bf16[128,768]{1,0:T(8,128)(2,1)S(1)}, bf16[128,768]{1,0:T(8,128)(2,1)S(1)}, u32[]{:S(2)}, u32[]{:S(2)}) collective-permute-start(bf16[128,768]{1,0:T(8,128)(2,1)S(1)} %constant_dynamic-update-slice_fusion), channel_id=1, source_target_pairs={{0,24},{8,16},{24,0},{16,8},{1,25},{9,17},{25,1},{17,9},{2,26},{10... | collective-permute-start | bytes 589832 | tf_op jit(solution)/shard_map/ppermute | solution.py:779
  17.3 28.7 %collective-permute-start.2 = (bf16[128,768]{1,0:T(8,128)(2,1)S(1)}, bf16[128,768]{1,0:T(8,128)(2,1)S(1)}, u32[]{:S(2)}, u32[]{:S(2)}) collective-permute-start(bf16[128,768]{1,0:T(8,128)(2,1)S(1)} %constant_dynamic-update-slice_fusion), channel_id=1, source_target_pairs={{0,16},{8,0},{24,8},{16,24},{1,17},{9,1},{25,9},{17,25},{2,18},{10... | collective-permute-start | bytes 589832 | tf_op jit(solution)/shard_map/ppermute | solution.py:779
  18.9 25.4 %all-to-all-start = ((bf16[8,128,768]{1,2,0:T(8,128)(2,1)}), bf16[8,128,768]{1,2,0:T(8,128)(2,1)}, u32[]{:S(2)}, u32[]{:S(2)}) async-start(bf16[8,128,768]{1,2,0:T(8,128)(2,1)} %bitcast.11), calls=%async_computation | async-start | bytes 3145728 | tf_op jit(solution)/shard_map/all_to_all | solution.py:790
  23.2 61.0 %all-gather.3.cloned.1.call-start = ((), (), s32[]{:S(2)}) async-start(), calls=%async_computation.4 | async-start | bytes 2359296 | tf_op jit(solution)/shard_map/all_gather | solution.py:824
  47.0 101.5 %all-gather.5.cloned.1.call-start = ((), (), s32[]{:S(2)}) async-start(), calls=%async_computation.5 | async-start | bytes 3932160 | tf_op jit(solution)/shard_map/all_gather | solution.py:826
  47.0 34.2 %collective-permute-start.8 = (bf16[1024,768]{1,0:T(8,128)(2,1)S(1)}, bf16[1024,768]{1,0:T(8,128)(2,1)}, u32[]{:S(2)}, u32[]{:S(2)}) collective-permute-start(bf16[1024,768]{1,0:T(8,128)(2,1)S(1)} %bitcast.27), channel_id=1, source_target_pairs={{0,8},{8,24},{24,16},{16,0},{1,9},{9,25},{25,17},{17,1},{2,10},{10... | collective-permute-start | bytes 4718600 | tf_op jit(solution)/shard_map/ppermute | solution.py:724
  83.9 37.9 %collective-permute-start.17 = (bf16[1024,768]{1,0:T(8,128)(2,1)}, bf16[1024,768]{1,0:T(8,128)(2,1)}, u32[]{:S(2)}, u32[]{:S(2)}) collective-permute-start(bf16[1024,768]{1,0:T(8,128)(2,1)} %collective-permute-done.8.refs_6_.refs_8_.refs_14_), channel_id=1, source_target_pairs={{0,8},{8,24},{24,16},{16,0},{1,9},{9,25},{25,17},{17,1},{2,10},{10... | collective-permute-start | bytes 4718600 | tf_op jit(solution)/shard_map/ppermute | solution.py:724
  95.9 51.5 %collective-permute-start.14 = (bf16[1024,768]{1,0:T(8,128)(2,1)}, bf16[1024,768]{1,0:T(8,128)(2,1)}, u32[]{:S(2)}, u32[]{:S(2)}) collective-permute-start(bf16[1024,768]{1,0:T(8,128)(2,1)} %collective-permute-done.8.refs_6_.refs_8_.refs_14_), channel_id=1, source_target_pairs={{0,1},{1,0},{2,3},{3,2},{4,5},{5,4},{6,7},{7,6},{8,9},{9,8},{10,11... | collective-permute-start | bytes 4718600 | tf_op jit(solution)/shard_map/ppermute | solution.py:736
  96.1 32.7 %collective-permute-start.15 = (bf16[384,1024]{1,0:T(8,128)(2,1)}, bf16[384,1024]{1,0:T(8,128)(2,1)S(1)}, u32[]{:S(2)}, u32[]{:S(2)}) collective-permute-start(bf16[384,1024]{1,0:T(8,128)(2,1)} %get-tuple-element.154.refs_0_.n2_h), channel_id=1, source_target_pairs={{0,2},{1,3},{2,0},{3,1},{4,6},{5,7},{6,4},{7,5},{8,10},{9,11},{10,... | collective-permute-start | bytes 2359304 | tf_op jit(solution)/shard_map/ppermute | solution.py:727
  100.3 31.0 %collective-permute-start.16 = (bf16[384,1024]{1,0:T(8,128)(2,1)}, bf16[384,1024]{1,0:T(8,128)(2,1)S(1)}, u32[]{:S(2)}, u32[]{:S(2)}) collective-permute-start(bf16[384,1024]{1,0:T(8,128)(2,1)} %get-tuple-element.154.refs_0_.n2_h), channel_id=1, source_target_pairs={{0,4},{1,5},{2,6},{3,7},{4,0},{5,1},{6,2},{7,3},{8,12},{9,13},{10,... | collective-permute-start | bytes 2359304 | tf_op jit(solution)/shard_map/ppermute | solution.py:730
  145.5 40.1 %collective-permute-start.24 = (bf16[1024,768]{1,0:T(8,128)(2,1)}, bf16[1024,768]{1,0:T(8,128)(2,1)}, u32[]{:S(2)}, u32[]{:S(2)}) collective-permute-start(bf16[1024,768]{1,0:T(8,128)(2,1)} %collective-permute-done.17.refs_8_.refs_10_.refs_16_), channel_id=1, source_target_pairs={{0,8},{8,24},{24,16},{16,0},{1,9},{9,25},{25,17},{17,1},{2,10},{10... | collective-permute-start | bytes 4718600 | tf_op jit(solution)/shard_map/ppermute | solution.py:724
  147.4 20.3 %collective-permute-start.20 = (bf16[1024,768]{1,0:T(8,128)(2,1)}, bf16[1024,768]{1,0:T(8,128)(2,1)}, u32[]{:S(2)}, u32[]{:S(2)}) collective-permute-start(bf16[1024,768]{1,0:T(8,128)(2,1)} %collective-permute-done.17.refs_8_.refs_10_.refs_16_), channel_id=1, source_target_pairs={{0,1},{1,0},{2,3},{3,2},{4,5},{5,4},{6,7},{7,6},{8,9},{9,8},{10,11... | collective-permute-start | bytes 4718600 | tf_op jit(solution)/shard_map/ppermute | solution.py:736
  190.8 44.4 %collective-permute-start.28 = (bf16[1024,768]{1,0:T(8,128)(2,1)}, bf16[1024,768]{1,0:T(8,128)(2,1)}, u32[]{:S(2)}, u32[]{:S(2)}) collective-permute-start(bf16[1024,768]{1,0:T(8,128)(2,1)} %add_convert_fusion.3), channel_id=1, source_target_pairs={{0,8},{8,24},{24,16},{16,0},{1,9},{9,25},{25,17},{17,1},{2,10},{10... | collective-permute-start | bytes 4718600 | tf_op jit(solution)/shard_map/ppermute | solution.py:724
  214.8 54.9 %all-to-all-start.1 = ((bf16[4,384,1152]{2,1,0:T(8,128)(2,1)}), bf16[4,384,1152]{2,1,0:T(8,128)(2,1)}, u32[]{:S(2)}, u32[]{:S(2)}) async-start(bf16[4,384,1152]{2,1,0:T(8,128)(2,1)} %get-tuple-element.201), calls=%async_computation.1 | async-start | bytes 7077888 | tf_op jit(solution)/shard_map/all_to_all | solution.py:746
  256.3 46.3 %collective-permute-start.29 = (bf16[1024,768]{1,0:T(8,128)(2,1)}, bf16[1024,768]{1,0:T(8,128)(2,1)}, u32[]{:S(2)}, u32[]{:S(2)}) collective-permute-start(bf16[1024,768]{1,0:T(8,128)(2,1)} %add_convert_fusion.2), channel_id=1, source_target_pairs={{0,8},{8,24},{24,16},{16,0},{1,9},{9,25},{25,17},{17,1},{2,10},{10... | collective-permute-start | bytes 4718600 | tf_op jit(solution)/shard_map/ppermute | solution.py:724
  269.7 41.5 %all-to-all-start.2 = ((bf16[4,384,1024]{2,1,0:T(8,128)(2,1)}), bf16[4,384,1024]{2,1,0:T(8,128)(2,1)}, u32[]{:S(2)}, u32[]{:S(2)}) async-start(bf16[4,384,1024]{2,1,0:T(8,128)(2,1)} %get-tuple-element.218), calls=%async_computation.2 | async-start | bytes 6291456 | tf_op jit(solution)/shard_map/all_to_all | solution.py:746
  283.5 26.3 %collective-permute-start.34 = (bf16[512,1152]{1,0:T(8,128)(2,1)}, bf16[512,1152]{1,0:T(8,128)(2,1)}, u32[]{:S(2)}, u32[]{:S(2)}) collective-permute-start(bf16[512,1152]{1,0:T(8,128)(2,1)} %get-tuple-element.217), channel_id=1, source_target_pairs={{0,1},{1,0},{2,3},{3,2},{4,5},{5,4},{6,7},{7,6},{8,9},{9,8},{10,11... | collective-permute-start | bytes 3538952 | tf_op jit(solution)/shard_map/ppermute | solution.py:736
  307.5 38.0 %collective-permute-start.35 = (bf16[1024,768]{1,0:T(8,128)(2,1)}, bf16[1024,768]{1,0:T(8,128)(2,1)}, u32[]{:S(2)}, u32[]{:S(2)}) collective-permute-start(bf16[1024,768]{1,0:T(8,128)(2,1)} %add_convert_fusion.1), channel_id=1, source_target_pairs={{0,8},{8,24},{24,16},{16,0},{1,9},{9,25},{25,17},{17,1},{2,10},{10... | collective-permute-start | bytes 4718600 | tf_op jit(solution)/shard_map/ppermute | solution.py:724
  314.5 35.2 %collective-permute-start.36 = (bf16[128,3200]{1,0:T(8,128)(2,1)S(1)}, bf16[128,3200]{1,0:T(8,128)(2,1)}, u32[]{:S(2)}, u32[]{:S(2)}) collective-permute-start(bf16[128,3200]{1,0:T(8,128)(2,1)S(1)} %pad_maximum_fusion.1), channel_id=1, source_target_pairs={{0,2},{1,3},{2,0},{3,1},{4,6},{5,7},{6,4},{7,5},{8,10},{9,11},{10,... | collective-permute-start | bytes 2457608 | tf_op jit(solution)/shard_map/ppermute | solution.py:727
  317.7 37.0 %collective-permute-start.37 = (bf16[128,3200]{1,0:T(8,128)(2,1)S(1)}, bf16[128,3200]{1,0:T(8,128)(2,1)}, u32[]{:S(2)}, u32[]{:S(2)}) collective-permute-start(bf16[128,3200]{1,0:T(8,128)(2,1)S(1)} %pad_maximum_fusion.2), channel_id=1, source_target_pairs={{0,4},{1,5},{2,6},{3,7},{4,0},{5,1},{6,2},{7,3},{8,12},{9,13},{10,... | collective-permute-start | bytes 2457608 | tf_op jit(solution)/shard_map/ppermute | solution.py:730
  319.0 35.7 %collective-permute-start.38 = (bf16[128,3200]{1,0:T(8,128)(2,1)S(1)}, bf16[128,3200]{1,0:T(8,128)(2,1)}, u32[]{:S(2)}, u32[]{:S(2)}) collective-permute-start(bf16[128,3200]{1,0:T(8,128)(2,1)S(1)} %pad_maximum_fusion.3), channel_id=1, source_target_pairs={{0,6},{1,7},{2,4},{3,5},{4,2},{5,3},{6,0},{7,1},{8,14},{9,15},{10,... | collective-permute-start | bytes 2457608 | tf_op jit(solution)/shard_map/ppermute | solution.py:733
  357.8 19.2 %collective-permute-start.41 = (bf16[128,896]{1,0:T(8,128)(2,1)}, bf16[128,896]{1,0:T(8,128)(2,1)S(1)}, u32[]{:S(2)}, u32[]{:S(2)}) collective-permute-start(bf16[128,896]{1,0:T(8,128)(2,1)} %get-tuple-element.239), channel_id=1, source_target_pairs={{0,8},{8,24},{24,16},{16,0},{1,9},{9,25},{25,17},{17,1},{2,10},{10... | collective-permute-start | bytes 688136 | tf_op jit(solution)/shard_map/ppermute | solution.py:754
  362.3 24.7 %all-to-all-start.3 = ((bf16[8,128,768]{2,1,0:T(8,128)(2,1)}), bf16[8,128,768]{2,1,0:T(8,128)(2,1)S(1)}, u32[]{:S(2)}, u32[]{:S(2)}) async-start(bf16[8,128,768]{2,1,0:T(8,128)(2,1)} %bitcast.33), calls=%async_computation.3 | async-start | bytes 3145728 | tf_op jit(solution)/shard_map/all_to_all | solution.py:749
  (62 other events, 628.6 us)
Sparse Core Ops, SparseCore 0:
  47.1 30.3 all-gather.2
  79.3 61.6 all-gather.4

commit v7 on v6

--- a/solution.py
+++ b/solution.py
@@ -204,8 +204,7 @@
     ]
 
 
-def act(t, e, X, Y, W, GT, GH, DGU):
-    rows = TREE[t]
+def act(rows, e, X, Y, W, GT, GH, DGU):
     lanes = lax.broadcasted_iota(jnp.int32, (T, LANES), 1)
     gate = jnp.sum(jnp.where(lanes == e, GT[rows, :], 0.0), axis=1, keepdims=True)
     dgate = jnp.zeros((T, 1), F32)
@@ -281,7 +280,7 @@
     for t in range(4):
         wait(trees[t])
         GT[TREE[t], :] = soft_gates(X[TREE[t], :], router, route_mask(routes[t][...].astype(F32)))
-        DG[TREE[t], :] = act(t, e_ref[1], X, Y, W.at[0], GT, GH.at[0], DGU.at[0])
+        DG[TREE[t], :] = act(TREE[t], e_ref[1], X, Y, W.at[0], GT, GH.at[0], DGU.at[0])
     outs = fetch([(GH.at[0], gh_h), (DGU.at[0], dgu_h), (GT, gates_h), (DG, dgate_h)], so)
     wgrad(X, Y, GH.at[0], DGU.at[0], DW)
     outs += fetch([(DW.at[0], dwo_h), (DW.at[1], dws_h)], so, 4)
@@ -314,11 +313,11 @@
     )
     for t in range(4):
         wait(trees[t])
-        DG[TREE[t], :] += act(t, e_ref[0], X, Y, W.at[0], GT, GH.at[0], DGU.at[0])
+        DG[TREE[t], :] += act(TREE[t], e_ref[0], X, Y, W.at[0], GT, GH.at[0], DGU.at[0])
     outs = fetch([(GH.at[0], gh0_h), (DGU.at[0], dgu0_h)], so)
     wait(second)
     for t in range(4):
-        DG[TREE[t], :] += act(t, e_ref[2], X, Y, W.at[1], GT, GH.at[1], DGU.at[1])
+        DG[TREE[t], :] += act(TREE[t], e_ref[2], X, Y, W.at[1], GT, GH.at[1], DGU.at[1])
     outs += fetch([(GH.at[1], gh2_h), (DGU.at[1], dgu2_h), (DG, dgate_h)], so, 2)
     wait(outs)
 
@@ -342,9 +341,16 @@
         xs, dyg, e_ref[4], X, Y,
         [(ws[6 + i], W.at[0, i]) for i in range(2)] + [(gates_h, GT), (dgate_i, DG)], late, si,
     )
-    for t in range(4):
-        wait(trees[t])
-        DG[TREE[t], :] += act(t, e_ref[3], X, Y, W.at[0], GT, GH.at[0], DGU.at[0])
+    def tree(t, carry):
+        for k in range(1, 4):
+            @pl.when(t == k)
+            def _():
+                wait(trees[k])
+        rows = pl.ds(pl.multiple_of(t * T, T), T)
+        DG[rows, :] += act(rows, e_ref[3], X, Y, W.at[0], GT, GH.at[0], DGU.at[0])
+        return carry
+
+    lax.fori_loop(0, 4, tree, 0)
     outs = fetch([(GH.at[0], gh_h), (DGU.at[0], dgu_h), (DG, dgate_h)], so)
     wait(late)
     w = jnp.concatenate([WB[...]] + [W[0, i, :, 0:WIDE] for i in range(2)], axis=1)

time: 405 us -> 405 us (level)
  no operation moved by 1% of the time
where the time goes in v7:
time: 405 us; the launch traced here: 400 us
  Pallas kernels  148 us (37%)
  waiting for transfers between devices  129 us (32%)
  starting transfers between devices  56.6 us (14%)
  other arithmetic  32.3 us (8%)
  local copies, waits for them, and re-layouts  18.1 us (4%)
  between operations  15.5 us (4%)
    pallas_call x11, Pallas kernels, call(): pl.pallas_call(body, out_shape=[jax.ShapeDtypeStruct(s, d) for s, d in ou...  148 us
    ppermute x6, waiting for transfers between devices, z_next(): return lax.ppermute(a, 'grp', shifted(1))  47.6 us
    ppermute x6, waiting for transfers between devices, to_x(): return lax.ppermute(a, 'fsdp', flip(2))  38.8 us
    all_to_all x1, waiting for transfers between devices, shards(): unit = lax.all_to_all(parts, 'fsdp', 0, 0, axis_index_groups=low_groups)  15 us
    convert_element_type x4, other arithmetic, chip_sum(): return total.astype(BF)  14.9 us
    ppermute x6, waiting for transfers between devices, to_y(): return lax.ppermute(a, 'fsdp', flip(4))  11.3 us
    unnamed x85, local copies, waits for them, and re-layouts  10.7 us
    all_to_all x2, starting transfers between devices, swap(): return lax.all_to_all(a, 'fsdp', 0, 0, axis_index_groups=core_groups)  10 us
  transfers between devices with their start and end apart: 48, of which 19 were waited for; matrix products, arithmetic and copies ran while one was open for 10% of the time, Pallas kernels for 35%

profile of v7, /device:TPU:0, one launch (start us, length us, event | category | flops | bytes accessed | tf_op | source)
XLA Modules:
  0.0 399.9 jit_solution(13919590063334311559)
XLA Ops:
  18.9 4.3 %all-to-all-start = ((bf16[8,128,768]{1,2,0:T(8,128)(2,1)}), bf16[8,128,768]{1,2,0:T(8,128)(2,1)}, u32[]{:S(2)}, u32[]{:S(2)}) async-start(bf16[8,128,768]{1,2,0:T(8,128)(2,1)} %bitcast.11), calls=%async_computation | async-start | bytes 3145728 | tf_op jit(solution)/shard_map/all_to_all | solution.py:796
  29.2 15.0 %all-to-all-done = bf16[8,128,768]{1,2,0:T(8,128)(2,1)} async-done(((bf16[8,128,768]{1,2,0:T(8,128)(2,1)}), bf16[8,128,768]{1,2,0:T(8,128)(2,1)}, u32[]{:S(2)}, u32[]{:S(2)}) %all-to-all-start) | async-done | bytes 1572896 | tf_op jit(solution)/shard_map/all_to_all | solution.py:796
  52.0 15.6 %collective-permute-done.3.refs_1_ = bf16[128,2176]{1,0:T(8,128)(2,1)S(1)} collective-permute-done((bf16[128,2176]{1,0:T(8,128)(2,1)}, bf16[128,2176]{1,0:T(8,128)(2,1)S(1)}, u32[]{:S(2)}, u32[]{:S(2)}) %collective-permute-start.3) | collective-permute-done | bytes 557088 | tf_op jit(solution)/shard_map/ppermute | solution.py:733
  71.1 7.8 %collective-permute-done.6.refs_3_ = bf16[64,2176]{1,0:T(8,128)(2,1)S(1)} collective-permute-done((bf16[64,2176]{1,0:T(8,128)(2,1)S(1)}, bf16[64,2176]{1,0:T(8,128)(2,1)S(1)}, u32[]{:S(2)}, u32[]{:S(2)}) %collective-permute-start.6) | collective-permute-done | bytes 278560 | tf_op jit(solution)/shard_map/ppermute | solution.py:733
  84.2 11.7 %attn_fwd.1 = (bf16[1024,2048]{1,0:T(8,128)(2,1)}, bf16[384,1024]{1,0:T(8,128)(2,1)}, bf16[4,384,512]{2,1,0:T(8,128)(2,1)}, bf16[4,384,256]{2,1,0:T(8,128)(2,1)}...) custom-call(s32[1]{0:T(128)} %bitcast.mine_ref, ...), custom_call_target="tpu_custom_call" | custom-call | flops 4000000000 | bytes 18546692 | tf_op jit(solution)/shard_map/attn_fwd/pallas_call | solution.py:46
  96.1 4.2 %collective-permute-start.15 = (bf16[384,1024]{1,0:T(8,128)(2,1)}, bf16[384,1024]{1,0:T(8,128)(2,1)S(1)}, u32[]{:S(2)}, u32[]{:S(2)}) collective-permute-start(bf16[384,1024]{1,0:T(8,128)(2,1)} %get-tuple-element.154.refs_0_.n2_h), channel_id=1, source_target_pairs={{0,2},{1,3},{2,0},{3,1},{4,6},{5,7},{6,4},{7,5},{8,10},{9,11},{10,... | collective-permute-start | bytes 2359304 | tf_op jit(solution)/shard_map/ppermute | solution.py:733
  100.3 21.5 %collective-permute-done.17.refs_8_.refs_10_.refs_16_ = bf16[1024,768]{1,0:T(8,128)(2,1)} collective-permute-done((bf16[1024,768]{1,0:T(8,128)(2,1)}, bf16[1024,768]{1,0:T(8,128)(2,1)}, u32[]{:S(2)}, u32[]{:S(2)}) %collective-permute-start.17) | collective-permute-done | bytes 1572896 | tf_op jit(solution)/shard_map/ppermute | solution.py:730
  121.8 7.0 %collective-permute-done.15.refs_1_ = bf16[384,1024]{1,0:T(8,128)(2,1)S(1)} collective-permute-done((bf16[384,1024]{1,0:T(8,128)(2,1)}, bf16[384,1024]{1,0:T(8,128)(2,1)S(1)}, u32[]{:S(2)}, u32[]{:S(2)}) %collective-permute-start.15) | collective-permute-done | bytes 786464 | tf_op jit(solution)/shard_map/ppermute | solution.py:733
  135.7 8.3 %collective-permute-done.18.refs_3_ = bf16[192,1024]{1,0:T(8,128)(2,1)S(1)} collective-permute-done((bf16[192,1024]{1,0:T(8,128)(2,1)S(1)}, bf16[192,1024]{1,0:T(8,128)(2,1)S(1)}, u32[]{:S(2)}, u32[]{:S(2)}) %collective-permute-start.18) | collective-permute-done | bytes 393248 | tf_op jit(solution)/shard_map/ppermute | solution.py:733
  149.1 18.4 %stage_a.1 = (bf16[1536,512]{1,0:T(8,128)(2,1)}, bf16[1536,1024]{1,0:T(8,128)(2,1)}, bf16[1024,768]{1,0:T(8,128)(2,1)}, bf16[1024,768]{1,0:T(8,128)(2,1)}, f32[1536,128]{1,0:T(8,128)}, /*index=5*/f32[1536,128]{1,0:T(8,128)}) custom-call(s32[6]{0:T(128)} %pad_add_fusion.e_ref, bf16[384,1024]{1,0:T(8,128)(2,1)} %get-tuple-element.154.refs_0_.n2_h, ...), custom_call_target="tpu_custom_call" | custom-call | flops 9663676416 | bytes 19423256 | tf_op jit(solution)/shard_map/stage_a/pallas_call | solution.py:46
  167.7 17.9 %stage_b.1 = (bf16[1536,512]{1,0:T(8,128)(2,1)}, bf16[1536,1024]{1,0:T(8,128)(2,1)}, bf16[1536,512]{1,0:T(8,128)(2,1)}, bf16[1536,1024]{1,0:T(8,128)(2,1)}, f32[1536,128]{1,0:T(8,128)}) custom-call(s32[6]{0:T(128)} %pad_add_fusion.e_ref, bf16[384,1024]{1,0:T(8,128)(2,1)} %get-tuple-element.154.refs_0_.n2_h, bf16[384,1024]{1,0:T(8,128)(2,1)} %copy-done.4, ...), custom_call_target="tpu_custom_call" | custom-call | flops 9663676416 | bytes 24379416 | tf_op jit(solution)/shard_map/stage_b/pallas_call | solution.py:46
  193.5 20.9 %stage_c.1 = (bf16[1536,512]{1,0:T(8,128)(2,1)}, bf16[1536,1024]{1,0:T(8,128)(2,1)}, f32[1536,128]{1,0:T(8,128)}, bf16[4,384,1152]{2,1,0:T(8,128)(2,1)}) custom-call(s32[6]{0:T(128)} %pad_add_fusion.e_ref, bf16[384,1024]{1,0:T(8,128)(2,1)} %get-tuple-element.154.refs_0_.n2_h, bf16[384,1024]{1,0:T(8,128)(2,1)} %copy-done.4, bf16[384,1024]{1,0:T(8,128)(2,1)} %copy-done.5, ...), custom_call_target="tpu_custom_call" | custom-call | flops 9663676416 | bytes 38928408 | tf_op jit(solution)/shard_map/stage_c/pallas_call | solution.py:46
  214.4 5.2 %all-to-all-start.1 = ((bf16[4,384,1152]{2,1,0:T(8,128)(2,1)}), bf16[4,384,1152]{2,1,0:T(8,128)(2,1)}, u32[]{:S(2)}, u32[]{:S(2)}) async-start(bf16[4,384,1152]{2,1,0:T(8,128)(2,1)} %get-tuple-element.201), calls=%async_computation.1 | async-start | bytes 7077888 | tf_op jit(solution)/shard_map/all_to_all | solution.py:752
  219.6 15.5 %late_stage.1 = (bf16[1024,768]{1,0:T(8,128)(2,1)}, bf16[1024,768]{1,0:T(8,128)(2,1)}, f32[384,1152]{1,0:T(8,128)}) custom-call(s32[6]{0:T(128)} %pad_add_fusion.e_ref, bf16[384,1024]{1,0:T(8,128)(2,1)} %get-tuple-element.154.refs_0_.n2_h, bf16[384,1024]{1,0:T(8,128)(2,1)} %copy-done.4, bf16[384,1024]{1,0:T(8,128)(2,1)} %copy-done.5, ...), custom_call_target="tpu_custom_call" | custom-call | flops 9663676416 | bytes 41877528 | tf_op jit(solution)/shard_map/late_stage/pallas_call | solution.py:46
  235.2 16.4 %grads_stage.1 = (bf16[1024,768]{1,0:T(8,128)(2,1)}, bf16[1024,768]{1,0:T(8,128)(2,1)}, bf16[1024,768]{1,0:T(8,128)(2,1)}, bf16[1024,768]{1,0:T(8,128)(2,1)}) custom-call(s32[6]{0:T(128)} %pad_add_fusion.e_ref, bf16[384,1024]{1,0:T(8,128)(2,1)} %get-tuple-element.154.refs_0_.n2_h, bf16[384,1024]{1,0:T(8,128)(2,1)} %copy-done.4, bf16[384,1024]{1,0:T(8,128)(2,1)} %copy-done.5, ...), custom_call_target="tpu_custom_call" | custom-call | flops 9663676416 | bytes 22020120 | tf_op jit(solution)/shard_map/grads_stage/pallas_call | solution.py:46
  257.6 12.0 %out_stage.1 = (bf16[4,384,1024]{2,1,0:T(8,128)(2,1)}, f32[384,1024]{1,0:T(8,128)}) custom-call(s32[6]{0:T(128)} %pad_add_fusion.e_ref, bf16[1536,512]{1,0:T(8,128)(2,1)} %get-tuple-element.194.refs_8_.refs_0_, bf16[1536,512]{1,0:T(8,128)(2,1)} %get-tuple-element.195.refs_1_, bf16[1536,512]{1,0:T(8,128)(2,1)} %get-tuple-element.168.refs_6_.refs_2_, ...), custom_call_target="tpu_custom_call" | custom-call | flops 6442450944 | bytes 23592984 | tf_op jit(solution)/shard_map/out_stage/pallas_call | solution.py:46
  269.7 4.9 %all-to-all-start.2 = ((bf16[4,384,1024]{2,1,0:T(8,128)(2,1)}), bf16[4,384,1024]{2,1,0:T(8,128)(2,1)}, u32[]{:S(2)}, u32[]{:S(2)}) async-start(bf16[4,384,1024]{2,1,0:T(8,128)(2,1)} %get-tuple-element.218), calls=%async_computation.2 | async-start | bytes 6291456 | tf_op jit(solution)/shard_map/all_to_all | solution.py:752
  274.6 8.9 %join.1 = (f32[384,1024]{1,0:T(8,128)}, bf16[4,384,256]{2,1,0:T(8,128)(2,1)}, bf16[512,1152]{1,0:T(8,128)(2,1)}, bf16[512,1152]{1,0:T(8,128)(2,1)}) custom-call(s32[6]{0:T(128)} %pad_add_fusion.e_ref, f32[384,1152]{1,0:T(8,128)} %get-tuple-element.206.p_h, bf16[4,384,1152]{2,1,0:T(8,128)(2,1)} %all-to-all-done.1.parts_h, ...), custom_call_target="tpu_custom_call" | custom-call | flops 2000000000 | bytes 17367064 | tf_op jit(solution)/shard_map/join/pallas_call | solution.py:46
  283.6 19.0 %attn_bwd.1 = (f32[384,1024]{1,0:T(8,128)}, bf16[256,2176]{1,0:T(8,128)(2,1)}, bf16[256,2176]{1,0:T(8,128)(2,1)}, bf16[256,2176]{1,0:T(8,128)(2,1)}, bf16[256,2176]{1,0:T(8,128)(2,1)}) custom-call(s32[1]{0:T(128)} %bitcast.mine_ref, bf16[384,1024]{1,0:T(8,128)(2,1)} %x_h.1, bf16[1024,2048]{1,0:T(8,128)(2,1)} %get-tuple-element.198.w_h, ...), custom_call_target="tpu_custom_call" | custom-call | flops 6000000000 | bytes 17235972 | tf_op jit(solution)/shard_map/attn_bwd/pallas_call | solution.py:46
  320.5 24.9 %collective-permute-done.35 = bf16[1024,768]{1,0:T(8,128)(2,1)} collective-permute-done((bf16[1024,768]{1,0:T(8,128)(2,1)}, bf16[1024,768]{1,0:T(8,128)(2,1)}, u32[]{:S(2)}, u32[]{:S(2)}) %collective-permute-start.35) | collective-permute-done | bytes 1572896 | tf_op jit(solution)/shard_map/ppermute | solution.py:730
  349.7 5.1 %collective-permute-done.37.refs_2_ = bf16[128,3200]{1,0:T(8,128)(2,1)} collective-permute-done((bf16[128,3200]{1,0:T(8,128)(2,1)S(1)}, bf16[128,3200]{1,0:T(8,128)(2,1)}, u32[]{:S(2)}, u32[]{:S(2)}) %collective-permute-start.37) | collective-permute-done | bytes 819232 | tf_op jit(solution)/shard_map/ppermute | solution.py:736
  369.7 7.4 %collective-permute-done.41 = bf16[128,896]{1,0:T(8,128)(2,1)S(1)} collective-permute-done((bf16[128,896]{1,0:T(8,128)(2,1)}, bf16[128,896]{1,0:T(8,128)(2,1)S(1)}, u32[]{:S(2)}, u32[]{:S(2)}) %collective-permute-start.41) | collective-permute-done | bytes 229408 | tf_op jit(solution)/shard_map/ppermute | solution.py:760
  382.0 5.0 %all-to-all-done.3.home_h = bf16[8,128,768]{2,1,0:T(8,128)(2,1)S(1)} async-done(((bf16[8,128,768]{2,1,0:T(8,128)(2,1)}), bf16[8,128,768]{2,1,0:T(8,128)(2,1)S(1)}, u32[]{:S(2)}, u32[]{:S(2)}) %all-to-all-start.3) | async-done | bytes 1572896 | tf_op jit(solution)/shard_map/all_to_all | solution.py:755
  388.2 4.5 %settle.1 = (f32[128,4,1024]{2,1,0:T(4,128)}, f32[128,4,512]{2,1,0:T(4,128)}) custom-call(bf16[8,128,768]{2,1,0:T(8,128)(2,1)} %copy-done.3), custom_call_target="tpu_custom_call" | custom-call | bytes 4718592 | tf_op jit(solution)/shard_map/settle/pallas_call | solution.py:46
  (237 shorter events, 103.1 us)
Async XLA Ops:
  11.7 34.2 %collective-permute-start = (bf16[128,768]{1,0:T(8,128)(2,1)S(1)}, bf16[128,768]{1,0:T(8,128)(2,1)S(1)}, u32[]{:S(2)}, u32[]{:S(2)}) collective-permute-start(bf16[128,768]{1,0:T(8,128)(2,1)S(1)} %constant_dynamic-update-slice_fusion), channel_id=1, source_target_pairs={{0,8},{8,24},{24,16},{16,0},{1,9},{9,25},{25,17},{17,1},{2,10},{10... | collective-permute-start | bytes 589832 | tf_op jit(solution)/shard_map/ppermute | solution.py:785
  14.8 31.1 %collective-permute-start.1 = (bf16[128,768]{1,0:T(8,128)(2,1)S(1)}, bf16[128,768]{1,0:T(8,128)(2,1)S(1)}, u32[]{:S(2)}, u32[]{:S(2)}) collective-permute-start(bf16[128,768]{1,0:T(8,128)(2,1)S(1)} %constant_dynamic-update-slice_fusion), channel_id=1, source_target_pairs={{0,24},{8,16},{24,0},{16,8},{1,25},{9,17},{25,1},{17,9},{2,26},{10... | collective-permute-start | bytes 589832 | tf_op jit(solution)/shard_map/ppermute | solution.py:785
  17.3 28.7 %collective-permute-start.2 = (bf16[128,768]{1,0:T(8,128)(2,1)S(1)}, bf16[128,768]{1,0:T(8,128)(2,1)S(1)}, u32[]{:S(2)}, u32[]{:S(2)}) collective-permute-start(bf16[128,768]{1,0:T(8,128)(2,1)S(1)} %constant_dynamic-update-slice_fusion), channel_id=1, source_target_pairs={{0,16},{8,0},{24,8},{16,24},{1,17},{9,1},{25,9},{17,25},{2,18},{10... | collective-permute-start | bytes 589832 | tf_op jit(solution)/shard_map/ppermute | solution.py:785
  18.9 25.4 %all-to-all-start = ((bf16[8,128,768]{1,2,0:T(8,128)(2,1)}), bf16[8,128,768]{1,2,0:T(8,128)(2,1)}, u32[]{:S(2)}, u32[]{:S(2)}) async-start(bf16[8,128,768]{1,2,0:T(8,128)(2,1)} %bitcast.11), calls=%async_computation | async-start | bytes 3145728 | tf_op jit(solution)/shard_map/all_to_all | solution.py:796
  23.2 61.0 %all-gather.3.cloned.1.call-start = ((), (), s32[]{:S(2)}) async-start(), calls=%async_computation.4 | async-start | bytes 2359296 | tf_op jit(solution)/shard_map/all_gather | solution.py:830
  47.0 101.5 %all-gather.5.cloned.1.call-start = ((), (), s32[]{:S(2)}) async-start(), calls=%async_computation.5 | async-start | bytes 3932160 | tf_op jit(solution)/shard_map/all_gather | solution.py:832
  47.0 34.2 %collective-permute-start.8 = (bf16[1024,768]{1,0:T(8,128)(2,1)S(1)}, bf16[1024,768]{1,0:T(8,128)(2,1)}, u32[]{:S(2)}, u32[]{:S(2)}) collective-permute-start(bf16[1024,768]{1,0:T(8,128)(2,1)S(1)} %bitcast.27), channel_id=1, source_target_pairs={{0,8},{8,24},{24,16},{16,0},{1,9},{9,25},{25,17},{17,1},{2,10},{10... | collective-permute-start | bytes 4718600 | tf_op jit(solution)/shard_map/ppermute | solution.py:730
  83.9 37.9 %collective-permute-start.17 = (bf16[1024,768]{1,0:T(8,128)(2,1)}, bf16[1024,768]{1,0:T(8,128)(2,1)}, u32[]{:S(2)}, u32[]{:S(2)}) collective-permute-start(bf16[1024,768]{1,0:T(8,128)(2,1)} %collective-permute-done.8.refs_6_.refs_8_.refs_14_), channel_id=1, source_target_pairs={{0,8},{8,24},{24,16},{16,0},{1,9},{9,25},{25,17},{17,1},{2,10},{10... | collective-permute-start | bytes 4718600 | tf_op jit(solution)/shard_map/ppermute | solution.py:730
  95.9 51.5 %collective-permute-start.14 = (bf16[1024,768]{1,0:T(8,128)(2,1)}, bf16[1024,768]{1,0:T(8,128)(2,1)}, u32[]{:S(2)}, u32[]{:S(2)}) collective-permute-start(bf16[1024,768]{1,0:T(8,128)(2,1)} %collective-permute-done.8.refs_6_.refs_8_.refs_14_), channel_id=1, source_target_pairs={{0,1},{1,0},{2,3},{3,2},{4,5},{5,4},{6,7},{7,6},{8,9},{9,8},{10,11... | collective-permute-start | bytes 4718600 | tf_op jit(solution)/shard_map/ppermute | solution.py:742
  96.1 32.7 %collective-permute-start.15 = (bf16[384,1024]{1,0:T(8,128)(2,1)}, bf16[384,1024]{1,0:T(8,128)(2,1)S(1)}, u32[]{:S(2)}, u32[]{:S(2)}) collective-permute-start(bf16[384,1024]{1,0:T(8,128)(2,1)} %get-tuple-element.154.refs_0_.n2_h), channel_id=1, source_target_pairs={{0,2},{1,3},{2,0},{3,1},{4,6},{5,7},{6,4},{7,5},{8,10},{9,11},{10,... | collective-permute-start | bytes 2359304 | tf_op jit(solution)/shard_map/ppermute | solution.py:733
  100.3 31.0 %collective-permute-start.16 = (bf16[384,1024]{1,0:T(8,128)(2,1)}, bf16[384,1024]{1,0:T(8,128)(2,1)S(1)}, u32[]{:S(2)}, u32[]{:S(2)}) collective-permute-start(bf16[384,1024]{1,0:T(8,128)(2,1)} %get-tuple-element.154.refs_0_.n2_h), channel_id=1, source_target_pairs={{0,4},{1,5},{2,6},{3,7},{4,0},{5,1},{6,2},{7,3},{8,12},{9,13},{10,... | collective-permute-start | bytes 2359304 | tf_op jit(solution)/shard_map/ppermute | solution.py:736
  145.5 40.1 %collective-permute-start.24 = (bf16[1024,768]{1,0:T(8,128)(2,1)}, bf16[1024,768]{1,0:T(8,128)(2,1)}, u32[]{:S(2)}, u32[]{:S(2)}) collective-permute-start(bf16[1024,768]{1,0:T(8,128)(2,1)} %collective-permute-done.17.refs_8_.refs_10_.refs_16_), channel_id=1, source_target_pairs={{0,8},{8,24},{24,16},{16,0},{1,9},{9,25},{25,17},{17,1},{2,10},{10... | collective-permute-start | bytes 4718600 | tf_op jit(solution)/shard_map/ppermute | solution.py:730
  147.4 20.3 %collective-permute-start.20 = (bf16[1024,768]{1,0:T(8,128)(2,1)}, bf16[1024,768]{1,0:T(8,128)(2,1)}, u32[]{:S(2)}, u32[]{:S(2)}) collective-permute-start(bf16[1024,768]{1,0:T(8,128)(2,1)} %collective-permute-done.17.refs_8_.refs_10_.refs_16_), channel_id=1, source_target_pairs={{0,1},{1,0},{2,3},{3,2},{4,5},{5,4},{6,7},{7,6},{8,9},{9,8},{10,11... | collective-permute-start | bytes 4718600 | tf_op jit(solution)/shard_map/ppermute | solution.py:742
  190.8 44.4 %collective-permute-start.28 = (bf16[1024,768]{1,0:T(8,128)(2,1)}, bf16[1024,768]{1,0:T(8,128)(2,1)}, u32[]{:S(2)}, u32[]{:S(2)}) collective-permute-start(bf16[1024,768]{1,0:T(8,128)(2,1)} %add_convert_fusion.3), channel_id=1, source_target_pairs={{0,8},{8,24},{24,16},{16,0},{1,9},{9,25},{25,17},{17,1},{2,10},{10... | collective-permute-start | bytes 4718600 | tf_op jit(solution)/shard_map/ppermute | solution.py:730
  214.4 55.3 %all-to-all-start.1 = ((bf16[4,384,1152]{2,1,0:T(8,128)(2,1)}), bf16[4,384,1152]{2,1,0:T(8,128)(2,1)}, u32[]{:S(2)}, u32[]{:S(2)}) async-start(bf16[4,384,1152]{2,1,0:T(8,128)(2,1)} %get-tuple-element.201), calls=%async_computation.1 | async-start | bytes 7077888 | tf_op jit(solution)/shard_map/all_to_all | solution.py:752
  256.3 46.3 %collective-permute-start.29 = (bf16[1024,768]{1,0:T(8,128)(2,1)}, bf16[1024,768]{1,0:T(8,128)(2,1)}, u32[]{:S(2)}, u32[]{:S(2)}) collective-permute-start(bf16[1024,768]{1,0:T(8,128)(2,1)} %add_convert_fusion.2), channel_id=1, source_target_pairs={{0,8},{8,24},{24,16},{16,0},{1,9},{9,25},{25,17},{17,1},{2,10},{10... | collective-permute-start | bytes 4718600 | tf_op jit(solution)/shard_map/ppermute | solution.py:730
  269.7 41.6 %all-to-all-start.2 = ((bf16[4,384,1024]{2,1,0:T(8,128)(2,1)}), bf16[4,384,1024]{2,1,0:T(8,128)(2,1)}, u32[]{:S(2)}, u32[]{:S(2)}) async-start(bf16[4,384,1024]{2,1,0:T(8,128)(2,1)} %get-tuple-element.218), calls=%async_computation.2 | async-start | bytes 6291456 | tf_op jit(solution)/shard_map/all_to_all | solution.py:752
  283.5 26.3 %collective-permute-start.34 = (bf16[512,1152]{1,0:T(8,128)(2,1)}, bf16[512,1152]{1,0:T(8,128)(2,1)}, u32[]{:S(2)}, u32[]{:S(2)}) collective-permute-start(bf16[512,1152]{1,0:T(8,128)(2,1)} %get-tuple-element.217), channel_id=1, source_target_pairs={{0,1},{1,0},{2,3},{3,2},{4,5},{5,4},{6,7},{7,6},{8,9},{9,8},{10,11... | collective-permute-start | bytes 3538952 | tf_op jit(solution)/shard_map/ppermute | solution.py:742
  307.5 38.0 %collective-permute-start.35 = (bf16[1024,768]{1,0:T(8,128)(2,1)}, bf16[1024,768]{1,0:T(8,128)(2,1)}, u32[]{:S(2)}, u32[]{:S(2)}) collective-permute-start(bf16[1024,768]{1,0:T(8,128)(2,1)} %add_convert_fusion.1), channel_id=1, source_target_pairs={{0,8},{8,24},{24,16},{16,0},{1,9},{9,25},{25,17},{17,1},{2,10},{10... | collective-permute-start | bytes 4718600 | tf_op jit(solution)/shard_map/ppermute | solution.py:730
  314.5 35.1 %collective-permute-start.36 = (bf16[128,3200]{1,0:T(8,128)(2,1)S(1)}, bf16[128,3200]{1,0:T(8,128)(2,1)}, u32[]{:S(2)}, u32[]{:S(2)}) collective-permute-start(bf16[128,3200]{1,0:T(8,128)(2,1)S(1)} %pad_maximum_fusion.1), channel_id=1, source_target_pairs={{0,2},{1,3},{2,0},{3,1},{4,6},{5,7},{6,4},{7,5},{8,10},{9,11},{10,... | collective-permute-start | bytes 2457608 | tf_op jit(solution)/shard_map/ppermute | solution.py:733
  317.7 37.0 %collective-permute-start.37 = (bf16[128,3200]{1,0:T(8,128)(2,1)S(1)}, bf16[128,3200]{1,0:T(8,128)(2,1)}, u32[]{:S(2)}, u32[]{:S(2)}) collective-permute-start(bf16[128,3200]{1,0:T(8,128)(2,1)S(1)} %pad_maximum_fusion.2), channel_id=1, source_target_pairs={{0,4},{1,5},{2,6},{3,7},{4,0},{5,1},{6,2},{7,3},{8,12},{9,13},{10,... | collective-permute-start | bytes 2457608 | tf_op jit(solution)/shard_map/ppermute | solution.py:736
  319.0 35.7 %collective-permute-start.38 = (bf16[128,3200]{1,0:T(8,128)(2,1)S(1)}, bf16[128,3200]{1,0:T(8,128)(2,1)}, u32[]{:S(2)}, u32[]{:S(2)}) collective-permute-start(bf16[128,3200]{1,0:T(8,128)(2,1)S(1)} %pad_maximum_fusion.3), channel_id=1, source_target_pairs={{0,6},{1,7},{2,4},{3,5},{4,2},{5,3},{6,0},{7,1},{8,14},{9,15},{10,... | collective-permute-start | bytes 2457608 | tf_op jit(solution)/shard_map/ppermute | solution.py:739
  357.8 19.2 %collective-permute-start.41 = (bf16[128,896]{1,0:T(8,128)(2,1)}, bf16[128,896]{1,0:T(8,128)(2,1)S(1)}, u32[]{:S(2)}, u32[]{:S(2)}) collective-permute-start(bf16[128,896]{1,0:T(8,128)(2,1)} %get-tuple-element.239), channel_id=1, source_target_pairs={{0,8},{8,24},{24,16},{16,0},{1,9},{9,25},{25,17},{17,1},{2,10},{10... | collective-permute-start | bytes 688136 | tf_op jit(solution)/shard_map/ppermute | solution.py:760
  362.3 24.7 %all-to-all-start.3 = ((bf16[8,128,768]{2,1,0:T(8,128)(2,1)}), bf16[8,128,768]{2,1,0:T(8,128)(2,1)S(1)}, u32[]{:S(2)}, u32[]{:S(2)}) async-start(bf16[8,128,768]{2,1,0:T(8,128)(2,1)} %bitcast.33), calls=%async_computation.3 | async-start | bytes 3145728 | tf_op jit(solution)/shard_map/all_to_all | solution.py:755
  (62 other events, 628.6 us)
Sparse Core Ops, SparseCore 0:
  47.1 30.3 all-gather.2
  79.3 61.6 all-gather.4
